TPU v7x, 256 devices: a whole 4x4x8 slice. The times are simulated.
256 devices in a mesh: vel: 16 (over y_hi, x, core), gx: 16 (over z, y_lo).
Axes of the slice: x: 4, y: 4 (y_hi: 2, y_lo: 2; y = y_hi * 2 + y_lo), z: 8, core: 2. Of those that a mesh axis runs over, the one named last changes fastest.
Arguments:
- distribution: float32 [4096, 32768], P('vel', 'gx'), as said below
- wall_mask: int32 [64, 512], replicated, may hold values 0 or 1
- boundary_kind: int32 [2, 512], replicated, may hold values from 0 to 1
- inflow: float32 [4096], P('vel'), may hold values from 0.5 to 3
Outputs:
- evolved: float32 [4096, 32768], P('vel', 'gx')
Inputs may be any that keep to these rules, and one draw needn't show every extreme that they name: `distribution`: every entry is positive. `wall_mask`: 1 marks a solid cell. `boundary_kind`: 0 is an outflow face, 1 an inflow face.
All inputs are finite; a program needn't handle non-finite values.
Results may differ from a plain program's by a relative error of at most 0.0003.
Values sent between devices are 32-bit elements; how exact they have to be, the bound alone decides.
No kernel may reach another device: no remote copies, remote signals or barrier semaphores. Data moves between devices by JAX's collectives and lax.ppermute only.
A program may use at most 64 MiB of HBM per device.

v0:
```python
import jax
import jax.numpy as jnp
from jax import lax
from jax.sharding import PartitionSpec as P

VS = 16
NY = 16
NZ = 32
STEPS = 3


vel_limit = 4.5
time_step = 0.075
relax_rate = 0.6
viscous_thermal_ratio = 0.6666667


def passed_along(array, axis, by):
    peers = lax.axis_size(axis)
    pairs = [(i, i + by) for i in range(peers) if 0 <= i + by < peers]
    return lax.ppermute(array, axis, pairs)


def velocity_rows(lattice_lines):
    square = VS * VS
    half = square // 2
    across = lattice_lines // square
    rest = lattice_lines % square
    upper = rest // half
    inner = rest % half
    along = jnp.where(upper == 1, VS // 2 + inner // VS, VS // 2 - 1 - inner // VS)
    depth = inner % VS
    spacing = 2.0 * vel_limit / VS

    def coord(index):
        return -vel_limit + (index.astype(jnp.float32) + 0.5) * spacing

    return (coord(along), coord(across), coord(depth))


def poly_basis(speed_x, speed_y, speed_z):
    energy = speed_x * speed_x + speed_y * speed_y + speed_z * speed_z
    return jnp.stack(
        [
            jnp.ones_like(speed_x),
            speed_x,
            speed_y,
            speed_z,
            speed_x * speed_x,
            speed_y * speed_y,
            speed_z * speed_z,
            speed_x * speed_y,
            speed_x * speed_z,
            speed_y * speed_z,
            energy * speed_x,
            energy * speed_y,
            energy * speed_z,
        ],
        axis=1,
    )


def exp_basis(speed_x, speed_y, speed_z):
    energy = speed_x * speed_x + speed_y * speed_y + speed_z * speed_z
    return jnp.stack([jnp.ones_like(speed_x), speed_x, speed_y, speed_z, energy], axis=1)


def shakhov_coefficients(moments):
    particle_concentration = moments[0]
    mean_drift_first = moments[1] / particle_concentration
    mean_drift_second = moments[2] / particle_concentration
    mean_drift_third_dir = moments[3] / particle_concentration
    second = moments[4:10]
    motion_work_content = (
        mean_drift_first * mean_drift_first
        + mean_drift_second * mean_drift_second
        + mean_drift_third_dir * mean_drift_third_dir
    )
    pressure_diagonal_sum = second[0] + second[1] + second[2]
    thermal_level = (pressure_diagonal_sum / particle_concentration - motion_work_content) / 3.0
    press_x = (
        second[0] * mean_drift_first
        + second[3] * mean_drift_second
        + second[4] * mean_drift_third_dir
    )
    press_y = (
        second[3] * mean_drift_first
        + second[1] * mean_drift_second
        + second[5] * mean_drift_third_dir
    )
    press_z = (
        second[4] * mean_drift_first
        + second[5] * mean_drift_second
        + second[2] * mean_drift_third_dir
    )
    heat_x = 0.5 * (
        moments[10]
        - 2.0 * press_x
        - mean_drift_first * pressure_diagonal_sum
        + 2.0 * particle_concentration * motion_work_content * mean_drift_first
    )
    heat_y = 0.5 * (
        moments[11]
        - 2.0 * press_y
        - mean_drift_second * pressure_diagonal_sum
        + 2.0 * particle_concentration * motion_work_content * mean_drift_second
    )
    heat_z = 0.5 * (
        moments[12]
        - 2.0 * press_z
        - mean_drift_third_dir * pressure_diagonal_sum
        + 2.0 * particle_concentration * motion_work_content * mean_drift_third_dir
    )
    heat_diffusivity_coef = (1.0 - viscous_thermal_ratio) / (
        5.0 * particle_concentration * thermal_level * thermal_level
    )
    quadrature_scale = heat_diffusivity_coef / thermal_level
    mixed = mean_drift_first * heat_x + mean_drift_second * heat_y + mean_drift_third_dir * heat_z
    foremost_dimension = (
        jnp.log(particle_concentration)
        - 1.5 * jnp.log(2.0 * jnp.pi * thermal_level)
        - motion_work_content / (2.0 * thermal_level)
    )
    lattice_lines = [
        foremost_dimension,
        mean_drift_first / thermal_level,
        mean_drift_second / thermal_level,
        mean_drift_third_dir / thermal_level,
        -0.5 / thermal_level,
        1.0 - quadrature_scale * mixed * motion_work_content + 5.0 * heat_diffusivity_coef * mixed,
        quadrature_scale * (heat_x * motion_work_content + 2.0 * mixed * mean_drift_first)
        - 5.0 * heat_diffusivity_coef * heat_x,
        quadrature_scale * (heat_y * motion_work_content + 2.0 * mixed * mean_drift_second)
        - 5.0 * heat_diffusivity_coef * heat_y,
        quadrature_scale * (heat_z * motion_work_content + 2.0 * mixed * mean_drift_third_dir)
        - 5.0 * heat_diffusivity_coef * heat_z,
        -2.0 * quadrature_scale * heat_x * mean_drift_first - quadrature_scale * mixed,
        -2.0 * quadrature_scale * heat_y * mean_drift_second - quadrature_scale * mixed,
        -2.0 * quadrature_scale * heat_z * mean_drift_third_dir - quadrature_scale * mixed,
        -2.0 * quadrature_scale * (heat_x * mean_drift_second + heat_y * mean_drift_first),
        -2.0 * quadrature_scale * (heat_x * mean_drift_third_dir + heat_z * mean_drift_first),
        -2.0 * quadrature_scale * (heat_y * mean_drift_third_dir + heat_z * mean_drift_second),
        quadrature_scale * heat_x,
        quadrature_scale * heat_y,
        quadrature_scale * heat_z,
    ]
    return jnp.stack(lattice_lines, axis=0)


def relax(moved, coefficients, expo_rows, poly_rows):
    power = jnp.dot(expo_rows, coefficients[0:5], precision=lax.Precision.HIGHEST)
    shape = jnp.dot(poly_rows, coefficients[5:18], precision=lax.Precision.HIGHEST)
    return moved + relax_rate * (jnp.exp(power) * shape - moved)


def per_device(distribution, wall_mask, boundary_kind, inflow):
    rows_dev = distribution.shape[0]
    cells_dev = distribution.shape[1]
    section = wall_mask.shape[1]
    depth = cells_dev // section
    half = VS * VS // 2
    blocks = rows_dev // (2 * half)
    position = lax.axis_index("gx")
    at_low = position == 0
    at_high = position == lax.axis_size("gx") - 1
    lattice_lines = lax.axis_index("vel") * rows_dev + jnp.arange(rows_dev, dtype=jnp.int32)
    speed_x, speed_y, speed_z = velocity_rows(lattice_lines)
    poly = poly_basis(speed_x, speed_y, speed_z)
    expo = exp_basis(speed_x, speed_y, speed_z)
    weight = (2.0 * vel_limit / VS) ** 3
    openness = (1 - wall_mask).astype(jnp.float32)
    open_pad = jnp.pad(openness, ((1, 1), (0, 0)), constant_values=1.0)
    local_open = lax.dynamic_slice_in_dim(open_pad, position * depth, depth + 2, 0)
    inner_open = local_open[1:-1]
    low_in = boundary_kind[0] == 1
    high_in = boundary_kind[1] == 1
    entering = inflow.reshape(blocks, 2, half)
    lanes = jnp.arange(section, dtype=jnp.int32)
    open_y = (
        inner_open * jnp.roll(inner_open, -NZ, axis=1) * (lanes // NZ < NY - 1).astype(jnp.float32)
    )
    open_z = (
        inner_open * jnp.roll(inner_open, -1, axis=1) * (lanes % NZ < NZ - 1).astype(jnp.float32)
    )
    open_x = local_open[:-1] * local_open[1:]

    def send_rims(state3):
        view = state3.reshape(blocks, 2, half, depth, section)
        from_left = passed_along(view[:, 1, :, depth - 1], "gx", 1)
        from_right = passed_along(view[:, 0, :, 0], "gx", -1)
        return (from_left, from_right)

    state = distribution.reshape(rows_dev, depth, section)
    from_left, from_right = send_rims(state)
    for step in range(STEPS):
        last = step + 1 == STEPS
        transport_view = state.reshape(blocks, 2, half, depth, section)
        low_value = jnp.where(
            low_in[None, None, :], entering[:, 1, :, None], transport_view[:, 1, :, 0]
        )
        ghost_upper = jnp.where(at_low, low_value, from_left)
        high_value = jnp.where(
            high_in[None, None, :], entering[:, 0, :, None], transport_view[:, 0, :, depth - 1]
        )
        ghost_lower = jnp.where(at_high, high_value, from_right)
        zeros = jnp.zeros_like(ghost_upper)
        left = jnp.stack([zeros, ghost_upper], axis=1).reshape(rows_dev, 1, section)
        right = jnp.stack([ghost_lower, zeros], axis=1).reshape(rows_dev, 1, section)
        extended = jnp.concatenate([left, state, right], axis=1)
        speed = speed_x[:, None, None]
        upwind = jnp.where(speed > 0, extended[:, :-1], extended[:, 1:])
        flux = speed * upwind * open_x
        change = flux[:, 1:] - flux[:, :-1]
        speed = speed_y[:, None, None]
        flux = speed * jnp.where(speed > 0, state, jnp.roll(state, -NZ, axis=2)) * open_y
        change = change + (flux - jnp.roll(flux, NZ, axis=2))
        speed = speed_z[:, None, None]
        flux = speed * jnp.where(speed > 0, state, jnp.roll(state, -1, axis=2)) * open_z
        change = change + (flux - jnp.roll(flux, 1, axis=2))
        moved = state - time_step * change
        moved2 = moved.reshape(rows_dev, cells_dev)
        partial_value = weight * jnp.dot(poly.T, moved2, precision=lax.Precision.HIGHEST)
        coefficients = shakhov_coefficients(lax.psum(partial_value, "vel"))
        state = relax(moved2, coefficients, expo, poly).reshape(rows_dev, depth, section)
        if not last:
            from_left, from_right = send_rims(state)
    return state.reshape(rows_dev, cells_dev)


def solution(mesh):
    placed = (P("vel", "gx"), P(), P(), P("vel"))
    return jax.shard_map(
        per_device, mesh=mesh, in_specs=placed, out_specs=P("vel", "gx"), check_vma=False
    )
```

profile of v0, /device:TPU:1, one launch (start us, length us, event | category | flops | bytes accessed | tf_op | source)
XLA Modules:
  0.0 605.4 jit_solution(14425497762548733683)
XLA Ops:
  6.5 3.8 reshape_reshape.15
  10.3 1.5 slice_bitcast_fusion.8
  11.8 1.3 collective-permute-start.1
  13.1 5.4 collective-permute-start
  25.7 2.7 reshape.864
  28.5 2.5 slice.461
  31.0 2.5 slice.457
  33.6 1.3 compare_reduce_fusion
  35.9 7.9 %fusion.30 = (f32[256,4,512]{2,1,0:T(4,128)}, f32[256,4,512]{2,1,0:T(4,128)}) fusion(f32[256,4,512]{2,1,0:T(4,128)S(1)} %reshape.864, f32[256,4,1]{2,1,0:T(4,128)S(1)} %slice.462, f32[256,4,511]{2,1,0:T(4,128)} %slice.461, f32[4,512]{1,0:T(4,128)S(1)} %get-tuple-element.97, f32[256]{0:T(256)} %get-tuple-element.134, pred[256]{0:T(512)(128)(4,1)} %get-tuple-element.136, ...), kind=kLoop, calls=%fused_computation.48 | loop fusion | flops 4194304 | bytes 10504704 | tf_op jit(solution)/shard_map/mul | solution.py:218
  44.0 1.4 slice.463
  45.4 1.4 slice.459
  47.0 1.7 fusion.42
  49.4 2.7 fusion.1
  52.1 3.2 fusion.26
  56.2 1.8 convolution_multiply_fusion.5
  58.3 147.4 %all-reduce.11.cloned.1.call-done = f32[13,2048]{1,0:T(8,128)} async-done(((f32[13,2048]{1,0:T(8,128)}), f32[13,2048]{1,0:T(8,128)}) %all-reduce.11.cloned.1.call-update) | async-done | bytes 106512 | tf_op jit(solution)/shard_map/psum | solution.py:223
  205.7 1.5 fusion.119
  207.1 1.3 fusion.123
  209.8 3.2 convolution_exponential_fusion.2
  213.2 5.0 fusion.10
  218.1 2.7 reshape.869
  220.8 3.6 reshape_reshape.13
  227.9 1.3 collective-permute-start.3
  229.2 4.4 collective-permute-start.2
  233.6 4.9 fusion.34
  239.3 3.3 collective-permute-done.2
  244.0 2.7 fusion.3
  246.7 3.2 fusion.22
  250.8 1.8 convolution_multiply_fusion.4
  252.8 142.7 %all-reduce.13.cloned.1.call-done = f32[13,2048]{1,0:T(8,128)} async-done(((f32[13,2048]{1,0:T(8,128)}), f32[13,2048]{1,0:T(8,128)}) %all-reduce.13.cloned.1.call-update) | async-done | bytes 106512 | tf_op jit(solution)/shard_map/psum | solution.py:223
  395.5 1.5 fusion.113
  397.0 1.3 fusion.117
  399.5 3.2 convolution_exponential_fusion.1
  403.0 5.0 fusion.12
  408.0 2.7 reshape.873
  410.7 4.7 reshape_reshape.16
  418.7 1.3 collective-permute-start.5
  420.0 4.2 collective-permute-start.4
  424.2 4.9 fusion.38
  429.8 3.6 collective-permute-done.4
  434.7 2.7 fusion.5
  437.4 3.2 fusion.18
  441.5 1.8 convolution_multiply_fusion.3
  443.2 142.9 %all-reduce.15.cloned.1.call-done = f32[13,2048]{1,0:T(8,128)} async-done(((f32[13,2048]{1,0:T(8,128)}), f32[13,2048]{1,0:T(8,128)}) %all-reduce.15.cloned.1.call-update) | async-done | bytes 106512 | tf_op jit(solution)/shard_map/psum | solution.py:223
  586.2 1.5 fusion.107
  587.7 1.3 fusion.111
  590.2 3.2 convolution_exponential_fusion
  593.7 5.0 fusion.14
  (153 shorter events, 27.3 us)
Async XLA Ops:
  6.5 17.9 %copy-start.9 = (s32[64,512]{1,0:T(8,128)S(1)}, s32[64,512]{1,0:T(8,128)}, u32[]{:S(2)}) copy-start(s32[64,512]{1,0:T(8,128)} %param.5) | copy-start | bytes 393220
  6.5 199.1 %all-reduce.11.cloned.1.call-start = ((), (), s32[]{:S(2)}) async-start(), calls=%async_computation | async-start | bytes 262144 | tf_op jit(solution)/shard_map/psum | solution.py:223
  10.3 15.3 %copy-start.2 = (f32[1,2,128,4,512]{4,0,3,2,1:T(1,128)}, f32[1,2,128,4,512]{4,0,3,2,1:T(1,128)S(1)}, u32[]{:S(2)}) copy-start(f32[1,2,128,4,512]{4,0,3,2,1:T(1,128)S(1)} %reshape_reshape.15) | copy-start | bytes 6291460
  11.8 35.2 %collective-permute-start.1 = (f32[1,128,512]{2,0,1:T(1,128)}, f32[1,128,512]{2,0,1:T(1,128)S(1)}, u32[]{:S(2)}, u32[]{:S(2)}) collective-permute-start(f32[1,128,512]{2,0,1:T(1,128)} %get-tuple-element.77), channel_id=1, source_target_pairs={{1,0},{2,1},{3,2},{4,3},{5,4},{6,5},{7,6},{8,7},{9,8},{10,9},{11,1... | collective-permute-start | bytes 786440 | tf_op jit(solution)/shard_map/ppermute | solution.py:21
  13.1 33.9 %collective-permute-start = (f32[1,128,512]{2,0,1:T(1,128)}, f32[1,128,512]{2,0,1:T(1,128)}, u32[]{:S(2)}, u32[]{:S(2)}) collective-permute-start(f32[1,128,512]{2,0,1:T(1,128)} %get-tuple-element.78), channel_id=1, source_target_pairs={{0,1},{1,2},{2,3},{3,4},{4,5},{5,6},{6,7},{7,8},{8,9},{9,10},{10,1... | collective-permute-start | bytes 786440 | tf_op jit(solution)/shard_map/ppermute | solution.py:21
  35.8 7.9 %copy-start.5 = (f32[4,512]{1,0:T(4,128)}, f32[4,512]{1,0:T(4,128)S(1)}, u32[]{:S(2)}) copy-start(f32[4,512]{1,0:T(4,128)S(1)} %get-tuple-element.97) | copy-start | bytes 24580
  35.9 7.9 %copy-start.7 = (f32[4,512]{1,0:T(4,128)}, f32[4,512]{1,0:T(4,128)S(1)}, u32[]{:S(2)}) copy-start(f32[4,512]{1,0:T(4,128)S(1)} %get-tuple-element.98) | copy-start | bytes 24580
  43.8 3.0 copy-start.14
  43.8 3.0 copy-start.15
  43.8 3.0 copy-start.16
  43.8 3.0 copy-start.29
  43.8 3.0 copy-start.30
  43.8 3.0 copy-start.31
  43.9 3.0 copy-start.32
  43.9 3.0 copy-start.33
  43.9 3.0 copy-start.34
  43.9 3.0 copy-start.35
  43.9 3.0 copy-start.36
  43.9 3.0 copy-start.37
  43.9 3.0 copy-start.38
  43.9 3.1 copy-start.17
  43.9 3.1 copy-start.19
  44.0 5.4 copy-start.27
  45.4 4.0 copy-start.12
  47.0 5.1 copy-start.21
  47.0 5.1 copy-start.23
  49.3 2.7 copy-start
  49.4 2.7 copy-start.1
  57.9 337.6 %all-reduce.13.cloned.1.call-start = ((), (), s32[]{:S(2)}) async-start(), calls=%async_computation.1 | async-start | bytes 262144 | tf_op jit(solution)/shard_map/psum | solution.py:223
  225.8 1.6 copy-start.4
  225.8 7.8 %copy-start.6 = (f32[4,512]{1,0:T(4,128)S(1)}, f32[4,512]{1,0:T(4,128)}, u32[]{:S(2)}) copy-start(f32[4,512]{1,0:T(4,128)} %copy-done.5) | copy-start | bytes 24580
  225.8 7.8 %copy-start.8 = (f32[4,512]{1,0:T(4,128)S(1)}, f32[4,512]{1,0:T(4,128)}, u32[]{:S(2)}) copy-start(f32[4,512]{1,0:T(4,128)} %copy-done.7) | copy-start | bytes 24580
  225.8 7.8 %copy-start.10 = (f32[256]{0:T(256)S(1)}, f32[256]{0:T(256)}, u32[]{:S(2)}) copy-start(f32[256]{0:T(256)} %get-tuple-element.134) | copy-start | bytes 3076
  225.8 7.8 %copy-start.11 = (f32[256]{0:T(256)S(1)}, f32[256]{0:T(256)}, u32[]{:S(2)}) copy-start(f32[256]{0:T(256)} %get-tuple-element.135) | copy-start | bytes 3076
  225.8 7.8 %copy-start.25 = (pred[256]{0:T(512)(128)(4,1)S(1)}, pred[256]{0:T(512)(128)(4,1)}, u32[]{:S(2)}) copy-start(pred[256]{0:T(512)(128)(4,1)} %get-tuple-element.136) | copy-start | bytes 772
  225.9 7.8 %copy-start.26 = (pred[256]{0:T(512)(128)(4,1)S(1)}, pred[256]{0:T(512)(128)(4,1)}, u32[]{:S(2)}) copy-start(pred[256]{0:T(512)(128)(4,1)} %get-tuple-element.137) | copy-start | bytes 772
  227.9 11.4 %collective-permute-start.3 = (f32[1,128,512]{2,0,1:T(1,128)S(1)}, f32[1,128,512]{2,0,1:T(1,128)S(1)}, u32[]{:S(2)}, u32[]{:S(2)}) collective-permute-start(f32[1,128,512]{2,0,1:T(1,128)S(1)} %get-tuple-element.71), channel_id=1, source_target_pairs={{1,0},{2,1},{3,2},{4,3},{5,4},{6,5},{7,6},{8,7},{9,8},{10,9},{11,1... | collective-permute-start | bytes 786440 | tf_op jit(solution)/shard_map/ppermute | solution.py:21
  229.2 13.4 %collective-permute-start.2 = (f32[1,128,512]{2,0,1:T(1,128)S(1)}, f32[1,128,512]{2,0,1:T(1,128)S(1)}, u32[]{:S(2)}, u32[]{:S(2)}) collective-permute-start(f32[1,128,512]{2,0,1:T(1,128)S(1)} %get-tuple-element.72), channel_id=1, source_target_pairs={{0,1},{1,2},{2,3},{3,4},{4,5},{5,6},{6,7},{7,8},{8,9},{9,10},{10,1... | collective-permute-start | bytes 786440 | tf_op jit(solution)/shard_map/ppermute | solution.py:21
  238.6 4.0 copy-start.18
  238.6 4.0 copy-start.20
  238.6 4.0 copy-start.22
  238.6 4.0 copy-start.24
  238.9 5.1 copy-start.13
  238.9 5.1 copy-start.28
  252.5 333.6 %all-reduce.15.cloned.1.call-start = ((), (), s32[]{:S(2)}) async-start(), calls=%async_computation.2 | async-start | bytes 262144 | tf_op jit(solution)/shard_map/psum | solution.py:223
  416.7 1.6 copy-start.3
  418.7 11.1 %collective-permute-start.5 = (f32[1,128,512]{2,0,1:T(1,128)S(1)}, f32[1,128,512]{2,0,1:T(1,128)S(1)}, u32[]{:S(2)}, u32[]{:S(2)}) collective-permute-start(f32[1,128,512]{2,0,1:T(1,128)S(1)} %get-tuple-element.65), channel_id=1, source_target_pairs={{1,0},{2,1},{3,2},{4,3},{5,4},{6,5},{7,6},{8,7},{9,8},{10,9},{11,1... | collective-permute-start | bytes 786440 | tf_op jit(solution)/shard_map/ppermute | solution.py:21
  420.0 13.4 %collective-permute-start.4 = (f32[1,128,512]{2,0,1:T(1,128)S(1)}, f32[1,128,512]{2,0,1:T(1,128)S(1)}, u32[]{:S(2)}, u32[]{:S(2)}) collective-permute-start(f32[1,128,512]{2,0,1:T(1,128)S(1)} %get-tuple-element.66), channel_id=1, source_target_pairs={{0,1},{1,2},{2,3},{3,4},{4,5},{5,6},{6,7},{7,8},{8,9},{9,10},{10,1... | collective-permute-start | bytes 786440 | tf_op jit(solution)/shard_map/ppermute | solution.py:21
Sparse Core Ops, SparseCore 0:
  58.1 147.5 all-reduce.10
  252.7 142.7 all-reduce.12
  443.4 142.7 all-reduce.14
where the time goes:
time: 616 us; the launch traced here: 605 us
  waiting for transfers between devices  440 us (71%)
  other arithmetic  58.5 us (9%)
  local copies, waits for them, and re-layouts  44.4 us (7%)
  matrix products  29.9 us (5%)
  starting transfers between devices  18.3 us (3%)
  between operations  14.3 us (2%)
    psum x3, waiting for transfers between devices, per_device(): coefficients = shakhov_coefficients(lax.psum(partial_value, 'vel'))  433 us
    ppermute x6, starting transfers between devices, passed_along(): return lax.ppermute(array, axis, pairs)  17.8 us
    mul x3, other arithmetic, per_device(): speed * jnp.where(speed > 0, state, jnp.roll(state, -1, axis=2)) * open_z  17.8 us
    dot_general x3, matrix products, relax(): jnp.dot(poly_rows, coefficients[5:18], precision=lax.Precision.HIGHEST)  14.9 us
  transfers between devices with their start and end apart: 9, of which 5 were waited for; matrix products, arithmetic and copies ran while one was open for 7% of the time, Pallas kernels for 0%

commit v1 on v0

v1 whole, which is shorter than its diff:
```python
import functools
import math

import jax
import jax.numpy as jnp
from jax import lax
from jax.experimental import pallas as pl
from jax.experimental.pallas import tpu as pltpu
from jax.sharding import PartitionSpec as P

VS = 16
NY = 16
NZ = 32
STEPS = 3
SEC = NY * NZ
DEPTH = 4
TILES = SEC // 128

LIMIT = 4.5
DT = 0.075
RATE = 0.6
KEEP = 1.0 - RATE
RATIO = 0.6666667
H = 2.0 * LIMIT / VS
WEIGHT = H**3
HALF = VS * VS // 2
ROWS = VS * VS
OWN = DEPTH * TILES


def vy_of(index):
    return -LIMIT + (index.astype(jnp.float32) + 0.5) * H


def sub_iota():
    return lax.broadcasted_iota(jnp.int32, (8, 128), 0).astype(jnp.float32)


def vz_tile(b):
    q = sub_iota()
    return (q + 0.5) * H if b else (q - 7.5) * H


def row(ref, *index):
    return jnp.broadcast_to(ref[index], (8, 128))


def prepare_masks(wall_ref, faces, position, count, forward):
    opened = []
    for slot in range(DEPTH + 2):
        at = position * DEPTH + slot - 1
        inside = jnp.logical_and(at >= 0, at < count * DEPTH)
        line = wall_ref[pl.ds(jnp.clip(at, 0, count * DEPTH - 1), 1), :]
        opened.append(jnp.where(inside, (1 - line).astype(jnp.float32), 1.0))
    zero = jnp.zeros_like(opened[0])
    o = jnp.concatenate(opened + [zero, zero], axis=0)
    cell = lax.broadcasted_iota(jnp.int32, (8, SEC), 1)
    up_x = o * pltpu.roll(o, 7, 0)
    up_y = o * pltpu.roll(o, SEC - NZ, 1) * (cell < SEC - NZ).astype(jnp.float32)
    up_z = o * pltpu.roll(o, SEC - 1, 1) * ((cell & (NZ - 1)) < NZ - 1).astype(jnp.float32)
    down_y = pltpu.roll(up_y, NZ, 1)
    down_z = pltpu.roll(up_z, 1, 1)
    planes = [
        up_x, jnp.where(forward, up_y, down_y), jnp.where(forward, down_y, up_y), down_z, up_z
    ]
    for k, plane in enumerate(planes):
        for slot in range(DEPTH + 1):
            for t in range(TILES):
                line = plane[slot : slot + 1, t * 128 : (t + 1) * 128]
                faces[k, slot, t] = jnp.broadcast_to(line, (8, 128))


def fill_ends(state, inflow_ref, kind_ref, position, count):
    lane = lax.broadcasted_iota(jnp.int32, (8, 128), 1)
    sub = lax.broadcasted_iota(jnp.int32, (8, 128), 0)

    def one(side, base, inner, outer):
        @pl.when(position == (0 if side == 0 else count - 1))
        def _():
            for tile in range(HALF // 8):
                start = base + tile * 8
                line = row(inflow_ref, pl.ds(start // 128, 1), slice(None))
                picked = jnp.where(lane == sub + start % 128, line, 0.0)
                column = jnp.sum(picked, axis=1, keepdims=True)
                for t in range(TILES):
                    kind = row(kind_ref, pl.ds(side, 1), pl.ds(t * 128, 128))
                    inside = state[pl.ds(start, 8), pl.ds(inner * SEC + t * 128, 128)]
                    state[pl.ds(start, 8), pl.ds(outer * SEC + t * 128, 128)] = jnp.where(
                        kind == 1, jnp.broadcast_to(column, (8, 128)), inside
                    )

    one(0, HALF, 1, 0)
    one(1, 0, DEPTH, DEPTH + 1)


def transport(state, faces, moved, sums, iy):
    forward = iy >= VS // 2
    speed_y = jnp.abs(vy_of(iy)) * (KEEP * DT)
    lane = lax.broadcasted_iota(jnp.int32, (8, 128), 1)
    take = jnp.logical_or(
        jnp.logical_and(forward, lane < NZ), jnp.logical_and(~forward, lane >= 128 - NZ)
    )
    shift_y = jnp.where(forward, NZ, 128 - NZ)

    def section(i, carry):
        total = [[None] * 8 for _ in range(TILES)]
        tiles = [jnp.where(forward, k, TILES - 1 - k) for k in range(TILES)]
        lanes = [pl.multiple_of(t * 128, 128) for t in tiles]
        for b in range(2):
            vz = vz_tile(b)
            az = jnp.abs(vz) * (KEEP * DT)
            below = [faces[0, i, t] for t in tiles]
            above = [faces[0, i + 1, t] for t in tiles]
            keep, in_y, in_z = [], [], []
            for t in tiles:
                out_y = faces[1, i + 1, t]
                out_z = faces[4 if b else 3, i + 1, t]
                keep.append(KEEP - speed_y * out_y - az * out_z)
                in_y.append(speed_y * faces[2, i + 1, t])
                in_z.append(az * faces[3 if b else 4, i + 1, t])
            acc = [[None] * 4 for _ in range(TILES)]
            for a in range(VS // 2):
                speed = (a + 0.5) * H
                cx = KEEP * DT * speed
                lo = [cx * x for x in below]
                hi = [cx * x for x in above]
                both = []
                for sign in range(2):
                    start = sign * HALF + a * VS + 8 * b
                    here, shifted = [], []
                    for l in lanes:
                        at = pl.multiple_of((i + 1) * SEC + l, 128)
                        value = state[start : start + 8, pl.ds(at, 128)]
                        here.append(value)
                        shifted.append(pltpu.roll(value, shift_y, 1))
                    result = []
                    for k, l in enumerate(lanes):
                        at = pl.multiple_of((i + (0 if sign else 2)) * SEC + l, 128)
                        before = state[start : start + 8, pl.ds(at, 128)]
                        out_x, in_x = (hi[k], lo[k]) if sign else (lo[k], hi[k])
                        along_y = jnp.where(take, shifted[k - 1], shifted[k]) if k else shifted[k]
                        along_z = pltpu.roll(here[k], 1 if b else 127, 1)
                        value = (
                            here[k] * (keep[k] - out_x)
                            + before * in_x
                            + along_y * in_y[k]
                            + along_z * in_z[k]
                        )
                        at = pl.multiple_of(i * SEC + l, 128)
                        moved[start : start + 8, pl.ds(at, 128)] = value
                        result.append(value)
                    both.append(result)
                for k in range(TILES):
                    even = both[1][k] + both[0][k]
                    odd = both[1][k] - both[0][k]
                    terms = [even, speed * odd, (speed * speed) * even, (speed**3) * odd]
                    for p in range(4):
                        acc[k][p] = terms[p] if acc[k][p] is None else acc[k][p] + terms[p]
            vz2 = vz * vz
            for k in range(TILES):
                a0, a1, a2, a3 = acc[k]
                terms = [
                    a0, a1, vz * a0, a2, vz2 * a0, vz * a1,
                    a3 + vz2 * a1, vz * (a2 + vz2 * a0),
                ]
                for p in range(8):
                    total[k][p] = terms[p] if b == 0 else total[k][p] + terms[p]
        for k, t in enumerate(tiles):
            for p in range(8):
                sums[p, i * TILES + t] = total[k][p]
        return carry

    lax.fori_loop(0, DEPTH, section, 0)


def fold(sums, p, first):
    sub = lax.broadcasted_iota(jnp.int32, (8, 128), 0)
    values = [sums[p, first + t] for t in range(8)]
    for step in (4, 2, 1):
        low = (sub & step) == 0
        merged = []
        for t in range(step):
            a, b = values[t], values[t + step]
            a = a + pltpu.roll(a, 8 - step, 0)
            b = b + pltpu.roll(b, step, 0)
            merged.append(jnp.where(low, a, b))
        values = merged
    return values[0]


def expand(sums, vy):
    s0, sx, sz, sxx, szz, sxz, ex, ez = sums
    y2 = vy * vy
    return [
        s0, sx, vy * s0, sz, sxx, y2 * s0, szz, vy * sx, sxz, vy * sz,
        ex + y2 * sx, vy * (sxx + szz + y2 * s0), ez + y2 * sz,
    ]


def coefficients(m, vy):
    n = m[0]
    inverse = 1.0 / n
    ux, uy, uz = m[1] * inverse, m[2] * inverse, m[3] * inverse
    xx, yy, zz, xy, xz, yz = m[4:10]
    u2 = ux * ux + uy * uy + uz * uz
    trace = xx + yy + zz
    temp = (trace * inverse - u2) / 3.0
    px = xx * ux + xy * uy + xz * uz
    py = xy * ux + yy * uy + yz * uz
    pz = xz * ux + yz * uy + zz * uz
    common = 2.0 * n * u2 - trace
    qx = 0.5 * (m[10] - 2.0 * px + common * ux)
    qy = 0.5 * (m[11] - 2.0 * py + common * uy)
    qz = 0.5 * (m[12] - 2.0 * pz + common * uz)
    inv_t = 1.0 / temp
    kappa = (1.0 - RATIO) / 5.0 * inverse * inv_t * inv_t
    s = kappa * inv_t
    i2t = 0.5 * inv_t
    cy = vy - uy
    level = 0.5 * (
        jnp.log(n) - 1.5 * jnp.log((2.0 * math.pi) * temp) - cy * cy * i2t
    )
    return [ux, uz, i2t, level, qx, qz, s, qy * cy, s * cy * cy - 5.0 * kappa]


def relax(moved, coefs, lines, state, count):
    q = sub_iota()

    def tile(j, carry):
        ux, uz, i2t, level, qx, qz, s, qyc, rest = [coefs[k, j] for k in range(9)]
        for sign in range(2):
            cx = (q + 0.5) * (H if sign else -H) - ux
            c2 = cx * cx
            lines[sign, 0] = jnp.exp(level - c2 * i2t) * RATE
            lines[sign, 1] = qx * cx + qyc
            lines[sign, 2] = s * c2 + rest
        along = []
        for b in range(2):
            cz = vz_tile(b) - uz
            c2 = cz * cz
            along.append((jnp.exp(level - c2 * i2t), qz * cz, s * c2))
        at = pl.multiple_of(j * 128, 128)
        for sign in range(2):
            for a in range(VS // 2):
                ex = row(lines, sign, 0, pl.ds(a, 1), slice(None))
                qa = row(lines, sign, 1, pl.ds(a, 1), slice(None))
                sa = row(lines, sign, 2, pl.ds(a, 1), slice(None))
                for b in range(2):
                    ez, qb, sb = along[b]
                    start = sign * HALF + a * VS + 8 * b
                    value = moved[start : start + 8, pl.ds(at, 128)]
                    state[start : start + 8, pl.ds(at, 128)] = value + (ex * ez) * (
                        1.0 + (qa + qb) * (sa + sb)
                    )
        return carry

    lax.fori_loop(0, count, tile, 0)


def move_kernel(
    count, dist, left, right, wall, kind, inflow, moved, mine, other, state, faces, sums, sems
):
    iy = lax.axis_index("vel")
    position = lax.axis_index("gx")
    copies = [
        pltpu.make_async_copy(dist, state.at[:, pl.ds(SEC, DEPTH * SEC)], sems.at[0]),
        pltpu.make_async_copy(left, state.at[pl.ds(HALF, HALF), pl.ds(0, SEC)], sems.at[1]),
        pltpu.make_async_copy(
            right, state.at[pl.ds(0, HALF), pl.ds((DEPTH + 1) * SEC, SEC)], sems.at[2]
        ),
    ]
    for copy in copies:
        copy.start()
    prepare_masks(wall, faces, position, count, iy >= VS // 2)
    for copy in copies:
        copy.wait()
    fill_ends(state, inflow, kind, position, count)
    transport(state, faces, moved, sums, iy)
    core = lax.rem(iy, 2)
    for p in range(8):
        mine[p] = fold(sums, p, core * 8)
        other[p] = fold(sums, p, 8 - core * 8)


VM = pl.BlockSpec(memory_space=pltpu.VMEM)
ANY = pl.BlockSpec(memory_space=pl.ANY)


def move(dist, left, right, wall, kind, inflow, count):
    part = jax.ShapeDtypeStruct((8, 8, 128), jnp.float32)
    return pl.pallas_call(
        functools.partial(move_kernel, count),
        out_shape=(jax.ShapeDtypeStruct((ROWS, DEPTH * SEC), jnp.float32), part, part),
        in_specs=[ANY, ANY, ANY, VM, VM, VM],
        out_specs=(VM, VM, VM),
        scratch_shapes=[
            pltpu.VMEM((ROWS, (DEPTH + 2) * SEC), jnp.float32),
            pltpu.VMEM((5, DEPTH + 1, TILES, 8, 128), jnp.float32),
            pltpu.VMEM((8, OWN, 8, 128), jnp.float32),
            pltpu.SemaphoreType.DMA((3,)),
        ],
        name="move",
    )(dist, left, right, wall, kind, inflow)


def join_kernel(mine, other, out):
    iy = lax.axis_index("vel")
    mate = iy + 1 - 2 * lax.rem(iy, 2)
    a = expand([mine[p] for p in range(8)], vy_of(iy))
    b = expand([other[p] for p in range(8)], vy_of(mate))
    for k in range(13):
        value = a[k] + b[k]
        for chip in range(8):
            out[chip, k] = value


def total_kernel(parts, out):
    for k in range(13):
        value = parts[0, k]
        for chip in range(1, 8):
            value = value + parts[chip, k]
        out[k] = value * (WEIGHT / KEEP)


def swap_cores(array):
    return lax.ppermute(array, "vel", [(i, i ^ 1) for i in range(VS)])


def all_moments(mine, other):
    got = swap_cores(other)
    shape = jax.ShapeDtypeStruct((8, 13, 8, 128), jnp.float32)
    sent = pl.pallas_call(
        join_kernel, out_shape=shape, in_specs=[VM, VM], out_specs=VM, name="join"
    )(mine, got)
    groups = [[2 * i + c for i in range(VS // 2)] for c in range(2)]
    parts = lax.all_to_all(sent, "vel", 0, 0, axis_index_groups=groups, tiled=True)
    own = pl.pallas_call(
        total_kernel,
        out_shape=jax.ShapeDtypeStruct((13, 8, 128), jnp.float32),
        in_specs=[VM],
        out_specs=VM,
        name="total",
    )(parts)
    return own, swap_cores(own)


def relax_kernel(last, moved, mine, other, *refs):
    if last:
        state, coefs, lines = refs
    else:
        state, to_right, to_left, coefs, lines = refs
    iy = lax.axis_index("vel")
    core = lax.rem(iy, 2)
    vy = vy_of(iy)
    for ref, half in ((mine, core), (other, 1 - core)):
        values = coefficients([ref[k] for k in range(13)], vy)
        for k, value in enumerate(values):
            for t in range(8):
                coefs[k, half * 8 + t] = jnp.broadcast_to(value[t : t + 1], (8, 128))
    relax(moved, coefs, lines, state, OWN)
    if not last:
        to_right[...] = state[HALF:, (DEPTH - 1) * SEC :]
        to_left[...] = state[:HALF, :SEC]


def relaxed(moved, mine, other, last):
    whole = jax.ShapeDtypeStruct((ROWS, DEPTH * SEC), jnp.float32)
    rim = jax.ShapeDtypeStruct((HALF, SEC), jnp.float32)
    outs = (whole,) if last else (whole, rim, rim)
    return pl.pallas_call(
        functools.partial(relax_kernel, last),
        out_shape=outs,
        in_specs=[VM, VM, VM],
        out_specs=(VM,) * len(outs),
        scratch_shapes=[
            pltpu.VMEM((9, OWN, 8, 128), jnp.float32),
            pltpu.VMEM((2, 3, 8, 128), jnp.float32),
        ],
        name="relax",
    )(moved, mine, other)


def send_rims(to_right, to_left, peers):
    from_left = lax.ppermute(to_right, "gx", [(i, i + 1) for i in range(peers - 1)])
    from_right = lax.ppermute(to_left, "gx", [(i + 1, i) for i in range(peers - 1)])
    return from_left, from_right


def per_device(distribution, wall_mask, boundary_kind, inflow):
    count = lax.axis_size("gx")
    inflow = inflow.reshape(2, 128)
    state = distribution
    left, right = send_rims(state[HALF:, (DEPTH - 1) * SEC :], state[:HALF, :SEC], count)
    for step in range(STEPS):
        last = step + 1 == STEPS
        moved, mine, other = move(state, left, right, wall_mask, boundary_kind, inflow, count)
        own, got = all_moments(mine, other)
        outs = relaxed(moved, own, got, last)
        state = outs[0]
        if not last:
            left, right = send_rims(outs[1], outs[2], count)
    return state


def solution(mesh):
    placed = (P("vel", "gx"), P(), P(), P("vel"))
    return jax.shard_map(
        per_device, mesh=mesh, in_specs=placed, out_specs=P("vel", "gx"), check_vma=False
    )
```

time: 616 us -> 156 us (0.25)
  the two profiles are of different devices: /device:TPU:1 before, /device:TPU:107 now
where the time goes in v1:
time: 156 us; the launch traced here: 153 us
  blocking collectives  43.7 us (28%)
  Pallas kernels  38.2 us (24%)
  waiting for transfers between devices  35.9 us (23%)
  starting transfers between devices  28.3 us (18%)
  local copies, waits for them, and re-layouts  6.81 us (4%)
    all_to_all x3, blocking collectives, all_moments(): lax.all_to_all(sent, 'vel', 0, 0, axis_index_groups=groups, tiled=True)  43.7 us
    pallas_call x3, Pallas kernels, move(): pl.pallas_call(functools.partial(move_kernel, count), out_shape=(jax.Shap...  16.8 us
    ppermute x3, waiting for transfers between devices, send_rims(): lax.ppermute(to_left, 'gx', [(i + 1, i) for i in range(peers - 1)])  16.3 us
    ppermute x3, starting transfers between devices, send_rims(): lax.ppermute(to_right, 'gx', [(i, i + 1) for i in range(peers - 1)])  14.4 us
    ppermute x3, waiting for transfers between devices, send_rims(): lax.ppermute(to_right, 'gx', [(i, i + 1) for i in range(peers - 1)])  13.1 us
    pallas_call x3, Pallas kernels, relaxed(): pl.pallas_call(functools.partial(relax_kernel, last), out_shape=outs, in_...  11.7 us
    ppermute x6, starting transfers between devices, swap_cores(): return lax.ppermute(array, 'vel', [(i, i ^ 1) for i in range(VS)])  7.93 us
    ppermute x6, waiting for transfers between devices, swap_cores(): return lax.ppermute(array, 'vel', [(i, i ^ 1) for i in range(VS)])  6.5 us
  transfers between devices with their start and end apart: 12, of which 12 were waited for; matrix products, arithmetic and copies ran while one was open for 0% of the time, Pallas kernels for 0%

profile of v1, /device:TPU:107, one launch (start us, length us, event | category | flops | bytes accessed | tf_op | source)
XLA Modules:
  0.0 153.0 jit_solution(1535517401749588959)
XLA Ops:
  0.0 1.1 fusion
  1.1 2.1 %collective-permute-start.1 = (f32[128,512]{1,0:T(8,128)S(1)}, f32[128,512]{1,0:T(8,128)S(1)}, u32[]{:S(2)}, u32[]{:S(2)}) collective-permute-start(f32[128,512]{1,0:T(8,128)S(1)} %get-tuple-element.35), channel_id=1, source_target_pairs={{1,0},{2,1},{3,2},{4,3},{5,4},{6,5},{7,6},{8,7},{9,8},{10,9},{11,1... | collective-permute-start | bytes 786440 | tf_op jit(solution)/shard_map/ppermute | solution.py:385
  3.2 5.3 %collective-permute-start = (f32[128,512]{1,0:T(8,128)S(1)}, f32[128,512]{1,0:T(8,128)S(1)}, u32[]{:S(2)}, u32[]{:S(2)}) collective-permute-start(f32[128,512]{1,0:T(8,128)S(1)} %get-tuple-element.36), channel_id=1, source_target_pairs={{0,1},{1,2},{2,3},{3,4},{4,5},{5,6},{6,7},{7,8},{8,9},{9,10},{10,1... | collective-permute-start | bytes 786440 | tf_op jit(solution)/shard_map/ppermute | solution.py:384
  8.5 5.1 %collective-permute-done.1.right = f32[128,512]{1,0:T(8,128)S(1)} collective-permute-done((f32[128,512]{1,0:T(8,128)S(1)}, f32[128,512]{1,0:T(8,128)S(1)}, u32[]{:S(2)}, u32[]{:S(2)}) %collective-permute-start.1) | collective-permute-done | bytes 262176 | tf_op jit(solution)/shard_map/ppermute | solution.py:385
  13.6 5.3 %collective-permute-done.left = f32[128,512]{1,0:T(8,128)S(1)} collective-permute-done((f32[128,512]{1,0:T(8,128)S(1)}, f32[128,512]{1,0:T(8,128)S(1)}, u32[]{:S(2)}, u32[]{:S(2)}) %collective-permute-start) | collective-permute-done | bytes 262176 | tf_op jit(solution)/shard_map/ppermute | solution.py:384
  18.9 0.7 copy-done.5
  19.6 5.6 %move.3 = (f32[256,2048]{1,0:T(8,128)}, f32[8,8,128]{2,1,0:T(8,128)}, f32[8,8,128]{2,1,0:T(8,128)}) custom-call(f32[256,2048]{1,0:T(8,128)} %dist.1, f32[128,512]{1,0:T(8,128)} %copy-done.5, f32[128,512]{1,0:T(8,128)} %copy-done.2, s32[64,512]{1,0:T(8,128)} %wall.5, s32[2,512]{1,0:T(2,128)} %kind.5, f32[2,128]{1,0:T(2,128)} %bitcast.1), custom_call_target="tpu_custom_call" | custom-call | tf_op jit(solution)/shard_map/move/pallas_call | solution.py:291
  25.2 0.6 collective-permute-start.2
  25.8 1.1 collective-permute-done.2.other
  27.4 1.6 %join.3 = f32[8,13,8,128]{3,2,1,0:T(8,128)} custom-call(f32[8,8,128]{2,1,0:T(8,128)} %get-tuple-element.21.mine, f32[8,8,128]{2,1,0:T(8,128)} %copy-done.9), custom_call_target="tpu_custom_call" | custom-call | tf_op jit(solution)/shard_map/join/pallas_call | solution.py:332
  29.0 15.2 %all_to_all.15.parts = f32[8,13,8,128]{3,2,1,0:T(8,128)} all-to-all(f32[8,13,8,128]{3,2,1,0:T(8,128)} %join.3), channel_id=1, replica_groups={{0,32,64,96,128,160,192,224},{16,48,80,112,144,176,208,240},{1,33,65,97..., dimensions={0} | all-to-all | bytes 851968 | tf_op jit(solution)/shard_map/all_to_all | solution.py:336
  44.2 1.6 %total.3.mine = f32[13,8,128]{2,1,0:T(8,128)} custom-call(f32[8,13,8,128]{3,2,1,0:T(8,128)} %all_to_all.15.parts), custom_call_target="tpu_custom_call" | custom-call | tf_op jit(solution)/shard_map/total/pallas_call | solution.py:337
  45.9 1.5 collective-permute-start.3
  47.4 1.1 collective-permute-done.3.other
  48.5 0.6 copy-done.6
  49.1 4.0 %relax.3 = (f32[256,2048]{1,0:T(8,128)}, f32[128,512]{1,0:T(8,128)}, f32[128,512]{1,0:T(8,128)}) custom-call(f32[256,2048]{1,0:T(8,128)} %get-tuple-element.20.moved, f32[13,8,128]{2,1,0:T(8,128)} %total.3.mine, f32[13,8,128]{2,1,0:T(8,128)} %copy-done.6), custom_call_target="tpu_custom_call" | custom-call | tf_op jit(solution)/shard_map/relax/pallas_call | solution.py:370
  53.1 3.5 %collective-permute-start.4 = (f32[128,512]{1,0:T(8,128)}, f32[128,512]{1,0:T(8,128)S(1)}, u32[]{:S(2)}, u32[]{:S(2)}) collective-permute-start(f32[128,512]{1,0:T(8,128)} %get-tuple-element.24), channel_id=1, source_target_pairs={{0,1},{1,2},{2,3},{3,4},{4,5},{5,6},{6,7},{7,8},{8,9},{9,10},{10,1... | collective-permute-start | bytes 786440 | tf_op jit(solution)/shard_map/ppermute | solution.py:384
  56.6 1.9 %collective-permute-start.5 = (f32[128,512]{1,0:T(8,128)}, f32[128,512]{1,0:T(8,128)S(1)}, u32[]{:S(2)}, u32[]{:S(2)}) collective-permute-start(f32[128,512]{1,0:T(8,128)} %get-tuple-element.25), channel_id=1, source_target_pairs={{1,0},{2,1},{3,2},{4,3},{5,4},{6,5},{7,6},{8,7},{9,8},{10,9},{11,1... | collective-permute-start | bytes 786440 | tf_op jit(solution)/shard_map/ppermute | solution.py:385
  58.6 4.1 %collective-permute-done.4.left = f32[128,512]{1,0:T(8,128)S(1)} collective-permute-done((f32[128,512]{1,0:T(8,128)}, f32[128,512]{1,0:T(8,128)S(1)}, u32[]{:S(2)}, u32[]{:S(2)}) %collective-permute-start.4) | collective-permute-done | bytes 262176 | tf_op jit(solution)/shard_map/ppermute | solution.py:384
  62.7 5.4 %collective-permute-done.5.right = f32[128,512]{1,0:T(8,128)S(1)} collective-permute-done((f32[128,512]{1,0:T(8,128)}, f32[128,512]{1,0:T(8,128)S(1)}, u32[]{:S(2)}, u32[]{:S(2)}) %collective-permute-start.5) | collective-permute-done | bytes 262176 | tf_op jit(solution)/shard_map/ppermute | solution.py:385
  68.1 0.7 copy-done.3
  68.8 5.6 %move.4 = (f32[256,2048]{1,0:T(8,128)}, f32[8,8,128]{2,1,0:T(8,128)}, f32[8,8,128]{2,1,0:T(8,128)}) custom-call(f32[256,2048]{1,0:T(8,128)} %get-tuple-element.23.dist, f32[128,512]{1,0:T(8,128)} %copy-done, f32[128,512]{1,0:T(8,128)} %copy-done.3, s32[64,512]{1,0:T(8,128)} %wall.5, s32[2,512]{1,0:T(2,128)} %kind.5, f32[2,128]{1,0:T(2,128)} %bitcast.2), custom_call_target="tpu_custom_call" | custom-call | tf_op jit(solution)/shard_map/move/pallas_call | solution.py:291
  74.4 1.6 %collective-permute-start.6 = (f32[8,8,128]{2,1,0:T(8,128)}, f32[8,8,128]{2,1,0:T(8,128)S(1)}, u32[]{:S(2)}, u32[]{:S(2)}) collective-permute-start(f32[8,8,128]{2,1,0:T(8,128)} %get-tuple-element.28), channel_id=1, source_target_pairs={{0,16},{16,0},{32,48},{48,32},{64,80},{80,64},{96,112},{112,96},{1... | collective-permute-start | bytes 98312 | tf_op jit(solution)/shard_map/ppermute | solution.py:326
  76.0 1.1 collective-permute-done.6.other
  77.0 0.6 copy-done.10
  77.6 1.6 %join.4 = f32[8,13,8,128]{3,2,1,0:T(8,128)} custom-call(f32[8,8,128]{2,1,0:T(8,128)} %get-tuple-element.27.mine, f32[8,8,128]{2,1,0:T(8,128)} %copy-done.10), custom_call_target="tpu_custom_call" | custom-call | tf_op jit(solution)/shard_map/join/pallas_call | solution.py:332
  79.2 14.2 %all_to_all.16.parts = f32[8,13,8,128]{3,2,1,0:T(8,128)} all-to-all(f32[8,13,8,128]{3,2,1,0:T(8,128)} %join.4), channel_id=1, replica_groups={{0,32,64,96,128,160,192,224},{16,48,80,112,144,176,208,240},{1,33,65,97..., dimensions={0} | all-to-all | bytes 851968 | tf_op jit(solution)/shard_map/all_to_all | solution.py:336
  93.4 1.6 %total.4.mine = f32[13,8,128]{2,1,0:T(8,128)} custom-call(f32[8,13,8,128]{3,2,1,0:T(8,128)} %all_to_all.16.parts), custom_call_target="tpu_custom_call" | custom-call | tf_op jit(solution)/shard_map/total/pallas_call | solution.py:337
  95.1 1.3 collective-permute-start.7
  96.4 1.1 collective-permute-done.7.other
  97.5 0.6 copy-done.7
  98.1 3.9 %relax.4 = (f32[256,2048]{1,0:T(8,128)}, f32[128,512]{1,0:T(8,128)}, f32[128,512]{1,0:T(8,128)}) custom-call(f32[256,2048]{1,0:T(8,128)} %get-tuple-element.26.moved, f32[13,8,128]{2,1,0:T(8,128)} %total.4.mine, f32[13,8,128]{2,1,0:T(8,128)} %copy-done.7), custom_call_target="tpu_custom_call" | custom-call | tf_op jit(solution)/shard_map/relax/pallas_call | solution.py:370
  102.1 5.6 %collective-permute-start.8 = (f32[128,512]{1,0:T(8,128)}, f32[128,512]{1,0:T(8,128)S(1)}, u32[]{:S(2)}, u32[]{:S(2)}) collective-permute-start(f32[128,512]{1,0:T(8,128)} %get-tuple-element.30), channel_id=1, source_target_pairs={{0,1},{1,2},{2,3},{3,4},{4,5},{5,6},{6,7},{7,8},{8,9},{9,10},{10,1... | collective-permute-start | bytes 786440 | tf_op jit(solution)/shard_map/ppermute | solution.py:384
  107.7 1.9 %collective-permute-start.9 = (f32[128,512]{1,0:T(8,128)}, f32[128,512]{1,0:T(8,128)S(1)}, u32[]{:S(2)}, u32[]{:S(2)}) collective-permute-start(f32[128,512]{1,0:T(8,128)} %get-tuple-element.31), channel_id=1, source_target_pairs={{1,0},{2,1},{3,2},{4,3},{5,4},{6,5},{7,6},{8,7},{9,8},{10,9},{11,1... | collective-permute-start | bytes 786440 | tf_op jit(solution)/shard_map/ppermute | solution.py:385
  109.6 3.7 %collective-permute-done.8.left = f32[128,512]{1,0:T(8,128)S(1)} collective-permute-done((f32[128,512]{1,0:T(8,128)}, f32[128,512]{1,0:T(8,128)S(1)}, u32[]{:S(2)}, u32[]{:S(2)}) %collective-permute-start.8) | collective-permute-done | bytes 262176 | tf_op jit(solution)/shard_map/ppermute | solution.py:384
  113.3 5.8 %collective-permute-done.9.right = f32[128,512]{1,0:T(8,128)S(1)} collective-permute-done((f32[128,512]{1,0:T(8,128)}, f32[128,512]{1,0:T(8,128)S(1)}, u32[]{:S(2)}, u32[]{:S(2)}) %collective-permute-start.9) | collective-permute-done | bytes 262176 | tf_op jit(solution)/shard_map/ppermute | solution.py:385
  119.1 0.7 copy-done.4
  119.8 5.6 %move.5 = (f32[256,2048]{1,0:T(8,128)}, f32[8,8,128]{2,1,0:T(8,128)}, f32[8,8,128]{2,1,0:T(8,128)}) custom-call(f32[256,2048]{1,0:T(8,128)} %get-tuple-element.29.dist, f32[128,512]{1,0:T(8,128)} %copy-done.1, f32[128,512]{1,0:T(8,128)} %copy-done.4, s32[64,512]{1,0:T(8,128)} %wall.5, s32[2,512]{1,0:T(2,128)} %kind.5, f32[2,128]{1,0:T(2,128)} %bitcast.3), custom_call_target="tpu_custom_call" | custom-call | tf_op jit(solution)/shard_map/move/pallas_call | solution.py:291
  125.5 1.6 %collective-permute-start.10 = (f32[8,8,128]{2,1,0:T(8,128)}, f32[8,8,128]{2,1,0:T(8,128)S(1)}, u32[]{:S(2)}, u32[]{:S(2)}) collective-permute-start(f32[8,8,128]{2,1,0:T(8,128)} %get-tuple-element.34), channel_id=1, source_target_pairs={{0,16},{16,0},{32,48},{48,32},{64,80},{80,64},{96,112},{112,96},{1... | collective-permute-start | bytes 98312 | tf_op jit(solution)/shard_map/ppermute | solution.py:326
  127.0 1.1 collective-permute-done.10.other
  128.1 0.6 copy-done.11
  128.7 1.6 %join.5 = f32[8,13,8,128]{3,2,1,0:T(8,128)} custom-call(f32[8,8,128]{2,1,0:T(8,128)} %get-tuple-element.33.mine, f32[8,8,128]{2,1,0:T(8,128)} %copy-done.11), custom_call_target="tpu_custom_call" | custom-call | tf_op jit(solution)/shard_map/join/pallas_call | solution.py:332
  130.3 14.2 %all_to_all.17.parts = f32[8,13,8,128]{3,2,1,0:T(8,128)} all-to-all(f32[8,13,8,128]{3,2,1,0:T(8,128)} %join.5), channel_id=1, replica_groups={{0,32,64,96,128,160,192,224},{16,48,80,112,144,176,208,240},{1,33,65,97..., dimensions={0} | all-to-all | bytes 851968 | tf_op jit(solution)/shard_map/all_to_all | solution.py:336
  144.5 1.6 %total.5.mine = f32[13,8,128]{2,1,0:T(8,128)} custom-call(f32[8,13,8,128]{3,2,1,0:T(8,128)} %all_to_all.17.parts), custom_call_target="tpu_custom_call" | custom-call | tf_op jit(solution)/shard_map/total/pallas_call | solution.py:337
  146.2 1.3 collective-permute-start.11
  147.5 1.1 collective-permute-done.11.other
  148.6 0.6 copy-done.8
  149.2 3.8 %relax.5 = f32[256,2048]{1,0:T(8,128)} custom-call(f32[256,2048]{1,0:T(8,128)} %get-tuple-element.32.moved, f32[13,8,128]{2,1,0:T(8,128)} %total.5.mine, f32[13,8,128]{2,1,0:T(8,128)} %copy-done.8), custom_call_target="tpu_custom_call" | custom-call | tf_op jit(solution)/shard_map/relax/pallas_call | solution.py:370
  (16 shorter events, 0.6 us)
Async XLA Ops:
  1.1 12.5 %collective-permute-start.1 = (f32[128,512]{1,0:T(8,128)S(1)}, f32[128,512]{1,0:T(8,128)S(1)}, u32[]{:S(2)}, u32[]{:S(2)}) collective-permute-start(f32[128,512]{1,0:T(8,128)S(1)} %get-tuple-element.35), channel_id=1, source_target_pairs={{1,0},{2,1},{3,2},{4,3},{5,4},{6,5},{7,6},{8,7},{9,8},{10,9},{11,1... | collective-permute-start | bytes 786440 | tf_op jit(solution)/shard_map/ppermute | solution.py:385
  3.2 15.7 %collective-permute-start = (f32[128,512]{1,0:T(8,128)S(1)}, f32[128,512]{1,0:T(8,128)S(1)}, u32[]{:S(2)}, u32[]{:S(2)}) collective-permute-start(f32[128,512]{1,0:T(8,128)S(1)} %get-tuple-element.36), channel_id=1, source_target_pairs={{0,1},{1,2},{2,3},{3,4},{4,5},{5,6},{6,7},{7,8},{8,9},{9,10},{10,1... | collective-permute-start | bytes 786440 | tf_op jit(solution)/shard_map/ppermute | solution.py:384
  13.6 5.3 %copy-start.2 = (f32[128,512]{1,0:T(8,128)}, f32[128,512]{1,0:T(8,128)S(1)}, u32[]{:S(2)}) copy-start(f32[128,512]{1,0:T(8,128)S(1)} %collective-permute-done.1.right) | copy-start | bytes 786436
  18.9 0.7 copy-start.5
  25.2 1.7 %collective-permute-start.2 = (f32[8,8,128]{2,1,0:T(8,128)}, f32[8,8,128]{2,1,0:T(8,128)S(1)}, u32[]{:S(2)}, u32[]{:S(2)}) collective-permute-start(f32[8,8,128]{2,1,0:T(8,128)} %get-tuple-element.22), channel_id=1, source_target_pairs={{0,16},{16,0},{32,48},{48,32},{64,80},{80,64},{96,112},{112,96},{1... | collective-permute-start | bytes 98312 | tf_op jit(solution)/shard_map/ppermute | solution.py:326
  26.8 0.6 copy-start.9
  45.9 2.6 %collective-permute-start.3 = (f32[13,8,128]{2,1,0:T(8,128)}, f32[13,8,128]{2,1,0:T(8,128)S(1)}, u32[]{:S(2)}, u32[]{:S(2)}) collective-permute-start(f32[13,8,128]{2,1,0:T(8,128)} %total.3.mine), channel_id=1, source_target_pairs={{0,16},{16,0},{32,48},{48,32},{64,80},{80,64},{96,112},{112,96},{1... | collective-permute-start | bytes 159752 | tf_op jit(solution)/shard_map/ppermute | solution.py:326
  48.5 0.6 copy-start.6
  53.1 9.6 %collective-permute-start.4 = (f32[128,512]{1,0:T(8,128)}, f32[128,512]{1,0:T(8,128)S(1)}, u32[]{:S(2)}, u32[]{:S(2)}) collective-permute-start(f32[128,512]{1,0:T(8,128)} %get-tuple-element.24), channel_id=1, source_target_pairs={{0,1},{1,2},{2,3},{3,4},{4,5},{5,6},{6,7},{7,8},{8,9},{9,10},{10,1... | collective-permute-start | bytes 786440 | tf_op jit(solution)/shard_map/ppermute | solution.py:384
  56.6 11.4 %collective-permute-start.5 = (f32[128,512]{1,0:T(8,128)}, f32[128,512]{1,0:T(8,128)S(1)}, u32[]{:S(2)}, u32[]{:S(2)}) collective-permute-start(f32[128,512]{1,0:T(8,128)} %get-tuple-element.25), channel_id=1, source_target_pairs={{1,0},{2,1},{3,2},{4,3},{5,4},{6,5},{7,6},{8,7},{9,8},{10,9},{11,1... | collective-permute-start | bytes 786440 | tf_op jit(solution)/shard_map/ppermute | solution.py:385
  62.7 5.4 %copy-start = (f32[128,512]{1,0:T(8,128)}, f32[128,512]{1,0:T(8,128)S(1)}, u32[]{:S(2)}) copy-start(f32[128,512]{1,0:T(8,128)S(1)} %collective-permute-done.4.left) | copy-start | bytes 786436
  68.1 0.7 copy-start.3
  74.4 2.6 %collective-permute-start.6 = (f32[8,8,128]{2,1,0:T(8,128)}, f32[8,8,128]{2,1,0:T(8,128)S(1)}, u32[]{:S(2)}, u32[]{:S(2)}) collective-permute-start(f32[8,8,128]{2,1,0:T(8,128)} %get-tuple-element.28), channel_id=1, source_target_pairs={{0,16},{16,0},{32,48},{48,32},{64,80},{80,64},{96,112},{112,96},{1... | collective-permute-start | bytes 98312 | tf_op jit(solution)/shard_map/ppermute | solution.py:326
  77.0 0.6 copy-start.10
  95.1 2.4 %collective-permute-start.7 = (f32[13,8,128]{2,1,0:T(8,128)}, f32[13,8,128]{2,1,0:T(8,128)S(1)}, u32[]{:S(2)}, u32[]{:S(2)}) collective-permute-start(f32[13,8,128]{2,1,0:T(8,128)} %total.4.mine), channel_id=1, source_target_pairs={{0,16},{16,0},{32,48},{48,32},{64,80},{80,64},{96,112},{112,96},{1... | collective-permute-start | bytes 159752 | tf_op jit(solution)/shard_map/ppermute | solution.py:326
  97.5 0.6 copy-start.7
  102.1 11.3 %collective-permute-start.8 = (f32[128,512]{1,0:T(8,128)}, f32[128,512]{1,0:T(8,128)S(1)}, u32[]{:S(2)}, u32[]{:S(2)}) collective-permute-start(f32[128,512]{1,0:T(8,128)} %get-tuple-element.30), channel_id=1, source_target_pairs={{0,1},{1,2},{2,3},{3,4},{4,5},{5,6},{6,7},{7,8},{8,9},{9,10},{10,1... | collective-permute-start | bytes 786440 | tf_op jit(solution)/shard_map/ppermute | solution.py:384
  107.7 11.4 %collective-permute-start.9 = (f32[128,512]{1,0:T(8,128)}, f32[128,512]{1,0:T(8,128)S(1)}, u32[]{:S(2)}, u32[]{:S(2)}) collective-permute-start(f32[128,512]{1,0:T(8,128)} %get-tuple-element.31), channel_id=1, source_target_pairs={{1,0},{2,1},{3,2},{4,3},{5,4},{6,5},{7,6},{8,7},{9,8},{10,9},{11,1... | collective-permute-start | bytes 786440 | tf_op jit(solution)/shard_map/ppermute | solution.py:385
  113.3 5.8 %copy-start.1 = (f32[128,512]{1,0:T(8,128)}, f32[128,512]{1,0:T(8,128)S(1)}, u32[]{:S(2)}) copy-start(f32[128,512]{1,0:T(8,128)S(1)} %collective-permute-done.8.left) | copy-start | bytes 786436
  119.1 0.7 copy-start.4
  125.5 2.6 %collective-permute-start.10 = (f32[8,8,128]{2,1,0:T(8,128)}, f32[8,8,128]{2,1,0:T(8,128)S(1)}, u32[]{:S(2)}, u32[]{:S(2)}) collective-permute-start(f32[8,8,128]{2,1,0:T(8,128)} %get-tuple-element.34), channel_id=1, source_target_pairs={{0,16},{16,0},{32,48},{48,32},{64,80},{80,64},{96,112},{112,96},{1... | collective-permute-start | bytes 98312 | tf_op jit(solution)/shard_map/ppermute | solution.py:326
  128.1 0.6 copy-start.11
  146.2 2.4 %collective-permute-start.11 = (f32[13,8,128]{2,1,0:T(8,128)}, f32[13,8,128]{2,1,0:T(8,128)S(1)}, u32[]{:S(2)}, u32[]{:S(2)}) collective-permute-start(f32[13,8,128]{2,1,0:T(8,128)} %total.5.mine), channel_id=1, source_target_pairs={{0,16},{16,0},{32,48},{48,32},{64,80},{80,64},{96,112},{112,96},{1... | collective-permute-start | bytes 159752 | tf_op jit(solution)/shard_map/ppermute | solution.py:326
  148.6 0.6 copy-start.8

commit v2 on v1

--- a/solution.py
+++ b/solution.py
@@ -223,183 +223,296 @@
     return [ux, uz, i2t, level, qx, qz, s, qy * cy, s * cy * cy - 5.0 * kappa]
 
 
-def relax(moved, coefs, lines, state, count):
-    q = sub_iota()
-
+def point(coefs, j):
+    return [coefs[k, j] for k in range(9)]
+
+
+def across(values, sign):
+    ux, uz, i2t, level, qx, qz, s, qyc, rest = values
+    cx = (sub_iota() + 0.5) * (H if sign else -H) - ux
+    c2 = cx * cx
+    return jnp.exp(level - c2 * i2t) * RATE, qx * cx + qyc, s * c2 + rest
+
+
+def along(values, b):
+    ux, uz, i2t, level, qx, qz, s, qyc, rest = values
+    cz = vz_tile(b) - uz
+    c2 = cz * cz
+    return jnp.exp(level - c2 * i2t), qz * cz, s * c2
+
+
+def store_lines(lines, values, sign):
+    for k, value in enumerate(across(values, sign)):
+        lines[sign, k] = value
+
+
+def relax_rows(read, write, lines, fixed, sign):
+    for a in range(VS // 2):
+        ex, qa, sa = [row(lines, sign, k, pl.ds(a, 1), slice(None)) for k in range(3)]
+        for b in range(2):
+            ez, qb, sb = fixed[b]
+            start = a * VS + 8 * b
+            write(start, read(start) + (ex * ez) * (1.0 + (qa + qb) * (sa + sb)))
+
+
+def relax(moved, coefs, lines, state, shift):
     def tile(j, carry):
-        ux, uz, i2t, level, qx, qz, s, qyc, rest = [coefs[k, j] for k in range(9)]
+        values = point(coefs, j)
         for sign in range(2):
-            cx = (q + 0.5) * (H if sign else -H) - ux
-            c2 = cx * cx
-            lines[sign, 0] = jnp.exp(level - c2 * i2t) * RATE
-            lines[sign, 1] = qx * cx + qyc
-            lines[sign, 2] = s * c2 + rest
-        along = []
-        for b in range(2):
-            cz = vz_tile(b) - uz
-            c2 = cz * cz
-            along.append((jnp.exp(level - c2 * i2t), qz * cz, s * c2))
+            store_lines(lines, values, sign)
+        fixed = [along(values, b) for b in range(2)]
         at = pl.multiple_of(j * 128, 128)
+        to = pl.multiple_of(j * 128 + shift, 128)
         for sign in range(2):
-            for a in range(VS // 2):
-                ex = row(lines, sign, 0, pl.ds(a, 1), slice(None))
-                qa = row(lines, sign, 1, pl.ds(a, 1), slice(None))
-                sa = row(lines, sign, 2, pl.ds(a, 1), slice(None))
-                for b in range(2):
-                    ez, qb, sb = along[b]
-                    start = sign * HALF + a * VS + 8 * b
-                    value = moved[start : start + 8, pl.ds(at, 128)]
-                    state[start : start + 8, pl.ds(at, 128)] = value + (ex * ez) * (
-                        1.0 + (qa + qb) * (sa + sb)
-                    )
+            base = sign * HALF
+
+            def read(start):
+                return moved[base + start : base + start + 8, pl.ds(at, 128)]
+
+            def write(start, value):
+                state[base + start : base + start + 8, pl.ds(to, 128)] = value
+
+            relax_rows(read, write, lines, fixed, sign)
         return carry
 
-    lax.fori_loop(0, count, tile, 0)
-
-
-def move_kernel(
-    count, dist, left, right, wall, kind, inflow, moved, mine, other, state, faces, sums, sems
-):
+    lax.fori_loop(0, OWN, tile, 0)
+
+
+def relax_ghosts(ghosts, coefs, lines, state):
+    def tile(t, carry):
+        at = pl.multiple_of(t * 128, 128)
+        for sign in range(2):
+            values = point(coefs, t + TILES * sign)
+            store_lines(lines, values, sign)
+            fixed = [along(values, b) for b in range(2)]
+            base = sign * HALF
+            to = pl.multiple_of(t * 128 + (0 if sign else (DEPTH + 1) * SEC), 128)
+
+            def read(start):
+                return ghosts[sign, start : start + 8, pl.ds(at, 128)]
+
+            def write(start, value):
+                state[base + start : base + start + 8, pl.ds(to, 128)] = value
+
+            relax_rows(read, write, lines, fixed, sign)
+        return carry
+
+    lax.fori_loop(0, TILES, tile, 0)
+
+
+def spread(coefs, values, first):
+    for k, value in enumerate(values):
+        for t in range(8):
+            coefs[k, first + t] = jnp.broadcast_to(value[t : t + 1], (8, 128))
+
+
+def finish(state, faces, sums, wall, kind, inflow, moved, mine, other, rims, count):
     iy = lax.axis_index("vel")
     position = lax.axis_index("gx")
+    fill_ends(state, inflow, kind, position, count)
+    transport(state, faces, moved, sums, iy)
+    core = lax.rem(iy, 2)
+    vy = vy_of(iy)
+    for ref, first in ((mine, core * 8), (other, 8 - core * 8)):
+        values = expand([fold(sums, p, first) * (WEIGHT / KEEP) for p in range(8)], vy)
+        for k, value in enumerate(values):
+            ref[k] = value
+    if rims:
+        even = lax.rem(position, 2) == 0
+        up = (slice(HALF, ROWS), slice((DEPTH - 1) * SEC, DEPTH * SEC))
+        down = (slice(0, HALF), slice(0, SEC))
+
+        @pl.when(even)
+        def _():
+            rims[0][...] = moved[up]
+            rims[1][...] = moved[down]
+
+        @pl.when(~even)
+        def _():
+            rims[0][...] = moved[down]
+            rims[1][...] = moved[up]
+
+
+def first_kernel(count, dist, pair_a, pair_b, wall, kind, inflow, *refs):
+    moved, mine, other, rim_a, rim_b, state, faces, sums, sems = refs
+    iy = lax.axis_index("vel")
+    position = lax.axis_index("gx")
+    even = lax.rem(position, 2) == 0
+    left = state.at[pl.ds(HALF, HALF), pl.ds(0, SEC)]
+    right = state.at[pl.ds(0, HALF), pl.ds((DEPTH + 1) * SEC, SEC)]
+    main = pltpu.make_async_copy(dist, state.at[:, pl.ds(SEC, DEPTH * SEC)], sems.at[0])
+    main.start()
+    prepare_masks(wall, faces, position, count, iy >= VS // 2)
+
+    def bring(one, two):
+        copies = [
+            pltpu.make_async_copy(pair_a, one, sems.at[1]),
+            pltpu.make_async_copy(pair_b, two, sems.at[2]),
+        ]
+        for copy in copies:
+            copy.start()
+        for copy in copies:
+            copy.wait()
+
+    pl.when(even)(lambda: bring(right, left))
+    pl.when(~even)(lambda: bring(left, right))
+    main.wait()
+    finish(
+        state, faces, sums, wall, kind, inflow, moved, mine, other, (rim_a, rim_b), count
+    )
+
+
+def middle_kernel(count, rims, old, pair_a, pair_b, got, swapped, wall, kind, inflow, *refs):
+    state, moved, mine, other = refs[:4]
+    out_rims = refs[4 : 4 + 2 * rims]
+    ghosts, coefs, lines, faces, sums, sems = refs[4 + 2 * rims :]
+    iy = lax.axis_index("vel")
+    position = lax.axis_index("gx")
+    odd = lax.rem(position, 2)
     copies = [
-        pltpu.make_async_copy(dist, state.at[:, pl.ds(SEC, DEPTH * SEC)], sems.at[0]),
-        pltpu.make_async_copy(left, state.at[pl.ds(HALF, HALF), pl.ds(0, SEC)], sems.at[1]),
-        pltpu.make_async_copy(
-            right, state.at[pl.ds(0, HALF), pl.ds((DEPTH + 1) * SEC, SEC)], sems.at[2]
-        ),
+        pltpu.make_async_copy(pair_a, ghosts.at[odd], sems.at[0]),
+        pltpu.make_async_copy(pair_b, ghosts.at[1 - odd], sems.at[1]),
     ]
     for copy in copies:
         copy.start()
     prepare_masks(wall, faces, position, count, iy >= VS // 2)
+    sub = lax.broadcasted_iota(jnp.int32, (8, 128), 0)
+    pick = (sub >= TILES) == (lax.rem(iy, 2) == 0)
+    values = [jnp.where(pick, got[k], swapped[k]) for k in range(13)]
+    spread(coefs, coefficients(values, vy_of(iy)), 0)
     for copy in copies:
         copy.wait()
-    fill_ends(state, inflow, kind, position, count)
-    transport(state, faces, moved, sums, iy)
-    core = lax.rem(iy, 2)
-    for p in range(8):
-        mine[p] = fold(sums, p, core * 8)
-        other[p] = fold(sums, p, 8 - core * 8)
+    relax_ghosts(ghosts, coefs, lines, state)
+    finish(state, faces, sums, wall, kind, inflow, moved, mine, other, out_rims, count)
 
 
 VM = pl.BlockSpec(memory_space=pltpu.VMEM)
 ANY = pl.BlockSpec(memory_space=pl.ANY)
-
-
-def move(dist, left, right, wall, kind, inflow, count):
-    part = jax.ShapeDtypeStruct((8, 8, 128), jnp.float32)
+PARAMS = pltpu.CompilerParams(vmem_limit_bytes=12 << 20)
+F32 = jnp.float32
+WHOLE = jax.ShapeDtypeStruct((ROWS, DEPTH * SEC), F32)
+WIDE = jax.ShapeDtypeStruct((ROWS, (DEPTH + 2) * SEC), F32)
+RIM = jax.ShapeDtypeStruct((HALF, SEC), F32)
+PART = jax.ShapeDtypeStruct((13, 8, 128), F32)
+FACES = pltpu.VMEM((5, DEPTH + 1, TILES, 8, 128), F32)
+SUMS = pltpu.VMEM((8, OWN, 8, 128), F32)
+LINES = pltpu.VMEM((2, 3, 8, 128), F32)
+
+
+def move_first(dist, pair_a, pair_b, wall, kind, inflow, count):
+    outs = (WHOLE, PART, PART, RIM, RIM)
     return pl.pallas_call(
-        functools.partial(move_kernel, count),
-        out_shape=(jax.ShapeDtypeStruct((ROWS, DEPTH * SEC), jnp.float32), part, part),
+        functools.partial(first_kernel, count),
+        out_shape=outs,
         in_specs=[ANY, ANY, ANY, VM, VM, VM],
-        out_specs=(VM, VM, VM),
+        out_specs=(VM,) * len(outs),
         scratch_shapes=[
-            pltpu.VMEM((ROWS, (DEPTH + 2) * SEC), jnp.float32),
-            pltpu.VMEM((5, DEPTH + 1, TILES, 8, 128), jnp.float32),
-            pltpu.VMEM((8, OWN, 8, 128), jnp.float32),
-            pltpu.SemaphoreType.DMA((3,)),
+            pltpu.VMEM(WIDE.shape, F32), FACES, SUMS, pltpu.SemaphoreType.DMA((3,))
         ],
-        name="move",
-    )(dist, left, right, wall, kind, inflow)
-
-
-def join_kernel(mine, other, out):
-    iy = lax.axis_index("vel")
-    mate = iy + 1 - 2 * lax.rem(iy, 2)
-    a = expand([mine[p] for p in range(8)], vy_of(iy))
-    b = expand([other[p] for p in range(8)], vy_of(mate))
-    for k in range(13):
-        value = a[k] + b[k]
-        for chip in range(8):
-            out[chip, k] = value
-
-
-def total_kernel(parts, out):
-    for k in range(13):
-        value = parts[0, k]
-        for chip in range(1, 8):
-            value = value + parts[chip, k]
-        out[k] = value * (WEIGHT / KEEP)
-
-
-def swap_cores(array):
-    return lax.ppermute(array, "vel", [(i, i ^ 1) for i in range(VS)])
-
-
-def all_moments(mine, other):
-    got = swap_cores(other)
-    shape = jax.ShapeDtypeStruct((8, 13, 8, 128), jnp.float32)
-    sent = pl.pallas_call(
-        join_kernel, out_shape=shape, in_specs=[VM, VM], out_specs=VM, name="join"
-    )(mine, got)
-    groups = [[2 * i + c for i in range(VS // 2)] for c in range(2)]
-    parts = lax.all_to_all(sent, "vel", 0, 0, axis_index_groups=groups, tiled=True)
-    own = pl.pallas_call(
-        total_kernel,
-        out_shape=jax.ShapeDtypeStruct((13, 8, 128), jnp.float32),
-        in_specs=[VM],
-        out_specs=VM,
-        name="total",
-    )(parts)
-    return own, swap_cores(own)
-
-
-def relax_kernel(last, moved, mine, other, *refs):
-    if last:
-        state, coefs, lines = refs
-    else:
-        state, to_right, to_left, coefs, lines = refs
+        compiler_params=PARAMS,
+        name="move_first",
+    )(dist, pair_a, pair_b, wall, kind, inflow)
+
+
+def move_middle(state, pairs, got, swapped, wall, kind, inflow, count, rims):
+    outs = (WIDE, WHOLE, PART, PART) + (RIM, RIM) * rims
+    return pl.pallas_call(
+        functools.partial(middle_kernel, count, rims),
+        out_shape=outs,
+        in_specs=[VM, ANY, ANY] + [VM] * 5,
+        out_specs=(VM,) * len(outs),
+        input_output_aliases={0: 0},
+        scratch_shapes=[
+            pltpu.VMEM((2, HALF, SEC), F32),
+            pltpu.VMEM((9, 8, 8, 128), F32),
+            LINES,
+            FACES,
+            SUMS,
+            pltpu.SemaphoreType.DMA((2,)),
+        ],
+        compiler_params=PARAMS,
+        name="move_middle",
+    )(state, *pairs, got, swapped, wall, kind, inflow)[1:]
+
+
+def relax_kernel(shift, moved, mine, other, state, coefs, lines):
     iy = lax.axis_index("vel")
     core = lax.rem(iy, 2)
     vy = vy_of(iy)
     for ref, half in ((mine, core), (other, 1 - core)):
-        values = coefficients([ref[k] for k in range(13)], vy)
-        for k, value in enumerate(values):
-            for t in range(8):
-                coefs[k, half * 8 + t] = jnp.broadcast_to(value[t : t + 1], (8, 128))
-    relax(moved, coefs, lines, state, OWN)
-    if not last:
-        to_right[...] = state[HALF:, (DEPTH - 1) * SEC :]
-        to_left[...] = state[:HALF, :SEC]
+        spread(coefs, coefficients([ref[k] for k in range(13)], vy), half * 8)
+    relax(moved, coefs, lines, state, shift)
 
 
 def relaxed(moved, mine, other, last):
-    whole = jax.ShapeDtypeStruct((ROWS, DEPTH * SEC), jnp.float32)
-    rim = jax.ShapeDtypeStruct((HALF, SEC), jnp.float32)
-    outs = (whole,) if last else (whole, rim, rim)
     return pl.pallas_call(
-        functools.partial(relax_kernel, last),
-        out_shape=outs,
+        functools.partial(relax_kernel, 0 if last else SEC),
+        out_shape=WHOLE if last else WIDE,
         in_specs=[VM, VM, VM],
-        out_specs=(VM,) * len(outs),
-        scratch_shapes=[
-            pltpu.VMEM((9, OWN, 8, 128), jnp.float32),
-            pltpu.VMEM((2, 3, 8, 128), jnp.float32),
-        ],
-        name="relax",
+        out_specs=VM,
+        scratch_shapes=[pltpu.VMEM((9, OWN, 8, 128), F32), LINES],
+        compiler_params=PARAMS,
+        name="relax_last" if last else "relax",
     )(moved, mine, other)
 
 
-def send_rims(to_right, to_left, peers):
-    from_left = lax.ppermute(to_right, "gx", [(i, i + 1) for i in range(peers - 1)])
-    from_right = lax.ppermute(to_left, "gx", [(i + 1, i) for i in range(peers - 1)])
-    return from_left, from_right
+def swap_cores(array):
+    return lax.ppermute(array, "vel", [(i, i ^ 1) for i in range(VS)])
+
+
+def shift_x(array, by):
+    def mate(i):
+        return i ^ (2 * by)
+
+    return lax.ppermute(array, "vel", [(i, mate(i)) for i in range(VS)])
+
+
+def all_moments(mine, other):
+    value = mine + swap_cores(other)
+    parts = [shift_x(value, by) for by in (1, 3, 2)]
+    value = (value + parts[2]) + (parts[0] + parts[1])
+    return value + lax.ppermute(value, "vel", [(i, i ^ 8) for i in range(VS)])
+
+
+def swap_rims(pair_a, pair_b, count):
+    near = [(i, i ^ 1) for i in range(count)]
+    far = []
+    for i in range(1, count - 1, 2):
+        far += [(i, i + 1), (i + 1, i)]
+    return lax.ppermute(pair_a, "gx", near), lax.ppermute(pair_b, "gx", far)
+
+
+def swap_moments(half, count):
+    pairs = []
+    for v in range(0, VS, 2):
+        for g in range(count - 1):
+            one, two = (v + 1) * count + g, v * count + g + 1
+            pairs += [(one, two), (two, one)]
+    return lax.ppermute(half, ("vel", "gx"), pairs)
 
 
 def per_device(distribution, wall_mask, boundary_kind, inflow):
     count = lax.axis_size("gx")
     inflow = inflow.reshape(2, 128)
-    state = distribution
-    left, right = send_rims(state[HALF:, (DEPTH - 1) * SEC :], state[:HALF, :SEC], count)
+    even = lax.rem(lax.axis_index("gx"), 2) == 0
+    up = distribution[HALF:, (DEPTH - 1) * SEC :]
+    down = distribution[:HALF, :SEC]
+    pairs = swap_rims(jnp.where(even, up, down), jnp.where(even, down, up), count)
+    outs = move_first(distribution, *pairs, wall_mask, boundary_kind, inflow, count)
     for step in range(STEPS):
+        moved, mine, other = outs[:3]
         last = step + 1 == STEPS
-        moved, mine, other = move(state, left, right, wall_mask, boundary_kind, inflow, count)
-        own, got = all_moments(mine, other)
-        outs = relaxed(moved, own, got, last)
-        state = outs[0]
         if not last:
-            left, right = send_rims(outs[1], outs[2], count)
-    return state
+            pairs = swap_rims(outs[3], outs[4], count)
+        half = all_moments(mine, other)
+        if last:
+            return relaxed(moved, half, swap_cores(half), True)
+        halo = swap_moments(half, count)
+        state = relaxed(moved, half, swap_cores(half), False)
+        outs = move_middle(
+            state, pairs, halo, swap_cores(halo), wall_mask, boundary_kind, inflow, count,
+            rims=step + 2 < STEPS,
+        )
 
 
 def solution(mesh):

time: 156 us -> 108 us (0.69); the launches traced: 153 us -> 107 us
  blocking collectives: 43.7 us -> 0 us
  Pallas kernels: 38.2 us -> 10.7 us
  starting transfers between devices: 28.3 us -> 48.5 us
  waiting for transfers between devices: 35.9 us -> 42.3 us
  local copies, waits for them, and re-layouts: 6.81 us -> 3.87 us
    all_to_all x3 -> x0, blocking collectives: 43.7 us -> none  [all_moments(): lax.all_to_all(sent, 'vel', 0, 0, axis_index_groups=groups, tiled=True)]
    pallas_call x12 -> x6, Pallas kernels: 38.2 us -> 10.7 us  [the longest x2 4.52 us: move_middle(): pl.pallas_call(functools.partial(middle_kernel, count, rims), out_shape=o...]
    ppermute x6 -> x20, starting transfers between devices: 20.4 us -> 43.8 us  [the longest x6 14.9 us: swap_rims(): return (lax.ppermute(pair_a, 'gx', near), lax.ppermute(pair_b, 'gx', far))]
    ppermute x6 -> x20, waiting for transfers between devices: 29.4 us -> 38 us  [the longest x3 17 us: all_moments(): return value + lax.ppermute(value, 'vel', [(i, i ^ 8) for i in range(VS)])]
    ppermute x6 -> x8, starting transfers between devices: 7.93 us -> 4.63 us  [swap_cores(): return lax.ppermute(array, 'vel', [(i, i ^ 1) for i in range(VS)])]
    ppermute x6 -> x8, waiting for transfers between devices: 6.5 us -> 4.32 us  [swap_cores(): return lax.ppermute(array, 'vel', [(i, i ^ 1) for i in range(VS)])]
    unnamed x24 -> x12, local copies, waits for them, and re-layouts: 5.75 us -> 3.87 us
  transfers between devices with their start and end apart: 12 -> 28, of which waited for: 12 -> 15; matrix products, arithmetic and copies ran while one was open for 0% -> 0% of each run, Pallas kernels for 0% -> 2%
where the time goes in v2:
time: 108 us; the launch traced here: 107 us
  starting transfers between devices  48.5 us (45%)
  waiting for transfers between devices  42.3 us (39%)
  Pallas kernels  10.7 us (10%)
  local copies, waits for them, and re-layouts  3.87 us (4%)
  other arithmetic  1.17 us (1%)
    ppermute x3, waiting for transfers between devices, all_moments(): return value + lax.ppermute(value, 'vel', [(i, i ^ 8) for i in range(VS)])  17 us
    ppermute x6, starting transfers between devices, swap_rims(): return (lax.ppermute(pair_a, 'gx', near), lax.ppermute(pair_b, 'gx', far))  14.9 us
    ppermute x2, starting transfers between devices, swap_moments(): return lax.ppermute(half, ('vel', 'gx'), pairs)  13.7 us
    ppermute x6, waiting for transfers between devices, swap_rims(): return (lax.ppermute(pair_a, 'gx', near), lax.ppermute(pair_b, 'gx', far))  13.1 us
    ppermute x9, starting transfers between devices, shift_x(): return lax.ppermute(array, 'vel', [(i, mate(i)) for i in range(VS)])  10.7 us
    ppermute x8, starting transfers between devices, swap_cores(): return lax.ppermute(array, 'vel', [(i, i ^ 1) for i in range(VS)])  4.63 us
    ppermute x3, starting transfers between devices, all_moments(): return value + lax.ppermute(value, 'vel', [(i, i ^ 8) for i in range(VS)])  4.61 us
    pallas_call x2, Pallas kernels, move_middle(): pl.pallas_call(functools.partial(middle_kernel, count, rims), out_shape=o...  4.52 us
  transfers between devices with their start and end apart: 28, of which 15 were waited for; matrix products, arithmetic and copies ran while one was open for 0% of the time, Pallas kernels for 2%

profile of v2, /device:TPU:107, one launch (start us, length us, event | category | flops | bytes accessed | tf_op | source)
XLA Modules:
  0.0 106.7 jit_solution(13263344266489825963)
XLA Ops:
  0.0 1.1 %slice_select_fusion = (f32[128,512]{1,0:T(8,128)S(1)}, f32[128,512]{1,0:T(8,128)S(1)}) fusion(f32[256,2048]{1,0:T(8,128)} %dist.1, pred[]{:T(512)S(6)} %eq.3), kind=kLoop, calls=%fused_computation | loop fusion | flops 131072 | bytes 1048577 | tf_op jit(solution)/shard_map/jit(_where)/select_n | solution.py:500
  1.1 4.6 %collective-permute-start.1 = (f32[128,512]{1,0:T(8,128)S(1)}, f32[128,512]{1,0:T(8,128)S(1)}, u32[]{:S(2)}, u32[]{:S(2)}) collective-permute-start(f32[128,512]{1,0:T(8,128)S(1)} %get-tuple-element.31), channel_id=1, source_target_pairs={{1,2},{2,1},{3,4},{4,3},{5,6},{6,5},{7,8},{8,7},{9,10},{10,9},{11,... | collective-permute-start | bytes 786440 | tf_op jit(solution)/shard_map/ppermute | solution.py:482
  5.7 0.1 collective-permute-start
  5.8 6.5 %collective-permute-done.1.pair_b = f32[128,512]{1,0:T(8,128)S(1)} collective-permute-done((f32[128,512]{1,0:T(8,128)S(1)}, f32[128,512]{1,0:T(8,128)S(1)}, u32[]{:S(2)}, u32[]{:S(2)}) %collective-permute-start.1) | collective-permute-done | bytes 262176 | tf_op jit(solution)/shard_map/ppermute | solution.py:482
  12.3 6.6 %collective-permute-done.pair_a = f32[128,512]{1,0:T(8,128)S(1)} collective-permute-done((f32[128,512]{1,0:T(8,128)S(1)}, f32[128,512]{1,0:T(8,128)S(1)}, u32[]{:S(2)}, u32[]{:S(2)}) %collective-permute-start) | collective-permute-done | bytes 262176 | tf_op jit(solution)/shard_map/ppermute | solution.py:482
  18.9 1.6 %copy-done = f32[256,2048]{1,0:T(8,128)S(1)} copy-done((f32[256,2048]{1,0:T(8,128)S(1)}, f32[256,2048]{1,0:T(8,128)}, u32[]{:S(2)}) %copy-start) | copy-done | bytes 2097176
  20.5 0.9 copy-done.1
  21.4 0.7 copy-done.2
  22.1 0.7 copy-done.4
  22.8 2.1 %move_first.1 = (f32[256,2048]{1,0:T(8,128)S(1)}, f32[13,8,128]{2,1,0:T(8,128)S(1)}, f32[13,8,128]{2,1,0:T(8,128)S(1)}, f32[128,512]{1,0:T(8,128)S(1)}, f32[128,512]{1,0:T(8,128)S(1)}) custom-call(f32[256,2048]{1,0:T(8,128)S(1)} %copy-done, f32[128,512]{1,0:T(8,128)S(1)} %collective-permute-done.pair_a, f32[128,512]{1,0:T(8,128)S(1)} %collective-permute-done.1.pair_b, ...), custom_call_target="tpu_custom_call" | custom-call | tf_op jit(solution)/shard_map/move_first/pallas_call | solution.py:404
  24.9 0.6 collective-permute-start.2
  25.5 0.9 collective-permute-done.2
  26.4 1.3 %collective-permute-start.5 = (f32[13,8,128]{2,1,0:T(8,128)S(1)}, f32[13,8,128]{2,1,0:T(8,128)S(1)}, u32[]{:S(2)}, u32[]{:S(2)}) collective-permute-start(f32[13,8,128]{2,1,0:T(8,128)S(1)} %add.45), channel_id=1, source_target_pairs={{0,96},{16,112},{32,64},{48,80},{64,32},{80,48},{96,0},{112,16},{1... | collective-permute-start | bytes 159752 | tf_op jit(solution)/shard_map/ppermute | solution.py:467
  27.6 1.5 %collective-permute-start.4 = (f32[13,8,128]{2,1,0:T(8,128)S(1)}, f32[13,8,128]{2,1,0:T(8,128)S(1)}, u32[]{:S(2)}, u32[]{:S(2)}) collective-permute-start(f32[13,8,128]{2,1,0:T(8,128)S(1)} %add.45), channel_id=1, source_target_pairs={{0,32},{16,48},{32,0},{48,16},{64,96},{80,112},{96,64},{112,80},{1... | collective-permute-start | bytes 159752 | tf_op jit(solution)/shard_map/ppermute | solution.py:467
  29.2 4.5 %collective-permute-start.9 = (f32[128,512]{1,0:T(8,128)S(1)}, f32[128,512]{1,0:T(8,128)S(1)}, u32[]{:S(2)}, u32[]{:S(2)}) collective-permute-start(f32[128,512]{1,0:T(8,128)S(1)} %get-tuple-element.22), channel_id=1, source_target_pairs={{1,2},{2,1},{3,4},{4,3},{5,6},{6,5},{7,8},{8,7},{9,10},{10,9},{11,... | collective-permute-start | bytes 786440 | tf_op jit(solution)/shard_map/ppermute | solution.py:482
  33.8 2.3 %collective-permute-start.6 = (f32[13,8,128]{2,1,0:T(8,128)S(1)}, f32[13,8,128]{2,1,0:T(8,128)S(1)}, u32[]{:S(2)}, u32[]{:S(2)}) collective-permute-start(f32[13,8,128]{2,1,0:T(8,128)S(1)} %add_add_fusion.2), channel_id=1, source_target_pairs={{0,128},{16,144},{32,160},{48,176},{64,192},{80,208},{96,224},{112... | collective-permute-start | bytes 159752 | tf_op jit(solution)/shard_map/ppermute | solution.py:474
  36.1 7.2 %collective-permute-done.6 = f32[13,8,128]{2,1,0:T(8,128)S(1)} collective-permute-done((f32[13,8,128]{2,1,0:T(8,128)S(1)}, f32[13,8,128]{2,1,0:T(8,128)S(1)}, u32[]{:S(2)}, u32[]{:S(2)}) %collective-permute-start.6) | collective-permute-done | bytes 53280 | tf_op jit(solution)/shard_map/ppermute | solution.py:474
  43.2 7.2 %collective-permute-start.10 = (f32[13,8,128]{2,1,0:T(8,128)S(1)}, f32[13,8,128]{2,1,0:T(8,128)S(1)}, u32[]{:S(2)}, u32[]{:S(2)}) collective-permute-start(f32[13,8,128]{2,1,0:T(8,128)S(1)} %add.49.mine), channel_id=1, source_target_pairs={{16,1},{1,16},{17,2},{2,17},{18,3},{3,18},{19,4},{4,19},{20,5},{5,... | collective-permute-start | bytes 159752 | tf_op jit(solution)/shard_map/ppermute | solution.py:491
  50.4 0.1 collective-permute-start.7
  50.5 1.7 %collective-permute-done.10.got = f32[13,8,128]{2,1,0:T(8,128)S(1)} collective-permute-done((f32[13,8,128]{2,1,0:T(8,128)S(1)}, f32[13,8,128]{2,1,0:T(8,128)S(1)}, u32[]{:S(2)}, u32[]{:S(2)}) %collective-permute-start.10) | collective-permute-done | bytes 53280 | tf_op jit(solution)/shard_map/ppermute | solution.py:491
  52.2 0.9 relax.2.old
  53.2 0.3 collective-permute-done.11.swapped
  53.5 2.2 %move_middle.2 = (f32[256,3072]{1,0:T(8,128)S(1)}, f32[256,2048]{1,0:T(8,128)S(1)}, f32[13,8,128]{2,1,0:T(8,128)S(1)}, f32[13,8,128]{2,1,0:T(8,128)S(1)}, f32[12...) custom-call(f32[256,3072]{1,0:T(8,128)S(1)} %relax.2.old, ...), custom_call_target="tpu_custom_call", output_to_operand_aliasing={{0}: (0, {})} | custom-call | tf_op jit(solution)/shard_map/move_middle/pallas_call | solution.py:419
  55.7 0.3 collective-permute-start.12
  56.0 1.0 collective-permute-done.12
  57.0 1.3 %collective-permute-start.15 = (f32[13,8,128]{2,1,0:T(8,128)S(1)}, f32[13,8,128]{2,1,0:T(8,128)S(1)}, u32[]{:S(2)}, u32[]{:S(2)}) collective-permute-start(f32[13,8,128]{2,1,0:T(8,128)S(1)} %add.50), channel_id=1, source_target_pairs={{0,96},{16,112},{32,64},{48,80},{64,32},{80,48},{96,0},{112,16},{1... | collective-permute-start | bytes 159752 | tf_op jit(solution)/shard_map/ppermute | solution.py:467
  58.3 2.7 %collective-permute-start.14 = (f32[13,8,128]{2,1,0:T(8,128)S(1)}, f32[13,8,128]{2,1,0:T(8,128)S(1)}, u32[]{:S(2)}, u32[]{:S(2)}) collective-permute-start(f32[13,8,128]{2,1,0:T(8,128)S(1)} %add.50), channel_id=1, source_target_pairs={{0,32},{16,48},{32,0},{48,16},{64,96},{80,112},{96,64},{112,80},{1... | collective-permute-start | bytes 159752 | tf_op jit(solution)/shard_map/ppermute | solution.py:467
  61.0 1.1 %collective-permute-start.18 = (f32[128,512]{1,0:T(8,128)S(1)}, f32[128,512]{1,0:T(8,128)S(1)}, u32[]{:S(2)}, u32[]{:S(2)}) collective-permute-start(f32[128,512]{1,0:T(8,128)S(1)} %get-tuple-element.26), channel_id=1, source_target_pairs={{0,1},{1,0},{2,3},{3,2},{4,5},{5,4},{6,7},{7,6},{8,9},{9,8},{10,11... | collective-permute-start | bytes 786440 | tf_op jit(solution)/shard_map/ppermute | solution.py:482
  62.1 4.5 %collective-permute-start.19 = (f32[128,512]{1,0:T(8,128)S(1)}, f32[128,512]{1,0:T(8,128)S(1)}, u32[]{:S(2)}, u32[]{:S(2)}) collective-permute-start(f32[128,512]{1,0:T(8,128)S(1)} %get-tuple-element.27), channel_id=1, source_target_pairs={{1,2},{2,1},{3,4},{4,3},{5,6},{6,5},{7,8},{8,7},{9,10},{10,9},{11,... | collective-permute-start | bytes 786440 | tf_op jit(solution)/shard_map/ppermute | solution.py:482
  66.6 0.1 collective-permute-start.16
  66.7 7.5 %collective-permute-done.16 = f32[13,8,128]{2,1,0:T(8,128)S(1)} collective-permute-done((f32[13,8,128]{2,1,0:T(8,128)S(1)}, f32[13,8,128]{2,1,0:T(8,128)S(1)}, u32[]{:S(2)}, u32[]{:S(2)}) %collective-permute-start.16) | collective-permute-done | bytes 53280 | tf_op jit(solution)/shard_map/ppermute | solution.py:474
  74.2 6.5 %collective-permute-start.20 = (f32[13,8,128]{2,1,0:T(8,128)S(1)}, f32[13,8,128]{2,1,0:T(8,128)S(1)}, u32[]{:S(2)}, u32[]{:S(2)}) collective-permute-start(f32[13,8,128]{2,1,0:T(8,128)S(1)} %add.54.mine), channel_id=1, source_target_pairs={{16,1},{1,16},{17,2},{2,17},{18,3},{3,18},{19,4},{4,19},{20,5},{5,... | collective-permute-start | bytes 159752 | tf_op jit(solution)/shard_map/ppermute | solution.py:491
  80.7 0.1 collective-permute-start.17
  80.8 1.7 %collective-permute-done.20.got = f32[13,8,128]{2,1,0:T(8,128)S(1)} collective-permute-done((f32[13,8,128]{2,1,0:T(8,128)S(1)}, f32[13,8,128]{2,1,0:T(8,128)S(1)}, u32[]{:S(2)}, u32[]{:S(2)}) %collective-permute-start.20) | collective-permute-done | bytes 53280 | tf_op jit(solution)/shard_map/ppermute | solution.py:491
  82.5 0.9 relax.3.old
  83.4 0.3 collective-permute-done.21.swapped
  83.7 2.3 %move_middle.3 = (f32[256,3072]{1,0:T(8,128)S(1)}, f32[256,2048]{1,0:T(8,128)S(1)}, f32[13,8,128]{2,1,0:T(8,128)S(1)}, f32[13,8,128]{2,1,0:T(8,128)S(1)}) custom-call(f32[256,3072]{1,0:T(8,128)S(1)} %relax.3.old, f32[128,512]{1,0:T(8,128)S(1)} %collective-permute-done.18.pair_a, ...), custom_call_target="tpu_custom_call", output_to_operand_aliasing={{0}: (0, {})} | custom-call | tf_op jit(solution)/shard_map/move_middle/pallas_call | solution.py:419
  86.0 0.3 collective-permute-start.22
  86.4 1.0 collective-permute-done.22
  87.4 1.3 %collective-permute-start.25 = (f32[13,8,128]{2,1,0:T(8,128)S(1)}, f32[13,8,128]{2,1,0:T(8,128)S(1)}, u32[]{:S(2)}, u32[]{:S(2)}) collective-permute-start(f32[13,8,128]{2,1,0:T(8,128)S(1)} %add.55), channel_id=1, source_target_pairs={{0,96},{16,112},{32,64},{48,80},{64,32},{80,48},{96,0},{112,16},{1... | collective-permute-start | bytes 159752 | tf_op jit(solution)/shard_map/ppermute | solution.py:467
  88.7 2.7 %collective-permute-start.24 = (f32[13,8,128]{2,1,0:T(8,128)S(1)}, f32[13,8,128]{2,1,0:T(8,128)S(1)}, u32[]{:S(2)}, u32[]{:S(2)}) collective-permute-start(f32[13,8,128]{2,1,0:T(8,128)S(1)} %add.55), channel_id=1, source_target_pairs={{0,32},{16,48},{32,0},{48,16},{64,96},{80,112},{96,64},{112,80},{1... | collective-permute-start | bytes 159752 | tf_op jit(solution)/shard_map/ppermute | solution.py:467
  91.3 1.5 %collective-permute-done.24 = f32[13,8,128]{2,1,0:T(8,128)S(1)} collective-permute-done((f32[13,8,128]{2,1,0:T(8,128)S(1)}, f32[13,8,128]{2,1,0:T(8,128)S(1)}, u32[]{:S(2)}, u32[]{:S(2)}) %collective-permute-start.24) | collective-permute-done | bytes 53280 | tf_op jit(solution)/shard_map/ppermute | solution.py:467
  92.8 3.0 %collective-permute-done.23 = f32[13,8,128]{2,1,0:T(8,128)S(1)} collective-permute-done((f32[13,8,128]{2,1,0:T(8,128)S(1)}, f32[13,8,128]{2,1,0:T(8,128)S(1)}, u32[]{:S(2)}, u32[]{:S(2)}) %collective-permute-start.23) | collective-permute-done | bytes 53280 | tf_op jit(solution)/shard_map/ppermute | solution.py:467
  95.8 2.3 %collective-permute-start.26 = (f32[13,8,128]{2,1,0:T(8,128)S(1)}, f32[13,8,128]{2,1,0:T(8,128)S(1)}, u32[]{:S(2)}, u32[]{:S(2)}) collective-permute-start(f32[13,8,128]{2,1,0:T(8,128)S(1)} %add_add_fusion), channel_id=1, source_target_pairs={{0,128},{16,144},{32,160},{48,176},{64,192},{80,208},{96,224},{112... | collective-permute-start | bytes 159752 | tf_op jit(solution)/shard_map/ppermute | solution.py:474
  98.1 2.3 %collective-permute-done.26 = f32[13,8,128]{2,1,0:T(8,128)S(1)} collective-permute-done((f32[13,8,128]{2,1,0:T(8,128)S(1)}, f32[13,8,128]{2,1,0:T(8,128)S(1)}, u32[]{:S(2)}, u32[]{:S(2)}) %collective-permute-start.26) | collective-permute-done | bytes 53280 | tf_op jit(solution)/shard_map/ppermute | solution.py:474
  100.4 3.2 %collective-permute-start.27 = (f32[13,8,128]{2,1,0:T(8,128)S(1)}, f32[13,8,128]{2,1,0:T(8,128)S(1)}, u32[]{:S(2)}, u32[]{:S(2)}) collective-permute-start(f32[13,8,128]{2,1,0:T(8,128)S(1)} %add.59.mine), channel_id=1, source_target_pairs={{0,16},{16,0},{32,48},{48,32},{64,80},{80,64},{96,112},{112,96},{1... | collective-permute-start | bytes 159752 | tf_op jit(solution)/shard_map/ppermute | solution.py:460
  103.6 0.9 collective-permute-done.27.other
  104.5 2.2 %relax_last.1 = f32[256,2048]{1,0:T(8,128)} custom-call(f32[256,2048]{1,0:T(8,128)S(1)} %get-tuple-element.28.moved, f32[13,8,128]{2,1,0:T(8,128)S(1)} %add.59.mine, f32[13,8,128]{2,1,0:T(8,128)S(1)} %collective-permute-done.27.other), custom_call_target="tpu_custom_call" | custom-call | tf_op jit(solution)/shard_map/relax_last/pallas_call | solution.py:448
  (36 shorter events, 0.2 us)
Async XLA Ops:
  1.1 11.2 %collective-permute-start.1 = (f32[128,512]{1,0:T(8,128)S(1)}, f32[128,512]{1,0:T(8,128)S(1)}, u32[]{:S(2)}, u32[]{:S(2)}) collective-permute-start(f32[128,512]{1,0:T(8,128)S(1)} %get-tuple-element.31), channel_id=1, source_target_pairs={{1,2},{2,1},{3,4},{4,3},{5,6},{6,5},{7,8},{8,7},{9,10},{10,9},{11,... | collective-permute-start | bytes 786440 | tf_op jit(solution)/shard_map/ppermute | solution.py:482
  5.7 13.2 %collective-permute-start = (f32[128,512]{1,0:T(8,128)S(1)}, f32[128,512]{1,0:T(8,128)S(1)}, u32[]{:S(2)}, u32[]{:S(2)}) collective-permute-start(f32[128,512]{1,0:T(8,128)S(1)} %get-tuple-element.32), channel_id=1, source_target_pairs={{0,1},{1,0},{2,3},{3,2},{4,5},{5,4},{6,7},{7,6},{8,9},{9,8},{10,11... | collective-permute-start | bytes 786440 | tf_op jit(solution)/shard_map/ppermute | solution.py:482
  18.9 1.6 %copy-start = (f32[256,2048]{1,0:T(8,128)S(1)}, f32[256,2048]{1,0:T(8,128)}, u32[]{:S(2)}) copy-start(f32[256,2048]{1,0:T(8,128)} %dist.1) | copy-start | bytes 6291460
  20.5 0.9 copy-start.1
  21.4 0.7 copy-start.2
  22.1 0.7 copy-start.4
  24.9 1.5 %collective-permute-start.2 = (f32[13,8,128]{2,1,0:T(8,128)S(1)}, f32[13,8,128]{2,1,0:T(8,128)S(1)}, u32[]{:S(2)}, u32[]{:S(2)}) collective-permute-start(f32[13,8,128]{2,1,0:T(8,128)S(1)} %get-tuple-element.20), channel_id=1, source_target_pairs={{0,16},{16,0},{32,48},{48,32},{64,80},{80,64},{96,112},{112,96},{1... | collective-permute-start | bytes 159752 | tf_op jit(solution)/shard_map/ppermute | solution.py:460
  26.4 7.3 %collective-permute-start.5 = (f32[13,8,128]{2,1,0:T(8,128)S(1)}, f32[13,8,128]{2,1,0:T(8,128)S(1)}, u32[]{:S(2)}, u32[]{:S(2)}) collective-permute-start(f32[13,8,128]{2,1,0:T(8,128)S(1)} %add.45), channel_id=1, source_target_pairs={{0,96},{16,112},{32,64},{48,80},{64,32},{80,48},{96,0},{112,16},{1... | collective-permute-start | bytes 159752 | tf_op jit(solution)/shard_map/ppermute | solution.py:467
  27.6 6.1 %collective-permute-start.4 = (f32[13,8,128]{2,1,0:T(8,128)S(1)}, f32[13,8,128]{2,1,0:T(8,128)S(1)}, u32[]{:S(2)}, u32[]{:S(2)}) collective-permute-start(f32[13,8,128]{2,1,0:T(8,128)S(1)} %add.45), channel_id=1, source_target_pairs={{0,32},{16,48},{32,0},{48,16},{64,96},{80,112},{96,64},{112,80},{1... | collective-permute-start | bytes 159752 | tf_op jit(solution)/shard_map/ppermute | solution.py:467
  29.2 4.6 %collective-permute-start.3 = (f32[13,8,128]{2,1,0:T(8,128)S(1)}, f32[13,8,128]{2,1,0:T(8,128)S(1)}, u32[]{:S(2)}, u32[]{:S(2)}) collective-permute-start(f32[13,8,128]{2,1,0:T(8,128)S(1)} %add.45), channel_id=1, source_target_pairs={{0,64},{16,80},{32,96},{48,112},{64,0},{80,16},{96,32},{112,48},{1... | collective-permute-start | bytes 159752 | tf_op jit(solution)/shard_map/ppermute | solution.py:467
  29.2 24.0 %collective-permute-start.8 = (f32[128,512]{1,0:T(8,128)S(1)}, f32[128,512]{1,0:T(8,128)S(1)}, u32[]{:S(2)}, u32[]{:S(2)}) collective-permute-start(f32[128,512]{1,0:T(8,128)S(1)} %get-tuple-element.21), channel_id=1, source_target_pairs={{0,1},{1,0},{2,3},{3,2},{4,5},{5,4},{6,7},{7,6},{8,9},{9,8},{10,11... | collective-permute-start | bytes 786440 | tf_op jit(solution)/shard_map/ppermute | solution.py:482
  29.2 24.0 %collective-permute-start.9 = (f32[128,512]{1,0:T(8,128)S(1)}, f32[128,512]{1,0:T(8,128)S(1)}, u32[]{:S(2)}, u32[]{:S(2)}) collective-permute-start(f32[128,512]{1,0:T(8,128)S(1)} %get-tuple-element.22), channel_id=1, source_target_pairs={{1,2},{2,1},{3,4},{4,3},{5,6},{6,5},{7,8},{8,7},{9,10},{10,9},{11,... | collective-permute-start | bytes 786440 | tf_op jit(solution)/shard_map/ppermute | solution.py:482
  33.8 9.4 %collective-permute-start.6 = (f32[13,8,128]{2,1,0:T(8,128)S(1)}, f32[13,8,128]{2,1,0:T(8,128)S(1)}, u32[]{:S(2)}, u32[]{:S(2)}) collective-permute-start(f32[13,8,128]{2,1,0:T(8,128)S(1)} %add_add_fusion.2), channel_id=1, source_target_pairs={{0,128},{16,144},{32,160},{48,176},{64,192},{80,208},{96,224},{112... | collective-permute-start | bytes 159752 | tf_op jit(solution)/shard_map/ppermute | solution.py:474
  43.2 9.0 %collective-permute-start.10 = (f32[13,8,128]{2,1,0:T(8,128)S(1)}, f32[13,8,128]{2,1,0:T(8,128)S(1)}, u32[]{:S(2)}, u32[]{:S(2)}) collective-permute-start(f32[13,8,128]{2,1,0:T(8,128)S(1)} %add.49.mine), channel_id=1, source_target_pairs={{16,1},{1,16},{17,2},{2,17},{18,3},{3,18},{19,4},{4,19},{20,5},{5,... | collective-permute-start | bytes 159752 | tf_op jit(solution)/shard_map/ppermute | solution.py:491
  50.4 1.8 %collective-permute-start.7 = (f32[13,8,128]{2,1,0:T(8,128)S(1)}, f32[13,8,128]{2,1,0:T(8,128)S(1)}, u32[]{:S(2)}, u32[]{:S(2)}) collective-permute-start(f32[13,8,128]{2,1,0:T(8,128)S(1)} %add.49.mine), channel_id=1, source_target_pairs={{0,16},{16,0},{32,48},{48,32},{64,80},{80,64},{96,112},{112,96},{1... | collective-permute-start | bytes 159752 | tf_op jit(solution)/shard_map/ppermute | solution.py:460
  52.2 1.2 %collective-permute-start.11 = (f32[13,8,128]{2,1,0:T(8,128)S(1)}, f32[13,8,128]{2,1,0:T(8,128)S(1)}, u32[]{:S(2)}, u32[]{:S(2)}) collective-permute-start(f32[13,8,128]{2,1,0:T(8,128)S(1)} %collective-permute-done.10.got), channel_id=1, source_target_pairs={{0,16},{16,0},{32,48},{48,32},{64,80},{80,64},{96,112},{112,96},{1... | collective-permute-start | bytes 159752 | tf_op jit(solution)/shard_map/ppermute | solution.py:460
  55.7 1.3 %collective-permute-start.12 = (f32[13,8,128]{2,1,0:T(8,128)S(1)}, f32[13,8,128]{2,1,0:T(8,128)S(1)}, u32[]{:S(2)}, u32[]{:S(2)}) collective-permute-start(f32[13,8,128]{2,1,0:T(8,128)S(1)} %get-tuple-element.25), channel_id=1, source_target_pairs={{0,16},{16,0},{32,48},{48,32},{64,80},{80,64},{96,112},{112,96},{1... | collective-permute-start | bytes 159752 | tf_op jit(solution)/shard_map/ppermute | solution.py:460
  57.0 9.6 %collective-permute-start.15 = (f32[13,8,128]{2,1,0:T(8,128)S(1)}, f32[13,8,128]{2,1,0:T(8,128)S(1)}, u32[]{:S(2)}, u32[]{:S(2)}) collective-permute-start(f32[13,8,128]{2,1,0:T(8,128)S(1)} %add.50), channel_id=1, source_target_pairs={{0,96},{16,112},{32,64},{48,80},{64,32},{80,48},{96,0},{112,16},{1... | collective-permute-start | bytes 159752 | tf_op jit(solution)/shard_map/ppermute | solution.py:467
  58.3 8.3 %collective-permute-start.14 = (f32[13,8,128]{2,1,0:T(8,128)S(1)}, f32[13,8,128]{2,1,0:T(8,128)S(1)}, u32[]{:S(2)}, u32[]{:S(2)}) collective-permute-start(f32[13,8,128]{2,1,0:T(8,128)S(1)} %add.50), channel_id=1, source_target_pairs={{0,32},{16,48},{32,0},{48,16},{64,96},{80,112},{96,64},{112,80},{1... | collective-permute-start | bytes 159752 | tf_op jit(solution)/shard_map/ppermute | solution.py:467
  60.9 5.6 %collective-permute-start.13 = (f32[13,8,128]{2,1,0:T(8,128)S(1)}, f32[13,8,128]{2,1,0:T(8,128)S(1)}, u32[]{:S(2)}, u32[]{:S(2)}) collective-permute-start(f32[13,8,128]{2,1,0:T(8,128)S(1)} %add.50), channel_id=1, source_target_pairs={{0,64},{16,80},{32,96},{48,112},{64,0},{80,16},{96,32},{112,48},{1... | collective-permute-start | bytes 159752 | tf_op jit(solution)/shard_map/ppermute | solution.py:467
  61.0 22.4 %collective-permute-start.18 = (f32[128,512]{1,0:T(8,128)S(1)}, f32[128,512]{1,0:T(8,128)S(1)}, u32[]{:S(2)}, u32[]{:S(2)}) collective-permute-start(f32[128,512]{1,0:T(8,128)S(1)} %get-tuple-element.26), channel_id=1, source_target_pairs={{0,1},{1,0},{2,3},{3,2},{4,5},{5,4},{6,7},{7,6},{8,9},{9,8},{10,11... | collective-permute-start | bytes 786440 | tf_op jit(solution)/shard_map/ppermute | solution.py:482
  62.1 21.3 %collective-permute-start.19 = (f32[128,512]{1,0:T(8,128)S(1)}, f32[128,512]{1,0:T(8,128)S(1)}, u32[]{:S(2)}, u32[]{:S(2)}) collective-permute-start(f32[128,512]{1,0:T(8,128)S(1)} %get-tuple-element.27), channel_id=1, source_target_pairs={{1,2},{2,1},{3,4},{4,3},{5,6},{6,5},{7,8},{8,7},{9,10},{10,9},{11,... | collective-permute-start | bytes 786440 | tf_op jit(solution)/shard_map/ppermute | solution.py:482
  66.6 7.6 %collective-permute-start.16 = (f32[13,8,128]{2,1,0:T(8,128)S(1)}, f32[13,8,128]{2,1,0:T(8,128)S(1)}, u32[]{:S(2)}, u32[]{:S(2)}) collective-permute-start(f32[13,8,128]{2,1,0:T(8,128)S(1)} %add_add_fusion.1), channel_id=1, source_target_pairs={{0,128},{16,144},{32,160},{48,176},{64,192},{80,208},{96,224},{112... | collective-permute-start | bytes 159752 | tf_op jit(solution)/shard_map/ppermute | solution.py:474
  74.2 8.3 %collective-permute-start.20 = (f32[13,8,128]{2,1,0:T(8,128)S(1)}, f32[13,8,128]{2,1,0:T(8,128)S(1)}, u32[]{:S(2)}, u32[]{:S(2)}) collective-permute-start(f32[13,8,128]{2,1,0:T(8,128)S(1)} %add.54.mine), channel_id=1, source_target_pairs={{16,1},{1,16},{17,2},{2,17},{18,3},{3,18},{19,4},{4,19},{20,5},{5,... | collective-permute-start | bytes 159752 | tf_op jit(solution)/shard_map/ppermute | solution.py:491
  80.7 1.8 %collective-permute-start.17 = (f32[13,8,128]{2,1,0:T(8,128)S(1)}, f32[13,8,128]{2,1,0:T(8,128)S(1)}, u32[]{:S(2)}, u32[]{:S(2)}) collective-permute-start(f32[13,8,128]{2,1,0:T(8,128)S(1)} %add.54.mine), channel_id=1, source_target_pairs={{0,16},{16,0},{32,48},{48,32},{64,80},{80,64},{96,112},{112,96},{1... | collective-permute-start | bytes 159752 | tf_op jit(solution)/shard_map/ppermute | solution.py:460
  82.5 1.2 %collective-permute-start.21 = (f32[13,8,128]{2,1,0:T(8,128)S(1)}, f32[13,8,128]{2,1,0:T(8,128)S(1)}, u32[]{:S(2)}, u32[]{:S(2)}) collective-permute-start(f32[13,8,128]{2,1,0:T(8,128)S(1)} %collective-permute-done.20.got), channel_id=1, source_target_pairs={{0,16},{16,0},{32,48},{48,32},{64,80},{80,64},{96,112},{112,96},{1... | collective-permute-start | bytes 159752 | tf_op jit(solution)/shard_map/ppermute | solution.py:460
  82.5 1.2 %copy-start.3 = (s32[2,512]{1,0:T(2,128)S(1)}, s32[2,512]{1,0:T(2,128)}, u32[]{:S(2)}) copy-start(s32[2,512]{1,0:T(2,128)} %kind.5) | copy-start | bytes 12292
  82.5 1.2 %copy-start.5 = (f32[256]{0:T(256)S(1)}, f32[256]{0:T(256)}, u32[]{:S(2)}) copy-start(f32[256]{0:T(256)} %param.7) | copy-start | bytes 3076
  86.0 1.3 %collective-permute-start.22 = (f32[13,8,128]{2,1,0:T(8,128)S(1)}, f32[13,8,128]{2,1,0:T(8,128)S(1)}, u32[]{:S(2)}, u32[]{:S(2)}) collective-permute-start(f32[13,8,128]{2,1,0:T(8,128)S(1)} %get-tuple-element.30), channel_id=1, source_target_pairs={{0,16},{16,0},{32,48},{48,32},{64,80},{80,64},{96,112},{112,96},{1... | collective-permute-start | bytes 159752 | tf_op jit(solution)/shard_map/ppermute | solution.py:460
  87.4 3.9 %collective-permute-start.25 = (f32[13,8,128]{2,1,0:T(8,128)S(1)}, f32[13,8,128]{2,1,0:T(8,128)S(1)}, u32[]{:S(2)}, u32[]{:S(2)}) collective-permute-start(f32[13,8,128]{2,1,0:T(8,128)S(1)} %add.55), channel_id=1, source_target_pairs={{0,96},{16,112},{32,64},{48,80},{64,32},{80,48},{96,0},{112,16},{1... | collective-permute-start | bytes 159752 | tf_op jit(solution)/shard_map/ppermute | solution.py:467
  88.7 4.2 %collective-permute-start.24 = (f32[13,8,128]{2,1,0:T(8,128)S(1)}, f32[13,8,128]{2,1,0:T(8,128)S(1)}, u32[]{:S(2)}, u32[]{:S(2)}) collective-permute-start(f32[13,8,128]{2,1,0:T(8,128)S(1)} %add.55), channel_id=1, source_target_pairs={{0,32},{16,48},{32,0},{48,16},{64,96},{80,112},{96,64},{112,80},{1... | collective-permute-start | bytes 159752 | tf_op jit(solution)/shard_map/ppermute | solution.py:467
  91.3 4.5 %collective-permute-start.23 = (f32[13,8,128]{2,1,0:T(8,128)S(1)}, f32[13,8,128]{2,1,0:T(8,128)S(1)}, u32[]{:S(2)}, u32[]{:S(2)}) collective-permute-start(f32[13,8,128]{2,1,0:T(8,128)S(1)} %add.55), channel_id=1, source_target_pairs={{0,64},{16,80},{32,96},{48,112},{64,0},{80,16},{96,32},{112,48},{1... | collective-permute-start | bytes 159752 | tf_op jit(solution)/shard_map/ppermute | solution.py:467
  95.8 4.6 %collective-permute-start.26 = (f32[13,8,128]{2,1,0:T(8,128)S(1)}, f32[13,8,128]{2,1,0:T(8,128)S(1)}, u32[]{:S(2)}, u32[]{:S(2)}) collective-permute-start(f32[13,8,128]{2,1,0:T(8,128)S(1)} %add_add_fusion), channel_id=1, source_target_pairs={{0,128},{16,144},{32,160},{48,176},{64,192},{80,208},{96,224},{112... | collective-permute-start | bytes 159752 | tf_op jit(solution)/shard_map/ppermute | solution.py:474
  100.4 4.1 %collective-permute-start.27 = (f32[13,8,128]{2,1,0:T(8,128)S(1)}, f32[13,8,128]{2,1,0:T(8,128)S(1)}, u32[]{:S(2)}, u32[]{:S(2)}) collective-permute-start(f32[13,8,128]{2,1,0:T(8,128)S(1)} %add.59.mine), channel_id=1, source_target_pairs={{0,16},{16,0},{32,48},{48,32},{64,80},{80,64},{96,112},{112,96},{1... | collective-permute-start | bytes 159752 | tf_op jit(solution)/shard_map/ppermute | solution.py:460

commit v3 on v2

--- a/solution.py
+++ b/solution.py
@@ -306,7 +306,7 @@
             coefs[k, first + t] = jnp.broadcast_to(value[t : t + 1], (8, 128))
 
 
-def finish(state, faces, sums, wall, kind, inflow, moved, mine, other, rims, count):
+def finish(state, faces, sums, kind, inflow, moved, mine, other, rims, count):
     iy = lax.axis_index("vel")
     position = lax.axis_index("gx")
     fill_ends(state, inflow, kind, position, count)
@@ -333,21 +333,24 @@
             rims[1][...] = moved[up]
 
 
-def first_kernel(count, dist, pair_a, pair_b, wall, kind, inflow, *refs):
-    moved, mine, other, rim_a, rim_b, state, faces, sums, sems = refs
-    iy = lax.axis_index("vel")
-    position = lax.axis_index("gx")
-    even = lax.rem(position, 2) == 0
+def prepare_kernel(count, dist, wall, state, faces, sem):
+    load = pltpu.make_async_copy(dist, state.at[:, pl.ds(SEC, DEPTH * SEC)], sem.at[0])
+    load.start()
+    forward = lax.axis_index("vel") >= VS // 2
+    prepare_masks(wall, faces, lax.axis_index("gx"), count, forward)
+    load.wait()
+
+
+def first_kernel(count, old, pair_a, pair_b, faces, kind, inflow, *refs):
+    state, moved, mine, other, rim_a, rim_b, sums, sems = refs
+    even = lax.rem(lax.axis_index("gx"), 2) == 0
     left = state.at[pl.ds(HALF, HALF), pl.ds(0, SEC)]
     right = state.at[pl.ds(0, HALF), pl.ds((DEPTH + 1) * SEC, SEC)]
-    main = pltpu.make_async_copy(dist, state.at[:, pl.ds(SEC, DEPTH * SEC)], sems.at[0])
-    main.start()
-    prepare_masks(wall, faces, position, count, iy >= VS // 2)
 
     def bring(one, two):
         copies = [
-            pltpu.make_async_copy(pair_a, one, sems.at[1]),
-            pltpu.make_async_copy(pair_b, two, sems.at[2]),
+            pltpu.make_async_copy(pair_a, one, sems.at[0]),
+            pltpu.make_async_copy(pair_b, two, sems.at[1]),
         ]
         for copy in copies:
             copy.start()
@@ -356,16 +359,13 @@
 
     pl.when(even)(lambda: bring(right, left))
     pl.when(~even)(lambda: bring(left, right))
-    main.wait()
-    finish(
-        state, faces, sums, wall, kind, inflow, moved, mine, other, (rim_a, rim_b), count
-    )
-
-
-def middle_kernel(count, rims, old, pair_a, pair_b, got, swapped, wall, kind, inflow, *refs):
+    finish(state, faces, sums, kind, inflow, moved, mine, other, (rim_a, rim_b), count)
+
+
+def middle_kernel(count, rims, old, pair_a, pair_b, got, swapped, faces, kind, inflow, *refs):
     state, moved, mine, other = refs[:4]
     out_rims = refs[4 : 4 + 2 * rims]
-    ghosts, coefs, lines, faces, sums, sems = refs[4 + 2 * rims :]
+    ghosts, coefs, lines, sums, sems = refs[4 + 2 * rims :]
     iy = lax.axis_index("vel")
     position = lax.axis_index("gx")
     odd = lax.rem(position, 2)
@@ -375,7 +375,6 @@
     ]
     for copy in copies:
         copy.start()
-    prepare_masks(wall, faces, position, count, iy >= VS // 2)
     sub = lax.broadcasted_iota(jnp.int32, (8, 128), 0)
     pick = (sub >= TILES) == (lax.rem(iy, 2) == 0)
     values = [jnp.where(pick, got[k], swapped[k]) for k in range(13)]
@@ -383,7 +382,7 @@
     for copy in copies:
         copy.wait()
     relax_ghosts(ghosts, coefs, lines, state)
-    finish(state, faces, sums, wall, kind, inflow, moved, mine, other, out_rims, count)
+    finish(state, faces, sums, kind, inflow, moved, mine, other, out_rims, count)
 
 
 VM = pl.BlockSpec(memory_space=pltpu.VMEM)
@@ -394,27 +393,38 @@
 WIDE = jax.ShapeDtypeStruct((ROWS, (DEPTH + 2) * SEC), F32)
 RIM = jax.ShapeDtypeStruct((HALF, SEC), F32)
 PART = jax.ShapeDtypeStruct((13, 8, 128), F32)
-FACES = pltpu.VMEM((5, DEPTH + 1, TILES, 8, 128), F32)
+FACES = jax.ShapeDtypeStruct((5, DEPTH + 1, TILES, 8, 128), F32)
 SUMS = pltpu.VMEM((8, OWN, 8, 128), F32)
 LINES = pltpu.VMEM((2, 3, 8, 128), F32)
 
 
-def move_first(dist, pair_a, pair_b, wall, kind, inflow, count):
-    outs = (WHOLE, PART, PART, RIM, RIM)
+def prepare(dist, wall, count):
+    return pl.pallas_call(
+        functools.partial(prepare_kernel, count),
+        out_shape=(WIDE, FACES),
+        in_specs=[ANY, VM],
+        out_specs=(VM, VM),
+        scratch_shapes=[pltpu.SemaphoreType.DMA((1,))],
+        compiler_params=pltpu.CompilerParams(vmem_limit_bytes=16 << 20),
+        name="prepare",
+    )(dist, wall)
+
+
+def move_first(state, pair_a, pair_b, faces, kind, inflow, count):
+    outs = (WIDE, WHOLE, PART, PART, RIM, RIM)
     return pl.pallas_call(
         functools.partial(first_kernel, count),
         out_shape=outs,
-        in_specs=[ANY, ANY, ANY, VM, VM, VM],
+        in_specs=[VM, ANY, ANY, VM, VM, VM],
         out_specs=(VM,) * len(outs),
-        scratch_shapes=[
-            pltpu.VMEM(WIDE.shape, F32), FACES, SUMS, pltpu.SemaphoreType.DMA((3,))
-        ],
+        input_output_aliases={0: 0},
+        scratch_shapes=[SUMS, pltpu.SemaphoreType.DMA((2,))],
         compiler_params=PARAMS,
         name="move_first",
-    )(dist, pair_a, pair_b, wall, kind, inflow)
-
-
-def move_middle(state, pairs, got, swapped, wall, kind, inflow, count, rims):
+    )(state, pair_a, pair_b, faces, kind, inflow)[1:]
+
+
+def move_middle(state, pairs, got, swapped, faces, kind, inflow, count, rims):
     outs = (WIDE, WHOLE, PART, PART) + (RIM, RIM) * rims
     return pl.pallas_call(
         functools.partial(middle_kernel, count, rims),
@@ -426,13 +436,12 @@
             pltpu.VMEM((2, HALF, SEC), F32),
             pltpu.VMEM((9, 8, 8, 128), F32),
             LINES,
-            FACES,
             SUMS,
             pltpu.SemaphoreType.DMA((2,)),
         ],
         compiler_params=PARAMS,
         name="move_middle",
-    )(state, *pairs, got, swapped, wall, kind, inflow)[1:]
+    )(state, *pairs, got, swapped, faces, kind, inflow)[1:]
 
 
 def relax_kernel(shift, moved, mine, other, state, coefs, lines):
@@ -467,11 +476,13 @@
     return lax.ppermute(array, "vel", [(i, mate(i)) for i in range(VS)])
 
 
-def all_moments(mine, other):
+def all_moments(mine, other, rims):
     value = mine + swap_cores(other)
+    value = value + lax.ppermute(value, "vel", [(i, i ^ 8) for i in range(VS)])
+    if rims:
+        value, *rims = lax.optimization_barrier((value, *rims))
     parts = [shift_x(value, by) for by in (1, 3, 2)]
-    value = (value + parts[2]) + (parts[0] + parts[1])
-    return value + lax.ppermute(value, "vel", [(i, i ^ 8) for i in range(VS)])
+    return (value + parts[2]) + (parts[0] + parts[1]), rims
 
 
 def swap_rims(pair_a, pair_b, count):
@@ -498,19 +509,20 @@
     up = distribution[HALF:, (DEPTH - 1) * SEC :]
     down = distribution[:HALF, :SEC]
     pairs = swap_rims(jnp.where(even, up, down), jnp.where(even, down, up), count)
-    outs = move_first(distribution, *pairs, wall_mask, boundary_kind, inflow, count)
+    state, faces = prepare(distribution, wall_mask, count)
+    outs = move_first(state, *pairs, faces, boundary_kind, inflow, count)
     for step in range(STEPS):
         moved, mine, other = outs[:3]
         last = step + 1 == STEPS
-        if not last:
-            pairs = swap_rims(outs[3], outs[4], count)
-        half = all_moments(mine, other)
+        half, rims = all_moments(mine, other, outs[3:])
         if last:
             return relaxed(moved, half, swap_cores(half), True)
+        pairs = swap_rims(*rims, count)
         halo = swap_moments(half, count)
         state = relaxed(moved, half, swap_cores(half), False)
+        halo, state = lax.optimization_barrier((halo, state))
         outs = move_middle(
-            state, pairs, halo, swap_cores(halo), wall_mask, boundary_kind, inflow, count,
+            state, pairs, halo, swap_cores(halo), faces, boundary_kind, inflow, count,
             rims=step + 2 < STEPS,
         )
 

time: 108 us -> 96.8 us (0.90)
  waiting for transfers between devices: 42.3 us -> 36.5 us
  starting transfers between devices: 48.5 us -> 45.3 us
  local copies, waits for them, and re-layouts: 3.87 us -> 2.5 us
    ppermute x3, waiting for transfers between devices: 17 us -> 7.21 us  [all_moments(): value = value + lax.ppermute(value, 'vel', [(i, i ^ 8) for i in range(VS)])]
    ppermute x2, starting transfers between devices: 13.7 us -> 6.38 us  [swap_moments(): return lax.ppermute(half, ('vel', 'gx'), pairs)]
    ppermute x8, starting transfers between devices: 4.63 us -> 10.6 us  [swap_cores(): return lax.ppermute(array, 'vel', [(i, i ^ 1) for i in range(VS)])]
    ppermute x2, waiting for transfers between devices: 3.41 us -> 6.89 us  [swap_moments(): return lax.ppermute(half, ('vel', 'gx'), pairs)]
    ppermute x6, waiting for transfers between devices: 13.1 us -> 10.3 us  [swap_rims(): return (lax.ppermute(pair_a, 'gx', near), lax.ppermute(pair_b, 'gx', far))]
    ppermute x6, starting transfers between devices: 14.9 us -> 12.5 us  [swap_rims(): return (lax.ppermute(pair_a, 'gx', near), lax.ppermute(pair_b, 'gx', far))]
    ppermute x8, waiting for transfers between devices: 4.32 us -> 6.4 us  [swap_cores(): return lax.ppermute(array, 'vel', [(i, i ^ 1) for i in range(VS)])]
    ppermute x3, starting transfers between devices: 4.61 us -> 6.47 us  [all_moments(): value = value + lax.ppermute(value, 'vel', [(i, i ^ 8) for i in range(VS)])]
  transfers between devices with their start and end apart: 28 -> 28, of which waited for: 15 -> 17; matrix products, arithmetic and copies ran while one was open for 0% -> 0% of each run, Pallas kernels for 2% -> 2%
where the time goes in v3:
time: 96.8 us; the launch traced here: 96 us
  starting transfers between devices  45.3 us (47%)
  waiting for transfers between devices  36.5 us (38%)
  Pallas kernels  10.3 us (11%)
  local copies, waits for them, and re-layouts  2.5 us (3%)
  other arithmetic  1.19 us (1%)
    ppermute x6, starting transfers between devices, swap_rims(): return (lax.ppermute(pair_a, 'gx', near), lax.ppermute(pair_b, 'gx', far))  12.5 us
    ppermute x8, starting transfers between devices, swap_cores(): return lax.ppermute(array, 'vel', [(i, i ^ 1) for i in range(VS)])  10.6 us
    ppermute x6, waiting for transfers between devices, swap_rims(): return (lax.ppermute(pair_a, 'gx', near), lax.ppermute(pair_b, 'gx', far))  10.3 us
    ppermute x9, starting transfers between devices, shift_x(): return lax.ppermute(array, 'vel', [(i, mate(i)) for i in range(VS)])  9.34 us
    ppermute x3, waiting for transfers between devices, all_moments(): value = value + lax.ppermute(value, 'vel', [(i, i ^ 8) for i in range(VS)])  7.21 us
    ppermute x2, waiting for transfers between devices, swap_moments(): return lax.ppermute(half, ('vel', 'gx'), pairs)  6.89 us
    ppermute x3, starting transfers between devices, all_moments(): value = value + lax.ppermute(value, 'vel', [(i, i ^ 8) for i in range(VS)])  6.47 us
    ppermute x8, waiting for transfers between devices, swap_cores(): return lax.ppermute(array, 'vel', [(i, i ^ 1) for i in range(VS)])  6.4 us
  transfers between devices with their start and end apart: 28, of which 17 were waited for; matrix products, arithmetic and copies ran while one was open for 0% of the time, Pallas kernels for 2%

profile of v3, /device:TPU:107, one launch (start us, length us, event | category | flops | bytes accessed | tf_op | source)
XLA Modules:
  0.0 96.0 jit_solution(948238603588112748)
XLA Ops:
  0.0 1.1 %slice_select_fusion = (f32[128,512]{1,0:T(8,128)S(1)}, f32[128,512]{1,0:T(8,128)S(1)}) fusion(f32[256,2048]{1,0:T(8,128)} %dist.1, pred[]{:T(512)S(6)} %eq.3), kind=kLoop, calls=%fused_computation | loop fusion | flops 131072 | bytes 1048577 | tf_op jit(solution)/shard_map/jit(_where)/select_n | solution.py:511
  1.1 4.6 %collective-permute-start.1 = (f32[128,512]{1,0:T(8,128)S(1)}, f32[128,512]{1,0:T(8,128)S(1)}, u32[]{:S(2)}, u32[]{:S(2)}) collective-permute-start(f32[128,512]{1,0:T(8,128)S(1)} %get-tuple-element.55), channel_id=1, source_target_pairs={{1,2},{2,1},{3,4},{4,3},{5,6},{6,5},{7,8},{8,7},{9,10},{10,9},{11,... | collective-permute-start | bytes 786440 | tf_op jit(solution)/shard_map/ppermute | solution.py:493
  5.8 0.1 collective-permute-start
  5.9 1.6 %copy-done = f32[256,2048]{1,0:T(8,128)S(1)} copy-done((f32[256,2048]{1,0:T(8,128)S(1)}, f32[256,2048]{1,0:T(8,128)}, u32[]{:S(2)}) %copy-start) | copy-done | bytes 2097176
  7.4 0.9 copy-done.1
  8.4 0.3 prepare.1
  8.7 3.6 %collective-permute-done.1.pair_b = f32[128,512]{1,0:T(8,128)S(1)} collective-permute-done((f32[128,512]{1,0:T(8,128)S(1)}, f32[128,512]{1,0:T(8,128)S(1)}, u32[]{:S(2)}, u32[]{:S(2)}) %collective-permute-start.1) | collective-permute-done | bytes 262176 | tf_op jit(solution)/shard_map/ppermute | solution.py:493
  12.3 6.6 %collective-permute-done.pair_a = f32[128,512]{1,0:T(8,128)S(1)} collective-permute-done((f32[128,512]{1,0:T(8,128)S(1)}, f32[128,512]{1,0:T(8,128)S(1)}, u32[]{:S(2)}, u32[]{:S(2)}) %collective-permute-start) | collective-permute-done | bytes 262176 | tf_op jit(solution)/shard_map/ppermute | solution.py:493
  19.0 1.8 %move_first.1 = (f32[256,3072]{1,0:T(8,128)S(1)}, f32[256,2048]{1,0:T(8,128)S(1)}, f32[13,8,128]{2,1,0:T(8,128)S(1)}, f32[13,8,128]{2,1,0:T(8,128)S(1)}, f32[128,512]{1,0:T(8,128)S(1)}, /*index=5*/f32[128,512]{1,0:T(8,128)S(1)}) custom-call(f32[256,3072]{1,0:T(8,128)S(1)} %get-tuple-element.30.old, ...), custom_call_target="tpu_custom_call", output_to_operand_aliasing={{0}: (0, {})} | custom-call | tf_op jit(solution)/shard_map/move_first/pallas_call | solution.py:415
  20.8 0.6 collective-permute-start.2
  21.3 0.9 collective-permute-done.2
  22.2 2.1 %collective-permute-start.3 = (f32[13,8,128]{2,1,0:T(8,128)S(1)}, f32[13,8,128]{2,1,0:T(8,128)S(1)}, u32[]{:S(2)}, u32[]{:S(2)}) collective-permute-start(f32[13,8,128]{2,1,0:T(8,128)S(1)} %add.45), channel_id=1, source_target_pairs={{0,128},{16,144},{32,160},{48,176},{64,192},{80,208},{96,224},{112... | collective-permute-start | bytes 159752 | tf_op jit(solution)/shard_map/ppermute | solution.py:481
  24.3 2.5 %collective-permute-done.3 = f32[13,8,128]{2,1,0:T(8,128)S(1)} collective-permute-done((f32[13,8,128]{2,1,0:T(8,128)S(1)}, f32[13,8,128]{2,1,0:T(8,128)S(1)}, u32[]{:S(2)}, u32[]{:S(2)}) %collective-permute-start.3) | collective-permute-done | bytes 53280 | tf_op jit(solution)/shard_map/ppermute | solution.py:481
  26.8 1.3 %collective-permute-start.6 = (f32[13,8,128]{2,1,0:T(8,128)S(1)}, f32[13,8,128]{2,1,0:T(8,128)S(1)}, u32[]{:S(2)}, u32[]{:S(2)}) collective-permute-start(f32[13,8,128]{2,1,0:T(8,128)S(1)} %add.46), channel_id=1, source_target_pairs={{0,96},{16,112},{32,64},{48,80},{64,32},{80,48},{96,0},{112,16},{1... | collective-permute-start | bytes 159752 | tf_op jit(solution)/shard_map/ppermute | solution.py:476
  28.1 1.5 %collective-permute-start.5 = (f32[13,8,128]{2,1,0:T(8,128)S(1)}, f32[13,8,128]{2,1,0:T(8,128)S(1)}, u32[]{:S(2)}, u32[]{:S(2)}) collective-permute-start(f32[13,8,128]{2,1,0:T(8,128)S(1)} %add.46), channel_id=1, source_target_pairs={{0,32},{16,48},{32,0},{48,16},{64,96},{80,112},{96,64},{112,80},{1... | collective-permute-start | bytes 159752 | tf_op jit(solution)/shard_map/ppermute | solution.py:476
  29.6 4.6 %collective-permute-start.10 = (f32[128,512]{1,0:T(8,128)S(1)}, f32[128,512]{1,0:T(8,128)S(1)}, u32[]{:S(2)}, u32[]{:S(2)}) collective-permute-start(f32[128,512]{1,0:T(8,128)S(1)} %get-tuple-element.40), channel_id=1, source_target_pairs={{1,2},{2,1},{3,4},{4,3},{5,6},{6,5},{7,8},{8,7},{9,10},{10,9},{11,... | collective-permute-start | bytes 786440 | tf_op jit(solution)/shard_map/ppermute | solution.py:493
  34.2 3.2 %collective-permute-start.8 = (f32[13,8,128]{2,1,0:T(8,128)S(1)}, f32[13,8,128]{2,1,0:T(8,128)S(1)}, u32[]{:S(2)}, u32[]{:S(2)}) collective-permute-start(f32[13,8,128]{2,1,0:T(8,128)S(1)} %add_add_fusion.2.mine), channel_id=1, source_target_pairs={{0,16},{16,0},{32,48},{48,32},{64,80},{80,64},{96,112},{112,96},{1... | collective-permute-start | bytes 159752 | tf_op jit(solution)/shard_map/ppermute | solution.py:469
  37.4 3.4 %collective-permute-start.7 = (f32[13,8,128]{2,1,0:T(8,128)S(1)}, f32[13,8,128]{2,1,0:T(8,128)S(1)}, u32[]{:S(2)}, u32[]{:S(2)}) collective-permute-start(f32[13,8,128]{2,1,0:T(8,128)S(1)} %add_add_fusion.2.mine), channel_id=1, source_target_pairs={{16,1},{1,16},{17,2},{2,17},{18,3},{3,18},{19,4},{4,19},{20,5},{5,... | collective-permute-start | bytes 159752 | tf_op jit(solution)/shard_map/ppermute | solution.py:502
  40.8 0.9 relax.2.old
  41.7 3.3 %collective-permute-done.7.got = f32[13,8,128]{2,1,0:T(8,128)S(1)} collective-permute-done((f32[13,8,128]{2,1,0:T(8,128)S(1)}, f32[13,8,128]{2,1,0:T(8,128)S(1)}, u32[]{:S(2)}, u32[]{:S(2)}) %collective-permute-start.7) | collective-permute-done | bytes 53280 | tf_op jit(solution)/shard_map/ppermute | solution.py:502
  45.0 1.2 %collective-permute-done.11.swapped = f32[13,8,128]{2,1,0:T(8,128)S(1)} collective-permute-done((f32[13,8,128]{2,1,0:T(8,128)S(1)}, f32[13,8,128]{2,1,0:T(8,128)S(1)}, u32[]{:S(2)}, u32[]{:S(2)}) %collective-permute-start.11) | collective-permute-done | bytes 53280 | tf_op jit(solution)/shard_map/ppermute | solution.py:469
  46.2 2.0 %move_middle.2 = (f32[256,3072]{1,0:T(8,128)S(1)}, f32[256,2048]{1,0:T(8,128)S(1)}, f32[13,8,128]{2,1,0:T(8,128)S(1)}, f32[13,8,128]{2,1,0:T(8,128)S(1)}, f32[12...) custom-call(f32[256,3072]{1,0:T(8,128)S(1)} %relax.2.old, ...), custom_call_target="tpu_custom_call", output_to_operand_aliasing={{0}: (0, {})} | custom-call | tf_op jit(solution)/shard_map/move_middle/pallas_call | solution.py:429
  48.3 0.2 collective-permute-start.12
  48.5 1.1 %collective-permute-done.12 = f32[13,8,128]{2,1,0:T(8,128)S(1)} collective-permute-done((f32[13,8,128]{2,1,0:T(8,128)S(1)}, f32[13,8,128]{2,1,0:T(8,128)S(1)}, u32[]{:S(2)}, u32[]{:S(2)}) %collective-permute-start.12) | collective-permute-done | bytes 53280 | tf_op jit(solution)/shard_map/ppermute | solution.py:469
  49.6 2.1 %collective-permute-start.13 = (f32[13,8,128]{2,1,0:T(8,128)S(1)}, f32[13,8,128]{2,1,0:T(8,128)S(1)}, u32[]{:S(2)}, u32[]{:S(2)}) collective-permute-start(f32[13,8,128]{2,1,0:T(8,128)S(1)} %add.50), channel_id=1, source_target_pairs={{0,128},{16,144},{32,160},{48,176},{64,192},{80,208},{96,224},{112... | collective-permute-start | bytes 159752 | tf_op jit(solution)/shard_map/ppermute | solution.py:481
  51.7 2.5 %collective-permute-done.13 = f32[13,8,128]{2,1,0:T(8,128)S(1)} collective-permute-done((f32[13,8,128]{2,1,0:T(8,128)S(1)}, f32[13,8,128]{2,1,0:T(8,128)S(1)}, u32[]{:S(2)}, u32[]{:S(2)}) %collective-permute-start.13) | collective-permute-done | bytes 53280 | tf_op jit(solution)/shard_map/ppermute | solution.py:481
  54.2 1.0 %collective-permute-start.16 = (f32[13,8,128]{2,1,0:T(8,128)S(1)}, f32[13,8,128]{2,1,0:T(8,128)S(1)}, u32[]{:S(2)}, u32[]{:S(2)}) collective-permute-start(f32[13,8,128]{2,1,0:T(8,128)S(1)} %add.51), channel_id=1, source_target_pairs={{0,96},{16,112},{32,64},{48,80},{64,32},{80,48},{96,0},{112,16},{1... | collective-permute-start | bytes 159752 | tf_op jit(solution)/shard_map/ppermute | solution.py:476
  55.2 2.7 %collective-permute-start.15 = (f32[13,8,128]{2,1,0:T(8,128)S(1)}, f32[13,8,128]{2,1,0:T(8,128)S(1)}, u32[]{:S(2)}, u32[]{:S(2)}) collective-permute-start(f32[13,8,128]{2,1,0:T(8,128)S(1)} %add.51), channel_id=1, source_target_pairs={{0,32},{16,48},{32,0},{48,16},{64,96},{80,112},{96,64},{112,80},{1... | collective-permute-start | bytes 159752 | tf_op jit(solution)/shard_map/ppermute | solution.py:476
  58.0 3.2 %collective-permute-start.20 = (f32[128,512]{1,0:T(8,128)S(1)}, f32[128,512]{1,0:T(8,128)S(1)}, u32[]{:S(2)}, u32[]{:S(2)}) collective-permute-start(f32[128,512]{1,0:T(8,128)S(1)} %get-tuple-element.50), channel_id=1, source_target_pairs={{1,2},{2,1},{3,4},{4,3},{5,6},{6,5},{7,8},{8,7},{9,10},{10,9},{11,... | collective-permute-start | bytes 786440 | tf_op jit(solution)/shard_map/ppermute | solution.py:493
  61.2 1.2 %collective-permute-done.14 = f32[13,8,128]{2,1,0:T(8,128)S(1)} collective-permute-done((f32[13,8,128]{2,1,0:T(8,128)S(1)}, f32[13,8,128]{2,1,0:T(8,128)S(1)}, u32[]{:S(2)}, u32[]{:S(2)}) %collective-permute-start.14) | collective-permute-done | bytes 53280 | tf_op jit(solution)/shard_map/ppermute | solution.py:476
  62.5 3.1 %collective-permute-start.18 = (f32[13,8,128]{2,1,0:T(8,128)S(1)}, f32[13,8,128]{2,1,0:T(8,128)S(1)}, u32[]{:S(2)}, u32[]{:S(2)}) collective-permute-start(f32[13,8,128]{2,1,0:T(8,128)S(1)} %add_add_fusion.1.mine), channel_id=1, source_target_pairs={{0,16},{16,0},{32,48},{48,32},{64,80},{80,64},{96,112},{112,96},{1... | collective-permute-start | bytes 159752 | tf_op jit(solution)/shard_map/ppermute | solution.py:469
  65.6 3.0 %collective-permute-start.17 = (f32[13,8,128]{2,1,0:T(8,128)S(1)}, f32[13,8,128]{2,1,0:T(8,128)S(1)}, u32[]{:S(2)}, u32[]{:S(2)}) collective-permute-start(f32[13,8,128]{2,1,0:T(8,128)S(1)} %add_add_fusion.1.mine), channel_id=1, source_target_pairs={{16,1},{1,16},{17,2},{2,17},{18,3},{3,18},{19,4},{4,19},{20,5},{5,... | collective-permute-start | bytes 159752 | tf_op jit(solution)/shard_map/ppermute | solution.py:502
  68.6 0.9 relax.3.old
  69.5 3.6 %collective-permute-done.17.got = f32[13,8,128]{2,1,0:T(8,128)S(1)} collective-permute-done((f32[13,8,128]{2,1,0:T(8,128)S(1)}, f32[13,8,128]{2,1,0:T(8,128)S(1)}, u32[]{:S(2)}, u32[]{:S(2)}) %collective-permute-start.17) | collective-permute-done | bytes 53280 | tf_op jit(solution)/shard_map/ppermute | solution.py:502
  73.1 1.2 %collective-permute-done.21.swapped = f32[13,8,128]{2,1,0:T(8,128)S(1)} collective-permute-done((f32[13,8,128]{2,1,0:T(8,128)S(1)}, f32[13,8,128]{2,1,0:T(8,128)S(1)}, u32[]{:S(2)}, u32[]{:S(2)}) %collective-permute-start.21) | collective-permute-done | bytes 53280 | tf_op jit(solution)/shard_map/ppermute | solution.py:469
  74.4 2.2 %move_middle.3 = (f32[256,3072]{1,0:T(8,128)S(1)}, f32[256,2048]{1,0:T(8,128)S(1)}, f32[13,8,128]{2,1,0:T(8,128)S(1)}, f32[13,8,128]{2,1,0:T(8,128)S(1)}) custom-call(f32[256,3072]{1,0:T(8,128)S(1)} %relax.3.old, f32[128,512]{1,0:T(8,128)S(1)} %collective-permute-done.19.pair_a, ...), custom_call_target="tpu_custom_call", output_to_operand_aliasing={{0}: (0, {})} | custom-call | tf_op jit(solution)/shard_map/move_middle/pallas_call | solution.py:429
  76.5 0.2 collective-permute-start.22
  76.8 1.1 %collective-permute-done.22 = f32[13,8,128]{2,1,0:T(8,128)S(1)} collective-permute-done((f32[13,8,128]{2,1,0:T(8,128)S(1)}, f32[13,8,128]{2,1,0:T(8,128)S(1)}, u32[]{:S(2)}, u32[]{:S(2)}) %collective-permute-start.22) | collective-permute-done | bytes 53280 | tf_op jit(solution)/shard_map/ppermute | solution.py:469
  77.9 2.3 %collective-permute-start.23 = (f32[13,8,128]{2,1,0:T(8,128)S(1)}, f32[13,8,128]{2,1,0:T(8,128)S(1)}, u32[]{:S(2)}, u32[]{:S(2)}) collective-permute-start(f32[13,8,128]{2,1,0:T(8,128)S(1)} %add.55), channel_id=1, source_target_pairs={{0,128},{16,144},{32,160},{48,176},{64,192},{80,208},{96,224},{112... | collective-permute-start | bytes 159752 | tf_op jit(solution)/shard_map/ppermute | solution.py:481
  80.2 2.3 %collective-permute-done.23 = f32[13,8,128]{2,1,0:T(8,128)S(1)} collective-permute-done((f32[13,8,128]{2,1,0:T(8,128)S(1)}, f32[13,8,128]{2,1,0:T(8,128)S(1)}, u32[]{:S(2)}, u32[]{:S(2)}) %collective-permute-start.23) | collective-permute-done | bytes 53280 | tf_op jit(solution)/shard_map/ppermute | solution.py:481
  82.5 0.3 collective-permute-start.26
  82.7 2.5 %collective-permute-start.25 = (f32[13,8,128]{2,1,0:T(8,128)S(1)}, f32[13,8,128]{2,1,0:T(8,128)S(1)}, u32[]{:S(2)}, u32[]{:S(2)}) collective-permute-start(f32[13,8,128]{2,1,0:T(8,128)S(1)} %add.56), channel_id=1, source_target_pairs={{0,32},{16,48},{32,0},{48,16},{64,96},{80,112},{96,64},{112,80},{1... | collective-permute-start | bytes 159752 | tf_op jit(solution)/shard_map/ppermute | solution.py:476
  85.2 0.3 collective-permute-done.26
  85.5 1.5 %collective-permute-done.25 = f32[13,8,128]{2,1,0:T(8,128)S(1)} collective-permute-done((f32[13,8,128]{2,1,0:T(8,128)S(1)}, f32[13,8,128]{2,1,0:T(8,128)S(1)}, u32[]{:S(2)}, u32[]{:S(2)}) %collective-permute-start.25) | collective-permute-done | bytes 53280 | tf_op jit(solution)/shard_map/ppermute | solution.py:476
  87.0 2.7 %collective-permute-done.24 = f32[13,8,128]{2,1,0:T(8,128)S(1)} collective-permute-done((f32[13,8,128]{2,1,0:T(8,128)S(1)}, f32[13,8,128]{2,1,0:T(8,128)S(1)}, u32[]{:S(2)}, u32[]{:S(2)}) %collective-permute-start.24) | collective-permute-done | bytes 53280 | tf_op jit(solution)/shard_map/ppermute | solution.py:476
  89.7 3.2 %collective-permute-start.27 = (f32[13,8,128]{2,1,0:T(8,128)S(1)}, f32[13,8,128]{2,1,0:T(8,128)S(1)}, u32[]{:S(2)}, u32[]{:S(2)}) collective-permute-start(f32[13,8,128]{2,1,0:T(8,128)S(1)} %add_add_fusion.mine), channel_id=1, source_target_pairs={{0,16},{16,0},{32,48},{48,32},{64,80},{80,64},{96,112},{112,96},{1... | collective-permute-start | bytes 159752 | tf_op jit(solution)/shard_map/ppermute | solution.py:469
  92.9 0.9 collective-permute-done.27.other
  93.8 2.2 %relax_last.1 = f32[256,2048]{1,0:T(8,128)} custom-call(f32[256,2048]{1,0:T(8,128)S(1)} %get-tuple-element.52.moved, f32[13,8,128]{2,1,0:T(8,128)S(1)} %add_add_fusion.mine, f32[13,8,128]{2,1,0:T(8,128)S(1)} %collective-permute-done.27.other), custom_call_target="tpu_custom_call" | custom-call | tf_op jit(solution)/shard_map/relax_last/pallas_call | solution.py:457
  (33 shorter events, 0.2 us)
Async XLA Ops:
  0.0 19.0 %copy-start.2 = (s32[2,512]{1,0:T(2,128)S(1)}, s32[2,512]{1,0:T(2,128)}, u32[]{:S(2)}) copy-start(s32[2,512]{1,0:T(2,128)} %kind.5) | copy-start | bytes 12292
  0.0 19.0 %copy-start.3 = (f32[256]{0:T(256)S(1)}, f32[256]{0:T(256)}, u32[]{:S(2)}) copy-start(f32[256]{0:T(256)} %param.7) | copy-start | bytes 3076
  1.1 11.2 %collective-permute-start.1 = (f32[128,512]{1,0:T(8,128)S(1)}, f32[128,512]{1,0:T(8,128)S(1)}, u32[]{:S(2)}, u32[]{:S(2)}) collective-permute-start(f32[128,512]{1,0:T(8,128)S(1)} %get-tuple-element.55), channel_id=1, source_target_pairs={{1,2},{2,1},{3,4},{4,3},{5,6},{6,5},{7,8},{8,7},{9,10},{10,9},{11,... | collective-permute-start | bytes 786440 | tf_op jit(solution)/shard_map/ppermute | solution.py:493
  5.8 13.2 %collective-permute-start = (f32[128,512]{1,0:T(8,128)S(1)}, f32[128,512]{1,0:T(8,128)S(1)}, u32[]{:S(2)}, u32[]{:S(2)}) collective-permute-start(f32[128,512]{1,0:T(8,128)S(1)} %get-tuple-element.56), channel_id=1, source_target_pairs={{0,1},{1,0},{2,3},{3,2},{4,5},{5,4},{6,7},{7,6},{8,9},{9,8},{10,11... | collective-permute-start | bytes 786440 | tf_op jit(solution)/shard_map/ppermute | solution.py:493
  5.9 1.6 %copy-start = (f32[256,2048]{1,0:T(8,128)S(1)}, f32[256,2048]{1,0:T(8,128)}, u32[]{:S(2)}) copy-start(f32[256,2048]{1,0:T(8,128)} %dist.1) | copy-start | bytes 6291460
  7.4 0.9 copy-start.1
  20.8 1.5 %collective-permute-start.2 = (f32[13,8,128]{2,1,0:T(8,128)S(1)}, f32[13,8,128]{2,1,0:T(8,128)S(1)}, u32[]{:S(2)}, u32[]{:S(2)}) collective-permute-start(f32[13,8,128]{2,1,0:T(8,128)S(1)} %get-tuple-element.33), channel_id=1, source_target_pairs={{0,16},{16,0},{32,48},{48,32},{64,80},{80,64},{96,112},{112,96},{1... | collective-permute-start | bytes 159752 | tf_op jit(solution)/shard_map/ppermute | solution.py:469
  22.2 4.5 %collective-permute-start.3 = (f32[13,8,128]{2,1,0:T(8,128)S(1)}, f32[13,8,128]{2,1,0:T(8,128)S(1)}, u32[]{:S(2)}, u32[]{:S(2)}) collective-permute-start(f32[13,8,128]{2,1,0:T(8,128)S(1)} %add.45), channel_id=1, source_target_pairs={{0,128},{16,144},{32,160},{48,176},{64,192},{80,208},{96,224},{112... | collective-permute-start | bytes 159752 | tf_op jit(solution)/shard_map/ppermute | solution.py:481
  26.8 7.4 %collective-permute-start.6 = (f32[13,8,128]{2,1,0:T(8,128)S(1)}, f32[13,8,128]{2,1,0:T(8,128)S(1)}, u32[]{:S(2)}, u32[]{:S(2)}) collective-permute-start(f32[13,8,128]{2,1,0:T(8,128)S(1)} %add.46), channel_id=1, source_target_pairs={{0,96},{16,112},{32,64},{48,80},{64,32},{80,48},{96,0},{112,16},{1... | collective-permute-start | bytes 159752 | tf_op jit(solution)/shard_map/ppermute | solution.py:476
  28.1 6.1 %collective-permute-start.5 = (f32[13,8,128]{2,1,0:T(8,128)S(1)}, f32[13,8,128]{2,1,0:T(8,128)S(1)}, u32[]{:S(2)}, u32[]{:S(2)}) collective-permute-start(f32[13,8,128]{2,1,0:T(8,128)S(1)} %add.46), channel_id=1, source_target_pairs={{0,32},{16,48},{32,0},{48,16},{64,96},{80,112},{96,64},{112,80},{1... | collective-permute-start | bytes 159752 | tf_op jit(solution)/shard_map/ppermute | solution.py:476
  29.6 4.6 %collective-permute-start.4 = (f32[13,8,128]{2,1,0:T(8,128)S(1)}, f32[13,8,128]{2,1,0:T(8,128)S(1)}, u32[]{:S(2)}, u32[]{:S(2)}) collective-permute-start(f32[13,8,128]{2,1,0:T(8,128)S(1)} %add.46), channel_id=1, source_target_pairs={{0,64},{16,80},{32,96},{48,112},{64,0},{80,16},{96,32},{112,48},{1... | collective-permute-start | bytes 159752 | tf_op jit(solution)/shard_map/ppermute | solution.py:476
  29.6 16.6 %collective-permute-start.9 = (f32[128,512]{1,0:T(8,128)S(1)}, f32[128,512]{1,0:T(8,128)S(1)}, u32[]{:S(2)}, u32[]{:S(2)}) collective-permute-start(f32[128,512]{1,0:T(8,128)S(1)} %get-tuple-element.39), channel_id=1, source_target_pairs={{0,1},{1,0},{2,3},{3,2},{4,5},{5,4},{6,7},{7,6},{8,9},{9,8},{10,11... | collective-permute-start | bytes 786440 | tf_op jit(solution)/shard_map/ppermute | solution.py:493
  29.6 16.6 %collective-permute-start.10 = (f32[128,512]{1,0:T(8,128)S(1)}, f32[128,512]{1,0:T(8,128)S(1)}, u32[]{:S(2)}, u32[]{:S(2)}) collective-permute-start(f32[128,512]{1,0:T(8,128)S(1)} %get-tuple-element.40), channel_id=1, source_target_pairs={{1,2},{2,1},{3,4},{4,3},{5,6},{6,5},{7,8},{8,7},{9,10},{10,9},{11,... | collective-permute-start | bytes 786440 | tf_op jit(solution)/shard_map/ppermute | solution.py:493
  34.2 6.6 %collective-permute-start.8 = (f32[13,8,128]{2,1,0:T(8,128)S(1)}, f32[13,8,128]{2,1,0:T(8,128)S(1)}, u32[]{:S(2)}, u32[]{:S(2)}) collective-permute-start(f32[13,8,128]{2,1,0:T(8,128)S(1)} %add_add_fusion.2.mine), channel_id=1, source_target_pairs={{0,16},{16,0},{32,48},{48,32},{64,80},{80,64},{96,112},{112,96},{1... | collective-permute-start | bytes 159752 | tf_op jit(solution)/shard_map/ppermute | solution.py:469
  37.4 7.6 %collective-permute-start.7 = (f32[13,8,128]{2,1,0:T(8,128)S(1)}, f32[13,8,128]{2,1,0:T(8,128)S(1)}, u32[]{:S(2)}, u32[]{:S(2)}) collective-permute-start(f32[13,8,128]{2,1,0:T(8,128)S(1)} %add_add_fusion.2.mine), channel_id=1, source_target_pairs={{16,1},{1,16},{17,2},{2,17},{18,3},{3,18},{19,4},{4,19},{20,5},{5,... | collective-permute-start | bytes 159752 | tf_op jit(solution)/shard_map/ppermute | solution.py:502
  45.0 1.2 %collective-permute-start.11 = (f32[13,8,128]{2,1,0:T(8,128)S(1)}, f32[13,8,128]{2,1,0:T(8,128)S(1)}, u32[]{:S(2)}, u32[]{:S(2)}) collective-permute-start(f32[13,8,128]{2,1,0:T(8,128)S(1)} %collective-permute-done.7.got), channel_id=1, source_target_pairs={{0,16},{16,0},{32,48},{48,32},{64,80},{80,64},{96,112},{112,96},{1... | collective-permute-start | bytes 159752 | tf_op jit(solution)/shard_map/ppermute | solution.py:469
  48.3 1.3 %collective-permute-start.12 = (f32[13,8,128]{2,1,0:T(8,128)S(1)}, f32[13,8,128]{2,1,0:T(8,128)S(1)}, u32[]{:S(2)}, u32[]{:S(2)}) collective-permute-start(f32[13,8,128]{2,1,0:T(8,128)S(1)} %get-tuple-element.43), channel_id=1, source_target_pairs={{0,16},{16,0},{32,48},{48,32},{64,80},{80,64},{96,112},{112,96},{1... | collective-permute-start | bytes 159752 | tf_op jit(solution)/shard_map/ppermute | solution.py:469
  49.6 4.6 %collective-permute-start.13 = (f32[13,8,128]{2,1,0:T(8,128)S(1)}, f32[13,8,128]{2,1,0:T(8,128)S(1)}, u32[]{:S(2)}, u32[]{:S(2)}) collective-permute-start(f32[13,8,128]{2,1,0:T(8,128)S(1)} %add.50), channel_id=1, source_target_pairs={{0,128},{16,144},{32,160},{48,176},{64,192},{80,208},{96,224},{112... | collective-permute-start | bytes 159752 | tf_op jit(solution)/shard_map/ppermute | solution.py:481
  54.2 7.0 %collective-permute-start.16 = (f32[13,8,128]{2,1,0:T(8,128)S(1)}, f32[13,8,128]{2,1,0:T(8,128)S(1)}, u32[]{:S(2)}, u32[]{:S(2)}) collective-permute-start(f32[13,8,128]{2,1,0:T(8,128)S(1)} %add.51), channel_id=1, source_target_pairs={{0,96},{16,112},{32,64},{48,80},{64,32},{80,48},{96,0},{112,16},{1... | collective-permute-start | bytes 159752 | tf_op jit(solution)/shard_map/ppermute | solution.py:476
  55.2 6.0 %collective-permute-start.15 = (f32[13,8,128]{2,1,0:T(8,128)S(1)}, f32[13,8,128]{2,1,0:T(8,128)S(1)}, u32[]{:S(2)}, u32[]{:S(2)}) collective-permute-start(f32[13,8,128]{2,1,0:T(8,128)S(1)} %add.51), channel_id=1, source_target_pairs={{0,32},{16,48},{32,0},{48,16},{64,96},{80,112},{96,64},{112,80},{1... | collective-permute-start | bytes 159752 | tf_op jit(solution)/shard_map/ppermute | solution.py:476
  57.9 4.5 %collective-permute-start.14 = (f32[13,8,128]{2,1,0:T(8,128)S(1)}, f32[13,8,128]{2,1,0:T(8,128)S(1)}, u32[]{:S(2)}, u32[]{:S(2)}) collective-permute-start(f32[13,8,128]{2,1,0:T(8,128)S(1)} %add.51), channel_id=1, source_target_pairs={{0,64},{16,80},{32,96},{48,112},{64,0},{80,16},{96,32},{112,48},{1... | collective-permute-start | bytes 159752 | tf_op jit(solution)/shard_map/ppermute | solution.py:476
  58.0 16.4 %collective-permute-start.19 = (f32[128,512]{1,0:T(8,128)S(1)}, f32[128,512]{1,0:T(8,128)S(1)}, u32[]{:S(2)}, u32[]{:S(2)}) collective-permute-start(f32[128,512]{1,0:T(8,128)S(1)} %get-tuple-element.49), channel_id=1, source_target_pairs={{0,1},{1,0},{2,3},{3,2},{4,5},{5,4},{6,7},{7,6},{8,9},{9,8},{10,11... | collective-permute-start | bytes 786440 | tf_op jit(solution)/shard_map/ppermute | solution.py:493
  58.0 16.4 %collective-permute-start.20 = (f32[128,512]{1,0:T(8,128)S(1)}, f32[128,512]{1,0:T(8,128)S(1)}, u32[]{:S(2)}, u32[]{:S(2)}) collective-permute-start(f32[128,512]{1,0:T(8,128)S(1)} %get-tuple-element.50), channel_id=1, source_target_pairs={{1,2},{2,1},{3,4},{4,3},{5,6},{6,5},{7,8},{8,7},{9,10},{10,9},{11,... | collective-permute-start | bytes 786440 | tf_op jit(solution)/shard_map/ppermute | solution.py:493
  62.5 6.1 %collective-permute-start.18 = (f32[13,8,128]{2,1,0:T(8,128)S(1)}, f32[13,8,128]{2,1,0:T(8,128)S(1)}, u32[]{:S(2)}, u32[]{:S(2)}) collective-permute-start(f32[13,8,128]{2,1,0:T(8,128)S(1)} %add_add_fusion.1.mine), channel_id=1, source_target_pairs={{0,16},{16,0},{32,48},{48,32},{64,80},{80,64},{96,112},{112,96},{1... | collective-permute-start | bytes 159752 | tf_op jit(solution)/shard_map/ppermute | solution.py:469
  65.6 7.6 %collective-permute-start.17 = (f32[13,8,128]{2,1,0:T(8,128)S(1)}, f32[13,8,128]{2,1,0:T(8,128)S(1)}, u32[]{:S(2)}, u32[]{:S(2)}) collective-permute-start(f32[13,8,128]{2,1,0:T(8,128)S(1)} %add_add_fusion.1.mine), channel_id=1, source_target_pairs={{16,1},{1,16},{17,2},{2,17},{18,3},{3,18},{19,4},{4,19},{20,5},{5,... | collective-permute-start | bytes 159752 | tf_op jit(solution)/shard_map/ppermute | solution.py:502
  73.1 1.2 %collective-permute-start.21 = (f32[13,8,128]{2,1,0:T(8,128)S(1)}, f32[13,8,128]{2,1,0:T(8,128)S(1)}, u32[]{:S(2)}, u32[]{:S(2)}) collective-permute-start(f32[13,8,128]{2,1,0:T(8,128)S(1)} %collective-permute-done.17.got), channel_id=1, source_target_pairs={{0,16},{16,0},{32,48},{48,32},{64,80},{80,64},{96,112},{112,96},{1... | collective-permute-start | bytes 159752 | tf_op jit(solution)/shard_map/ppermute | solution.py:469
  76.5 1.3 %collective-permute-start.22 = (f32[13,8,128]{2,1,0:T(8,128)S(1)}, f32[13,8,128]{2,1,0:T(8,128)S(1)}, u32[]{:S(2)}, u32[]{:S(2)}) collective-permute-start(f32[13,8,128]{2,1,0:T(8,128)S(1)} %get-tuple-element.54), channel_id=1, source_target_pairs={{0,16},{16,0},{32,48},{48,32},{64,80},{80,64},{96,112},{112,96},{1... | collective-permute-start | bytes 159752 | tf_op jit(solution)/shard_map/ppermute | solution.py:469
  77.9 4.6 %collective-permute-start.23 = (f32[13,8,128]{2,1,0:T(8,128)S(1)}, f32[13,8,128]{2,1,0:T(8,128)S(1)}, u32[]{:S(2)}, u32[]{:S(2)}) collective-permute-start(f32[13,8,128]{2,1,0:T(8,128)S(1)} %add.55), channel_id=1, source_target_pairs={{0,128},{16,144},{32,160},{48,176},{64,192},{80,208},{96,224},{112... | collective-permute-start | bytes 159752 | tf_op jit(solution)/shard_map/ppermute | solution.py:481
  82.5 3.1 %collective-permute-start.26 = (f32[13,8,128]{2,1,0:T(8,128)S(1)}, f32[13,8,128]{2,1,0:T(8,128)S(1)}, u32[]{:S(2)}, u32[]{:S(2)}) collective-permute-start(f32[13,8,128]{2,1,0:T(8,128)S(1)} %add.56), channel_id=1, source_target_pairs={{0,96},{16,112},{32,64},{48,80},{64,32},{80,48},{96,0},{112,16},{1... | collective-permute-start | bytes 159752 | tf_op jit(solution)/shard_map/ppermute | solution.py:476
  82.7 4.3 %collective-permute-start.25 = (f32[13,8,128]{2,1,0:T(8,128)S(1)}, f32[13,8,128]{2,1,0:T(8,128)S(1)}, u32[]{:S(2)}, u32[]{:S(2)}) collective-permute-start(f32[13,8,128]{2,1,0:T(8,128)S(1)} %add.56), channel_id=1, source_target_pairs={{0,32},{16,48},{32,0},{48,16},{64,96},{80,112},{96,64},{112,80},{1... | collective-permute-start | bytes 159752 | tf_op jit(solution)/shard_map/ppermute | solution.py:476
  85.2 4.5 %collective-permute-start.24 = (f32[13,8,128]{2,1,0:T(8,128)S(1)}, f32[13,8,128]{2,1,0:T(8,128)S(1)}, u32[]{:S(2)}, u32[]{:S(2)}) collective-permute-start(f32[13,8,128]{2,1,0:T(8,128)S(1)} %add.56), channel_id=1, source_target_pairs={{0,64},{16,80},{32,96},{48,112},{64,0},{80,16},{96,32},{112,48},{1... | collective-permute-start | bytes 159752 | tf_op jit(solution)/shard_map/ppermute | solution.py:476
  89.7 4.1 %collective-permute-start.27 = (f32[13,8,128]{2,1,0:T(8,128)S(1)}, f32[13,8,128]{2,1,0:T(8,128)S(1)}, u32[]{:S(2)}, u32[]{:S(2)}) collective-permute-start(f32[13,8,128]{2,1,0:T(8,128)S(1)} %add_add_fusion.mine), channel_id=1, source_target_pairs={{0,16},{16,0},{32,48},{48,32},{64,80},{80,64},{96,112},{112,96},{1... | collective-permute-start | bytes 159752 | tf_op jit(solution)/shard_map/ppermute | solution.py:469

commit v4 on v2

--- a/solution.py
+++ b/solution.py
@@ -306,7 +306,7 @@
             coefs[k, first + t] = jnp.broadcast_to(value[t : t + 1], (8, 128))
 
 
-def finish(state, faces, sums, wall, kind, inflow, moved, mine, other, rims, count):
+def finish(state, faces, sums, kind, inflow, moved, mine, other, rims, count):
     iy = lax.axis_index("vel")
     position = lax.axis_index("gx")
     fill_ends(state, inflow, kind, position, count)
@@ -333,126 +333,252 @@
             rims[1][...] = moved[up]
 
 
-def first_kernel(count, dist, pair_a, pair_b, wall, kind, inflow, *refs):
-    moved, mine, other, rim_a, rim_b, state, faces, sums, sems = refs
+def low_rows():
+    return lax.broadcasted_iota(jnp.int32, (8, 128), 0) < TILES
+
+
+def pack(values):
+    low = low_rows()
+    values = values + [jnp.zeros_like(values[0])]
+    return [jnp.where(low, values[k], values[k + 1]) for k in range(0, 14, 2)]
+
+
+def doubled(packed, k):
+    turned = pltpu.roll(packed, TILES, 0)
+    if k % 2:
+        return jnp.where(low_rows(), turned, packed)
+    return jnp.where(low_rows(), packed, turned)
+
+
+def rim_flux(state, sums):
+    def tile(t, carry):
+        for sign in range(2):
+            at = pl.multiple_of((DEPTH if sign else 1) * SEC + t * 128, 128)
+            total = [None] * 8
+            for b in range(2):
+                vz = vz_tile(b)
+                vz2 = vz * vz
+                acc = [None] * 4
+                for a in range(VS // 2):
+                    speed = (a + 0.5) * H
+                    start = sign * HALF + a * VS + 8 * b
+                    value = state[start : start + 8, pl.ds(at, 128)] * speed
+                    for p in range(4):
+                        acc[p] = value if acc[p] is None else acc[p] + value
+                        value = value * (speed if sign else -speed)
+                a0, a1, a2, a3 = acc
+                terms = [
+                    a0, a1, vz * a0, a2, vz2 * a0, vz * a1,
+                    a3 + vz2 * a1, vz * (a2 + vz2 * a0),
+                ]
+                total = terms if b == 0 else [x + y for x, y in zip(total, terms)]
+            for p in range(8):
+                sums[p, TILES * sign + t] = total[p]
+        return carry
+
+    lax.fori_loop(0, TILES, tile, 0)
+
+
+def first_kernel(count, dist, wall, kind, inflow, *refs):
+    faces, moved, mine, other, rim_a, rim_b, state, sums, flux, sems = refs
     iy = lax.axis_index("vel")
     position = lax.axis_index("gx")
-    even = lax.rem(position, 2) == 0
-    left = state.at[pl.ds(HALF, HALF), pl.ds(0, SEC)]
-    right = state.at[pl.ds(0, HALF), pl.ds((DEPTH + 1) * SEC, SEC)]
-    main = pltpu.make_async_copy(dist, state.at[:, pl.ds(SEC, DEPTH * SEC)], sems.at[0])
-    main.start()
+    loads = [
+        pltpu.make_async_copy(
+            dist.at[:, pl.ds(i * SEC, SEC)], state.at[:, pl.ds((i + 1) * SEC, SEC)], sems.at[i]
+        )
+        for i in range(DEPTH)
+    ]
+    for load in loads:
+        load.start()
     prepare_masks(wall, faces, position, count, iy >= VS // 2)
-
-    def bring(one, two):
-        copies = [
-            pltpu.make_async_copy(pair_a, one, sems.at[1]),
-            pltpu.make_async_copy(pair_b, two, sems.at[2]),
-        ]
-        for copy in copies:
-            copy.start()
-        for copy in copies:
-            copy.wait()
-
-    pl.when(even)(lambda: bring(right, left))
-    pl.when(~even)(lambda: bring(left, right))
-    main.wait()
-    finish(
-        state, faces, sums, wall, kind, inflow, moved, mine, other, (rim_a, rim_b), count
-    )
-
-
-def middle_kernel(count, rims, old, pair_a, pair_b, got, swapped, wall, kind, inflow, *refs):
-    state, moved, mine, other = refs[:4]
-    out_rims = refs[4 : 4 + 2 * rims]
-    ghosts, coefs, lines, faces, sums, sems = refs[4 + 2 * rims :]
+    state[HALF:, :SEC] = jnp.zeros((HALF, SEC), F32)
+    state[:HALF, (DEPTH + 1) * SEC :] = jnp.zeros((HALF, SEC), F32)
+    for load in loads:
+        load.wait()
+    finish(state, faces, sums, kind, inflow, moved, mine, other, (rim_a, rim_b), count)
+    rim_flux(state, flux)
+    values = expand([fold(flux, p, 0) * (WEIGHT / KEEP) for p in range(8)], vy_of(iy))
+    turned = [pltpu.roll(value, TILES, 0) for value in values]
+    low = low_rows()
+    halves = [
+        pack([value if k % 2 == 0 else turned[k] for k, value in enumerate(values)]),
+        pack([turned[k] if k % 2 == 0 else value for k, value in enumerate(values)]),
+    ]
+    inner = lax.rem(iy, 2) == 0
+    for k in range(7):
+        mine[13 + k] = jnp.where(inner, halves[0][k], halves[1][k])
+        other[13 + k] = jnp.where(inner, halves[1][k], halves[0][k])
+
+
+def y_kernel(first, value, across_y, near, far, *refs):
+    out = refs[-1]
+    low = low_rows()
+    inner = lax.rem(lax.axis_index("vel"), 2) == 0
+    own_rows = low == inner
+    own = [value[k] + across_y[k] for k in range(20 if first else 13)]
+    halo = [near[k] + far[k] for k in range(20 if first else 13)]
+    if first:
+        faces = refs[0]
+        sub = lax.broadcasted_iota(jnp.int32, (8, 128), 0)
+        edge = jnp.zeros((8, 128), F32)
+        for t in range(TILES):
+            edge = jnp.where(sub == t, faces[0, 0, t], edge)
+            edge = jnp.where(sub == t + TILES, faces[0, DEPTH, t], edge)
+        edge = edge * (KEEP * DT)
+        turned = pltpu.roll(edge, TILES, 0)
+        for k in range(13):
+            add = edge * doubled(halo[13 + k // 2], k)
+            own[k] = own[k] + jnp.where(own_rows, add, 0.0)
+        for k in range(13):
+            halo[k] = halo[k] + turned * doubled(own[13 + k // 2], k)
+    for k in range(13):
+        out[k] = own[k]
+    both = [jnp.where(own_rows, pltpu.roll(halo[k], TILES, 0), halo[k]) for k in range(13)]
+    for k, value in enumerate(pack(both)):
+        out[13 + k] = value
+
+
+def add_rims(ghosts, faces, state):
+    def tile(t, carry):
+        at = pl.multiple_of(t * 128, 128)
+        for sign in range(2):
+            to = pl.multiple_of((1 if sign else DEPTH) * SEC + t * 128, 128)
+            open_x = faces[0, 0 if sign else DEPTH, t]
+            for a in range(VS // 2):
+                scale = open_x * (KEEP * DT * (a + 0.5) * H)
+                for b in range(2):
+                    start = a * VS + 8 * b
+                    rows = slice(sign * HALF + start, sign * HALF + start + 8)
+                    state[rows, pl.ds(to, 128)] = state[rows, pl.ds(to, 128)] + scale * (
+                        ghosts[sign, start : start + 8, pl.ds(at, 128)]
+                    )
+        return carry
+
+    lax.fori_loop(0, TILES, tile, 0)
+
+
+def own_coefficients(mine, other, coefs):
     iy = lax.axis_index("vel")
-    position = lax.axis_index("gx")
-    odd = lax.rem(position, 2)
-    copies = [
-        pltpu.make_async_copy(pair_a, ghosts.at[odd], sems.at[0]),
-        pltpu.make_async_copy(pair_b, ghosts.at[1 - odd], sems.at[1]),
-    ]
+    core = lax.rem(iy, 2)
+    for ref, half in ((mine, core), (other, 1 - core)):
+        spread(coefs, coefficients([ref[k] for k in range(13)], vy_of(iy)), half * 8)
+
+
+def middle_kernel(count, first, source, mine_in, other_in, faces, kind, inflow, *refs):
+    pairs = refs[: 4 if first else 2]
+    refs = refs[len(pairs) :]
+    moved, mine, other = refs[:3]
+    out_rims = refs[3 : 3 + 2 * first]
+    state, ghosts, coefs, edges, lines, sums, sems = refs[3 + 2 * first :]
+    iy = lax.axis_index("vel")
+    odd = lax.rem(lax.axis_index("gx"), 2)
+    copies = []
+    for n in range(len(pairs) // 2):
+        for m in range(2):
+            at = 2 * n + (odd if m == 0 else 1 - odd)
+            copies.append(
+                pltpu.make_async_copy(pairs[2 * n + m], ghosts.at[at], sems.at[2 * n + m])
+            )
     for copy in copies:
         copy.start()
-    prepare_masks(wall, faces, position, count, iy >= VS // 2)
-    sub = lax.broadcasted_iota(jnp.int32, (8, 128), 0)
-    pick = (sub >= TILES) == (lax.rem(iy, 2) == 0)
-    values = [jnp.where(pick, got[k], swapped[k]) for k in range(13)]
-    spread(coefs, coefficients(values, vy_of(iy)), 0)
+    own_coefficients(mine_in, other_in, coefs)
+    inner = lax.rem(iy, 2) == 0
+    low = low_rows()
+    values = []
+    for k in range(13):
+        a, b = mine_in[13 + k // 2], other_in[13 + k // 2]
+        left, right = jnp.where(inner, a, b), jnp.where(inner, b, a)
+        values.append(jnp.where(low, doubled(right, k), doubled(left, k)))
+    spread(edges, coefficients(values, vy_of(iy)), 0)
+    relax(source, coefs, lines, state, SEC)
     for copy in copies:
         copy.wait()
-    relax_ghosts(ghosts, coefs, lines, state)
-    finish(state, faces, sums, wall, kind, inflow, moved, mine, other, out_rims, count)
+    relax_ghosts(ghosts, edges, lines, state)
+    if first:
+        add_rims(ghosts.at[pl.ds(2, 2)], faces, state)
+    finish(state, faces, sums, kind, inflow, moved, mine, other, out_rims, count)
 
 
 VM = pl.BlockSpec(memory_space=pltpu.VMEM)
 ANY = pl.BlockSpec(memory_space=pl.ANY)
+HBM = pl.BlockSpec(memory_space=pltpu.HBM)
 PARAMS = pltpu.CompilerParams(vmem_limit_bytes=12 << 20)
 F32 = jnp.float32
 WHOLE = jax.ShapeDtypeStruct((ROWS, DEPTH * SEC), F32)
 WIDE = jax.ShapeDtypeStruct((ROWS, (DEPTH + 2) * SEC), F32)
 RIM = jax.ShapeDtypeStruct((HALF, SEC), F32)
 PART = jax.ShapeDtypeStruct((13, 8, 128), F32)
-FACES = pltpu.VMEM((5, DEPTH + 1, TILES, 8, 128), F32)
+FULL = jax.ShapeDtypeStruct((20, 8, 128), F32)
+FACES = jax.ShapeDtypeStruct((5, DEPTH + 1, TILES, 8, 128), F32)
 SUMS = pltpu.VMEM((8, OWN, 8, 128), F32)
 LINES = pltpu.VMEM((2, 3, 8, 128), F32)
 
 
-def move_first(dist, pair_a, pair_b, wall, kind, inflow, count):
-    outs = (WHOLE, PART, PART, RIM, RIM)
+def move_first(dist, wall, kind, inflow, count):
+    outs = (FACES, WHOLE, FULL, FULL, RIM, RIM)
     return pl.pallas_call(
         functools.partial(first_kernel, count),
         out_shape=outs,
-        in_specs=[ANY, ANY, ANY, VM, VM, VM],
+        in_specs=[HBM, VM, VM, VM],
         out_specs=(VM,) * len(outs),
         scratch_shapes=[
-            pltpu.VMEM(WIDE.shape, F32), FACES, SUMS, pltpu.SemaphoreType.DMA((3,))
+            pltpu.VMEM(WIDE.shape, F32),
+            SUMS,
+            pltpu.VMEM((8, 8, 8, 128), F32),
+            pltpu.SemaphoreType.DMA((DEPTH,)),
         ],
         compiler_params=PARAMS,
         name="move_first",
-    )(dist, pair_a, pair_b, wall, kind, inflow)
-
-
-def move_middle(state, pairs, got, swapped, wall, kind, inflow, count, rims):
-    outs = (WIDE, WHOLE, PART, PART) + (RIM, RIM) * rims
+    )(dist, wall, kind, inflow)
+
+
+def y_sum(first, *arrays):
     return pl.pallas_call(
-        functools.partial(middle_kernel, count, rims),
+        functools.partial(y_kernel, first),
+        out_shape=FULL,
+        in_specs=[VM] * len(arrays),
+        out_specs=VM,
+        compiler_params=pltpu.CompilerParams(vmem_limit_bytes=4 << 20),
+        name="y_sum",
+    )(*arrays)
+
+
+def move_middle(source, mine, other, faces, kind, inflow, pairs, count, first):
+    outs = (WHOLE, PART, PART) + (RIM, RIM) * first
+    return pl.pallas_call(
+        functools.partial(middle_kernel, count, first),
         out_shape=outs,
-        in_specs=[VM, ANY, ANY] + [VM] * 5,
+        in_specs=[VM] * 6 + [ANY] * len(pairs),
         out_specs=(VM,) * len(outs),
-        input_output_aliases={0: 0},
         scratch_shapes=[
-            pltpu.VMEM((2, HALF, SEC), F32),
+            pltpu.VMEM(WIDE.shape, F32),
+            pltpu.VMEM((len(pairs), HALF, SEC), F32),
+            pltpu.VMEM((9, OWN, 8, 128), F32),
             pltpu.VMEM((9, 8, 8, 128), F32),
             LINES,
-            FACES,
             SUMS,
-            pltpu.SemaphoreType.DMA((2,)),
+            pltpu.SemaphoreType.DMA((len(pairs),)),
         ],
         compiler_params=PARAMS,
         name="move_middle",
-    )(state, *pairs, got, swapped, wall, kind, inflow)[1:]
-
-
-def relax_kernel(shift, moved, mine, other, state, coefs, lines):
-    iy = lax.axis_index("vel")
-    core = lax.rem(iy, 2)
-    vy = vy_of(iy)
-    for ref, half in ((mine, core), (other, 1 - core)):
-        spread(coefs, coefficients([ref[k] for k in range(13)], vy), half * 8)
-    relax(moved, coefs, lines, state, shift)
-
-
-def relaxed(moved, mine, other, last):
+    )(source, mine, other, faces, kind, inflow, *pairs)
+
+
+def last_kernel(moved, mine, other, state, coefs, lines):
+    own_coefficients(mine, other, coefs)
+    relax(moved, coefs, lines, state, 0)
+
+
+def relax_last(moved, mine, other):
     return pl.pallas_call(
-        functools.partial(relax_kernel, 0 if last else SEC),
-        out_shape=WHOLE if last else WIDE,
+        last_kernel,
+        out_shape=WHOLE,
         in_specs=[VM, VM, VM],
         out_specs=VM,
         scratch_shapes=[pltpu.VMEM((9, OWN, 8, 128), F32), LINES],
         compiler_params=PARAMS,
-        name="relax_last" if last else "relax",
+        name="relax_last",
     )(moved, mine, other)
 
 
@@ -467,11 +593,13 @@
     return lax.ppermute(array, "vel", [(i, mate(i)) for i in range(VS)])
 
 
-def all_moments(mine, other):
-    value = mine + swap_cores(other)
+def flip_y(array):
+    return lax.ppermute(array, "vel", [(i, i ^ 8) for i in range(VS)])
+
+
+def sum_x(value):
     parts = [shift_x(value, by) for by in (1, 3, 2)]
-    value = (value + parts[2]) + (parts[0] + parts[1])
-    return value + lax.ppermute(value, "vel", [(i, i ^ 8) for i in range(VS)])
+    return (value + parts[2]) + (parts[0] + parts[1])
 
 
 def swap_rims(pair_a, pair_b, count):
@@ -482,13 +610,18 @@
     return lax.ppermute(pair_a, "gx", near), lax.ppermute(pair_b, "gx", far)
 
 
-def swap_moments(half, count):
+def to_neighbours(half, count, flip):
     pairs = []
     for v in range(0, VS, 2):
         for g in range(count - 1):
-            one, two = (v + 1) * count + g, v * count + g + 1
+            one, two = (v + 1) * count + g, (v ^ flip) * count + g + 1
             pairs += [(one, two), (two, one)]
     return lax.ppermute(half, ("vel", "gx"), pairs)
+
+
+def stage_y(value, count, *faces):
+    moves = (flip_y(value), to_neighbours(value, count, 0), to_neighbours(value, count, 8))
+    return y_sum(bool(faces), value, *moves, *faces)
 
 
 def per_device(distribution, wall_mask, boundary_kind, inflow):
@@ -497,22 +630,28 @@
     even = lax.rem(lax.axis_index("gx"), 2) == 0
     up = distribution[HALF:, (DEPTH - 1) * SEC :]
     down = distribution[:HALF, :SEC]
-    pairs = swap_rims(jnp.where(even, up, down), jnp.where(even, down, up), count)
-    outs = move_first(distribution, *pairs, wall_mask, boundary_kind, inflow, count)
-    for step in range(STEPS):
-        moved, mine, other = outs[:3]
-        last = step + 1 == STEPS
-        if not last:
-            pairs = swap_rims(outs[3], outs[4], count)
-        half = all_moments(mine, other)
-        if last:
-            return relaxed(moved, half, swap_cores(half), True)
-        halo = swap_moments(half, count)
-        state = relaxed(moved, half, swap_cores(half), False)
-        outs = move_middle(
-            state, pairs, halo, swap_cores(halo), wall_mask, boundary_kind, inflow, count,
-            rims=step + 2 < STEPS,
-        )
+    start = swap_rims(jnp.where(even, up, down), jnp.where(even, down, up), count)
+    faces, *outs = move_first(distribution, wall_mask, boundary_kind, inflow, count)
+    moved, mine, other, *rims = outs
+    pairs = swap_rims(*rims, count)
+    half = stage_y(sum_x(mine + swap_cores(other)), count, faces)
+    outs = move_middle(
+        moved, half, swap_cores(half), faces, boundary_kind, inflow, (*pairs, *start), count, True
+    )
+    moved, mine, other, *rims = outs
+    half = stage_y(mine + swap_cores(other), count)
+    half, *rims = lax.optimization_barrier((half, *rims))
+    pairs = swap_rims(*rims, count)
+    half = sum_x(half)
+    moved, mine, other = move_middle(
+        moved, half, swap_cores(half), faces, boundary_kind, inflow, pairs, count, False
+    )
+    half = sum_x(flip_y_sum(mine + swap_cores(other)))
+    return relax_last(moved, half, swap_cores(half))
+
+
+def flip_y_sum(value):
+    return value + flip_y(value)
 
 
 def solution(mesh):

time: 108 us -> 119 us (1.10)
  starting transfers between devices: 48.5 us -> 56 us
  waiting for transfers between devices: 42.3 us -> 46.7 us
    ppermute x8 -> x6, starting transfers between devices: 4.63 us -> 14.2 us  [swap_cores(): return lax.ppermute(array, 'vel', [(i, i ^ 1) for i in range(VS)])]
    ppermute x6, waiting for transfers between devices: 13.1 us -> 6.32 us  [swap_rims(): return (lax.ppermute(pair_a, 'gx', near), lax.ppermute(pair_b, 'gx', far))]
    ppermute x9, waiting for transfers between devices: 4.5 us -> 10.2 us  [shift_x(): return lax.ppermute(array, 'vel', [(i, mate(i)) for i in range(VS)])]
    ppermute x5 -> x7, waiting for transfers between devices: 20.4 us -> 24.7 us  [the longest x3 17.1 us: flip_y(): return lax.ppermute(array, 'vel', [(i, i ^ 8) for i in range(VS)])]
    ppermute x6, starting transfers between devices: 14.9 us -> 13 us  [swap_rims(): return (lax.ppermute(pair_a, 'gx', near), lax.ppermute(pair_b, 'gx', far))]
    ppermute x9, starting transfers between devices: 10.7 us -> 9 us  [shift_x(): return lax.ppermute(array, 'vel', [(i, mate(i)) for i in range(VS)])]
    ppermute x5 -> x7, starting transfers between devices: 18.3 us -> 19.8 us  [the longest x4 19.3 us: to_neighbours(): return lax.ppermute(half, ('vel', 'gx'), pairs)]
    ppermute x8 -> x6, waiting for transfers between devices: 4.32 us -> 5.41 us  [swap_cores(): return lax.ppermute(array, 'vel', [(i, i ^ 1) for i in range(VS)])]
  transfers between devices with their start and end apart: 28 -> 28, of which waited for: 15 -> 18; matrix products, arithmetic and copies ran while one was open for 0% -> 1% of each run, Pallas kernels for 2% -> 0%
where the time goes in v4:
time: 119 us; the launch traced here: 118 us
  starting transfers between devices  56 us (47%)
  waiting for transfers between devices  46.7 us (39%)
  Pallas kernels  10.6 us (9%)
  local copies, waits for them, and re-layouts  3.87 us (3%)
    ppermute x4, starting transfers between devices, to_neighbours(): return lax.ppermute(half, ('vel', 'gx'), pairs)  19.3 us
    ppermute x3, waiting for transfers between devices, flip_y(): return lax.ppermute(array, 'vel', [(i, i ^ 8) for i in range(VS)])  17.1 us
    ppermute x6, starting transfers between devices, swap_cores(): return lax.ppermute(array, 'vel', [(i, i ^ 1) for i in range(VS)])  14.2 us
    ppermute x6, starting transfers between devices, swap_rims(): return (lax.ppermute(pair_a, 'gx', near), lax.ppermute(pair_b, 'gx', far))  13 us
    ppermute x9, waiting for transfers between devices, shift_x(): return lax.ppermute(array, 'vel', [(i, mate(i)) for i in range(VS)])  10.2 us
    ppermute x9, starting transfers between devices, shift_x(): return lax.ppermute(array, 'vel', [(i, mate(i)) for i in range(VS)])  9 us
    ppermute x4, waiting for transfers between devices, to_neighbours(): return lax.ppermute(half, ('vel', 'gx'), pairs)  7.59 us
    ppermute x6, waiting for transfers between devices, swap_rims(): return (lax.ppermute(pair_a, 'gx', near), lax.ppermute(pair_b, 'gx', far))  6.32 us
  transfers between devices with their start and end apart: 28, of which 18 were waited for; matrix products, arithmetic and copies ran while one was open for 1% of the time, Pallas kernels for 0%

profile of v4, /device:TPU:107, one launch (start us, length us, event | category | flops | bytes accessed | tf_op | source)
XLA Modules:
  0.0 118.5 jit_solution(12611243598614219375)
XLA Ops:
  0.0 1.6 %copy-done = f32[256,2048]{1,0:T(8,128)S(1)} copy-done((f32[256,2048]{1,0:T(8,128)S(1)}, f32[256,2048]{1,0:T(8,128)}, u32[]{:S(2)}) %copy-start) | copy-done | bytes 2097176
  1.6 0.9 copy-done.1
  2.5 0.7 copy-done.2
  3.2 0.7 copy-done.4
  3.9 2.3 %move_first.1 = (f32[5,5,4,8,128]{4,3,2,1,0:T(8,128)S(1)}, f32[256,2048]{1,0:T(8,128)S(1)}, f32[20,8,128]{2,1,0:T(8,128)S(1)}, f32[20,8,128]{2,1,0:T(8,128)S(1)}...) custom-call(f32[256,2048]{1,0:T(8,128)S(1)} %copy-done, s32[64,512]{1,0:T(8,128)S(1)} %copy-done.1, ...), custom_call_target="tpu_custom_call" | custom-call | tf_op jit(solution)/shard_map/move_first/pallas_call | solution.py:520
  6.2 0.8 collective-permute-start
  7.0 0.9 collective-permute-done
  7.9 1.3 %collective-permute-start.3 = (f32[20,8,128]{2,1,0:T(8,128)S(1)}, f32[20,8,128]{2,1,0:T(8,128)S(1)}, u32[]{:S(2)}, u32[]{:S(2)}) collective-permute-start(f32[20,8,128]{2,1,0:T(8,128)S(1)} %add.39), channel_id=1, source_target_pairs={{0,96},{16,112},{32,64},{48,80},{64,32},{80,48},{96,0},{112,16},{1... | collective-permute-start | bytes 245768 | tf_op jit(solution)/shard_map/ppermute | solution.py:593
  9.2 1.5 %collective-permute-start.2 = (f32[20,8,128]{2,1,0:T(8,128)S(1)}, f32[20,8,128]{2,1,0:T(8,128)S(1)}, u32[]{:S(2)}, u32[]{:S(2)}) collective-permute-start(f32[20,8,128]{2,1,0:T(8,128)S(1)} %add.39), channel_id=1, source_target_pairs={{0,32},{16,48},{32,0},{48,16},{64,96},{80,112},{96,64},{112,80},{1... | collective-permute-start | bytes 245768 | tf_op jit(solution)/shard_map/ppermute | solution.py:593
  10.7 0.9 collective-permute-done.3
  11.6 0.9 collective-permute-done.2
  12.6 3.0 %collective-permute-done.1 = f32[20,8,128]{2,1,0:T(8,128)S(1)} collective-permute-done((f32[20,8,128]{2,1,0:T(8,128)S(1)}, f32[20,8,128]{2,1,0:T(8,128)S(1)}, u32[]{:S(2)}, u32[]{:S(2)}) %collective-permute-start.1) | collective-permute-done | bytes 81952 | tf_op jit(solution)/shard_map/ppermute | solution.py:593
  15.6 7.7 %collective-permute-start.6 = (f32[20,8,128]{2,1,0:T(8,128)S(1)}, f32[20,8,128]{2,1,0:T(8,128)S(1)}, u32[]{:S(2)}, u32[]{:S(2)}) collective-permute-start(f32[20,8,128]{2,1,0:T(8,128)S(1)} %add_add_fusion.1.value), channel_id=1, source_target_pairs={{16,129},{129,16},{17,130},{130,17},{18,131},{131,18},{19,132},{13... | collective-permute-start | bytes 245768 | tf_op jit(solution)/shard_map/ppermute | solution.py:619
  23.3 1.1 slice_select_fusion
  24.4 3.5 %collective-permute-start.11 = (f32[128,512]{1,0:T(8,128)S(1)}, f32[128,512]{1,0:T(8,128)S(1)}, u32[]{:S(2)}, u32[]{:S(2)}) collective-permute-start(f32[128,512]{1,0:T(8,128)S(1)} %get-tuple-element.39), channel_id=1, source_target_pairs={{1,2},{2,1},{3,4},{4,3},{5,6},{6,5},{7,8},{8,7},{9,10},{10,9},{11,... | collective-permute-start | bytes 786440 | tf_op jit(solution)/shard_map/ppermute | solution.py:610
  28.0 1.5 %collective-permute-start.8 = (f32[128,512]{1,0:T(8,128)S(1)}, f32[128,512]{1,0:T(8,128)S(1)}, u32[]{:S(2)}, u32[]{:S(2)}) collective-permute-start(f32[128,512]{1,0:T(8,128)S(1)} %get-tuple-element.26), channel_id=1, source_target_pairs={{0,1},{1,0},{2,3},{3,2},{4,5},{5,4},{6,7},{7,6},{8,9},{9,8},{10,11... | collective-permute-start | bytes 786440 | tf_op jit(solution)/shard_map/ppermute | solution.py:610
  29.5 3.9 %collective-permute-start.9 = (f32[128,512]{1,0:T(8,128)S(1)}, f32[128,512]{1,0:T(8,128)S(1)}, u32[]{:S(2)}, u32[]{:S(2)}) collective-permute-start(f32[128,512]{1,0:T(8,128)S(1)} %get-tuple-element.27), channel_id=1, source_target_pairs={{1,2},{2,1},{3,4},{4,3},{5,6},{6,5},{7,8},{8,7},{9,10},{10,9},{11,... | collective-permute-start | bytes 786440 | tf_op jit(solution)/shard_map/ppermute | solution.py:610
  33.3 2.5 %collective-permute-start.5 = (f32[20,8,128]{2,1,0:T(8,128)S(1)}, f32[20,8,128]{2,1,0:T(8,128)S(1)}, u32[]{:S(2)}, u32[]{:S(2)}) collective-permute-start(f32[20,8,128]{2,1,0:T(8,128)S(1)} %add_add_fusion.1.value), channel_id=1, source_target_pairs={{16,1},{1,16},{17,2},{2,17},{18,3},{3,18},{19,4},{4,19},{20,5},{5,... | collective-permute-start | bytes 245768 | tf_op jit(solution)/shard_map/ppermute | solution.py:619
  35.9 5.9 %collective-permute-done.5.near = f32[20,8,128]{2,1,0:T(8,128)S(1)} collective-permute-done((f32[20,8,128]{2,1,0:T(8,128)S(1)}, f32[20,8,128]{2,1,0:T(8,128)S(1)}, u32[]{:S(2)}, u32[]{:S(2)}) %collective-permute-start.5) | collective-permute-done | bytes 81952 | tf_op jit(solution)/shard_map/ppermute | solution.py:619
  41.7 0.3 collective-permute-start.4
  42.1 9.9 %collective-permute-done.4.across_y = f32[20,8,128]{2,1,0:T(8,128)S(1)} collective-permute-done((f32[20,8,128]{2,1,0:T(8,128)S(1)}, f32[20,8,128]{2,1,0:T(8,128)S(1)}, u32[]{:S(2)}, u32[]{:S(2)}) %collective-permute-start.4) | collective-permute-done | bytes 81952 | tf_op jit(solution)/shard_map/ppermute | solution.py:597
  52.0 7.4 %collective-permute-start.7 = (f32[20,8,128]{2,1,0:T(8,128)S(1)}, f32[20,8,128]{2,1,0:T(8,128)S(1)}, u32[]{:S(2)}, u32[]{:S(2)}) collective-permute-start(f32[20,8,128]{2,1,0:T(8,128)S(1)} %y_sum.2.mine_in), channel_id=1, source_target_pairs={{0,16},{16,0},{32,48},{48,32},{64,80},{80,64},{96,112},{112,96},{1... | collective-permute-start | bytes 245768 | tf_op jit(solution)/shard_map/ppermute | solution.py:586
  59.4 0.9 collective-permute-done.7.other_in
  60.3 3.1 %move_middle.2 = (f32[256,2048]{1,0:T(8,128)S(1)}, f32[13,8,128]{2,1,0:T(8,128)S(1)}, f32[13,8,128]{2,1,0:T(8,128)S(1)}, f32[128,512]{1,0:T(8,128)S(1)}, f32[128,512]{1,0:T(8,128)S(1)}) custom-call(f32[256,2048]{1,0:T(8,128)S(1)} %get-tuple-element.22.source, f32[20,8,128]{2,1,0:T(8,128)S(1)} %y_sum.2.mine_in, ...), custom_call_target="tpu_custom_call" | custom-call | tf_op jit(solution)/shard_map/move_middle/pallas_call | solution.py:549
  63.4 0.4 collective-permute-start.12
  63.9 0.9 collective-permute-done.12
  64.7 2.6 %collective-permute-start.15 = (f32[13,8,128]{2,1,0:T(8,128)S(1)}, f32[13,8,128]{2,1,0:T(8,128)S(1)}, u32[]{:S(2)}, u32[]{:S(2)}) collective-permute-start(f32[13,8,128]{2,1,0:T(8,128)S(1)} %add.43.value), channel_id=1, source_target_pairs={{16,129},{129,16},{17,130},{130,17},{18,131},{131,18},{19,132},{13... | collective-permute-start | bytes 159752 | tf_op jit(solution)/shard_map/ppermute | solution.py:619
  67.3 6.5 %collective-permute-start.14 = (f32[13,8,128]{2,1,0:T(8,128)S(1)}, f32[13,8,128]{2,1,0:T(8,128)S(1)}, u32[]{:S(2)}, u32[]{:S(2)}) collective-permute-start(f32[13,8,128]{2,1,0:T(8,128)S(1)} %add.43.value), channel_id=1, source_target_pairs={{16,1},{1,16},{17,2},{2,17},{18,3},{3,18},{19,4},{4,19},{20,5},{5,... | collective-permute-start | bytes 159752 | tf_op jit(solution)/shard_map/ppermute | solution.py:619
  73.9 1.7 %collective-permute-done.14.near = f32[13,8,128]{2,1,0:T(8,128)S(1)} collective-permute-done((f32[13,8,128]{2,1,0:T(8,128)S(1)}, f32[13,8,128]{2,1,0:T(8,128)S(1)}, u32[]{:S(2)}, u32[]{:S(2)}) %collective-permute-start.14) | collective-permute-done | bytes 53280 | tf_op jit(solution)/shard_map/ppermute | solution.py:619
  75.6 2.8 %collective-permute-done.13.across_y = f32[13,8,128]{2,1,0:T(8,128)S(1)} collective-permute-done((f32[13,8,128]{2,1,0:T(8,128)S(1)}, f32[13,8,128]{2,1,0:T(8,128)S(1)}, u32[]{:S(2)}, u32[]{:S(2)}) %collective-permute-start.13) | collective-permute-done | bytes 53280 | tf_op jit(solution)/shard_map/ppermute | solution.py:597
  78.5 2.1 %collective-permute-start.17 = (f32[20,8,128]{2,1,0:T(8,128)S(1)}, f32[20,8,128]{2,1,0:T(8,128)S(1)}, u32[]{:S(2)}, u32[]{:S(2)}) collective-permute-start(f32[20,8,128]{2,1,0:T(8,128)S(1)} %y_sum.3), channel_id=1, source_target_pairs={{0,32},{16,48},{32,0},{48,16},{64,96},{80,112},{96,64},{112,80},{1... | collective-permute-start | bytes 245768 | tf_op jit(solution)/shard_map/ppermute | solution.py:593
  80.6 0.5 collective-permute-start.16
  81.1 4.1 %collective-permute-start.21 = (f32[128,512]{1,0:T(8,128)S(1)}, f32[128,512]{1,0:T(8,128)S(1)}, u32[]{:S(2)}, u32[]{:S(2)}) collective-permute-start(f32[128,512]{1,0:T(8,128)S(1)} %get-tuple-element.35), channel_id=1, source_target_pairs={{1,2},{2,1},{3,4},{4,3},{5,6},{6,5},{7,8},{8,7},{9,10},{10,9},{11,... | collective-permute-start | bytes 786440 | tf_op jit(solution)/shard_map/ppermute | solution.py:610
  85.2 1.0 collective-permute-done.16
  86.2 0.9 collective-permute-start.19
  87.1 0.9 collective-permute-done.19.other_in
  88.1 6.3 %collective-permute-done.20.refs_0_ = f32[128,512]{1,0:T(8,128)S(1)} collective-permute-done((f32[128,512]{1,0:T(8,128)S(1)}, f32[128,512]{1,0:T(8,128)S(1)}, u32[]{:S(2)}, u32[]{:S(2)}) %collective-permute-start.20) | collective-permute-done | bytes 262176 | tf_op jit(solution)/shard_map/ppermute | solution.py:610
  94.4 2.9 %move_middle.3 = (f32[256,2048]{1,0:T(8,128)S(1)}, f32[13,8,128]{2,1,0:T(8,128)S(1)}, f32[13,8,128]{2,1,0:T(8,128)S(1)}) custom-call(f32[256,2048]{1,0:T(8,128)S(1)} %get-tuple-element.28.source, f32[20,8,128]{2,1,0:T(8,128)S(1)} %add_add_fusion.mine_in, f32[20,8,128]{2,1,0:T(8,128)S(1)} %collective-permute-done.19.other_in, ...), custom_call_target="tpu_custom_call" | custom-call | tf_op jit(solution)/shard_map/move_middle/pallas_call | solution.py:549
  97.2 1.4 %collective-permute-start.22 = (f32[13,8,128]{2,1,0:T(8,128)S(1)}, f32[13,8,128]{2,1,0:T(8,128)S(1)}, u32[]{:S(2)}, u32[]{:S(2)}) collective-permute-start(f32[13,8,128]{2,1,0:T(8,128)S(1)} %get-tuple-element.38), channel_id=1, source_target_pairs={{0,16},{16,0},{32,48},{48,32},{64,80},{80,64},{96,112},{112,96},{1... | collective-permute-start | bytes 159752 | tf_op jit(solution)/shard_map/ppermute | solution.py:586
  98.6 0.9 collective-permute-done.22
  99.6 4.5 %collective-permute-done.23 = f32[13,8,128]{2,1,0:T(8,128)S(1)} collective-permute-done((f32[13,8,128]{2,1,0:T(8,128)S(1)}, f32[13,8,128]{2,1,0:T(8,128)S(1)}, u32[]{:S(2)}, u32[]{:S(2)}) %collective-permute-start.23) | collective-permute-done | bytes 53280 | tf_op jit(solution)/shard_map/ppermute | solution.py:597
  104.0 0.8 collective-permute-start.26
  104.8 2.7 %collective-permute-start.25 = (f32[13,8,128]{2,1,0:T(8,128)S(1)}, f32[13,8,128]{2,1,0:T(8,128)S(1)}, u32[]{:S(2)}, u32[]{:S(2)}) collective-permute-start(f32[13,8,128]{2,1,0:T(8,128)S(1)} %add.48), channel_id=1, source_target_pairs={{0,32},{16,48},{32,0},{48,16},{64,96},{80,112},{96,64},{112,80},{1... | collective-permute-start | bytes 159752 | tf_op jit(solution)/shard_map/ppermute | solution.py:593
  107.5 1.8 %collective-permute-done.25 = f32[13,8,128]{2,1,0:T(8,128)S(1)} collective-permute-done((f32[13,8,128]{2,1,0:T(8,128)S(1)}, f32[13,8,128]{2,1,0:T(8,128)S(1)}, u32[]{:S(2)}, u32[]{:S(2)}) %collective-permute-start.25) | collective-permute-done | bytes 53280 | tf_op jit(solution)/shard_map/ppermute | solution.py:593
  109.3 2.7 %collective-permute-done.24 = f32[13,8,128]{2,1,0:T(8,128)S(1)} collective-permute-done((f32[13,8,128]{2,1,0:T(8,128)S(1)}, f32[13,8,128]{2,1,0:T(8,128)S(1)}, u32[]{:S(2)}, u32[]{:S(2)}) %collective-permute-start.24) | collective-permute-done | bytes 53280 | tf_op jit(solution)/shard_map/ppermute | solution.py:593
  112.0 3.3 %collective-permute-start.27 = (f32[13,8,128]{2,1,0:T(8,128)S(1)}, f32[13,8,128]{2,1,0:T(8,128)S(1)}, u32[]{:S(2)}, u32[]{:S(2)}) collective-permute-start(f32[13,8,128]{2,1,0:T(8,128)S(1)} %add_add_fusion.2.mine), channel_id=1, source_target_pairs={{0,16},{16,0},{32,48},{48,32},{64,80},{80,64},{96,112},{112,96},{1... | collective-permute-start | bytes 159752 | tf_op jit(solution)/shard_map/ppermute | solution.py:586
  115.3 0.9 collective-permute-done.27.other
  116.2 2.2 %relax_last.1 = f32[256,2048]{1,0:T(8,128)} custom-call(f32[256,2048]{1,0:T(8,128)S(1)} %get-tuple-element.36.moved, f32[13,8,128]{2,1,0:T(8,128)S(1)} %add_add_fusion.2.mine, f32[13,8,128]{2,1,0:T(8,128)S(1)} %collective-permute-done.27.other), custom_call_target="tpu_custom_call" | custom-call | tf_op jit(solution)/shard_map/relax_last/pallas_call | solution.py:574
  (34 shorter events, 0.5 us)
Async XLA Ops:
  0.0 1.6 %copy-start = (f32[256,2048]{1,0:T(8,128)S(1)}, f32[256,2048]{1,0:T(8,128)}, u32[]{:S(2)}) copy-start(f32[256,2048]{1,0:T(8,128)} %dist.1) | copy-start | bytes 6291460
  1.6 0.9 copy-start.1
  2.5 0.7 copy-start.2
  3.2 0.7 copy-start.4
  3.9 56.4 %copy-start.3 = (s32[2,512]{1,0:T(2,128)S(1)}, s32[2,512]{1,0:T(2,128)}, u32[]{:S(2)}) copy-start(s32[2,512]{1,0:T(2,128)} %kind.5) | copy-start | bytes 12292
  3.9 56.4 %copy-start.5 = (f32[256]{0:T(256)S(1)}, f32[256]{0:T(256)}, u32[]{:S(2)}) copy-start(f32[256]{0:T(256)} %param.7) | copy-start | bytes 3076
  6.2 1.7 %collective-permute-start = (f32[20,8,128]{2,1,0:T(8,128)S(1)}, f32[20,8,128]{2,1,0:T(8,128)S(1)}, u32[]{:S(2)}, u32[]{:S(2)}) collective-permute-start(f32[20,8,128]{2,1,0:T(8,128)S(1)} %get-tuple-element.24), channel_id=1, source_target_pairs={{0,16},{16,0},{32,48},{48,32},{64,80},{80,64},{96,112},{112,96},{1... | collective-permute-start | bytes 245768 | tf_op jit(solution)/shard_map/ppermute | solution.py:586
  7.9 3.7 %collective-permute-start.3 = (f32[20,8,128]{2,1,0:T(8,128)S(1)}, f32[20,8,128]{2,1,0:T(8,128)S(1)}, u32[]{:S(2)}, u32[]{:S(2)}) collective-permute-start(f32[20,8,128]{2,1,0:T(8,128)S(1)} %add.39), channel_id=1, source_target_pairs={{0,96},{16,112},{32,64},{48,80},{64,32},{80,48},{96,0},{112,16},{1... | collective-permute-start | bytes 245768 | tf_op jit(solution)/shard_map/ppermute | solution.py:593
  9.2 3.4 %collective-permute-start.2 = (f32[20,8,128]{2,1,0:T(8,128)S(1)}, f32[20,8,128]{2,1,0:T(8,128)S(1)}, u32[]{:S(2)}, u32[]{:S(2)}) collective-permute-start(f32[20,8,128]{2,1,0:T(8,128)S(1)} %add.39), channel_id=1, source_target_pairs={{0,32},{16,48},{32,0},{48,16},{64,96},{80,112},{96,64},{112,80},{1... | collective-permute-start | bytes 245768 | tf_op jit(solution)/shard_map/ppermute | solution.py:593
  10.7 4.8 %collective-permute-start.1 = (f32[20,8,128]{2,1,0:T(8,128)S(1)}, f32[20,8,128]{2,1,0:T(8,128)S(1)}, u32[]{:S(2)}, u32[]{:S(2)}) collective-permute-start(f32[20,8,128]{2,1,0:T(8,128)S(1)} %add.39), channel_id=1, source_target_pairs={{0,64},{16,80},{32,96},{48,112},{64,0},{80,16},{96,32},{112,48},{1... | collective-permute-start | bytes 245768 | tf_op jit(solution)/shard_map/ppermute | solution.py:593
  15.6 17.8 %collective-permute-start.6 = (f32[20,8,128]{2,1,0:T(8,128)S(1)}, f32[20,8,128]{2,1,0:T(8,128)S(1)}, u32[]{:S(2)}, u32[]{:S(2)}) collective-permute-start(f32[20,8,128]{2,1,0:T(8,128)S(1)} %add_add_fusion.1.value), channel_id=1, source_target_pairs={{16,129},{129,16},{17,130},{130,17},{18,131},{131,18},{19,132},{13... | collective-permute-start | bytes 245768 | tf_op jit(solution)/shard_map/ppermute | solution.py:619
  24.4 35.0 %collective-permute-start.11 = (f32[128,512]{1,0:T(8,128)S(1)}, f32[128,512]{1,0:T(8,128)S(1)}, u32[]{:S(2)}, u32[]{:S(2)}) collective-permute-start(f32[128,512]{1,0:T(8,128)S(1)} %get-tuple-element.39), channel_id=1, source_target_pairs={{1,2},{2,1},{3,4},{4,3},{5,6},{6,5},{7,8},{8,7},{9,10},{10,9},{11,... | collective-permute-start | bytes 786440 | tf_op jit(solution)/shard_map/ppermute | solution.py:610
  27.9 31.5 %collective-permute-start.10 = (f32[128,512]{1,0:T(8,128)S(1)}, f32[128,512]{1,0:T(8,128)S(1)}, u32[]{:S(2)}, u32[]{:S(2)}) collective-permute-start(f32[128,512]{1,0:T(8,128)S(1)} %get-tuple-element.40), channel_id=1, source_target_pairs={{0,1},{1,0},{2,3},{3,2},{4,5},{5,4},{6,7},{7,6},{8,9},{9,8},{10,11... | collective-permute-start | bytes 786440 | tf_op jit(solution)/shard_map/ppermute | solution.py:610
  28.0 31.4 %collective-permute-start.8 = (f32[128,512]{1,0:T(8,128)S(1)}, f32[128,512]{1,0:T(8,128)S(1)}, u32[]{:S(2)}, u32[]{:S(2)}) collective-permute-start(f32[128,512]{1,0:T(8,128)S(1)} %get-tuple-element.26), channel_id=1, source_target_pairs={{0,1},{1,0},{2,3},{3,2},{4,5},{5,4},{6,7},{7,6},{8,9},{9,8},{10,11... | collective-permute-start | bytes 786440 | tf_op jit(solution)/shard_map/ppermute | solution.py:610
  29.5 29.9 %collective-permute-start.9 = (f32[128,512]{1,0:T(8,128)S(1)}, f32[128,512]{1,0:T(8,128)S(1)}, u32[]{:S(2)}, u32[]{:S(2)}) collective-permute-start(f32[128,512]{1,0:T(8,128)S(1)} %get-tuple-element.27), channel_id=1, source_target_pairs={{1,2},{2,1},{3,4},{4,3},{5,6},{6,5},{7,8},{8,7},{9,10},{10,9},{11,... | collective-permute-start | bytes 786440 | tf_op jit(solution)/shard_map/ppermute | solution.py:610
  33.3 8.4 %collective-permute-start.5 = (f32[20,8,128]{2,1,0:T(8,128)S(1)}, f32[20,8,128]{2,1,0:T(8,128)S(1)}, u32[]{:S(2)}, u32[]{:S(2)}) collective-permute-start(f32[20,8,128]{2,1,0:T(8,128)S(1)} %add_add_fusion.1.value), channel_id=1, source_target_pairs={{16,1},{1,16},{17,2},{2,17},{18,3},{3,18},{19,4},{4,19},{20,5},{5,... | collective-permute-start | bytes 245768 | tf_op jit(solution)/shard_map/ppermute | solution.py:619
  41.7 10.2 %collective-permute-start.4 = (f32[20,8,128]{2,1,0:T(8,128)S(1)}, f32[20,8,128]{2,1,0:T(8,128)S(1)}, u32[]{:S(2)}, u32[]{:S(2)}) collective-permute-start(f32[20,8,128]{2,1,0:T(8,128)S(1)} %add_add_fusion.1.value), channel_id=1, source_target_pairs={{0,128},{16,144},{32,160},{48,176},{64,192},{80,208},{96,224},{112... | collective-permute-start | bytes 245768 | tf_op jit(solution)/shard_map/ppermute | solution.py:597
  52.0 8.3 %collective-permute-start.7 = (f32[20,8,128]{2,1,0:T(8,128)S(1)}, f32[20,8,128]{2,1,0:T(8,128)S(1)}, u32[]{:S(2)}, u32[]{:S(2)}) collective-permute-start(f32[20,8,128]{2,1,0:T(8,128)S(1)} %y_sum.2.mine_in), channel_id=1, source_target_pairs={{0,16},{16,0},{32,48},{48,32},{64,80},{80,64},{96,112},{112,96},{1... | collective-permute-start | bytes 245768 | tf_op jit(solution)/shard_map/ppermute | solution.py:586
  63.4 1.3 %collective-permute-start.12 = (f32[13,8,128]{2,1,0:T(8,128)S(1)}, f32[13,8,128]{2,1,0:T(8,128)S(1)}, u32[]{:S(2)}, u32[]{:S(2)}) collective-permute-start(f32[13,8,128]{2,1,0:T(8,128)S(1)} %get-tuple-element.30), channel_id=1, source_target_pairs={{0,16},{16,0},{32,48},{48,32},{64,80},{80,64},{96,112},{112,96},{1... | collective-permute-start | bytes 159752 | tf_op jit(solution)/shard_map/ppermute | solution.py:586
  64.7 9.2 %collective-permute-start.15 = (f32[13,8,128]{2,1,0:T(8,128)S(1)}, f32[13,8,128]{2,1,0:T(8,128)S(1)}, u32[]{:S(2)}, u32[]{:S(2)}) collective-permute-start(f32[13,8,128]{2,1,0:T(8,128)S(1)} %add.43.value), channel_id=1, source_target_pairs={{16,129},{129,16},{17,130},{130,17},{18,131},{131,18},{19,132},{13... | collective-permute-start | bytes 159752 | tf_op jit(solution)/shard_map/ppermute | solution.py:619
  67.3 8.3 %collective-permute-start.14 = (f32[13,8,128]{2,1,0:T(8,128)S(1)}, f32[13,8,128]{2,1,0:T(8,128)S(1)}, u32[]{:S(2)}, u32[]{:S(2)}) collective-permute-start(f32[13,8,128]{2,1,0:T(8,128)S(1)} %add.43.value), channel_id=1, source_target_pairs={{16,1},{1,16},{17,2},{2,17},{18,3},{3,18},{19,4},{4,19},{20,5},{5,... | collective-permute-start | bytes 159752 | tf_op jit(solution)/shard_map/ppermute | solution.py:619
  73.8 4.6 %collective-permute-start.13 = (f32[13,8,128]{2,1,0:T(8,128)S(1)}, f32[13,8,128]{2,1,0:T(8,128)S(1)}, u32[]{:S(2)}, u32[]{:S(2)}) collective-permute-start(f32[13,8,128]{2,1,0:T(8,128)S(1)} %add.43.value), channel_id=1, source_target_pairs={{0,128},{16,144},{32,160},{48,176},{64,192},{80,208},{96,224},{112... | collective-permute-start | bytes 159752 | tf_op jit(solution)/shard_map/ppermute | solution.py:597
  78.4 6.8 %collective-permute-start.18 = (f32[20,8,128]{2,1,0:T(8,128)S(1)}, f32[20,8,128]{2,1,0:T(8,128)S(1)}, u32[]{:S(2)}, u32[]{:S(2)}) collective-permute-start(f32[20,8,128]{2,1,0:T(8,128)S(1)} %y_sum.3), channel_id=1, source_target_pairs={{0,96},{16,112},{32,64},{48,80},{64,32},{80,48},{96,0},{112,16},{1... | collective-permute-start | bytes 245768 | tf_op jit(solution)/shard_map/ppermute | solution.py:593
  78.5 6.7 %collective-permute-start.17 = (f32[20,8,128]{2,1,0:T(8,128)S(1)}, f32[20,8,128]{2,1,0:T(8,128)S(1)}, u32[]{:S(2)}, u32[]{:S(2)}) collective-permute-start(f32[20,8,128]{2,1,0:T(8,128)S(1)} %y_sum.3), channel_id=1, source_target_pairs={{0,32},{16,48},{32,0},{48,16},{64,96},{80,112},{96,64},{112,80},{1... | collective-permute-start | bytes 245768 | tf_op jit(solution)/shard_map/ppermute | solution.py:593
  80.6 5.6 %collective-permute-start.16 = (f32[20,8,128]{2,1,0:T(8,128)S(1)}, f32[20,8,128]{2,1,0:T(8,128)S(1)}, u32[]{:S(2)}, u32[]{:S(2)}) collective-permute-start(f32[20,8,128]{2,1,0:T(8,128)S(1)} %y_sum.3), channel_id=1, source_target_pairs={{0,64},{16,80},{32,96},{48,112},{64,0},{80,16},{96,32},{112,48},{1... | collective-permute-start | bytes 245768 | tf_op jit(solution)/shard_map/ppermute | solution.py:593
  81.1 13.2 %collective-permute-start.20 = (f32[128,512]{1,0:T(8,128)S(1)}, f32[128,512]{1,0:T(8,128)S(1)}, u32[]{:S(2)}, u32[]{:S(2)}) collective-permute-start(f32[128,512]{1,0:T(8,128)S(1)} %get-tuple-element.34), channel_id=1, source_target_pairs={{0,1},{1,0},{2,3},{3,2},{4,5},{5,4},{6,7},{7,6},{8,9},{9,8},{10,11... | collective-permute-start | bytes 786440 | tf_op jit(solution)/shard_map/ppermute | solution.py:610
  81.1 13.2 %collective-permute-start.21 = (f32[128,512]{1,0:T(8,128)S(1)}, f32[128,512]{1,0:T(8,128)S(1)}, u32[]{:S(2)}, u32[]{:S(2)}) collective-permute-start(f32[128,512]{1,0:T(8,128)S(1)} %get-tuple-element.35), channel_id=1, source_target_pairs={{1,2},{2,1},{3,4},{4,3},{5,6},{6,5},{7,8},{8,7},{9,10},{10,9},{11,... | collective-permute-start | bytes 786440 | tf_op jit(solution)/shard_map/ppermute | solution.py:610
  86.2 1.9 %collective-permute-start.19 = (f32[20,8,128]{2,1,0:T(8,128)S(1)}, f32[20,8,128]{2,1,0:T(8,128)S(1)}, u32[]{:S(2)}, u32[]{:S(2)}) collective-permute-start(f32[20,8,128]{2,1,0:T(8,128)S(1)} %add_add_fusion.mine_in), channel_id=1, source_target_pairs={{0,16},{16,0},{32,48},{48,32},{64,80},{80,64},{96,112},{112,96},{1... | collective-permute-start | bytes 245768 | tf_op jit(solution)/shard_map/ppermute | solution.py:586
  97.2 2.2 %collective-permute-start.22 = (f32[13,8,128]{2,1,0:T(8,128)S(1)}, f32[13,8,128]{2,1,0:T(8,128)S(1)}, u32[]{:S(2)}, u32[]{:S(2)}) collective-permute-start(f32[13,8,128]{2,1,0:T(8,128)S(1)} %get-tuple-element.38), channel_id=1, source_target_pairs={{0,16},{16,0},{32,48},{48,32},{64,80},{80,64},{96,112},{112,96},{1... | collective-permute-start | bytes 159752 | tf_op jit(solution)/shard_map/ppermute | solution.py:586
  99.5 4.5 %collective-permute-start.23 = (f32[13,8,128]{2,1,0:T(8,128)S(1)}, f32[13,8,128]{2,1,0:T(8,128)S(1)}, u32[]{:S(2)}, u32[]{:S(2)}) collective-permute-start(f32[13,8,128]{2,1,0:T(8,128)S(1)} %add.47), channel_id=1, source_target_pairs={{0,128},{16,144},{32,160},{48,176},{64,192},{80,208},{96,224},{112... | collective-permute-start | bytes 159752 | tf_op jit(solution)/shard_map/ppermute | solution.py:597
  104.0 3.5 %collective-permute-start.26 = (f32[13,8,128]{2,1,0:T(8,128)S(1)}, f32[13,8,128]{2,1,0:T(8,128)S(1)}, u32[]{:S(2)}, u32[]{:S(2)}) collective-permute-start(f32[13,8,128]{2,1,0:T(8,128)S(1)} %add.48), channel_id=1, source_target_pairs={{0,96},{16,112},{32,64},{48,80},{64,32},{80,48},{96,0},{112,16},{1... | collective-permute-start | bytes 159752 | tf_op jit(solution)/shard_map/ppermute | solution.py:593
  104.8 4.5 %collective-permute-start.25 = (f32[13,8,128]{2,1,0:T(8,128)S(1)}, f32[13,8,128]{2,1,0:T(8,128)S(1)}, u32[]{:S(2)}, u32[]{:S(2)}) collective-permute-start(f32[13,8,128]{2,1,0:T(8,128)S(1)} %add.48), channel_id=1, source_target_pairs={{0,32},{16,48},{32,0},{48,16},{64,96},{80,112},{96,64},{112,80},{1... | collective-permute-start | bytes 159752 | tf_op jit(solution)/shard_map/ppermute | solution.py:593
  107.5 4.5 %collective-permute-start.24 = (f32[13,8,128]{2,1,0:T(8,128)S(1)}, f32[13,8,128]{2,1,0:T(8,128)S(1)}, u32[]{:S(2)}, u32[]{:S(2)}) collective-permute-start(f32[13,8,128]{2,1,0:T(8,128)S(1)} %add.48), channel_id=1, source_target_pairs={{0,64},{16,80},{32,96},{48,112},{64,0},{80,16},{96,32},{112,48},{1... | collective-permute-start | bytes 159752 | tf_op jit(solution)/shard_map/ppermute | solution.py:593
  112.0 4.2 %collective-permute-start.27 = (f32[13,8,128]{2,1,0:T(8,128)S(1)}, f32[13,8,128]{2,1,0:T(8,128)S(1)}, u32[]{:S(2)}, u32[]{:S(2)}) collective-permute-start(f32[13,8,128]{2,1,0:T(8,128)S(1)} %add_add_fusion.2.mine), channel_id=1, source_target_pairs={{0,16},{16,0},{32,48},{48,32},{64,80},{80,64},{96,112},{112,96},{1... | collective-permute-start | bytes 159752 | tf_op jit(solution)/shard_map/ppermute | solution.py:586

commit v5 on v4

--- a/solution.py
+++ b/solution.py
@@ -8,10 +8,10 @@
 from jax.experimental.pallas import tpu as pltpu
 from jax.sharding import PartitionSpec as P
 
+
 VS = 16
 NY = 16
 NZ = 32
-STEPS = 3
 SEC = NY * NZ
 DEPTH = 4
 TILES = SEC // 128
@@ -228,14 +228,14 @@
 
 
 def across(values, sign):
-    ux, uz, i2t, level, qx, qz, s, qyc, rest = values
+    ux, _, i2t, level, qx, _, s, qyc, rest = values
     cx = (sub_iota() + 0.5) * (H if sign else -H) - ux
     c2 = cx * cx
     return jnp.exp(level - c2 * i2t) * RATE, qx * cx + qyc, s * c2 + rest
 
 
 def along(values, b):
-    ux, uz, i2t, level, qx, qz, s, qyc, rest = values
+    _, uz, i2t, level, _, qz, s, _, _ = values
     cz = vz_tile(b) - uz
     c2 = cz * cz
     return jnp.exp(level - c2 * i2t), qz * cz, s * c2
@@ -411,34 +411,6 @@
         other[13 + k] = jnp.where(inner, halves[1][k], halves[0][k])
 
 
-def y_kernel(first, value, across_y, near, far, *refs):
-    out = refs[-1]
-    low = low_rows()
-    inner = lax.rem(lax.axis_index("vel"), 2) == 0
-    own_rows = low == inner
-    own = [value[k] + across_y[k] for k in range(20 if first else 13)]
-    halo = [near[k] + far[k] for k in range(20 if first else 13)]
-    if first:
-        faces = refs[0]
-        sub = lax.broadcasted_iota(jnp.int32, (8, 128), 0)
-        edge = jnp.zeros((8, 128), F32)
-        for t in range(TILES):
-            edge = jnp.where(sub == t, faces[0, 0, t], edge)
-            edge = jnp.where(sub == t + TILES, faces[0, DEPTH, t], edge)
-        edge = edge * (KEEP * DT)
-        turned = pltpu.roll(edge, TILES, 0)
-        for k in range(13):
-            add = edge * doubled(halo[13 + k // 2], k)
-            own[k] = own[k] + jnp.where(own_rows, add, 0.0)
-        for k in range(13):
-            halo[k] = halo[k] + turned * doubled(own[13 + k // 2], k)
-    for k in range(13):
-        out[k] = own[k]
-    both = [jnp.where(own_rows, pltpu.roll(halo[k], TILES, 0), halo[k]) for k in range(13)]
-    for k, value in enumerate(pack(both)):
-        out[13 + k] = value
-
-
 def add_rims(ghosts, faces, state):
     def tile(t, carry):
         at = pl.multiple_of(t * 128, 128)
@@ -465,13 +437,36 @@
         spread(coefs, coefficients([ref[k] for k in range(13)], vy_of(iy)), half * 8)
 
 
-def middle_kernel(count, first, source, mine_in, other_in, faces, kind, inflow, *refs):
-    pairs = refs[: 4 if first else 2]
-    refs = refs[len(pairs) :]
-    moved, mine, other = refs[:3]
-    out_rims = refs[3 : 3 + 2 * first]
-    state, ghosts, coefs, edges, lines, sums, sems = refs[3 + 2 * first :]
-    iy = lax.axis_index("vel")
+def first_moments(mine, other, got, swapped, faces):
+    inner = lax.rem(lax.axis_index("vel"), 2) == 0
+    low = low_rows()
+    sub = lax.broadcasted_iota(jnp.int32, (8, 128), 0)
+    edge = jnp.zeros((8, 128), F32)
+    for t in range(TILES):
+        edge = jnp.where(sub == t, faces[0, 0, t], edge)
+        edge = jnp.where(sub == t + TILES, faces[0, DEPTH, t], edge)
+    edge = edge * (KEEP * DT)
+    turned = pltpu.roll(edge, TILES, 0)
+
+    def pair(a, b, k):
+        return jnp.where(inner, a[k], b[k]), jnp.where(inner, b[k], a[k])
+
+    start, end, halo = [], [], []
+    for k in range(13):
+        one, two = pair(mine, other, k)
+        one_flux, two_flux = pair(mine, other, 13 + k // 2)
+        left, right = pair(got, swapped, k)
+        left_flux, right_flux = pair(got, swapped, 13 + k // 2)
+        start.append(one + jnp.where(low, edge * doubled(left_flux, k), 0.0))
+        end.append(two + jnp.where(low, 0.0, edge * doubled(right_flux, k)))
+        halo.append(
+            jnp.where(low, right, left)
+            + turned * jnp.where(low, doubled(two_flux, k), doubled(one_flux, k))
+        )
+    return start, end, halo
+
+
+def bring_rims(pairs, ghosts, sems):
     odd = lax.rem(lax.axis_index("gx"), 2)
     copies = []
     for n in range(len(pairs) // 2):
@@ -482,22 +477,38 @@
             )
     for copy in copies:
         copy.start()
-    own_coefficients(mine_in, other_in, coefs)
-    inner = lax.rem(iy, 2) == 0
-    low = low_rows()
-    values = []
-    for k in range(13):
-        a, b = mine_in[13 + k // 2], other_in[13 + k // 2]
-        left, right = jnp.where(inner, a, b), jnp.where(inner, b, a)
-        values.append(jnp.where(low, doubled(right, k), doubled(left, k)))
-    spread(edges, coefficients(values, vy_of(iy)), 0)
+    return copies
+
+
+def second_kernel(count, source, mine_in, other_in, got, swapped, faces, kind, inflow, *refs):
+    pairs = refs[:4]
+    moved, mine, other, *out_rims = refs[4:9]
+    state, ghosts, coefs, edges, lines, sums, sems = refs[9:]
+    copies = bring_rims(pairs, ghosts, sems)
+    vy = vy_of(lax.axis_index("vel"))
+    start, end, halo = first_moments(mine_in, other_in, got, swapped, faces)
+    spread(coefs, coefficients(start, vy), 0)
+    spread(coefs, coefficients(end, vy), 8)
+    spread(edges, coefficients(halo, vy), 0)
     relax(source, coefs, lines, state, SEC)
     for copy in copies:
         copy.wait()
     relax_ghosts(ghosts, edges, lines, state)
-    if first:
-        add_rims(ghosts.at[pl.ds(2, 2)], faces, state)
+    add_rims(ghosts.at[pl.ds(2, 2)], faces, state)
     finish(state, faces, sums, kind, inflow, moved, mine, other, out_rims, count)
+
+
+def third_kernel(count, old, pair_a, pair_b, got, swapped, faces, kind, inflow, *refs):
+    state, moved, mine, other, ghosts, edges, lines, sums, sems = refs
+    copies = bring_rims((pair_a, pair_b), ghosts, sems)
+    iy = lax.axis_index("vel")
+    pick = low_rows() != (lax.rem(iy, 2) == 0)
+    values = [jnp.where(pick, got[k], swapped[k]) for k in range(13)]
+    spread(edges, coefficients(values, vy_of(iy)), 0)
+    for copy in copies:
+        copy.wait()
+    relax_ghosts(ghosts, edges, lines, state)
+    finish(state, faces, sums, kind, inflow, moved, mine, other, (), count)
 
 
 VM = pl.BlockSpec(memory_space=pltpu.VMEM)
@@ -533,52 +544,61 @@
     )(dist, wall, kind, inflow)
 
 
-def y_sum(first, *arrays):
+def move_second(source, halves, faces, kind, inflow, pairs, count):
+    outs = (WHOLE, PART, PART, RIM, RIM)
     return pl.pallas_call(
-        functools.partial(y_kernel, first),
-        out_shape=FULL,
-        in_specs=[VM] * len(arrays),
-        out_specs=VM,
-        compiler_params=pltpu.CompilerParams(vmem_limit_bytes=4 << 20),
-        name="y_sum",
-    )(*arrays)
-
-
-def move_middle(source, mine, other, faces, kind, inflow, pairs, count, first):
-    outs = (WHOLE, PART, PART) + (RIM, RIM) * first
-    return pl.pallas_call(
-        functools.partial(middle_kernel, count, first),
+        functools.partial(second_kernel, count),
         out_shape=outs,
-        in_specs=[VM] * 6 + [ANY] * len(pairs),
+        in_specs=[VM] * 8 + [ANY] * 4,
         out_specs=(VM,) * len(outs),
         scratch_shapes=[
             pltpu.VMEM(WIDE.shape, F32),
-            pltpu.VMEM((len(pairs), HALF, SEC), F32),
+            pltpu.VMEM((4, HALF, SEC), F32),
             pltpu.VMEM((9, OWN, 8, 128), F32),
             pltpu.VMEM((9, 8, 8, 128), F32),
             LINES,
             SUMS,
-            pltpu.SemaphoreType.DMA((len(pairs),)),
+            pltpu.SemaphoreType.DMA((4,)),
         ],
         compiler_params=PARAMS,
-        name="move_middle",
-    )(source, mine, other, faces, kind, inflow, *pairs)
-
-
-def last_kernel(moved, mine, other, state, coefs, lines):
+        name="move_second",
+    )(source, *halves, faces, kind, inflow, *pairs)
+
+
+def move_third(state, pairs, got, swapped, faces, kind, inflow, count):
+    outs = (WIDE, WHOLE, PART, PART)
+    return pl.pallas_call(
+        functools.partial(third_kernel, count),
+        out_shape=outs,
+        in_specs=[VM, ANY, ANY] + [VM] * 5,
+        out_specs=(VM,) * len(outs),
+        input_output_aliases={0: 0},
+        scratch_shapes=[
+            pltpu.VMEM((2, HALF, SEC), F32),
+            pltpu.VMEM((9, 8, 8, 128), F32),
+            LINES,
+            SUMS,
+            pltpu.SemaphoreType.DMA((2,)),
+        ],
+        compiler_params=PARAMS,
+        name="move_third",
+    )(state, *pairs, got, swapped, faces, kind, inflow)[1:]
+
+
+def relax_kernel(shift, moved, mine, other, state, coefs, lines):
     own_coefficients(mine, other, coefs)
-    relax(moved, coefs, lines, state, 0)
-
-
-def relax_last(moved, mine, other):
+    relax(moved, coefs, lines, state, shift)
+
+
+def relaxed(moved, mine, other, last):
     return pl.pallas_call(
-        last_kernel,
-        out_shape=WHOLE,
+        functools.partial(relax_kernel, 0 if last else SEC),
+        out_shape=WHOLE if last else WIDE,
         in_specs=[VM, VM, VM],
         out_specs=VM,
         scratch_shapes=[pltpu.VMEM((9, OWN, 8, 128), F32), LINES],
         compiler_params=PARAMS,
-        name="relax_last",
+        name="relax_last" if last else "relax",
     )(moved, mine, other)
 
 
@@ -598,8 +618,15 @@
 
 
 def sum_x(value):
-    parts = [shift_x(value, by) for by in (1, 3, 2)]
+    parts = []
+    for by in (1, 3, 2):
+        parts.append(shift_x(value, by))
     return (value + parts[2]) + (parts[0] + parts[1])
+
+
+def sum_chips(value):
+    value = sum_x(value)
+    return value + flip_y(value)
 
 
 def swap_rims(pair_a, pair_b, count):
@@ -607,21 +634,18 @@
     far = []
     for i in range(1, count - 1, 2):
         far += [(i, i + 1), (i + 1, i)]
-    return lax.ppermute(pair_a, "gx", near), lax.ppermute(pair_b, "gx", far)
-
-
-def to_neighbours(half, count, flip):
+    pair_a = lax.ppermute(pair_a, "gx", near)
+    pair_b = lax.ppermute(pair_b, "gx", far)
+    return pair_a, pair_b
+
+
+def swap_moments(half, count):
     pairs = []
     for v in range(0, VS, 2):
         for g in range(count - 1):
-            one, two = (v + 1) * count + g, (v ^ flip) * count + g + 1
+            one, two = (v + 1) * count + g, v * count + g + 1
             pairs += [(one, two), (two, one)]
     return lax.ppermute(half, ("vel", "gx"), pairs)
-
-
-def stage_y(value, count, *faces):
-    moves = (flip_y(value), to_neighbours(value, count, 0), to_neighbours(value, count, 8))
-    return y_sum(bool(faces), value, *moves, *faces)
 
 
 def per_device(distribution, wall_mask, boundary_kind, inflow):
@@ -631,27 +655,26 @@
     up = distribution[HALF:, (DEPTH - 1) * SEC :]
     down = distribution[:HALF, :SEC]
     start = swap_rims(jnp.where(even, up, down), jnp.where(even, down, up), count)
-    faces, *outs = move_first(distribution, wall_mask, boundary_kind, inflow, count)
-    moved, mine, other, *rims = outs
+    outs = move_first(distribution, wall_mask, boundary_kind, inflow, count)
+    faces, moved, mine, other, *rims = outs
     pairs = swap_rims(*rims, count)
-    half = stage_y(sum_x(mine + swap_cores(other)), count, faces)
-    outs = move_middle(
-        moved, half, swap_cores(half), faces, boundary_kind, inflow, (*pairs, *start), count, True
+    half = sum_chips(mine + swap_cores(other))
+    halo = swap_moments(half, count)
+    swapped = swap_cores(half)
+    halves = (half, swapped, halo, swap_cores(halo))
+    moved, mine, other, *rims = move_second(
+        moved, halves, faces, boundary_kind, inflow, (*pairs, *start), count
     )
-    moved, mine, other, *rims = outs
-    half = stage_y(mine + swap_cores(other), count)
-    half, *rims = lax.optimization_barrier((half, *rims))
     pairs = swap_rims(*rims, count)
-    half = sum_x(half)
-    moved, mine, other = move_middle(
-        moved, half, swap_cores(half), faces, boundary_kind, inflow, pairs, count, False
+    half = sum_chips(mine + swap_cores(other))
+    halo = swap_moments(half, count)
+    state = relaxed(moved, half, swap_cores(half), False)
+    halo, state = lax.optimization_barrier((halo, state))
+    moved, mine, other = move_third(
+        state, pairs, halo, swap_cores(halo), faces, boundary_kind, inflow, count
     )
-    half = sum_x(flip_y_sum(mine + swap_cores(other)))
-    return relax_last(moved, half, swap_cores(half))
-
-
-def flip_y_sum(value):
-    return value + flip_y(value)
+    half = sum_chips(mine + swap_cores(other))
+    return relaxed(moved, half, swap_cores(half), True)
 
 
 def solution(mesh):

time: 119 us -> 109 us (0.916); the launches traced: 118 us -> 107 us
  starting transfers between devices: 56 us -> 47.9 us
  waiting for transfers between devices: 46.7 us -> 43.3 us
    ppermute x3, waiting for transfers between devices: 17.1 us -> 28.5 us  [flip_y(): return lax.ppermute(array, 'vel', [(i, i ^ 8) for i in range(VS)])]
    ppermute x10 -> x8, waiting for transfers between devices: 13.9 us -> 3.91 us  [the longest x2 3.89 us: swap_moments(): return lax.ppermute(half, ('vel', 'gx'), pairs)]
    ppermute x6 -> x8, starting transfers between devices: 14.2 us -> 6.03 us  [swap_cores(): return lax.ppermute(array, 'vel', [(i, i ^ 1) for i in range(VS)])]
    ppermute x10 -> x8, starting transfers between devices: 32.3 us -> 25.6 us  [the longest x3 11.7 us: swap_rims(): pair_b = lax.ppermute(pair_b, 'gx', far)]
    ppermute x9, waiting for transfers between devices: 10.2 us -> 4.5 us  [shift_x(): return lax.ppermute(array, 'vel', [(i, mate(i)) for i in range(VS)])]
    ppermute x3, starting transfers between devices: 0.48 us -> 5.55 us  [flip_y(): return lax.ppermute(array, 'vel', [(i, i ^ 8) for i in range(VS)])]
    ppermute x9, starting transfers between devices: 9 us -> 10.7 us  [shift_x(): return lax.ppermute(array, 'vel', [(i, mate(i)) for i in range(VS)])]
    ppermute x6 -> x8, waiting for transfers between devices: 5.41 us -> 6.44 us  [swap_cores(): return lax.ppermute(array, 'vel', [(i, i ^ 1) for i in range(VS)])]
  transfers between devices with their start and end apart: 28 -> 28, of which waited for: 18 -> 13; matrix products, arithmetic and copies ran while one was open for 1% -> 1% of each run, Pallas kernels for 0% -> 1%
where the time goes in v5:
time: 109 us; the launch traced here: 107 us
  starting transfers between devices  47.9 us (44%)
  waiting for transfers between devices  43.3 us (40%)
  Pallas kernels  10.7 us (10%)
  local copies, waits for them, and re-layouts  3.87 us (4%)
  other arithmetic  1.18 us (1%)
    ppermute x3, waiting for transfers between devices, flip_y(): return lax.ppermute(array, 'vel', [(i, i ^ 8) for i in range(VS)])  28.5 us
    ppermute x3, starting transfers between devices, swap_rims(): pair_b = lax.ppermute(pair_b, 'gx', far)  11.7 us
    ppermute x2, starting transfers between devices, swap_moments(): return lax.ppermute(half, ('vel', 'gx'), pairs)  11.2 us
    ppermute x9, starting transfers between devices, shift_x(): return lax.ppermute(array, 'vel', [(i, mate(i)) for i in range(VS)])  10.7 us
    ppermute x8, waiting for transfers between devices, swap_cores(): return lax.ppermute(array, 'vel', [(i, i ^ 1) for i in range(VS)])  6.44 us
    ppermute x8, starting transfers between devices, swap_cores(): return lax.ppermute(array, 'vel', [(i, i ^ 1) for i in range(VS)])  6.03 us
    ppermute x3, starting transfers between devices, flip_y(): return lax.ppermute(array, 'vel', [(i, i ^ 8) for i in range(VS)])  5.55 us
    ppermute x9, waiting for transfers between devices, shift_x(): return lax.ppermute(array, 'vel', [(i, mate(i)) for i in range(VS)])  4.5 us
  transfers between devices with their start and end apart: 28, of which 13 were waited for; matrix products, arithmetic and copies ran while one was open for 1% of the time, Pallas kernels for 1%

profile of v5, /device:TPU:107, one launch (start us, length us, event | category | flops | bytes accessed | tf_op | source)
XLA Modules:
  0.0 107.1 jit_solution(1222544186713436280)
XLA Ops:
  0.0 1.6 %copy-done = f32[256,2048]{1,0:T(8,128)S(1)} copy-done((f32[256,2048]{1,0:T(8,128)S(1)}, f32[256,2048]{1,0:T(8,128)}, u32[]{:S(2)}) %copy-start) | copy-done | bytes 2097176
  1.6 0.9 copy-done.1
  2.5 0.7 copy-done.2
  3.2 0.7 copy-done.4
  3.9 2.3 %move_first.1 = (f32[5,5,4,8,128]{4,3,2,1,0:T(8,128)S(1)}, f32[256,2048]{1,0:T(8,128)S(1)}, f32[20,8,128]{2,1,0:T(8,128)S(1)}, f32[20,8,128]{2,1,0:T(8,128)S(1)}...) custom-call(f32[256,2048]{1,0:T(8,128)S(1)} %copy-done, s32[64,512]{1,0:T(8,128)S(1)} %copy-done.1, ...), custom_call_target="tpu_custom_call" | custom-call | tf_op jit(solution)/shard_map/move_first/pallas_call | solution.py:531
  6.2 0.8 collective-permute-start
  7.0 0.9 collective-permute-done
  7.9 1.3 %collective-permute-start.3 = (f32[20,8,128]{2,1,0:T(8,128)S(1)}, f32[20,8,128]{2,1,0:T(8,128)S(1)}, u32[]{:S(2)}, u32[]{:S(2)}) collective-permute-start(f32[20,8,128]{2,1,0:T(8,128)S(1)} %add.45), channel_id=1, source_target_pairs={{0,96},{16,112},{32,64},{48,80},{64,32},{80,48},{96,0},{112,16},{1... | collective-permute-start | bytes 245768 | tf_op jit(solution)/shard_map/ppermute | solution.py:613
  9.2 1.5 %collective-permute-start.2 = (f32[20,8,128]{2,1,0:T(8,128)S(1)}, f32[20,8,128]{2,1,0:T(8,128)S(1)}, u32[]{:S(2)}, u32[]{:S(2)}) collective-permute-start(f32[20,8,128]{2,1,0:T(8,128)S(1)} %add.45), channel_id=1, source_target_pairs={{0,32},{16,48},{32,0},{48,16},{64,96},{80,112},{96,64},{112,80},{1... | collective-permute-start | bytes 245768 | tf_op jit(solution)/shard_map/ppermute | solution.py:613
  10.7 0.0 collective-permute-start.1
  10.7 1.1 slice_select_fusion
  11.8 4.6 %collective-permute-start.11 = (f32[128,512]{1,0:T(8,128)S(1)}, f32[128,512]{1,0:T(8,128)S(1)}, u32[]{:S(2)}, u32[]{:S(2)}) collective-permute-start(f32[128,512]{1,0:T(8,128)S(1)} %get-tuple-element.37), channel_id=1, source_target_pairs={{1,2},{2,1},{3,4},{4,3},{5,6},{6,5},{7,8},{8,7},{9,10},{10,9},{11,... | collective-permute-start | bytes 786440 | tf_op jit(solution)/shard_map/ppermute | solution.py:638
  16.5 0.1 collective-permute-start.10
  16.6 1.4 %collective-permute-start.8 = (f32[128,512]{1,0:T(8,128)S(1)}, f32[128,512]{1,0:T(8,128)S(1)}, u32[]{:S(2)}, u32[]{:S(2)}) collective-permute-start(f32[128,512]{1,0:T(8,128)S(1)} %get-tuple-element.25), channel_id=1, source_target_pairs={{0,1},{1,0},{2,3},{3,2},{4,5},{5,4},{6,7},{7,6},{8,9},{9,8},{10,11... | collective-permute-start | bytes 786440 | tf_op jit(solution)/shard_map/ppermute | solution.py:637
  18.0 2.7 %collective-permute-start.9 = (f32[128,512]{1,0:T(8,128)S(1)}, f32[128,512]{1,0:T(8,128)S(1)}, u32[]{:S(2)}, u32[]{:S(2)}) collective-permute-start(f32[128,512]{1,0:T(8,128)S(1)} %get-tuple-element.26), channel_id=1, source_target_pairs={{1,2},{2,1},{3,4},{4,3},{5,6},{6,5},{7,8},{8,7},{9,10},{10,9},{11,... | collective-permute-start | bytes 786440 | tf_op jit(solution)/shard_map/ppermute | solution.py:638
  20.8 2.1 %collective-permute-start.4 = (f32[20,8,128]{2,1,0:T(8,128)S(1)}, f32[20,8,128]{2,1,0:T(8,128)S(1)}, u32[]{:S(2)}, u32[]{:S(2)}) collective-permute-start(f32[20,8,128]{2,1,0:T(8,128)S(1)} %add_add_fusion), channel_id=1, source_target_pairs={{0,128},{16,144},{32,160},{48,176},{64,192},{80,208},{96,224},{112... | collective-permute-start | bytes 245768 | tf_op jit(solution)/shard_map/ppermute | solution.py:617
  22.9 19.5 %collective-permute-done.4 = f32[20,8,128]{2,1,0:T(8,128)S(1)} collective-permute-done((f32[20,8,128]{2,1,0:T(8,128)S(1)}, f32[20,8,128]{2,1,0:T(8,128)S(1)}, u32[]{:S(2)}, u32[]{:S(2)}) %collective-permute-start.4) | collective-permute-done | bytes 81952 | tf_op jit(solution)/shard_map/ppermute | solution.py:617
  42.5 6.5 %collective-permute-start.6 = (f32[20,8,128]{2,1,0:T(8,128)S(1)}, f32[20,8,128]{2,1,0:T(8,128)S(1)}, u32[]{:S(2)}, u32[]{:S(2)}) collective-permute-start(f32[20,8,128]{2,1,0:T(8,128)S(1)} %add.49.mine_in), channel_id=1, source_target_pairs={{16,1},{1,16},{17,2},{2,17},{18,3},{3,18},{19,4},{4,19},{20,5},{5,... | collective-permute-start | bytes 245768 | tf_op jit(solution)/shard_map/ppermute | solution.py:648
  49.0 0.1 collective-permute-start.5
  49.1 2.0 %collective-permute-done.6.got = f32[20,8,128]{2,1,0:T(8,128)S(1)} collective-permute-done((f32[20,8,128]{2,1,0:T(8,128)S(1)}, f32[20,8,128]{2,1,0:T(8,128)S(1)}, u32[]{:S(2)}, u32[]{:S(2)}) %collective-permute-start.6) | collective-permute-done | bytes 81952 | tf_op jit(solution)/shard_map/ppermute | solution.py:648
  51.1 1.2 %collective-permute-done.7.swapped = f32[20,8,128]{2,1,0:T(8,128)S(1)} collective-permute-done((f32[20,8,128]{2,1,0:T(8,128)S(1)}, f32[20,8,128]{2,1,0:T(8,128)S(1)}, u32[]{:S(2)}, u32[]{:S(2)}) %collective-permute-start.7) | collective-permute-done | bytes 81952 | tf_op jit(solution)/shard_map/ppermute | solution.py:606
  52.3 3.2 %move_second.1 = (f32[256,2048]{1,0:T(8,128)S(1)}, f32[13,8,128]{2,1,0:T(8,128)S(1)}, f32[13,8,128]{2,1,0:T(8,128)S(1)}, f32[128,512]{1,0:T(8,128)S(1)}, f32[128,512]{1,0:T(8,128)S(1)}) custom-call(f32[256,2048]{1,0:T(8,128)S(1)} %get-tuple-element.21.source, f32[20,8,128]{2,1,0:T(8,128)S(1)} %add.49.mine_in, ...), custom_call_target="tpu_custom_call" | custom-call | tf_op jit(solution)/shard_map/move_second/pallas_call | solution.py:549
  55.5 0.2 collective-permute-start.12
  55.8 1.1 %collective-permute-done.12 = f32[13,8,128]{2,1,0:T(8,128)S(1)} collective-permute-done((f32[13,8,128]{2,1,0:T(8,128)S(1)}, f32[13,8,128]{2,1,0:T(8,128)S(1)}, u32[]{:S(2)}, u32[]{:S(2)}) %collective-permute-start.12) | collective-permute-done | bytes 53280 | tf_op jit(solution)/shard_map/ppermute | solution.py:606
  56.9 1.3 %collective-permute-start.15 = (f32[13,8,128]{2,1,0:T(8,128)S(1)}, f32[13,8,128]{2,1,0:T(8,128)S(1)}, u32[]{:S(2)}, u32[]{:S(2)}) collective-permute-start(f32[13,8,128]{2,1,0:T(8,128)S(1)} %add.50), channel_id=1, source_target_pairs={{0,96},{16,112},{32,64},{48,80},{64,32},{80,48},{96,0},{112,16},{1... | collective-permute-start | bytes 159752 | tf_op jit(solution)/shard_map/ppermute | solution.py:613
  58.1 2.7 %collective-permute-start.14 = (f32[13,8,128]{2,1,0:T(8,128)S(1)}, f32[13,8,128]{2,1,0:T(8,128)S(1)}, u32[]{:S(2)}, u32[]{:S(2)}) collective-permute-start(f32[13,8,128]{2,1,0:T(8,128)S(1)} %add.50), channel_id=1, source_target_pairs={{0,32},{16,48},{32,0},{48,16},{64,96},{80,112},{96,64},{112,80},{1... | collective-permute-start | bytes 159752 | tf_op jit(solution)/shard_map/ppermute | solution.py:613
  60.8 1.1 %collective-permute-start.19 = (f32[128,512]{1,0:T(8,128)S(1)}, f32[128,512]{1,0:T(8,128)S(1)}, u32[]{:S(2)}, u32[]{:S(2)}) collective-permute-start(f32[128,512]{1,0:T(8,128)S(1)} %get-tuple-element.31), channel_id=1, source_target_pairs={{0,1},{1,0},{2,3},{3,2},{4,5},{5,4},{6,7},{7,6},{8,9},{9,8},{10,11... | collective-permute-start | bytes 786440 | tf_op jit(solution)/shard_map/ppermute | solution.py:637
  61.9 4.4 %collective-permute-start.20 = (f32[128,512]{1,0:T(8,128)S(1)}, f32[128,512]{1,0:T(8,128)S(1)}, u32[]{:S(2)}, u32[]{:S(2)}) collective-permute-start(f32[128,512]{1,0:T(8,128)S(1)} %get-tuple-element.32), channel_id=1, source_target_pairs={{1,2},{2,1},{3,4},{4,3},{5,6},{6,5},{7,8},{8,7},{9,10},{10,9},{11,... | collective-permute-start | bytes 786440 | tf_op jit(solution)/shard_map/ppermute | solution.py:638
  66.4 0.1 collective-permute-start.16
  66.5 7.4 %collective-permute-done.16 = f32[13,8,128]{2,1,0:T(8,128)S(1)} collective-permute-done((f32[13,8,128]{2,1,0:T(8,128)S(1)}, f32[13,8,128]{2,1,0:T(8,128)S(1)}, u32[]{:S(2)}, u32[]{:S(2)}) %collective-permute-start.16) | collective-permute-done | bytes 53280 | tf_op jit(solution)/shard_map/ppermute | solution.py:617
  73.9 1.9 %collective-permute-start.18 = (f32[13,8,128]{2,1,0:T(8,128)S(1)}, f32[13,8,128]{2,1,0:T(8,128)S(1)}, u32[]{:S(2)}, u32[]{:S(2)}) collective-permute-start(f32[13,8,128]{2,1,0:T(8,128)S(1)} %add.54.mine), channel_id=1, source_target_pairs={{0,16},{16,0},{32,48},{48,32},{64,80},{80,64},{96,112},{112,96},{1... | collective-permute-start | bytes 159752 | tf_op jit(solution)/shard_map/ppermute | solution.py:606
  75.8 4.7 %collective-permute-start.17 = (f32[13,8,128]{2,1,0:T(8,128)S(1)}, f32[13,8,128]{2,1,0:T(8,128)S(1)}, u32[]{:S(2)}, u32[]{:S(2)}) collective-permute-start(f32[13,8,128]{2,1,0:T(8,128)S(1)} %add.54.mine), channel_id=1, source_target_pairs={{16,1},{1,16},{17,2},{2,17},{18,3},{3,18},{19,4},{4,19},{20,5},{5,... | collective-permute-start | bytes 159752 | tf_op jit(solution)/shard_map/ppermute | solution.py:648
  80.5 0.9 relax.1.old
  81.4 1.9 %collective-permute-done.17.got = f32[13,8,128]{2,1,0:T(8,128)S(1)} collective-permute-done((f32[13,8,128]{2,1,0:T(8,128)S(1)}, f32[13,8,128]{2,1,0:T(8,128)S(1)}, u32[]{:S(2)}, u32[]{:S(2)}) %collective-permute-start.17) | collective-permute-done | bytes 53280 | tf_op jit(solution)/shard_map/ppermute | solution.py:648
  83.3 0.0 collective-permute-start.21
  83.3 1.2 %collective-permute-done.21.swapped = f32[13,8,128]{2,1,0:T(8,128)S(1)} collective-permute-done((f32[13,8,128]{2,1,0:T(8,128)S(1)}, f32[13,8,128]{2,1,0:T(8,128)S(1)}, u32[]{:S(2)}, u32[]{:S(2)}) %collective-permute-start.21) | collective-permute-done | bytes 53280 | tf_op jit(solution)/shard_map/ppermute | solution.py:606
  84.6 2.0 %move_third.1 = (f32[256,3072]{1,0:T(8,128)S(1)}, f32[256,2048]{1,0:T(8,128)S(1)}, f32[13,8,128]{2,1,0:T(8,128)S(1)}, f32[13,8,128]{2,1,0:T(8,128)S(1)}) custom-call(f32[256,3072]{1,0:T(8,128)S(1)} %relax.1.old, f32[128,512]{1,0:T(8,128)S(1)} %collective-permute-done.19.pair_a, ...), custom_call_target="tpu_custom_call", output_to_operand_aliasing={{0}: (0, {})} | custom-call | tf_op jit(solution)/shard_map/move_third/pallas_call | solution.py:570
  86.6 0.2 collective-permute-start.22
  86.8 1.1 %collective-permute-done.22 = f32[13,8,128]{2,1,0:T(8,128)S(1)} collective-permute-done((f32[13,8,128]{2,1,0:T(8,128)S(1)}, f32[13,8,128]{2,1,0:T(8,128)S(1)}, u32[]{:S(2)}, u32[]{:S(2)}) %collective-permute-start.22) | collective-permute-done | bytes 53280 | tf_op jit(solution)/shard_map/ppermute | solution.py:606
  87.9 1.3 %collective-permute-start.25 = (f32[13,8,128]{2,1,0:T(8,128)S(1)}, f32[13,8,128]{2,1,0:T(8,128)S(1)}, u32[]{:S(2)}, u32[]{:S(2)}) collective-permute-start(f32[13,8,128]{2,1,0:T(8,128)S(1)} %add.55), channel_id=1, source_target_pairs={{0,96},{16,112},{32,64},{48,80},{64,32},{80,48},{96,0},{112,16},{1... | collective-permute-start | bytes 159752 | tf_op jit(solution)/shard_map/ppermute | solution.py:613
  89.2 2.7 %collective-permute-start.24 = (f32[13,8,128]{2,1,0:T(8,128)S(1)}, f32[13,8,128]{2,1,0:T(8,128)S(1)}, u32[]{:S(2)}, u32[]{:S(2)}) collective-permute-start(f32[13,8,128]{2,1,0:T(8,128)S(1)} %add.55), channel_id=1, source_target_pairs={{0,32},{16,48},{32,0},{48,16},{64,96},{80,112},{96,64},{112,80},{1... | collective-permute-start | bytes 159752 | tf_op jit(solution)/shard_map/ppermute | solution.py:613
  91.8 1.5 %collective-permute-done.24 = f32[13,8,128]{2,1,0:T(8,128)S(1)} collective-permute-done((f32[13,8,128]{2,1,0:T(8,128)S(1)}, f32[13,8,128]{2,1,0:T(8,128)S(1)}, u32[]{:S(2)}, u32[]{:S(2)}) %collective-permute-start.24) | collective-permute-done | bytes 53280 | tf_op jit(solution)/shard_map/ppermute | solution.py:613
  93.4 3.0 %collective-permute-done.23 = f32[13,8,128]{2,1,0:T(8,128)S(1)} collective-permute-done((f32[13,8,128]{2,1,0:T(8,128)S(1)}, f32[13,8,128]{2,1,0:T(8,128)S(1)}, u32[]{:S(2)}, u32[]{:S(2)}) %collective-permute-start.23) | collective-permute-done | bytes 53280 | tf_op jit(solution)/shard_map/ppermute | solution.py:613
  96.3 3.3 %collective-permute-start.26 = (f32[13,8,128]{2,1,0:T(8,128)S(1)}, f32[13,8,128]{2,1,0:T(8,128)S(1)}, u32[]{:S(2)}, u32[]{:S(2)}) collective-permute-start(f32[13,8,128]{2,1,0:T(8,128)S(1)} %add_add_fusion.1), channel_id=1, source_target_pairs={{0,128},{16,144},{32,160},{48,176},{64,192},{80,208},{96,224},{112... | collective-permute-start | bytes 159752 | tf_op jit(solution)/shard_map/ppermute | solution.py:617
  99.7 1.5 %collective-permute-done.26 = f32[13,8,128]{2,1,0:T(8,128)S(1)} collective-permute-done((f32[13,8,128]{2,1,0:T(8,128)S(1)}, f32[13,8,128]{2,1,0:T(8,128)S(1)}, u32[]{:S(2)}, u32[]{:S(2)}) %collective-permute-start.26) | collective-permute-done | bytes 53280 | tf_op jit(solution)/shard_map/ppermute | solution.py:617
  101.2 2.8 %collective-permute-start.27 = (f32[13,8,128]{2,1,0:T(8,128)S(1)}, f32[13,8,128]{2,1,0:T(8,128)S(1)}, u32[]{:S(2)}, u32[]{:S(2)}) collective-permute-start(f32[13,8,128]{2,1,0:T(8,128)S(1)} %add.59.mine), channel_id=1, source_target_pairs={{0,16},{16,0},{32,48},{48,32},{64,80},{80,64},{96,112},{112,96},{1... | collective-permute-start | bytes 159752 | tf_op jit(solution)/shard_map/ppermute | solution.py:606
  104.0 0.9 collective-permute-done.27.other
  104.9 2.2 %relax_last.1 = f32[256,2048]{1,0:T(8,128)} custom-call(f32[256,2048]{1,0:T(8,128)S(1)} %get-tuple-element.34.moved, f32[13,8,128]{2,1,0:T(8,128)S(1)} %add.59.mine, f32[13,8,128]{2,1,0:T(8,128)S(1)} %collective-permute-done.27.other), custom_call_target="tpu_custom_call" | custom-call | tf_op jit(solution)/shard_map/relax_last/pallas_call | solution.py:594
  (35 shorter events, 0.2 us)
Async XLA Ops:
  0.0 1.6 %copy-start = (f32[256,2048]{1,0:T(8,128)S(1)}, f32[256,2048]{1,0:T(8,128)}, u32[]{:S(2)}) copy-start(f32[256,2048]{1,0:T(8,128)} %dist.1) | copy-start | bytes 6291460
  1.6 0.9 copy-start.1
  2.5 0.7 copy-start.2
  3.2 0.7 copy-start.4
  3.9 48.5 %copy-start.3 = (s32[2,512]{1,0:T(2,128)S(1)}, s32[2,512]{1,0:T(2,128)}, u32[]{:S(2)}) copy-start(s32[2,512]{1,0:T(2,128)} %kind.5) | copy-start | bytes 12292
  3.9 48.5 %copy-start.5 = (f32[256]{0:T(256)S(1)}, f32[256]{0:T(256)}, u32[]{:S(2)}) copy-start(f32[256]{0:T(256)} %param.7) | copy-start | bytes 3076
  6.2 1.7 %collective-permute-start = (f32[20,8,128]{2,1,0:T(8,128)S(1)}, f32[20,8,128]{2,1,0:T(8,128)S(1)}, u32[]{:S(2)}, u32[]{:S(2)}) collective-permute-start(f32[20,8,128]{2,1,0:T(8,128)S(1)} %get-tuple-element.23), channel_id=1, source_target_pairs={{0,16},{16,0},{32,48},{48,32},{64,80},{80,64},{96,112},{112,96},{1... | collective-permute-start | bytes 245768 | tf_op jit(solution)/shard_map/ppermute | solution.py:606
  7.9 8.6 %collective-permute-start.3 = (f32[20,8,128]{2,1,0:T(8,128)S(1)}, f32[20,8,128]{2,1,0:T(8,128)S(1)}, u32[]{:S(2)}, u32[]{:S(2)}) collective-permute-start(f32[20,8,128]{2,1,0:T(8,128)S(1)} %add.45), channel_id=1, source_target_pairs={{0,96},{16,112},{32,64},{48,80},{64,32},{80,48},{96,0},{112,16},{1... | collective-permute-start | bytes 245768 | tf_op jit(solution)/shard_map/ppermute | solution.py:613
  9.2 8.8 %collective-permute-start.2 = (f32[20,8,128]{2,1,0:T(8,128)S(1)}, f32[20,8,128]{2,1,0:T(8,128)S(1)}, u32[]{:S(2)}, u32[]{:S(2)}) collective-permute-start(f32[20,8,128]{2,1,0:T(8,128)S(1)} %add.45), channel_id=1, source_target_pairs={{0,32},{16,48},{32,0},{48,16},{64,96},{80,112},{96,64},{112,80},{1... | collective-permute-start | bytes 245768 | tf_op jit(solution)/shard_map/ppermute | solution.py:613
  10.7 10.0 %collective-permute-start.1 = (f32[20,8,128]{2,1,0:T(8,128)S(1)}, f32[20,8,128]{2,1,0:T(8,128)S(1)}, u32[]{:S(2)}, u32[]{:S(2)}) collective-permute-start(f32[20,8,128]{2,1,0:T(8,128)S(1)} %add.45), channel_id=1, source_target_pairs={{0,64},{16,80},{32,96},{48,112},{64,0},{80,16},{96,32},{112,48},{1... | collective-permute-start | bytes 245768 | tf_op jit(solution)/shard_map/ppermute | solution.py:613
  11.8 37.1 %collective-permute-start.11 = (f32[128,512]{1,0:T(8,128)S(1)}, f32[128,512]{1,0:T(8,128)S(1)}, u32[]{:S(2)}, u32[]{:S(2)}) collective-permute-start(f32[128,512]{1,0:T(8,128)S(1)} %get-tuple-element.37), channel_id=1, source_target_pairs={{1,2},{2,1},{3,4},{4,3},{5,6},{6,5},{7,8},{8,7},{9,10},{10,9},{11,... | collective-permute-start | bytes 786440 | tf_op jit(solution)/shard_map/ppermute | solution.py:638
  16.5 34.6 %collective-permute-start.10 = (f32[128,512]{1,0:T(8,128)S(1)}, f32[128,512]{1,0:T(8,128)S(1)}, u32[]{:S(2)}, u32[]{:S(2)}) collective-permute-start(f32[128,512]{1,0:T(8,128)S(1)} %get-tuple-element.38), channel_id=1, source_target_pairs={{0,1},{1,0},{2,3},{3,2},{4,5},{5,4},{6,7},{7,6},{8,9},{9,8},{10,11... | collective-permute-start | bytes 786440 | tf_op jit(solution)/shard_map/ppermute | solution.py:637
  16.6 34.5 %collective-permute-start.8 = (f32[128,512]{1,0:T(8,128)S(1)}, f32[128,512]{1,0:T(8,128)S(1)}, u32[]{:S(2)}, u32[]{:S(2)}) collective-permute-start(f32[128,512]{1,0:T(8,128)S(1)} %get-tuple-element.25), channel_id=1, source_target_pairs={{0,1},{1,0},{2,3},{3,2},{4,5},{5,4},{6,7},{7,6},{8,9},{9,8},{10,11... | collective-permute-start | bytes 786440 | tf_op jit(solution)/shard_map/ppermute | solution.py:637
  18.0 33.1 %collective-permute-start.9 = (f32[128,512]{1,0:T(8,128)S(1)}, f32[128,512]{1,0:T(8,128)S(1)}, u32[]{:S(2)}, u32[]{:S(2)}) collective-permute-start(f32[128,512]{1,0:T(8,128)S(1)} %get-tuple-element.26), channel_id=1, source_target_pairs={{1,2},{2,1},{3,4},{4,3},{5,6},{6,5},{7,8},{8,7},{9,10},{10,9},{11,... | collective-permute-start | bytes 786440 | tf_op jit(solution)/shard_map/ppermute | solution.py:638
  20.8 21.6 %collective-permute-start.4 = (f32[20,8,128]{2,1,0:T(8,128)S(1)}, f32[20,8,128]{2,1,0:T(8,128)S(1)}, u32[]{:S(2)}, u32[]{:S(2)}) collective-permute-start(f32[20,8,128]{2,1,0:T(8,128)S(1)} %add_add_fusion), channel_id=1, source_target_pairs={{0,128},{16,144},{32,160},{48,176},{64,192},{80,208},{96,224},{112... | collective-permute-start | bytes 245768 | tf_op jit(solution)/shard_map/ppermute | solution.py:617
  42.5 8.6 %collective-permute-start.6 = (f32[20,8,128]{2,1,0:T(8,128)S(1)}, f32[20,8,128]{2,1,0:T(8,128)S(1)}, u32[]{:S(2)}, u32[]{:S(2)}) collective-permute-start(f32[20,8,128]{2,1,0:T(8,128)S(1)} %add.49.mine_in), channel_id=1, source_target_pairs={{16,1},{1,16},{17,2},{2,17},{18,3},{3,18},{19,4},{4,19},{20,5},{5,... | collective-permute-start | bytes 245768 | tf_op jit(solution)/shard_map/ppermute | solution.py:648
  49.0 2.1 %collective-permute-start.5 = (f32[20,8,128]{2,1,0:T(8,128)S(1)}, f32[20,8,128]{2,1,0:T(8,128)S(1)}, u32[]{:S(2)}, u32[]{:S(2)}) collective-permute-start(f32[20,8,128]{2,1,0:T(8,128)S(1)} %add.49.mine_in), channel_id=1, source_target_pairs={{0,16},{16,0},{32,48},{48,32},{64,80},{80,64},{96,112},{112,96},{1... | collective-permute-start | bytes 245768 | tf_op jit(solution)/shard_map/ppermute | solution.py:606
  51.1 1.3 %collective-permute-start.7 = (f32[20,8,128]{2,1,0:T(8,128)S(1)}, f32[20,8,128]{2,1,0:T(8,128)S(1)}, u32[]{:S(2)}, u32[]{:S(2)}) collective-permute-start(f32[20,8,128]{2,1,0:T(8,128)S(1)} %collective-permute-done.6.got), channel_id=1, source_target_pairs={{0,16},{16,0},{32,48},{48,32},{64,80},{80,64},{96,112},{112,96},{1... | collective-permute-start | bytes 245768 | tf_op jit(solution)/shard_map/ppermute | solution.py:606
  55.5 1.3 %collective-permute-start.12 = (f32[13,8,128]{2,1,0:T(8,128)S(1)}, f32[13,8,128]{2,1,0:T(8,128)S(1)}, u32[]{:S(2)}, u32[]{:S(2)}) collective-permute-start(f32[13,8,128]{2,1,0:T(8,128)S(1)} %get-tuple-element.28), channel_id=1, source_target_pairs={{0,16},{16,0},{32,48},{48,32},{64,80},{80,64},{96,112},{112,96},{1... | collective-permute-start | bytes 159752 | tf_op jit(solution)/shard_map/ppermute | solution.py:606
  56.9 9.5 %collective-permute-start.15 = (f32[13,8,128]{2,1,0:T(8,128)S(1)}, f32[13,8,128]{2,1,0:T(8,128)S(1)}, u32[]{:S(2)}, u32[]{:S(2)}) collective-permute-start(f32[13,8,128]{2,1,0:T(8,128)S(1)} %add.50), channel_id=1, source_target_pairs={{0,96},{16,112},{32,64},{48,80},{64,32},{80,48},{96,0},{112,16},{1... | collective-permute-start | bytes 159752 | tf_op jit(solution)/shard_map/ppermute | solution.py:613
  58.1 8.2 %collective-permute-start.14 = (f32[13,8,128]{2,1,0:T(8,128)S(1)}, f32[13,8,128]{2,1,0:T(8,128)S(1)}, u32[]{:S(2)}, u32[]{:S(2)}) collective-permute-start(f32[13,8,128]{2,1,0:T(8,128)S(1)} %add.50), channel_id=1, source_target_pairs={{0,32},{16,48},{32,0},{48,16},{64,96},{80,112},{96,64},{112,80},{1... | collective-permute-start | bytes 159752 | tf_op jit(solution)/shard_map/ppermute | solution.py:613
  60.8 5.5 %collective-permute-start.13 = (f32[13,8,128]{2,1,0:T(8,128)S(1)}, f32[13,8,128]{2,1,0:T(8,128)S(1)}, u32[]{:S(2)}, u32[]{:S(2)}) collective-permute-start(f32[13,8,128]{2,1,0:T(8,128)S(1)} %add.50), channel_id=1, source_target_pairs={{0,64},{16,80},{32,96},{48,112},{64,0},{80,16},{96,32},{112,48},{1... | collective-permute-start | bytes 159752 | tf_op jit(solution)/shard_map/ppermute | solution.py:613
  60.8 22.5 %collective-permute-start.19 = (f32[128,512]{1,0:T(8,128)S(1)}, f32[128,512]{1,0:T(8,128)S(1)}, u32[]{:S(2)}, u32[]{:S(2)}) collective-permute-start(f32[128,512]{1,0:T(8,128)S(1)} %get-tuple-element.31), channel_id=1, source_target_pairs={{0,1},{1,0},{2,3},{3,2},{4,5},{5,4},{6,7},{7,6},{8,9},{9,8},{10,11... | collective-permute-start | bytes 786440 | tf_op jit(solution)/shard_map/ppermute | solution.py:637
  61.9 21.4 %collective-permute-start.20 = (f32[128,512]{1,0:T(8,128)S(1)}, f32[128,512]{1,0:T(8,128)S(1)}, u32[]{:S(2)}, u32[]{:S(2)}) collective-permute-start(f32[128,512]{1,0:T(8,128)S(1)} %get-tuple-element.32), channel_id=1, source_target_pairs={{1,2},{2,1},{3,4},{4,3},{5,6},{6,5},{7,8},{8,7},{9,10},{10,9},{11,... | collective-permute-start | bytes 786440 | tf_op jit(solution)/shard_map/ppermute | solution.py:638
  66.4 7.5 %collective-permute-start.16 = (f32[13,8,128]{2,1,0:T(8,128)S(1)}, f32[13,8,128]{2,1,0:T(8,128)S(1)}, u32[]{:S(2)}, u32[]{:S(2)}) collective-permute-start(f32[13,8,128]{2,1,0:T(8,128)S(1)} %add_add_fusion.2), channel_id=1, source_target_pairs={{0,128},{16,144},{32,160},{48,176},{64,192},{80,208},{96,224},{112... | collective-permute-start | bytes 159752 | tf_op jit(solution)/shard_map/ppermute | solution.py:617
  73.9 6.6 %collective-permute-start.18 = (f32[13,8,128]{2,1,0:T(8,128)S(1)}, f32[13,8,128]{2,1,0:T(8,128)S(1)}, u32[]{:S(2)}, u32[]{:S(2)}) collective-permute-start(f32[13,8,128]{2,1,0:T(8,128)S(1)} %add.54.mine), channel_id=1, source_target_pairs={{0,16},{16,0},{32,48},{48,32},{64,80},{80,64},{96,112},{112,96},{1... | collective-permute-start | bytes 159752 | tf_op jit(solution)/shard_map/ppermute | solution.py:606
  75.8 7.6 %collective-permute-start.17 = (f32[13,8,128]{2,1,0:T(8,128)S(1)}, f32[13,8,128]{2,1,0:T(8,128)S(1)}, u32[]{:S(2)}, u32[]{:S(2)}) collective-permute-start(f32[13,8,128]{2,1,0:T(8,128)S(1)} %add.54.mine), channel_id=1, source_target_pairs={{16,1},{1,16},{17,2},{2,17},{18,3},{3,18},{19,4},{4,19},{20,5},{5,... | collective-permute-start | bytes 159752 | tf_op jit(solution)/shard_map/ppermute | solution.py:648
  83.3 1.2 %collective-permute-start.21 = (f32[13,8,128]{2,1,0:T(8,128)S(1)}, f32[13,8,128]{2,1,0:T(8,128)S(1)}, u32[]{:S(2)}, u32[]{:S(2)}) collective-permute-start(f32[13,8,128]{2,1,0:T(8,128)S(1)} %collective-permute-done.17.got), channel_id=1, source_target_pairs={{0,16},{16,0},{32,48},{48,32},{64,80},{80,64},{96,112},{112,96},{1... | collective-permute-start | bytes 159752 | tf_op jit(solution)/shard_map/ppermute | solution.py:606
  86.6 1.3 %collective-permute-start.22 = (f32[13,8,128]{2,1,0:T(8,128)S(1)}, f32[13,8,128]{2,1,0:T(8,128)S(1)}, u32[]{:S(2)}, u32[]{:S(2)}) collective-permute-start(f32[13,8,128]{2,1,0:T(8,128)S(1)} %get-tuple-element.36), channel_id=1, source_target_pairs={{0,16},{16,0},{32,48},{48,32},{64,80},{80,64},{96,112},{112,96},{1... | collective-permute-start | bytes 159752 | tf_op jit(solution)/shard_map/ppermute | solution.py:606
  87.9 3.9 %collective-permute-start.25 = (f32[13,8,128]{2,1,0:T(8,128)S(1)}, f32[13,8,128]{2,1,0:T(8,128)S(1)}, u32[]{:S(2)}, u32[]{:S(2)}) collective-permute-start(f32[13,8,128]{2,1,0:T(8,128)S(1)} %add.55), channel_id=1, source_target_pairs={{0,96},{16,112},{32,64},{48,80},{64,32},{80,48},{96,0},{112,16},{1... | collective-permute-start | bytes 159752 | tf_op jit(solution)/shard_map/ppermute | solution.py:613
  89.2 4.2 %collective-permute-start.24 = (f32[13,8,128]{2,1,0:T(8,128)S(1)}, f32[13,8,128]{2,1,0:T(8,128)S(1)}, u32[]{:S(2)}, u32[]{:S(2)}) collective-permute-start(f32[13,8,128]{2,1,0:T(8,128)S(1)} %add.55), channel_id=1, source_target_pairs={{0,32},{16,48},{32,0},{48,16},{64,96},{80,112},{96,64},{112,80},{1... | collective-permute-start | bytes 159752 | tf_op jit(solution)/shard_map/ppermute | solution.py:613
  91.8 4.5 %collective-permute-start.23 = (f32[13,8,128]{2,1,0:T(8,128)S(1)}, f32[13,8,128]{2,1,0:T(8,128)S(1)}, u32[]{:S(2)}, u32[]{:S(2)}) collective-permute-start(f32[13,8,128]{2,1,0:T(8,128)S(1)} %add.55), channel_id=1, source_target_pairs={{0,64},{16,80},{32,96},{48,112},{64,0},{80,16},{96,32},{112,48},{1... | collective-permute-start | bytes 159752 | tf_op jit(solution)/shard_map/ppermute | solution.py:613
  96.3 4.9 %collective-permute-start.26 = (f32[13,8,128]{2,1,0:T(8,128)S(1)}, f32[13,8,128]{2,1,0:T(8,128)S(1)}, u32[]{:S(2)}, u32[]{:S(2)}) collective-permute-start(f32[13,8,128]{2,1,0:T(8,128)S(1)} %add_add_fusion.1), channel_id=1, source_target_pairs={{0,128},{16,144},{32,160},{48,176},{64,192},{80,208},{96,224},{112... | collective-permute-start | bytes 159752 | tf_op jit(solution)/shard_map/ppermute | solution.py:617
  101.2 3.7 %collective-permute-start.27 = (f32[13,8,128]{2,1,0:T(8,128)S(1)}, f32[13,8,128]{2,1,0:T(8,128)S(1)}, u32[]{:S(2)}, u32[]{:S(2)}) collective-permute-start(f32[13,8,128]{2,1,0:T(8,128)S(1)} %add.59.mine), channel_id=1, source_target_pairs={{0,16},{16,0},{32,48},{48,32},{64,80},{80,64},{96,112},{112,96},{1... | collective-permute-start | bytes 159752 | tf_op jit(solution)/shard_map/ppermute | solution.py:606

commit v6 on v5

--- a/solution.py
+++ b/solution.py
@@ -255,7 +255,7 @@
             write(start, read(start) + (ex * ez) * (1.0 + (qa + qb) * (sa + sb)))
 
 
-def relax(moved, coefs, lines, state, shift):
+def relax(moved, coefs, lines, state, shift, first=0, size=OWN):
     def tile(j, carry):
         values = point(coefs, j)
         for sign in range(2):
@@ -275,7 +275,7 @@
             relax_rows(read, write, lines, fixed, sign)
         return carry
 
-    lax.fori_loop(0, OWN, tile, 0)
+    lax.fori_loop(first, first + size, tile, 0)
 
 
 def relax_ghosts(ghosts, coefs, lines, state):
@@ -380,7 +380,16 @@
 
 
 def first_kernel(count, dist, wall, kind, inflow, *refs):
-    faces, moved, mine, other, rim_a, rim_b, state, sums, flux, sems = refs
+    faces, moved, mine, other, rim_a, rim_b, state, sums, flux, wall_v, kind_v, inflow_v, sems = (
+        refs
+    )
+    small = [
+        pltpu.make_async_copy(wall, wall_v, sems.at[DEPTH]),
+        pltpu.make_async_copy(kind, kind_v, sems.at[DEPTH + 1]),
+        pltpu.make_async_copy(inflow, inflow_v, sems.at[DEPTH + 2]),
+    ]
+    for load in small:
+        load.start()
     iy = lax.axis_index("vel")
     position = lax.axis_index("gx")
     loads = [
@@ -391,12 +400,14 @@
     ]
     for load in loads:
         load.start()
-    prepare_masks(wall, faces, position, count, iy >= VS // 2)
     state[HALF:, :SEC] = jnp.zeros((HALF, SEC), F32)
     state[:HALF, (DEPTH + 1) * SEC :] = jnp.zeros((HALF, SEC), F32)
+    for load in small:
+        load.wait()
+    prepare_masks(wall_v, faces, position, count, iy >= VS // 2)
     for load in loads:
         load.wait()
-    finish(state, faces, sums, kind, inflow, moved, mine, other, (rim_a, rim_b), count)
+    finish(state, faces, sums, kind_v, inflow_v, moved, mine, other, (rim_a, rim_b), count)
     rim_flux(state, flux)
     values = expand([fold(flux, p, 0) * (WEIGHT / KEEP) for p in range(8)], vy_of(iy))
     turned = [pltpu.roll(value, TILES, 0) for value in values]
@@ -516,6 +527,7 @@
 HBM = pl.BlockSpec(memory_space=pltpu.HBM)
 PARAMS = pltpu.CompilerParams(vmem_limit_bytes=12 << 20)
 F32 = jnp.float32
+FIRST_LIMIT = 60_000_000
 WHOLE = jax.ShapeDtypeStruct((ROWS, DEPTH * SEC), F32)
 WIDE = jax.ShapeDtypeStruct((ROWS, (DEPTH + 2) * SEC), F32)
 RIM = jax.ShapeDtypeStruct((HALF, SEC), F32)
@@ -531,15 +543,18 @@
     return pl.pallas_call(
         functools.partial(first_kernel, count),
         out_shape=outs,
-        in_specs=[HBM, VM, VM, VM],
+        in_specs=[HBM] * 4,
         out_specs=(VM,) * len(outs),
         scratch_shapes=[
             pltpu.VMEM(WIDE.shape, F32),
             SUMS,
             pltpu.VMEM((8, 8, 8, 128), F32),
-            pltpu.SemaphoreType.DMA((DEPTH,)),
+            pltpu.VMEM(wall.shape, jnp.int32),
+            pltpu.VMEM(kind.shape, jnp.int32),
+            pltpu.VMEM(inflow.shape, F32),
+            pltpu.SemaphoreType.DMA((DEPTH + 3,)),
         ],
-        compiler_params=PARAMS,
+        compiler_params=pltpu.CompilerParams(vmem_limit_bytes=FIRST_LIMIT),
         name="move_first",
     )(dist, wall, kind, inflow)
 
@@ -585,20 +600,54 @@
     )(state, *pairs, got, swapped, faces, kind, inflow)[1:]
 
 
-def relax_kernel(shift, moved, mine, other, state, coefs, lines):
+def relax_kernel(moved, mine, other, state, coefs, lines):
     own_coefficients(mine, other, coefs)
-    relax(moved, coefs, lines, state, shift)
-
-
-def relaxed(moved, mine, other, last):
+    relax(moved, coefs, lines, state, SEC)
+
+
+def last_kernel(moved, mine, other, out, state, coefs, lines, sems):
+    own_coefficients(mine, other, coefs)
+
+    def store(i):
+        part = pl.ds(pl.multiple_of(i * SEC, SEC), SEC)
+        return pltpu.make_async_copy(state.at[:, part], out.at[:, part], sems.at[i])
+
+    def section(i, carry):
+        relax(moved, coefs, lines, state, 0, i * TILES, TILES)
+        store(i).start()
+        return carry
+
+    lax.fori_loop(0, DEPTH, section, 0)
+    for i in range(DEPTH):
+        store(i).wait()
+
+
+def relaxed(moved, mine, other):
     return pl.pallas_call(
-        functools.partial(relax_kernel, 0 if last else SEC),
-        out_shape=WHOLE if last else WIDE,
+        relax_kernel,
+        out_shape=WIDE,
         in_specs=[VM, VM, VM],
         out_specs=VM,
         scratch_shapes=[pltpu.VMEM((9, OWN, 8, 128), F32), LINES],
         compiler_params=PARAMS,
-        name="relax_last" if last else "relax",
+        name="relax",
+    )(moved, mine, other)
+
+
+def relax_last(moved, mine, other):
+    return pl.pallas_call(
+        last_kernel,
+        out_shape=WHOLE,
+        in_specs=[VM, VM, VM],
+        out_specs=HBM,
+        scratch_shapes=[
+            pltpu.VMEM(WHOLE.shape, F32),
+            pltpu.VMEM((9, OWN, 8, 128), F32),
+            LINES,
+            pltpu.SemaphoreType.DMA((DEPTH,)),
+        ],
+        compiler_params=PARAMS,
+        name="relax_last",
     )(moved, mine, other)
 
 
@@ -668,13 +717,13 @@
     pairs = swap_rims(*rims, count)
     half = sum_chips(mine + swap_cores(other))
     halo = swap_moments(half, count)
-    state = relaxed(moved, half, swap_cores(half), False)
+    state = relaxed(moved, half, swap_cores(half))
     halo, state = lax.optimization_barrier((halo, state))
     moved, mine, other = move_third(
         state, pairs, halo, swap_cores(halo), faces, boundary_kind, inflow, count
     )
     half = sum_chips(mine + swap_cores(other))
-    return relaxed(moved, half, swap_cores(half), True)
+    return relax_last(moved, half, swap_cores(half))
 
 
 def solution(mesh):

time: 109 us -> 110 us (level)
  Pallas kernels: 10.7 us -> 13.1 us
  local copies, waits for them, and re-layouts: 3.87 us -> 1.6 us
    pallas_call x1, Pallas kernels: 2.34 us -> 5.31 us  [move_first(): pl.pallas_call(functools.partial(first_kernel, count), out_shape=outs, in...]
    unnamed x12 -> x8, local copies, waits for them, and re-layouts: 3.87 us -> 1.6 us
where the time goes in v6:
time: 110 us; the launch traced here: 109 us
  starting transfers between devices  47.9 us (44%)
  waiting for transfers between devices  43.6 us (40%)
  Pallas kernels  13.1 us (12%)
  other arithmetic  2.07 us (2%)
  local copies, waits for them, and re-layouts  1.6 us (1%)
    ppermute x3, waiting for transfers between devices, flip_y(): return lax.ppermute(array, 'vel', [(i, i ^ 8) for i in range(VS)])  28.5 us
    ppermute x3, starting transfers between devices, swap_rims(): pair_b = lax.ppermute(pair_b, 'gx', far)  11.7 us
    ppermute x2, starting transfers between devices, swap_moments(): return lax.ppermute(half, ('vel', 'gx'), pairs)  11.2 us
    ppermute x9, starting transfers between devices, shift_x(): return lax.ppermute(array, 'vel', [(i, mate(i)) for i in range(VS)])  10.7 us
    ppermute x8, waiting for transfers between devices, swap_cores(): return lax.ppermute(array, 'vel', [(i, i ^ 1) for i in range(VS)])  6.66 us
    ppermute x8, starting transfers between devices, swap_cores(): return lax.ppermute(array, 'vel', [(i, i ^ 1) for i in range(VS)])  6.04 us
    ppermute x3, starting transfers between devices, flip_y(): return lax.ppermute(array, 'vel', [(i, i ^ 8) for i in range(VS)])  5.52 us
    pallas_call x1, Pallas kernels, move_first(): pl.pallas_call(functools.partial(first_kernel, count), out_shape=outs, in...  5.31 us
  transfers between devices with their start and end apart: 28, of which 13 were waited for; matrix products, arithmetic and copies ran while one was open for 1% of the time, Pallas kernels for 1%

profile of v6, /device:TPU:107, one launch (start us, length us, event | category | flops | bytes accessed | tf_op | source)
XLA Modules:
  0.0 108.6 jit_solution(16408816014512412355)
XLA Ops:
  0.0 5.3 %move_first.1 = (f32[5,5,4,8,128]{4,3,2,1,0:T(8,128)}, f32[256,2048]{1,0:T(8,128)}, f32[20,8,128]{2,1,0:T(8,128)}, f32[20,8,128]{2,1,0:T(8,128)}, f32[128,512]{1,0:T(8,128)}, /*index=5*/f32[128,512]{1,0:T(8,128)}) custom-call(f32[256,2048]{1,0:T(8,128)} %dist.1, s32[64,512]{1,0:T(8,128)} %wall.1, s32[2,512]{1,0:T(2,128)} %kind.5, f32[2,128]{1,0:T(2,128)} %bitcast.1), custom_call_target="tpu_custom_call" | custom-call | tf_op jit(solution)/shard_map/move_first/pallas_call | solution.py:543
  5.3 0.8 collective-permute-start
  6.1 1.1 %collective-permute-done = f32[20,8,128]{2,1,0:T(8,128)S(1)} collective-permute-done((f32[20,8,128]{2,1,0:T(8,128)}, f32[20,8,128]{2,1,0:T(8,128)S(1)}, u32[]{:S(2)}, u32[]{:S(2)}) %collective-permute-start) | collective-permute-done | bytes 81952 | tf_op jit(solution)/shard_map/ppermute | solution.py:655
  7.2 0.9 add.45
  8.1 1.3 %collective-permute-start.3 = (f32[20,8,128]{2,1,0:T(8,128)S(1)}, f32[20,8,128]{2,1,0:T(8,128)S(1)}, u32[]{:S(2)}, u32[]{:S(2)}) collective-permute-start(f32[20,8,128]{2,1,0:T(8,128)S(1)} %add.45), channel_id=1, source_target_pairs={{0,96},{16,112},{32,64},{48,80},{64,32},{80,48},{96,0},{112,16},{1... | collective-permute-start | bytes 245768 | tf_op jit(solution)/shard_map/ppermute | solution.py:662
  9.4 1.5 %collective-permute-start.2 = (f32[20,8,128]{2,1,0:T(8,128)S(1)}, f32[20,8,128]{2,1,0:T(8,128)S(1)}, u32[]{:S(2)}, u32[]{:S(2)}) collective-permute-start(f32[20,8,128]{2,1,0:T(8,128)S(1)} %add.45), channel_id=1, source_target_pairs={{0,32},{16,48},{32,0},{48,16},{64,96},{80,112},{96,64},{112,80},{1... | collective-permute-start | bytes 245768 | tf_op jit(solution)/shard_map/ppermute | solution.py:662
  11.0 1.1 slice_select_fusion
  12.0 4.6 %collective-permute-start.11 = (f32[128,512]{1,0:T(8,128)S(1)}, f32[128,512]{1,0:T(8,128)S(1)}, u32[]{:S(2)}, u32[]{:S(2)}) collective-permute-start(f32[128,512]{1,0:T(8,128)S(1)} %get-tuple-element.37), channel_id=1, source_target_pairs={{1,2},{2,1},{3,4},{4,3},{5,6},{6,5},{7,8},{8,7},{9,10},{10,9},{11,... | collective-permute-start | bytes 786440 | tf_op jit(solution)/shard_map/ppermute | solution.py:687
  16.7 0.1 collective-permute-start.10
  16.8 0.0 collective-permute-done.3
  16.8 1.4 %collective-permute-start.8 = (f32[128,512]{1,0:T(8,128)}, f32[128,512]{1,0:T(8,128)S(1)}, u32[]{:S(2)}, u32[]{:S(2)}) collective-permute-start(f32[128,512]{1,0:T(8,128)} %get-tuple-element.25), channel_id=1, source_target_pairs={{0,1},{1,0},{2,3},{3,2},{4,5},{5,4},{6,7},{7,6},{8,9},{9,8},{10,11... | collective-permute-start | bytes 786440 | tf_op jit(solution)/shard_map/ppermute | solution.py:686
  18.2 2.7 %collective-permute-start.9 = (f32[128,512]{1,0:T(8,128)}, f32[128,512]{1,0:T(8,128)S(1)}, u32[]{:S(2)}, u32[]{:S(2)}) collective-permute-start(f32[128,512]{1,0:T(8,128)} %get-tuple-element.26), channel_id=1, source_target_pairs={{1,2},{2,1},{3,4},{4,3},{5,6},{6,5},{7,8},{8,7},{9,10},{10,9},{11,... | collective-permute-start | bytes 786440 | tf_op jit(solution)/shard_map/ppermute | solution.py:687
  21.0 0.0 collective-permute-done.1
  21.0 2.1 %collective-permute-start.4 = (f32[20,8,128]{2,1,0:T(8,128)S(1)}, f32[20,8,128]{2,1,0:T(8,128)S(1)}, u32[]{:S(2)}, u32[]{:S(2)}) collective-permute-start(f32[20,8,128]{2,1,0:T(8,128)S(1)} %add_add_fusion), channel_id=1, source_target_pairs={{0,128},{16,144},{32,160},{48,176},{64,192},{80,208},{96,224},{112... | collective-permute-start | bytes 245768 | tf_op jit(solution)/shard_map/ppermute | solution.py:666
  23.1 19.5 %collective-permute-done.4 = f32[20,8,128]{2,1,0:T(8,128)S(1)} collective-permute-done((f32[20,8,128]{2,1,0:T(8,128)S(1)}, f32[20,8,128]{2,1,0:T(8,128)S(1)}, u32[]{:S(2)}, u32[]{:S(2)}) %collective-permute-start.4) | collective-permute-done | bytes 81952 | tf_op jit(solution)/shard_map/ppermute | solution.py:666
  42.7 6.5 %collective-permute-start.6 = (f32[20,8,128]{2,1,0:T(8,128)S(1)}, f32[20,8,128]{2,1,0:T(8,128)S(1)}, u32[]{:S(2)}, u32[]{:S(2)}) collective-permute-start(f32[20,8,128]{2,1,0:T(8,128)S(1)} %add.49.mine_in), channel_id=1, source_target_pairs={{16,1},{1,16},{17,2},{2,17},{18,3},{3,18},{19,4},{4,19},{20,5},{5,... | collective-permute-start | bytes 245768 | tf_op jit(solution)/shard_map/ppermute | solution.py:697
  49.2 0.1 collective-permute-start.5
  49.3 2.0 %collective-permute-done.6.got = f32[20,8,128]{2,1,0:T(8,128)S(1)} collective-permute-done((f32[20,8,128]{2,1,0:T(8,128)S(1)}, f32[20,8,128]{2,1,0:T(8,128)S(1)}, u32[]{:S(2)}, u32[]{:S(2)}) %collective-permute-start.6) | collective-permute-done | bytes 81952 | tf_op jit(solution)/shard_map/ppermute | solution.py:697
  51.3 1.2 %collective-permute-done.7.swapped = f32[20,8,128]{2,1,0:T(8,128)S(1)} collective-permute-done((f32[20,8,128]{2,1,0:T(8,128)S(1)}, f32[20,8,128]{2,1,0:T(8,128)S(1)}, u32[]{:S(2)}, u32[]{:S(2)}) %collective-permute-start.7) | collective-permute-done | bytes 81952 | tf_op jit(solution)/shard_map/ppermute | solution.py:655
  52.5 0.0 copy-start
  52.6 1.6 %copy-done = f32[256,2048]{1,0:T(8,128)S(1)} copy-done((f32[256,2048]{1,0:T(8,128)S(1)}, f32[256,2048]{1,0:T(8,128)}, u32[]{:S(2)}) %copy-start) | copy-done | bytes 2097176
  54.1 3.1 %move_second.1 = (f32[256,2048]{1,0:T(8,128)S(1)}, f32[13,8,128]{2,1,0:T(8,128)S(1)}, f32[13,8,128]{2,1,0:T(8,128)S(1)}, f32[128,512]{1,0:T(8,128)S(1)}, f32[128,512]{1,0:T(8,128)S(1)}) custom-call(f32[256,2048]{1,0:T(8,128)S(1)} %copy-done, f32[20,8,128]{2,1,0:T(8,128)S(1)} %add.49.mine_in, f32[20,8,128]{2,1,0:T(8,128)S(1)} %collective-permute-done.5.other_in, ...), custom_call_target="tpu_custom_call" | custom-call | tf_op jit(solution)/shard_map/move_second/pallas_call | solution.py:564
  57.3 0.2 collective-permute-start.12
  57.5 1.1 collective-permute-done.12
  58.6 1.3 %collective-permute-start.15 = (f32[13,8,128]{2,1,0:T(8,128)S(1)}, f32[13,8,128]{2,1,0:T(8,128)S(1)}, u32[]{:S(2)}, u32[]{:S(2)}) collective-permute-start(f32[13,8,128]{2,1,0:T(8,128)S(1)} %add.50), channel_id=1, source_target_pairs={{0,96},{16,112},{32,64},{48,80},{64,32},{80,48},{96,0},{112,16},{1... | collective-permute-start | bytes 159752 | tf_op jit(solution)/shard_map/ppermute | solution.py:662
  59.9 2.7 %collective-permute-start.14 = (f32[13,8,128]{2,1,0:T(8,128)S(1)}, f32[13,8,128]{2,1,0:T(8,128)S(1)}, u32[]{:S(2)}, u32[]{:S(2)}) collective-permute-start(f32[13,8,128]{2,1,0:T(8,128)S(1)} %add.50), channel_id=1, source_target_pairs={{0,32},{16,48},{32,0},{48,16},{64,96},{80,112},{96,64},{112,80},{1... | collective-permute-start | bytes 159752 | tf_op jit(solution)/shard_map/ppermute | solution.py:662
  62.6 1.1 %collective-permute-start.19 = (f32[128,512]{1,0:T(8,128)S(1)}, f32[128,512]{1,0:T(8,128)S(1)}, u32[]{:S(2)}, u32[]{:S(2)}) collective-permute-start(f32[128,512]{1,0:T(8,128)S(1)} %get-tuple-element.31), channel_id=1, source_target_pairs={{0,1},{1,0},{2,3},{3,2},{4,5},{5,4},{6,7},{7,6},{8,9},{9,8},{10,11... | collective-permute-start | bytes 786440 | tf_op jit(solution)/shard_map/ppermute | solution.py:686
  63.7 4.4 %collective-permute-start.20 = (f32[128,512]{1,0:T(8,128)S(1)}, f32[128,512]{1,0:T(8,128)S(1)}, u32[]{:S(2)}, u32[]{:S(2)}) collective-permute-start(f32[128,512]{1,0:T(8,128)S(1)} %get-tuple-element.32), channel_id=1, source_target_pairs={{1,2},{2,1},{3,4},{4,3},{5,6},{6,5},{7,8},{8,7},{9,10},{10,9},{11,... | collective-permute-start | bytes 786440 | tf_op jit(solution)/shard_map/ppermute | solution.py:687
  68.1 0.1 collective-permute-start.16
  68.2 7.4 %collective-permute-done.16 = f32[13,8,128]{2,1,0:T(8,128)S(1)} collective-permute-done((f32[13,8,128]{2,1,0:T(8,128)S(1)}, f32[13,8,128]{2,1,0:T(8,128)S(1)}, u32[]{:S(2)}, u32[]{:S(2)}) %collective-permute-start.16) | collective-permute-done | bytes 53280 | tf_op jit(solution)/shard_map/ppermute | solution.py:666
  75.7 1.9 %collective-permute-start.18 = (f32[13,8,128]{2,1,0:T(8,128)S(1)}, f32[13,8,128]{2,1,0:T(8,128)S(1)}, u32[]{:S(2)}, u32[]{:S(2)}) collective-permute-start(f32[13,8,128]{2,1,0:T(8,128)S(1)} %add.54.mine), channel_id=1, source_target_pairs={{0,16},{16,0},{32,48},{48,32},{64,80},{80,64},{96,112},{112,96},{1... | collective-permute-start | bytes 159752 | tf_op jit(solution)/shard_map/ppermute | solution.py:655
  77.5 4.7 %collective-permute-start.17 = (f32[13,8,128]{2,1,0:T(8,128)S(1)}, f32[13,8,128]{2,1,0:T(8,128)S(1)}, u32[]{:S(2)}, u32[]{:S(2)}) collective-permute-start(f32[13,8,128]{2,1,0:T(8,128)S(1)} %add.54.mine), channel_id=1, source_target_pairs={{16,1},{1,16},{17,2},{2,17},{18,3},{3,18},{19,4},{4,19},{20,5},{5,... | collective-permute-start | bytes 159752 | tf_op jit(solution)/shard_map/ppermute | solution.py:697
  82.3 0.9 relax.1.old
  83.2 1.9 %collective-permute-done.17.got = f32[13,8,128]{2,1,0:T(8,128)S(1)} collective-permute-done((f32[13,8,128]{2,1,0:T(8,128)S(1)}, f32[13,8,128]{2,1,0:T(8,128)S(1)}, u32[]{:S(2)}, u32[]{:S(2)}) %collective-permute-start.17) | collective-permute-done | bytes 53280 | tf_op jit(solution)/shard_map/ppermute | solution.py:697
  85.1 0.0 collective-permute-start.21
  85.1 1.2 %collective-permute-done.21.swapped = f32[13,8,128]{2,1,0:T(8,128)S(1)} collective-permute-done((f32[13,8,128]{2,1,0:T(8,128)S(1)}, f32[13,8,128]{2,1,0:T(8,128)S(1)}, u32[]{:S(2)}, u32[]{:S(2)}) %collective-permute-start.21) | collective-permute-done | bytes 53280 | tf_op jit(solution)/shard_map/ppermute | solution.py:655
  86.3 2.0 %move_third.1 = (f32[256,3072]{1,0:T(8,128)S(1)}, f32[256,2048]{1,0:T(8,128)S(1)}, f32[13,8,128]{2,1,0:T(8,128)S(1)}, f32[13,8,128]{2,1,0:T(8,128)S(1)}) custom-call(f32[256,3072]{1,0:T(8,128)S(1)} %relax.1.old, f32[128,512]{1,0:T(8,128)S(1)} %collective-permute-done.19.pair_a, ...), custom_call_target="tpu_custom_call", output_to_operand_aliasing={{0}: (0, {})} | custom-call | tf_op jit(solution)/shard_map/move_third/pallas_call | solution.py:585
  88.3 0.2 collective-permute-start.22
  88.6 1.1 collective-permute-done.22
  89.7 1.3 %collective-permute-start.25 = (f32[13,8,128]{2,1,0:T(8,128)S(1)}, f32[13,8,128]{2,1,0:T(8,128)S(1)}, u32[]{:S(2)}, u32[]{:S(2)}) collective-permute-start(f32[13,8,128]{2,1,0:T(8,128)S(1)} %add.55), channel_id=1, source_target_pairs={{0,96},{16,112},{32,64},{48,80},{64,32},{80,48},{96,0},{112,16},{1... | collective-permute-start | bytes 159752 | tf_op jit(solution)/shard_map/ppermute | solution.py:662
  90.9 2.7 %collective-permute-start.24 = (f32[13,8,128]{2,1,0:T(8,128)S(1)}, f32[13,8,128]{2,1,0:T(8,128)S(1)}, u32[]{:S(2)}, u32[]{:S(2)}) collective-permute-start(f32[13,8,128]{2,1,0:T(8,128)S(1)} %add.55), channel_id=1, source_target_pairs={{0,32},{16,48},{32,0},{48,16},{64,96},{80,112},{96,64},{112,80},{1... | collective-permute-start | bytes 159752 | tf_op jit(solution)/shard_map/ppermute | solution.py:662
  93.6 1.5 %collective-permute-done.24 = f32[13,8,128]{2,1,0:T(8,128)S(1)} collective-permute-done((f32[13,8,128]{2,1,0:T(8,128)S(1)}, f32[13,8,128]{2,1,0:T(8,128)S(1)}, u32[]{:S(2)}, u32[]{:S(2)}) %collective-permute-start.24) | collective-permute-done | bytes 53280 | tf_op jit(solution)/shard_map/ppermute | solution.py:662
  95.1 3.0 %collective-permute-done.23 = f32[13,8,128]{2,1,0:T(8,128)S(1)} collective-permute-done((f32[13,8,128]{2,1,0:T(8,128)S(1)}, f32[13,8,128]{2,1,0:T(8,128)S(1)}, u32[]{:S(2)}, u32[]{:S(2)}) %collective-permute-start.23) | collective-permute-done | bytes 53280 | tf_op jit(solution)/shard_map/ppermute | solution.py:662
  98.1 3.3 %collective-permute-start.26 = (f32[13,8,128]{2,1,0:T(8,128)S(1)}, f32[13,8,128]{2,1,0:T(8,128)S(1)}, u32[]{:S(2)}, u32[]{:S(2)}) collective-permute-start(f32[13,8,128]{2,1,0:T(8,128)S(1)} %add_add_fusion.1), channel_id=1, source_target_pairs={{0,128},{16,144},{32,160},{48,176},{64,192},{80,208},{96,224},{112... | collective-permute-start | bytes 159752 | tf_op jit(solution)/shard_map/ppermute | solution.py:666
  101.4 1.5 %collective-permute-done.26 = f32[13,8,128]{2,1,0:T(8,128)S(1)} collective-permute-done((f32[13,8,128]{2,1,0:T(8,128)S(1)}, f32[13,8,128]{2,1,0:T(8,128)S(1)}, u32[]{:S(2)}, u32[]{:S(2)}) %collective-permute-start.26) | collective-permute-done | bytes 53280 | tf_op jit(solution)/shard_map/ppermute | solution.py:666
  103.0 2.8 %collective-permute-start.27 = (f32[13,8,128]{2,1,0:T(8,128)S(1)}, f32[13,8,128]{2,1,0:T(8,128)S(1)}, u32[]{:S(2)}, u32[]{:S(2)}) collective-permute-start(f32[13,8,128]{2,1,0:T(8,128)S(1)} %add.59.mine), channel_id=1, source_target_pairs={{0,16},{16,0},{32,48},{48,32},{64,80},{80,64},{96,112},{112,96},{1... | collective-permute-start | bytes 159752 | tf_op jit(solution)/shard_map/ppermute | solution.py:655
  105.8 0.9 collective-permute-done.27.other
  106.7 1.8 %relax_last.1 = f32[256,2048]{1,0:T(8,128)} custom-call(f32[256,2048]{1,0:T(8,128)S(1)} %get-tuple-element.34.moved, f32[13,8,128]{2,1,0:T(8,128)S(1)} %add.59.mine, f32[13,8,128]{2,1,0:T(8,128)S(1)} %collective-permute-done.27.other), custom_call_target="tpu_custom_call" | custom-call | tf_op jit(solution)/shard_map/relax_last/pallas_call | solution.py:638
  (31 shorter events, 0.2 us)
Async XLA Ops:
  0.0 52.5 %copy-start.2 = (s32[2,512]{1,0:T(2,128)S(1)}, s32[2,512]{1,0:T(2,128)}, u32[]{:S(2)}) copy-start(s32[2,512]{1,0:T(2,128)} %kind.5) | copy-start | bytes 12292
  0.0 52.5 %copy-start.3 = (f32[256]{0:T(256)S(1)}, f32[256]{0:T(256)}, u32[]{:S(2)}) copy-start(f32[256]{0:T(256)} %param.7) | copy-start | bytes 3076
  5.3 47.2 %copy-start.1 = (f32[5,5,4,8,128]{4,3,2,1,0:T(8,128)S(1)}, f32[5,5,4,8,128]{4,3,2,1,0:T(8,128)}, u32[]{:S(2)}) copy-start(f32[5,5,4,8,128]{4,3,2,1,0:T(8,128)} %get-tuple-element.24.faces) | copy-start | bytes 1228804
  5.3 1.9 %collective-permute-start = (f32[20,8,128]{2,1,0:T(8,128)}, f32[20,8,128]{2,1,0:T(8,128)S(1)}, u32[]{:S(2)}, u32[]{:S(2)}) collective-permute-start(f32[20,8,128]{2,1,0:T(8,128)} %get-tuple-element.23), channel_id=1, source_target_pairs={{0,16},{16,0},{32,48},{48,32},{64,80},{80,64},{96,112},{112,96},{1... | collective-permute-start | bytes 245768 | tf_op jit(solution)/shard_map/ppermute | solution.py:655
  8.1 8.6 %collective-permute-start.3 = (f32[20,8,128]{2,1,0:T(8,128)S(1)}, f32[20,8,128]{2,1,0:T(8,128)S(1)}, u32[]{:S(2)}, u32[]{:S(2)}) collective-permute-start(f32[20,8,128]{2,1,0:T(8,128)S(1)} %add.45), channel_id=1, source_target_pairs={{0,96},{16,112},{32,64},{48,80},{64,32},{80,48},{96,0},{112,16},{1... | collective-permute-start | bytes 245768 | tf_op jit(solution)/shard_map/ppermute | solution.py:662
  9.4 8.8 %collective-permute-start.2 = (f32[20,8,128]{2,1,0:T(8,128)S(1)}, f32[20,8,128]{2,1,0:T(8,128)S(1)}, u32[]{:S(2)}, u32[]{:S(2)}) collective-permute-start(f32[20,8,128]{2,1,0:T(8,128)S(1)} %add.45), channel_id=1, source_target_pairs={{0,32},{16,48},{32,0},{48,16},{64,96},{80,112},{96,64},{112,80},{1... | collective-permute-start | bytes 245768 | tf_op jit(solution)/shard_map/ppermute | solution.py:662
  11.0 10.0 %collective-permute-start.1 = (f32[20,8,128]{2,1,0:T(8,128)S(1)}, f32[20,8,128]{2,1,0:T(8,128)S(1)}, u32[]{:S(2)}, u32[]{:S(2)}) collective-permute-start(f32[20,8,128]{2,1,0:T(8,128)S(1)} %add.45), channel_id=1, source_target_pairs={{0,64},{16,80},{32,96},{48,112},{64,0},{80,16},{96,32},{112,48},{1... | collective-permute-start | bytes 245768 | tf_op jit(solution)/shard_map/ppermute | solution.py:662
  12.0 37.1 %collective-permute-start.11 = (f32[128,512]{1,0:T(8,128)S(1)}, f32[128,512]{1,0:T(8,128)S(1)}, u32[]{:S(2)}, u32[]{:S(2)}) collective-permute-start(f32[128,512]{1,0:T(8,128)S(1)} %get-tuple-element.37), channel_id=1, source_target_pairs={{1,2},{2,1},{3,4},{4,3},{5,6},{6,5},{7,8},{8,7},{9,10},{10,9},{11,... | collective-permute-start | bytes 786440 | tf_op jit(solution)/shard_map/ppermute | solution.py:687
  16.7 34.6 %collective-permute-start.10 = (f32[128,512]{1,0:T(8,128)S(1)}, f32[128,512]{1,0:T(8,128)S(1)}, u32[]{:S(2)}, u32[]{:S(2)}) collective-permute-start(f32[128,512]{1,0:T(8,128)S(1)} %get-tuple-element.38), channel_id=1, source_target_pairs={{0,1},{1,0},{2,3},{3,2},{4,5},{5,4},{6,7},{7,6},{8,9},{9,8},{10,11... | collective-permute-start | bytes 786440 | tf_op jit(solution)/shard_map/ppermute | solution.py:686
  16.8 34.5 %collective-permute-start.8 = (f32[128,512]{1,0:T(8,128)}, f32[128,512]{1,0:T(8,128)S(1)}, u32[]{:S(2)}, u32[]{:S(2)}) collective-permute-start(f32[128,512]{1,0:T(8,128)} %get-tuple-element.25), channel_id=1, source_target_pairs={{0,1},{1,0},{2,3},{3,2},{4,5},{5,4},{6,7},{7,6},{8,9},{9,8},{10,11... | collective-permute-start | bytes 786440 | tf_op jit(solution)/shard_map/ppermute | solution.py:686
  18.2 33.0 %collective-permute-start.9 = (f32[128,512]{1,0:T(8,128)}, f32[128,512]{1,0:T(8,128)S(1)}, u32[]{:S(2)}, u32[]{:S(2)}) collective-permute-start(f32[128,512]{1,0:T(8,128)} %get-tuple-element.26), channel_id=1, source_target_pairs={{1,2},{2,1},{3,4},{4,3},{5,6},{6,5},{7,8},{8,7},{9,10},{10,9},{11,... | collective-permute-start | bytes 786440 | tf_op jit(solution)/shard_map/ppermute | solution.py:687
  21.0 21.6 %collective-permute-start.4 = (f32[20,8,128]{2,1,0:T(8,128)S(1)}, f32[20,8,128]{2,1,0:T(8,128)S(1)}, u32[]{:S(2)}, u32[]{:S(2)}) collective-permute-start(f32[20,8,128]{2,1,0:T(8,128)S(1)} %add_add_fusion), channel_id=1, source_target_pairs={{0,128},{16,144},{32,160},{48,176},{64,192},{80,208},{96,224},{112... | collective-permute-start | bytes 245768 | tf_op jit(solution)/shard_map/ppermute | solution.py:666
  42.7 8.6 %collective-permute-start.6 = (f32[20,8,128]{2,1,0:T(8,128)S(1)}, f32[20,8,128]{2,1,0:T(8,128)S(1)}, u32[]{:S(2)}, u32[]{:S(2)}) collective-permute-start(f32[20,8,128]{2,1,0:T(8,128)S(1)} %add.49.mine_in), channel_id=1, source_target_pairs={{16,1},{1,16},{17,2},{2,17},{18,3},{3,18},{19,4},{4,19},{20,5},{5,... | collective-permute-start | bytes 245768 | tf_op jit(solution)/shard_map/ppermute | solution.py:697
  49.2 2.1 %collective-permute-start.5 = (f32[20,8,128]{2,1,0:T(8,128)S(1)}, f32[20,8,128]{2,1,0:T(8,128)S(1)}, u32[]{:S(2)}, u32[]{:S(2)}) collective-permute-start(f32[20,8,128]{2,1,0:T(8,128)S(1)} %add.49.mine_in), channel_id=1, source_target_pairs={{0,16},{16,0},{32,48},{48,32},{64,80},{80,64},{96,112},{112,96},{1... | collective-permute-start | bytes 245768 | tf_op jit(solution)/shard_map/ppermute | solution.py:655
  51.3 1.3 %collective-permute-start.7 = (f32[20,8,128]{2,1,0:T(8,128)S(1)}, f32[20,8,128]{2,1,0:T(8,128)S(1)}, u32[]{:S(2)}, u32[]{:S(2)}) collective-permute-start(f32[20,8,128]{2,1,0:T(8,128)S(1)} %collective-permute-done.6.got), channel_id=1, source_target_pairs={{0,16},{16,0},{32,48},{48,32},{64,80},{80,64},{96,112},{112,96},{1... | collective-permute-start | bytes 245768 | tf_op jit(solution)/shard_map/ppermute | solution.py:655
  52.5 1.6 %copy-start = (f32[256,2048]{1,0:T(8,128)S(1)}, f32[256,2048]{1,0:T(8,128)}, u32[]{:S(2)}) copy-start(f32[256,2048]{1,0:T(8,128)} %get-tuple-element.21.source) | copy-start | bytes 6291460
  57.3 1.3 %collective-permute-start.12 = (f32[13,8,128]{2,1,0:T(8,128)S(1)}, f32[13,8,128]{2,1,0:T(8,128)S(1)}, u32[]{:S(2)}, u32[]{:S(2)}) collective-permute-start(f32[13,8,128]{2,1,0:T(8,128)S(1)} %get-tuple-element.28), channel_id=1, source_target_pairs={{0,16},{16,0},{32,48},{48,32},{64,80},{80,64},{96,112},{112,96},{1... | collective-permute-start | bytes 159752 | tf_op jit(solution)/shard_map/ppermute | solution.py:655
  58.6 9.4 %collective-permute-start.15 = (f32[13,8,128]{2,1,0:T(8,128)S(1)}, f32[13,8,128]{2,1,0:T(8,128)S(1)}, u32[]{:S(2)}, u32[]{:S(2)}) collective-permute-start(f32[13,8,128]{2,1,0:T(8,128)S(1)} %add.50), channel_id=1, source_target_pairs={{0,96},{16,112},{32,64},{48,80},{64,32},{80,48},{96,0},{112,16},{1... | collective-permute-start | bytes 159752 | tf_op jit(solution)/shard_map/ppermute | solution.py:662
  59.9 8.2 %collective-permute-start.14 = (f32[13,8,128]{2,1,0:T(8,128)S(1)}, f32[13,8,128]{2,1,0:T(8,128)S(1)}, u32[]{:S(2)}, u32[]{:S(2)}) collective-permute-start(f32[13,8,128]{2,1,0:T(8,128)S(1)} %add.50), channel_id=1, source_target_pairs={{0,32},{16,48},{32,0},{48,16},{64,96},{80,112},{96,64},{112,80},{1... | collective-permute-start | bytes 159752 | tf_op jit(solution)/shard_map/ppermute | solution.py:662
  62.6 5.5 %collective-permute-start.13 = (f32[13,8,128]{2,1,0:T(8,128)S(1)}, f32[13,8,128]{2,1,0:T(8,128)S(1)}, u32[]{:S(2)}, u32[]{:S(2)}) collective-permute-start(f32[13,8,128]{2,1,0:T(8,128)S(1)} %add.50), channel_id=1, source_target_pairs={{0,64},{16,80},{32,96},{48,112},{64,0},{80,16},{96,32},{112,48},{1... | collective-permute-start | bytes 159752 | tf_op jit(solution)/shard_map/ppermute | solution.py:662
  62.6 22.5 %collective-permute-start.19 = (f32[128,512]{1,0:T(8,128)S(1)}, f32[128,512]{1,0:T(8,128)S(1)}, u32[]{:S(2)}, u32[]{:S(2)}) collective-permute-start(f32[128,512]{1,0:T(8,128)S(1)} %get-tuple-element.31), channel_id=1, source_target_pairs={{0,1},{1,0},{2,3},{3,2},{4,5},{5,4},{6,7},{7,6},{8,9},{9,8},{10,11... | collective-permute-start | bytes 786440 | tf_op jit(solution)/shard_map/ppermute | solution.py:686
  63.7 21.4 %collective-permute-start.20 = (f32[128,512]{1,0:T(8,128)S(1)}, f32[128,512]{1,0:T(8,128)S(1)}, u32[]{:S(2)}, u32[]{:S(2)}) collective-permute-start(f32[128,512]{1,0:T(8,128)S(1)} %get-tuple-element.32), channel_id=1, source_target_pairs={{1,2},{2,1},{3,4},{4,3},{5,6},{6,5},{7,8},{8,7},{9,10},{10,9},{11,... | collective-permute-start | bytes 786440 | tf_op jit(solution)/shard_map/ppermute | solution.py:687
  68.1 7.5 %collective-permute-start.16 = (f32[13,8,128]{2,1,0:T(8,128)S(1)}, f32[13,8,128]{2,1,0:T(8,128)S(1)}, u32[]{:S(2)}, u32[]{:S(2)}) collective-permute-start(f32[13,8,128]{2,1,0:T(8,128)S(1)} %add_add_fusion.2), channel_id=1, source_target_pairs={{0,128},{16,144},{32,160},{48,176},{64,192},{80,208},{96,224},{112... | collective-permute-start | bytes 159752 | tf_op jit(solution)/shard_map/ppermute | solution.py:666
  75.7 6.6 %collective-permute-start.18 = (f32[13,8,128]{2,1,0:T(8,128)S(1)}, f32[13,8,128]{2,1,0:T(8,128)S(1)}, u32[]{:S(2)}, u32[]{:S(2)}) collective-permute-start(f32[13,8,128]{2,1,0:T(8,128)S(1)} %add.54.mine), channel_id=1, source_target_pairs={{0,16},{16,0},{32,48},{48,32},{64,80},{80,64},{96,112},{112,96},{1... | collective-permute-start | bytes 159752 | tf_op jit(solution)/shard_map/ppermute | solution.py:655
  77.5 7.6 %collective-permute-start.17 = (f32[13,8,128]{2,1,0:T(8,128)S(1)}, f32[13,8,128]{2,1,0:T(8,128)S(1)}, u32[]{:S(2)}, u32[]{:S(2)}) collective-permute-start(f32[13,8,128]{2,1,0:T(8,128)S(1)} %add.54.mine), channel_id=1, source_target_pairs={{16,1},{1,16},{17,2},{2,17},{18,3},{3,18},{19,4},{4,19},{20,5},{5,... | collective-permute-start | bytes 159752 | tf_op jit(solution)/shard_map/ppermute | solution.py:697
  85.1 1.2 %collective-permute-start.21 = (f32[13,8,128]{2,1,0:T(8,128)S(1)}, f32[13,8,128]{2,1,0:T(8,128)S(1)}, u32[]{:S(2)}, u32[]{:S(2)}) collective-permute-start(f32[13,8,128]{2,1,0:T(8,128)S(1)} %collective-permute-done.17.got), channel_id=1, source_target_pairs={{0,16},{16,0},{32,48},{48,32},{64,80},{80,64},{96,112},{112,96},{1... | collective-permute-start | bytes 159752 | tf_op jit(solution)/shard_map/ppermute | solution.py:655
  88.3 1.3 %collective-permute-start.22 = (f32[13,8,128]{2,1,0:T(8,128)S(1)}, f32[13,8,128]{2,1,0:T(8,128)S(1)}, u32[]{:S(2)}, u32[]{:S(2)}) collective-permute-start(f32[13,8,128]{2,1,0:T(8,128)S(1)} %get-tuple-element.36), channel_id=1, source_target_pairs={{0,16},{16,0},{32,48},{48,32},{64,80},{80,64},{96,112},{112,96},{1... | collective-permute-start | bytes 159752 | tf_op jit(solution)/shard_map/ppermute | solution.py:655
  89.7 3.9 %collective-permute-start.25 = (f32[13,8,128]{2,1,0:T(8,128)S(1)}, f32[13,8,128]{2,1,0:T(8,128)S(1)}, u32[]{:S(2)}, u32[]{:S(2)}) collective-permute-start(f32[13,8,128]{2,1,0:T(8,128)S(1)} %add.55), channel_id=1, source_target_pairs={{0,96},{16,112},{32,64},{48,80},{64,32},{80,48},{96,0},{112,16},{1... | collective-permute-start | bytes 159752 | tf_op jit(solution)/shard_map/ppermute | solution.py:662
  90.9 4.2 %collective-permute-start.24 = (f32[13,8,128]{2,1,0:T(8,128)S(1)}, f32[13,8,128]{2,1,0:T(8,128)S(1)}, u32[]{:S(2)}, u32[]{:S(2)}) collective-permute-start(f32[13,8,128]{2,1,0:T(8,128)S(1)} %add.55), channel_id=1, source_target_pairs={{0,32},{16,48},{32,0},{48,16},{64,96},{80,112},{96,64},{112,80},{1... | collective-permute-start | bytes 159752 | tf_op jit(solution)/shard_map/ppermute | solution.py:662
  93.6 4.5 %collective-permute-start.23 = (f32[13,8,128]{2,1,0:T(8,128)S(1)}, f32[13,8,128]{2,1,0:T(8,128)S(1)}, u32[]{:S(2)}, u32[]{:S(2)}) collective-permute-start(f32[13,8,128]{2,1,0:T(8,128)S(1)} %add.55), channel_id=1, source_target_pairs={{0,64},{16,80},{32,96},{48,112},{64,0},{80,16},{96,32},{112,48},{1... | collective-permute-start | bytes 159752 | tf_op jit(solution)/shard_map/ppermute | solution.py:662
  98.1 4.8 %collective-permute-start.26 = (f32[13,8,128]{2,1,0:T(8,128)S(1)}, f32[13,8,128]{2,1,0:T(8,128)S(1)}, u32[]{:S(2)}, u32[]{:S(2)}) collective-permute-start(f32[13,8,128]{2,1,0:T(8,128)S(1)} %add_add_fusion.1), channel_id=1, source_target_pairs={{0,128},{16,144},{32,160},{48,176},{64,192},{80,208},{96,224},{112... | collective-permute-start | bytes 159752 | tf_op jit(solution)/shard_map/ppermute | solution.py:666
  103.0 3.7 %collective-permute-start.27 = (f32[13,8,128]{2,1,0:T(8,128)S(1)}, f32[13,8,128]{2,1,0:T(8,128)S(1)}, u32[]{:S(2)}, u32[]{:S(2)}) collective-permute-start(f32[13,8,128]{2,1,0:T(8,128)S(1)} %add.59.mine), channel_id=1, source_target_pairs={{0,16},{16,0},{32,48},{48,32},{64,80},{80,64},{96,112},{112,96},{1... | collective-permute-start | bytes 159752 | tf_op jit(solution)/shard_map/ppermute | solution.py:655

commit v7 on v6

--- a/solution.py
+++ b/solution.py
@@ -47,13 +47,12 @@
 
 def prepare_masks(wall_ref, faces, position, count, forward):
     opened = []
-    for slot in range(DEPTH + 2):
-        at = position * DEPTH + slot - 1
+    for slot in range(DEPTH + 4):
+        at = position * DEPTH + slot - 2
         inside = jnp.logical_and(at >= 0, at < count * DEPTH)
         line = wall_ref[pl.ds(jnp.clip(at, 0, count * DEPTH - 1), 1), :]
         opened.append(jnp.where(inside, (1 - line).astype(jnp.float32), 1.0))
-    zero = jnp.zeros_like(opened[0])
-    o = jnp.concatenate(opened + [zero, zero], axis=0)
+    o = jnp.concatenate(opened, axis=0)
     cell = lax.broadcasted_iota(jnp.int32, (8, SEC), 1)
     up_x = o * pltpu.roll(o, 7, 0)
     up_y = o * pltpu.roll(o, SEC - NZ, 1) * (cell < SEC - NZ).astype(jnp.float32)
@@ -64,7 +63,7 @@
         up_x, jnp.where(forward, up_y, down_y), jnp.where(forward, down_y, up_y), down_z, up_z
     ]
     for k, plane in enumerate(planes):
-        for slot in range(DEPTH + 1):
+        for slot in range(DEPTH + 3):
             for t in range(TILES):
                 line = plane[slot : slot + 1, t * 128 : (t + 1) * 128]
                 faces[k, slot, t] = jnp.broadcast_to(line, (8, 128))
@@ -109,15 +108,15 @@
         for b in range(2):
             vz = vz_tile(b)
             az = jnp.abs(vz) * (KEEP * DT)
-            below = [faces[0, i, t] for t in tiles]
-            above = [faces[0, i + 1, t] for t in tiles]
+            below = [faces[0, i + 1, t] for t in tiles]
+            above = [faces[0, i + 2, t] for t in tiles]
             keep, in_y, in_z = [], [], []
             for t in tiles:
-                out_y = faces[1, i + 1, t]
-                out_z = faces[4 if b else 3, i + 1, t]
+                out_y = faces[1, i + 2, t]
+                out_z = faces[4 if b else 3, i + 2, t]
                 keep.append(KEEP - speed_y * out_y - az * out_z)
-                in_y.append(speed_y * faces[2, i + 1, t])
-                in_z.append(az * faces[3 if b else 4, i + 1, t])
+                in_y.append(speed_y * faces[2, i + 2, t])
+                in_z.append(az * faces[3 if b else 4, i + 2, t])
             acc = [[None] * 4 for _ in range(TILES)]
             for a in range(VS // 2):
                 speed = (a + 0.5) * H
@@ -173,6 +172,53 @@
     lax.fori_loop(0, DEPTH, section, 0)
 
 
+def move_ghosts(raw, faces, ghosts, iy):
+    forward = iy >= VS // 2
+    speed_y = jnp.abs(vy_of(iy)) * (KEEP * DT)
+    lane = lax.broadcasted_iota(jnp.int32, (8, 128), 1)
+    take = jnp.logical_or(
+        jnp.logical_and(forward, lane < NZ), jnp.logical_and(~forward, lane >= 128 - NZ)
+    )
+    shift_y = jnp.where(forward, NZ, 128 - NZ)
+    tiles = [jnp.where(forward, k, TILES - 1 - k) for k in range(TILES)]
+    lanes = [pl.multiple_of(t * 128, 128) for t in tiles]
+    for sign in range(2):
+        at = 1 if sign else DEPTH + 2
+        out_at, in_at = (1, 0) if sign else (DEPTH + 1, DEPTH + 2)
+        here_at, before_at = (SEC, 0) if sign else (0, SEC)
+        for b in range(2):
+            az = jnp.abs(vz_tile(b)) * (KEEP * DT)
+            keep, in_y, in_z = [], [], []
+            for t in tiles:
+                keep.append(KEEP - speed_y * faces[1, at, t] - az * faces[4 if b else 3, at, t])
+                in_y.append(speed_y * faces[2, at, t])
+                in_z.append(az * faces[3 if b else 4, at, t])
+
+            def rows(a, carry):
+                cx = (KEEP * DT * H) * (a.astype(F32) + 0.5)
+                start = pl.multiple_of(a * VS + 8 * b, 8)
+                here, shifted = [], []
+                for l in lanes:
+                    value = raw[sign, pl.ds(start, 8), pl.ds(pl.multiple_of(here_at + l, 128), 128)]
+                    here.append(value)
+                    shifted.append(pltpu.roll(value, shift_y, 1))
+                for k, (t, l) in enumerate(zip(tiles, lanes)):
+                    before = raw[
+                        sign, pl.ds(start, 8), pl.ds(pl.multiple_of(before_at + l, 128), 128)
+                    ]
+                    along_y = jnp.where(take, shifted[k - 1], shifted[k]) if k else shifted[k]
+                    along_z = pltpu.roll(here[k], 1 if b else 127, 1)
+                    ghosts[sign, pl.ds(start, 8), pl.ds(l, 128)] = (
+                        here[k] * (keep[k] - cx * faces[0, out_at, t])
+                        + before * (cx * faces[0, in_at, t])
+                        + along_y * in_y[k]
+                        + along_z * in_z[k]
+                    )
+                return carry
+
+            lax.fori_loop(0, VS // 2, rows, 0)
+
+
 def fold(sums, p, first):
     sub = lax.broadcasted_iota(jnp.int32, (8, 128), 0)
     values = [sums[p, first + t] for t in range(8)]
@@ -380,9 +426,7 @@
 
 
 def first_kernel(count, dist, wall, kind, inflow, *refs):
-    faces, moved, mine, other, rim_a, rim_b, state, sums, flux, wall_v, kind_v, inflow_v, sems = (
-        refs
-    )
+    faces, moved, mine, other, state, sums, flux, wall_v, kind_v, inflow_v, sems = refs
     small = [
         pltpu.make_async_copy(wall, wall_v, sems.at[DEPTH]),
         pltpu.make_async_copy(kind, kind_v, sems.at[DEPTH + 1]),
@@ -407,7 +451,7 @@
     prepare_masks(wall_v, faces, position, count, iy >= VS // 2)
     for load in loads:
         load.wait()
-    finish(state, faces, sums, kind_v, inflow_v, moved, mine, other, (rim_a, rim_b), count)
+    finish(state, faces, sums, kind_v, inflow_v, moved, mine, other, (), count)
     rim_flux(state, flux)
     values = expand([fold(flux, p, 0) * (WEIGHT / KEEP) for p in range(8)], vy_of(iy))
     turned = [pltpu.roll(value, TILES, 0) for value in values]
@@ -424,10 +468,10 @@
 
 def add_rims(ghosts, faces, state):
     def tile(t, carry):
-        at = pl.multiple_of(t * 128, 128)
         for sign in range(2):
+            at = pl.multiple_of(t * 128 + (SEC if sign else 0), 128)
             to = pl.multiple_of((1 if sign else DEPTH) * SEC + t * 128, 128)
-            open_x = faces[0, 0 if sign else DEPTH, t]
+            open_x = faces[0, 1 if sign else DEPTH + 1, t]
             for a in range(VS // 2):
                 scale = open_x * (KEEP * DT * (a + 0.5) * H)
                 for b in range(2):
@@ -454,8 +498,8 @@
     sub = lax.broadcasted_iota(jnp.int32, (8, 128), 0)
     edge = jnp.zeros((8, 128), F32)
     for t in range(TILES):
-        edge = jnp.where(sub == t, faces[0, 0, t], edge)
-        edge = jnp.where(sub == t + TILES, faces[0, DEPTH, t], edge)
+        edge = jnp.where(sub == t, faces[0, 1, t], edge)
+        edge = jnp.where(sub == t + TILES, faces[0, DEPTH + 1, t], edge)
     edge = edge * (KEEP * DT)
     turned = pltpu.roll(edge, TILES, 0)
 
@@ -492,10 +536,10 @@
 
 
 def second_kernel(count, source, mine_in, other_in, got, swapped, faces, kind, inflow, *refs):
-    pairs = refs[:4]
-    moved, mine, other, *out_rims = refs[4:9]
-    state, ghosts, coefs, edges, lines, sums, sems = refs[9:]
-    copies = bring_rims(pairs, ghosts, sems)
+    pairs = refs[:2]
+    moved, mine, other, *out_rims = refs[2:7]
+    state, raw, ghosts, coefs, edges, lines, sums, sems = refs[7:]
+    copies = bring_rims(pairs, raw, sems)
     vy = vy_of(lax.axis_index("vel"))
     start, end, halo = first_moments(mine_in, other_in, got, swapped, faces)
     spread(coefs, coefficients(start, vy), 0)
@@ -504,8 +548,9 @@
     relax(source, coefs, lines, state, SEC)
     for copy in copies:
         copy.wait()
+    move_ghosts(raw, faces, ghosts, lax.axis_index("vel"))
     relax_ghosts(ghosts, edges, lines, state)
-    add_rims(ghosts.at[pl.ds(2, 2)], faces, state)
+    add_rims(raw, faces, state)
     finish(state, faces, sums, kind, inflow, moved, mine, other, out_rims, count)
 
 
@@ -527,19 +572,19 @@
 HBM = pl.BlockSpec(memory_space=pltpu.HBM)
 PARAMS = pltpu.CompilerParams(vmem_limit_bytes=12 << 20)
 F32 = jnp.float32
-FIRST_LIMIT = 60_000_000
+FIRST_LIMIT = 12 << 20
 WHOLE = jax.ShapeDtypeStruct((ROWS, DEPTH * SEC), F32)
 WIDE = jax.ShapeDtypeStruct((ROWS, (DEPTH + 2) * SEC), F32)
 RIM = jax.ShapeDtypeStruct((HALF, SEC), F32)
 PART = jax.ShapeDtypeStruct((13, 8, 128), F32)
 FULL = jax.ShapeDtypeStruct((20, 8, 128), F32)
-FACES = jax.ShapeDtypeStruct((5, DEPTH + 1, TILES, 8, 128), F32)
+FACES = jax.ShapeDtypeStruct((5, DEPTH + 3, TILES, 8, 128), F32)
 SUMS = pltpu.VMEM((8, OWN, 8, 128), F32)
 LINES = pltpu.VMEM((2, 3, 8, 128), F32)
 
 
 def move_first(dist, wall, kind, inflow, count):
-    outs = (FACES, WHOLE, FULL, FULL, RIM, RIM)
+    outs = (FACES, WHOLE, FULL, FULL)
     return pl.pallas_call(
         functools.partial(first_kernel, count),
         out_shape=outs,
@@ -564,16 +609,17 @@
     return pl.pallas_call(
         functools.partial(second_kernel, count),
         out_shape=outs,
-        in_specs=[VM] * 8 + [ANY] * 4,
+        in_specs=[VM] * 8 + [ANY] * 2,
         out_specs=(VM,) * len(outs),
         scratch_shapes=[
             pltpu.VMEM(WIDE.shape, F32),
-            pltpu.VMEM((4, HALF, SEC), F32),
+            pltpu.VMEM((2, HALF, 2 * SEC), F32),
+            pltpu.VMEM((2, HALF, SEC), F32),
             pltpu.VMEM((9, OWN, 8, 128), F32),
             pltpu.VMEM((9, 8, 8, 128), F32),
             LINES,
             SUMS,
-            pltpu.SemaphoreType.DMA((4,)),
+            pltpu.SemaphoreType.DMA((2,)),
         ],
         compiler_params=PARAMS,
         name="move_second",
@@ -701,18 +747,17 @@
     count = lax.axis_size("gx")
     inflow = inflow.reshape(2, 128)
     even = lax.rem(lax.axis_index("gx"), 2) == 0
-    up = distribution[HALF:, (DEPTH - 1) * SEC :]
-    down = distribution[:HALF, :SEC]
+    up = distribution[HALF:, (DEPTH - 2) * SEC :]
+    down = distribution[:HALF, : 2 * SEC]
     start = swap_rims(jnp.where(even, up, down), jnp.where(even, down, up), count)
     outs = move_first(distribution, wall_mask, boundary_kind, inflow, count)
-    faces, moved, mine, other, *rims = outs
-    pairs = swap_rims(*rims, count)
+    faces, moved, mine, other = outs
     half = sum_chips(mine + swap_cores(other))
     halo = swap_moments(half, count)
     swapped = swap_cores(half)
     halves = (half, swapped, halo, swap_cores(halo))
     moved, mine, other, *rims = move_second(
-        moved, halves, faces, boundary_kind, inflow, (*pairs, *start), count
+        moved, halves, faces, boundary_kind, inflow, start, count
     )
     pairs = swap_rims(*rims, count)
     half = sum_chips(mine + swap_cores(other))

time: 110 us -> 112 us (1.018)
  starting transfers between devices: 47.9 us -> 43.9 us
  waiting for transfers between devices: 43.6 us -> 47.3 us
  local copies, waits for them, and re-layouts: 1.6 us -> 5.19 us
  other arithmetic: 2.07 us -> 0.18 us
    ppermute x3, waiting for transfers between devices: 28.5 us -> 32.4 us  [flip_y(): return lax.ppermute(array, 'vel', [(i, i ^ 8) for i in range(VS)])]
    unnamed x8 -> x18, local copies, waits for them, and re-layouts: 1.6 us -> 5.19 us
    ppermute x3 -> x2, starting transfers between devices: 11.7 us -> 9.01 us  [swap_rims(): pair_b = lax.ppermute(pair_b, 'gx', far)]
    pallas_call x1, Pallas kernels: 5.31 us -> 2.59 us  [move_first(): pl.pallas_call(functools.partial(first_kernel, count), out_shape=outs, in...]
    pallas_call x1, Pallas kernels: 3.13 us -> 5.69 us  [move_second(): pl.pallas_call(functools.partial(second_kernel, count), out_shape=outs, i...]
    ppermute x3 -> x2, starting transfers between devices: 2.67 us -> 1.22 us  [swap_rims(): pair_a = lax.ppermute(pair_a, 'gx', near)]
  transfers between devices with their start and end apart: 28 -> 26, of which waited for: 13 -> 13; matrix products, arithmetic and copies ran while one was open for 1% -> 0% of each run, Pallas kernels for 1% -> 1%
where the time goes in v7:
time: 112 us; the launch traced here: 110 us
  waiting for transfers between devices  47.3 us (42%)
  starting transfers between devices  43.9 us (39%)
  Pallas kernels  13.2 us (12%)
  local copies, waits for them, and re-layouts  5.19 us (5%)
    ppermute x3, waiting for transfers between devices, flip_y(): return lax.ppermute(array, 'vel', [(i, i ^ 8) for i in range(VS)])  32.4 us
    ppermute x2, starting transfers between devices, swap_moments(): return lax.ppermute(half, ('vel', 'gx'), pairs)  11.2 us
    ppermute x9, starting transfers between devices, shift_x(): return lax.ppermute(array, 'vel', [(i, mate(i)) for i in range(VS)])  10.7 us
    ppermute x2, starting transfers between devices, swap_rims(): pair_b = lax.ppermute(pair_b, 'gx', far)  9.01 us
    ppermute x8, waiting for transfers between devices, swap_cores(): return lax.ppermute(array, 'vel', [(i, i ^ 1) for i in range(VS)])  6.47 us
    ppermute x8, starting transfers between devices, swap_cores(): return lax.ppermute(array, 'vel', [(i, i ^ 1) for i in range(VS)])  5.98 us
    ppermute x3, starting transfers between devices, flip_y(): return lax.ppermute(array, 'vel', [(i, i ^ 8) for i in range(VS)])  5.77 us
    pallas_call x1, Pallas kernels, move_second(): pl.pallas_call(functools.partial(second_kernel, count), out_shape=outs, i...  5.69 us
  transfers between devices with their start and end apart: 26, of which 13 were waited for; matrix products, arithmetic and copies ran while one was open for 0% of the time, Pallas kernels for 1%

profile of v7, /device:TPU:107, one launch (start us, length us, event | category | flops | bytes accessed | tf_op | source)
XLA Modules:
  0.0 110.1 jit_solution(10923283612003937031)
XLA Ops:
  0.0 1.6 %copy-done = f32[256,2048]{1,0:T(8,128)S(1)} copy-done((f32[256,2048]{1,0:T(8,128)S(1)}, f32[256,2048]{1,0:T(8,128)}, u32[]{:S(2)}) %copy-start) | copy-done | bytes 2097176
  1.6 0.9 copy-done.4
  2.5 0.7 copy-done.5
  3.2 0.7 copy-done.7
  3.9 2.6 %move_first.1 = (f32[5,7,4,8,128]{4,3,2,1,0:T(8,128)S(1)}, f32[256,2048]{1,0:T(8,128)S(1)}, f32[20,8,128]{2,1,0:T(8,128)S(1)}, f32[20,8,128]{2,1,0:T(8,128)S(1)}) custom-call(f32[256,2048]{1,0:T(8,128)S(1)} %copy-done, s32[64,512]{1,0:T(8,128)S(1)} %copy-done.4, s32[2,512]{1,0:T(2,128)S(1)} %copy-done.5, f32[2,128]{1,0:T(2,128)S(1)} %bitcast.1), custom_call_target="tpu_custom_call" | custom-call | tf_op jit(solution)/shard_map/move_first/pallas_call | solution.py:588
  6.5 0.0 copy-start.2
  6.5 1.3 %copy-done.2 = f32[256,2048]{1,0:T(8,128)} copy-done((f32[256,2048]{1,0:T(8,128)}, f32[256,2048]{1,0:T(8,128)S(1)}, u32[]{:S(2)}) %copy-start.2) | copy-done | bytes 2097176
  7.8 0.7 collective-permute-start
  8.5 0.9 collective-permute-done
  9.4 1.3 %collective-permute-start.3 = (f32[20,8,128]{2,1,0:T(8,128)S(1)}, f32[20,8,128]{2,1,0:T(8,128)S(1)}, u32[]{:S(2)}, u32[]{:S(2)}) collective-permute-start(f32[20,8,128]{2,1,0:T(8,128)S(1)} %add.45), channel_id=1, source_target_pairs={{0,96},{16,112},{32,64},{48,80},{64,32},{80,48},{96,0},{112,16},{1... | collective-permute-start | bytes 245768 | tf_op jit(solution)/shard_map/ppermute | solution.py:708
  10.7 1.5 %collective-permute-start.2 = (f32[20,8,128]{2,1,0:T(8,128)S(1)}, f32[20,8,128]{2,1,0:T(8,128)S(1)}, u32[]{:S(2)}, u32[]{:S(2)}) collective-permute-start(f32[20,8,128]{2,1,0:T(8,128)S(1)} %add.45), channel_id=1, source_target_pairs={{0,32},{16,48},{32,0},{48,16},{64,96},{80,112},{96,64},{112,80},{1... | collective-permute-start | bytes 245768 | tf_op jit(solution)/shard_map/ppermute | solution.py:708
  12.2 0.1 slice_select_fusion
  12.3 4.6 %collective-permute-start.9 = (f32[128,1024]{1,0:T(8,128)S(1)}, f32[128,1024]{1,0:T(8,128)S(1)}, u32[]{:S(2)}, u32[]{:S(2)}) collective-permute-start(f32[128,1024]{1,0:T(8,128)S(1)} %get-tuple-element.33), channel_id=1, source_target_pairs={{1,2},{2,1},{3,4},{4,3},{5,6},{6,5},{7,8},{8,7},{9,10},{10,9},{11,... | collective-permute-start | bytes 1572872 | tf_op jit(solution)/shard_map/ppermute | solution.py:733
  17.0 0.1 collective-permute-start.8
  17.1 0.0 collective-permute-done.3
  17.1 0.0 collective-permute-done.1
  17.1 2.4 %collective-permute-start.4 = (f32[20,8,128]{2,1,0:T(8,128)S(1)}, f32[20,8,128]{2,1,0:T(8,128)S(1)}, u32[]{:S(2)}, u32[]{:S(2)}) collective-permute-start(f32[20,8,128]{2,1,0:T(8,128)S(1)} %add_add_fusion), channel_id=1, source_target_pairs={{0,128},{16,144},{32,160},{48,176},{64,192},{80,208},{96,224},{112... | collective-permute-start | bytes 245768 | tf_op jit(solution)/shard_map/ppermute | solution.py:712
  19.5 23.4 %collective-permute-done.4 = f32[20,8,128]{2,1,0:T(8,128)S(1)} collective-permute-done((f32[20,8,128]{2,1,0:T(8,128)S(1)}, f32[20,8,128]{2,1,0:T(8,128)S(1)}, u32[]{:S(2)}, u32[]{:S(2)}) %collective-permute-start.4) | collective-permute-done | bytes 81952 | tf_op jit(solution)/shard_map/ppermute | solution.py:712
  43.0 6.5 %collective-permute-start.6 = (f32[20,8,128]{2,1,0:T(8,128)S(1)}, f32[20,8,128]{2,1,0:T(8,128)S(1)}, u32[]{:S(2)}, u32[]{:S(2)}) collective-permute-start(f32[20,8,128]{2,1,0:T(8,128)S(1)} %add.49.mine_in), channel_id=1, source_target_pairs={{16,1},{1,16},{17,2},{2,17},{18,3},{3,18},{19,4},{4,19},{20,5},{5,... | collective-permute-start | bytes 245768 | tf_op jit(solution)/shard_map/ppermute | solution.py:743
  49.4 0.1 collective-permute-start.5
  49.5 2.0 %collective-permute-done.6.got = f32[20,8,128]{2,1,0:T(8,128)S(1)} collective-permute-done((f32[20,8,128]{2,1,0:T(8,128)S(1)}, f32[20,8,128]{2,1,0:T(8,128)S(1)}, u32[]{:S(2)}, u32[]{:S(2)}) %collective-permute-start.6) | collective-permute-done | bytes 81952 | tf_op jit(solution)/shard_map/ppermute | solution.py:743
  51.5 1.3 %collective-permute-done.7.swapped = f32[20,8,128]{2,1,0:T(8,128)S(1)} collective-permute-done((f32[20,8,128]{2,1,0:T(8,128)S(1)}, f32[20,8,128]{2,1,0:T(8,128)S(1)}, u32[]{:S(2)}, u32[]{:S(2)}) %collective-permute-start.7) | collective-permute-done | bytes 81952 | tf_op jit(solution)/shard_map/ppermute | solution.py:701
  52.8 5.7 %move_second.1 = (f32[256,2048]{1,0:T(8,128)S(1)}, f32[13,8,128]{2,1,0:T(8,128)S(1)}, f32[13,8,128]{2,1,0:T(8,128)S(1)}, f32[128,512]{1,0:T(8,128)S(1)}, f32[128,512]{1,0:T(8,128)S(1)}) custom-call(f32[256,2048]{1,0:T(8,128)S(1)} %copy-done.3, f32[20,8,128]{2,1,0:T(8,128)S(1)} %add.49.mine_in, f32[20,8,128]{2,1,0:T(8,128)S(1)} %collective-permute-done.5.other_in, ...), custom_call_target="tpu_custom_call" | custom-call | tf_op jit(solution)/shard_map/move_second/pallas_call | solution.py:609
  58.5 0.2 collective-permute-start.10
  58.8 1.1 collective-permute-done.10
  59.9 1.3 %collective-permute-start.13 = (f32[13,8,128]{2,1,0:T(8,128)S(1)}, f32[13,8,128]{2,1,0:T(8,128)S(1)}, u32[]{:S(2)}, u32[]{:S(2)}) collective-permute-start(f32[13,8,128]{2,1,0:T(8,128)S(1)} %add.50), channel_id=1, source_target_pairs={{0,96},{16,112},{32,64},{48,80},{64,32},{80,48},{96,0},{112,16},{1... | collective-permute-start | bytes 159752 | tf_op jit(solution)/shard_map/ppermute | solution.py:708
  61.1 2.7 %collective-permute-start.12 = (f32[13,8,128]{2,1,0:T(8,128)S(1)}, f32[13,8,128]{2,1,0:T(8,128)S(1)}, u32[]{:S(2)}, u32[]{:S(2)}) collective-permute-start(f32[13,8,128]{2,1,0:T(8,128)S(1)} %add.50), channel_id=1, source_target_pairs={{0,32},{16,48},{32,0},{48,16},{64,96},{80,112},{96,64},{112,80},{1... | collective-permute-start | bytes 159752 | tf_op jit(solution)/shard_map/ppermute | solution.py:708
  63.8 1.1 %collective-permute-start.17 = (f32[128,512]{1,0:T(8,128)S(1)}, f32[128,512]{1,0:T(8,128)S(1)}, u32[]{:S(2)}, u32[]{:S(2)}) collective-permute-start(f32[128,512]{1,0:T(8,128)S(1)} %get-tuple-element.27), channel_id=1, source_target_pairs={{0,1},{1,0},{2,3},{3,2},{4,5},{5,4},{6,7},{7,6},{8,9},{9,8},{10,11... | collective-permute-start | bytes 786440 | tf_op jit(solution)/shard_map/ppermute | solution.py:732
  65.0 4.4 %collective-permute-start.18 = (f32[128,512]{1,0:T(8,128)S(1)}, f32[128,512]{1,0:T(8,128)S(1)}, u32[]{:S(2)}, u32[]{:S(2)}) collective-permute-start(f32[128,512]{1,0:T(8,128)S(1)} %get-tuple-element.28), channel_id=1, source_target_pairs={{1,2},{2,1},{3,4},{4,3},{5,6},{6,5},{7,8},{8,7},{9,10},{10,9},{11,... | collective-permute-start | bytes 786440 | tf_op jit(solution)/shard_map/ppermute | solution.py:733
  69.4 0.1 collective-permute-start.14
  69.5 7.5 %collective-permute-done.14 = f32[13,8,128]{2,1,0:T(8,128)S(1)} collective-permute-done((f32[13,8,128]{2,1,0:T(8,128)S(1)}, f32[13,8,128]{2,1,0:T(8,128)S(1)}, u32[]{:S(2)}, u32[]{:S(2)}) %collective-permute-start.14) | collective-permute-done | bytes 53280 | tf_op jit(solution)/shard_map/ppermute | solution.py:712
  77.0 1.9 %collective-permute-start.16 = (f32[13,8,128]{2,1,0:T(8,128)S(1)}, f32[13,8,128]{2,1,0:T(8,128)S(1)}, u32[]{:S(2)}, u32[]{:S(2)}) collective-permute-start(f32[13,8,128]{2,1,0:T(8,128)S(1)} %add.54.mine), channel_id=1, source_target_pairs={{0,16},{16,0},{32,48},{48,32},{64,80},{80,64},{96,112},{112,96},{1... | collective-permute-start | bytes 159752 | tf_op jit(solution)/shard_map/ppermute | solution.py:701
  78.8 4.7 %collective-permute-start.15 = (f32[13,8,128]{2,1,0:T(8,128)S(1)}, f32[13,8,128]{2,1,0:T(8,128)S(1)}, u32[]{:S(2)}, u32[]{:S(2)}) collective-permute-start(f32[13,8,128]{2,1,0:T(8,128)S(1)} %add.54.mine), channel_id=1, source_target_pairs={{16,1},{1,16},{17,2},{2,17},{18,3},{3,18},{19,4},{4,19},{20,5},{5,... | collective-permute-start | bytes 159752 | tf_op jit(solution)/shard_map/ppermute | solution.py:743
  83.6 0.9 relax.1.old
  84.5 1.9 %collective-permute-done.15.got = f32[13,8,128]{2,1,0:T(8,128)S(1)} collective-permute-done((f32[13,8,128]{2,1,0:T(8,128)S(1)}, f32[13,8,128]{2,1,0:T(8,128)S(1)}, u32[]{:S(2)}, u32[]{:S(2)}) %collective-permute-start.15) | collective-permute-done | bytes 53280 | tf_op jit(solution)/shard_map/ppermute | solution.py:743
  86.4 1.2 %collective-permute-done.19.swapped = f32[13,8,128]{2,1,0:T(8,128)S(1)} collective-permute-done((f32[13,8,128]{2,1,0:T(8,128)S(1)}, f32[13,8,128]{2,1,0:T(8,128)S(1)}, u32[]{:S(2)}, u32[]{:S(2)}) %collective-permute-start.19) | collective-permute-done | bytes 53280 | tf_op jit(solution)/shard_map/ppermute | solution.py:701
  87.6 2.2 %move_third.1 = (f32[256,3072]{1,0:T(8,128)S(1)}, f32[256,2048]{1,0:T(8,128)S(1)}, f32[13,8,128]{2,1,0:T(8,128)S(1)}, f32[13,8,128]{2,1,0:T(8,128)S(1)}) custom-call(f32[256,3072]{1,0:T(8,128)S(1)} %relax.1.old, f32[128,512]{1,0:T(8,128)S(1)} %collective-permute-done.17.pair_a, ...), custom_call_target="tpu_custom_call", output_to_operand_aliasing={{0}: (0, {})} | custom-call | tf_op jit(solution)/shard_map/move_third/pallas_call | solution.py:631
  89.8 0.2 collective-permute-start.20
  90.0 1.1 collective-permute-done.20
  91.1 1.3 %collective-permute-start.23 = (f32[13,8,128]{2,1,0:T(8,128)S(1)}, f32[13,8,128]{2,1,0:T(8,128)S(1)}, u32[]{:S(2)}, u32[]{:S(2)}) collective-permute-start(f32[13,8,128]{2,1,0:T(8,128)S(1)} %add.55), channel_id=1, source_target_pairs={{0,96},{16,112},{32,64},{48,80},{64,32},{80,48},{96,0},{112,16},{1... | collective-permute-start | bytes 159752 | tf_op jit(solution)/shard_map/ppermute | solution.py:708
  92.4 2.7 %collective-permute-start.22 = (f32[13,8,128]{2,1,0:T(8,128)S(1)}, f32[13,8,128]{2,1,0:T(8,128)S(1)}, u32[]{:S(2)}, u32[]{:S(2)}) collective-permute-start(f32[13,8,128]{2,1,0:T(8,128)S(1)} %add.55), channel_id=1, source_target_pairs={{0,32},{16,48},{32,0},{48,16},{64,96},{80,112},{96,64},{112,80},{1... | collective-permute-start | bytes 159752 | tf_op jit(solution)/shard_map/ppermute | solution.py:708
  95.1 1.5 %collective-permute-done.22 = f32[13,8,128]{2,1,0:T(8,128)S(1)} collective-permute-done((f32[13,8,128]{2,1,0:T(8,128)S(1)}, f32[13,8,128]{2,1,0:T(8,128)S(1)}, u32[]{:S(2)}, u32[]{:S(2)}) %collective-permute-start.22) | collective-permute-done | bytes 53280 | tf_op jit(solution)/shard_map/ppermute | solution.py:708
  96.6 3.0 %collective-permute-done.21 = f32[13,8,128]{2,1,0:T(8,128)S(1)} collective-permute-done((f32[13,8,128]{2,1,0:T(8,128)S(1)}, f32[13,8,128]{2,1,0:T(8,128)S(1)}, u32[]{:S(2)}, u32[]{:S(2)}) %collective-permute-start.21) | collective-permute-done | bytes 53280 | tf_op jit(solution)/shard_map/ppermute | solution.py:708
  99.6 3.3 %collective-permute-start.24 = (f32[13,8,128]{2,1,0:T(8,128)S(1)}, f32[13,8,128]{2,1,0:T(8,128)S(1)}, u32[]{:S(2)}, u32[]{:S(2)}) collective-permute-start(f32[13,8,128]{2,1,0:T(8,128)S(1)} %add_add_fusion.1), channel_id=1, source_target_pairs={{0,128},{16,144},{32,160},{48,176},{64,192},{80,208},{96,224},{112... | collective-permute-start | bytes 159752 | tf_op jit(solution)/shard_map/ppermute | solution.py:712
  102.9 1.5 %collective-permute-done.24 = f32[13,8,128]{2,1,0:T(8,128)S(1)} collective-permute-done((f32[13,8,128]{2,1,0:T(8,128)S(1)}, f32[13,8,128]{2,1,0:T(8,128)S(1)}, u32[]{:S(2)}, u32[]{:S(2)}) %collective-permute-start.24) | collective-permute-done | bytes 53280 | tf_op jit(solution)/shard_map/ppermute | solution.py:712
  104.4 2.9 %collective-permute-start.25 = (f32[13,8,128]{2,1,0:T(8,128)S(1)}, f32[13,8,128]{2,1,0:T(8,128)S(1)}, u32[]{:S(2)}, u32[]{:S(2)}) collective-permute-start(f32[13,8,128]{2,1,0:T(8,128)S(1)} %add.59.mine), channel_id=1, source_target_pairs={{0,16},{16,0},{32,48},{48,32},{64,80},{80,64},{96,112},{112,96},{1... | collective-permute-start | bytes 159752 | tf_op jit(solution)/shard_map/ppermute | solution.py:701
  107.3 0.9 collective-permute-done.25.other
  108.2 1.8 %relax_last.1 = f32[256,2048]{1,0:T(8,128)} custom-call(f32[256,2048]{1,0:T(8,128)S(1)} %get-tuple-element.30.moved, f32[13,8,128]{2,1,0:T(8,128)S(1)} %add.59.mine, f32[13,8,128]{2,1,0:T(8,128)S(1)} %collective-permute-done.25.other), custom_call_target="tpu_custom_call" | custom-call | tf_op jit(solution)/shard_map/relax_last/pallas_call | solution.py:684
  (37 shorter events, 0.2 us)
Async XLA Ops:
  0.0 1.6 %copy-start = (f32[256,2048]{1,0:T(8,128)S(1)}, f32[256,2048]{1,0:T(8,128)}, u32[]{:S(2)}) copy-start(f32[256,2048]{1,0:T(8,128)} %dist.1) | copy-start | bytes 6291460
  1.6 0.9 copy-start.4
  2.5 0.7 copy-start.5
  3.2 0.7 copy-start.7
  3.9 8.4 %copy-start.1 = (f32[256,2048]{1,0:T(8,128)S(1)}, f32[256,2048]{1,0:T(8,128)}, u32[]{:S(2)}) copy-start(f32[256,2048]{1,0:T(8,128)} %dist.1) | copy-start | bytes 6291460
  3.9 49.0 %copy-start.6 = (s32[2,512]{1,0:T(2,128)S(1)}, s32[2,512]{1,0:T(2,128)}, u32[]{:S(2)}) copy-start(s32[2,512]{1,0:T(2,128)} %kind.5) | copy-start | bytes 12292
  3.9 49.0 %copy-start.8 = (f32[256]{0:T(256)S(1)}, f32[256]{0:T(256)}, u32[]{:S(2)}) copy-start(f32[256]{0:T(256)} %param.7) | copy-start | bytes 3076
  6.5 1.3 %copy-start.2 = (f32[256,2048]{1,0:T(8,128)}, f32[256,2048]{1,0:T(8,128)S(1)}, u32[]{:S(2)}) copy-start(f32[256,2048]{1,0:T(8,128)S(1)} %get-tuple-element.19.source) | copy-start | bytes 6291460
  7.8 1.6 %collective-permute-start = (f32[20,8,128]{2,1,0:T(8,128)S(1)}, f32[20,8,128]{2,1,0:T(8,128)S(1)}, u32[]{:S(2)}, u32[]{:S(2)}) collective-permute-start(f32[20,8,128]{2,1,0:T(8,128)S(1)} %get-tuple-element.21), channel_id=1, source_target_pairs={{0,16},{16,0},{32,48},{48,32},{64,80},{80,64},{96,112},{112,96},{1... | collective-permute-start | bytes 245768 | tf_op jit(solution)/shard_map/ppermute | solution.py:701
  8.5 44.4 %copy-start.3 = (f32[256,2048]{1,0:T(8,128)S(1)}, f32[256,2048]{1,0:T(8,128)}, u32[]{:S(2)}) copy-start(f32[256,2048]{1,0:T(8,128)} %copy-done.2) | copy-start | bytes 6291460
  9.4 7.7 %collective-permute-start.3 = (f32[20,8,128]{2,1,0:T(8,128)S(1)}, f32[20,8,128]{2,1,0:T(8,128)S(1)}, u32[]{:S(2)}, u32[]{:S(2)}) collective-permute-start(f32[20,8,128]{2,1,0:T(8,128)S(1)} %add.45), channel_id=1, source_target_pairs={{0,96},{16,112},{32,64},{48,80},{64,32},{80,48},{96,0},{112,16},{1... | collective-permute-start | bytes 245768 | tf_op jit(solution)/shard_map/ppermute | solution.py:708
  10.7 6.4 %collective-permute-start.2 = (f32[20,8,128]{2,1,0:T(8,128)S(1)}, f32[20,8,128]{2,1,0:T(8,128)S(1)}, u32[]{:S(2)}, u32[]{:S(2)}) collective-permute-start(f32[20,8,128]{2,1,0:T(8,128)S(1)} %add.45), channel_id=1, source_target_pairs={{0,32},{16,48},{32,0},{48,16},{64,96},{80,112},{96,64},{112,80},{1... | collective-permute-start | bytes 245768 | tf_op jit(solution)/shard_map/ppermute | solution.py:708
  12.2 4.9 %collective-permute-start.1 = (f32[20,8,128]{2,1,0:T(8,128)S(1)}, f32[20,8,128]{2,1,0:T(8,128)S(1)}, u32[]{:S(2)}, u32[]{:S(2)}) collective-permute-start(f32[20,8,128]{2,1,0:T(8,128)S(1)} %add.45), channel_id=1, source_target_pairs={{0,64},{16,80},{32,96},{48,112},{64,0},{80,16},{96,32},{112,48},{1... | collective-permute-start | bytes 245768 | tf_op jit(solution)/shard_map/ppermute | solution.py:708
  12.3 40.5 %collective-permute-start.9 = (f32[128,1024]{1,0:T(8,128)S(1)}, f32[128,1024]{1,0:T(8,128)S(1)}, u32[]{:S(2)}, u32[]{:S(2)}) collective-permute-start(f32[128,1024]{1,0:T(8,128)S(1)} %get-tuple-element.33), channel_id=1, source_target_pairs={{1,2},{2,1},{3,4},{4,3},{5,6},{6,5},{7,8},{8,7},{9,10},{10,9},{11,... | collective-permute-start | bytes 1572872 | tf_op jit(solution)/shard_map/ppermute | solution.py:733
  17.0 35.9 %collective-permute-start.8 = (f32[128,1024]{1,0:T(8,128)S(1)}, f32[128,1024]{1,0:T(8,128)S(1)}, u32[]{:S(2)}, u32[]{:S(2)}) collective-permute-start(f32[128,1024]{1,0:T(8,128)S(1)} %get-tuple-element.34), channel_id=1, source_target_pairs={{0,1},{1,0},{2,3},{3,2},{4,5},{5,4},{6,7},{7,6},{8,9},{9,8},{10,11... | collective-permute-start | bytes 1572872 | tf_op jit(solution)/shard_map/ppermute | solution.py:732
  17.1 25.8 %collective-permute-start.4 = (f32[20,8,128]{2,1,0:T(8,128)S(1)}, f32[20,8,128]{2,1,0:T(8,128)S(1)}, u32[]{:S(2)}, u32[]{:S(2)}) collective-permute-start(f32[20,8,128]{2,1,0:T(8,128)S(1)} %add_add_fusion), channel_id=1, source_target_pairs={{0,128},{16,144},{32,160},{48,176},{64,192},{80,208},{96,224},{112... | collective-permute-start | bytes 245768 | tf_op jit(solution)/shard_map/ppermute | solution.py:712
  43.0 8.6 %collective-permute-start.6 = (f32[20,8,128]{2,1,0:T(8,128)S(1)}, f32[20,8,128]{2,1,0:T(8,128)S(1)}, u32[]{:S(2)}, u32[]{:S(2)}) collective-permute-start(f32[20,8,128]{2,1,0:T(8,128)S(1)} %add.49.mine_in), channel_id=1, source_target_pairs={{16,1},{1,16},{17,2},{2,17},{18,3},{3,18},{19,4},{4,19},{20,5},{5,... | collective-permute-start | bytes 245768 | tf_op jit(solution)/shard_map/ppermute | solution.py:743
  49.4 2.1 %collective-permute-start.5 = (f32[20,8,128]{2,1,0:T(8,128)S(1)}, f32[20,8,128]{2,1,0:T(8,128)S(1)}, u32[]{:S(2)}, u32[]{:S(2)}) collective-permute-start(f32[20,8,128]{2,1,0:T(8,128)S(1)} %add.49.mine_in), channel_id=1, source_target_pairs={{0,16},{16,0},{32,48},{48,32},{64,80},{80,64},{96,112},{112,96},{1... | collective-permute-start | bytes 245768 | tf_op jit(solution)/shard_map/ppermute | solution.py:701
  51.5 1.3 %collective-permute-start.7 = (f32[20,8,128]{2,1,0:T(8,128)S(1)}, f32[20,8,128]{2,1,0:T(8,128)S(1)}, u32[]{:S(2)}, u32[]{:S(2)}) collective-permute-start(f32[20,8,128]{2,1,0:T(8,128)S(1)} %collective-permute-done.6.got), channel_id=1, source_target_pairs={{0,16},{16,0},{32,48},{48,32},{64,80},{80,64},{96,112},{112,96},{1... | collective-permute-start | bytes 245768 | tf_op jit(solution)/shard_map/ppermute | solution.py:701
  58.5 1.3 %collective-permute-start.10 = (f32[13,8,128]{2,1,0:T(8,128)S(1)}, f32[13,8,128]{2,1,0:T(8,128)S(1)}, u32[]{:S(2)}, u32[]{:S(2)}) collective-permute-start(f32[13,8,128]{2,1,0:T(8,128)S(1)} %get-tuple-element.24), channel_id=1, source_target_pairs={{0,16},{16,0},{32,48},{48,32},{64,80},{80,64},{96,112},{112,96},{1... | collective-permute-start | bytes 159752 | tf_op jit(solution)/shard_map/ppermute | solution.py:701
  59.9 9.5 %collective-permute-start.13 = (f32[13,8,128]{2,1,0:T(8,128)S(1)}, f32[13,8,128]{2,1,0:T(8,128)S(1)}, u32[]{:S(2)}, u32[]{:S(2)}) collective-permute-start(f32[13,8,128]{2,1,0:T(8,128)S(1)} %add.50), channel_id=1, source_target_pairs={{0,96},{16,112},{32,64},{48,80},{64,32},{80,48},{96,0},{112,16},{1... | collective-permute-start | bytes 159752 | tf_op jit(solution)/shard_map/ppermute | solution.py:708
  61.1 8.2 %collective-permute-start.12 = (f32[13,8,128]{2,1,0:T(8,128)S(1)}, f32[13,8,128]{2,1,0:T(8,128)S(1)}, u32[]{:S(2)}, u32[]{:S(2)}) collective-permute-start(f32[13,8,128]{2,1,0:T(8,128)S(1)} %add.50), channel_id=1, source_target_pairs={{0,32},{16,48},{32,0},{48,16},{64,96},{80,112},{96,64},{112,80},{1... | collective-permute-start | bytes 159752 | tf_op jit(solution)/shard_map/ppermute | solution.py:708
  63.8 5.5 %collective-permute-start.11 = (f32[13,8,128]{2,1,0:T(8,128)S(1)}, f32[13,8,128]{2,1,0:T(8,128)S(1)}, u32[]{:S(2)}, u32[]{:S(2)}) collective-permute-start(f32[13,8,128]{2,1,0:T(8,128)S(1)} %add.50), channel_id=1, source_target_pairs={{0,64},{16,80},{32,96},{48,112},{64,0},{80,16},{96,32},{112,48},{1... | collective-permute-start | bytes 159752 | tf_op jit(solution)/shard_map/ppermute | solution.py:708
  63.8 22.6 %collective-permute-start.17 = (f32[128,512]{1,0:T(8,128)S(1)}, f32[128,512]{1,0:T(8,128)S(1)}, u32[]{:S(2)}, u32[]{:S(2)}) collective-permute-start(f32[128,512]{1,0:T(8,128)S(1)} %get-tuple-element.27), channel_id=1, source_target_pairs={{0,1},{1,0},{2,3},{3,2},{4,5},{5,4},{6,7},{7,6},{8,9},{9,8},{10,11... | collective-permute-start | bytes 786440 | tf_op jit(solution)/shard_map/ppermute | solution.py:732
  65.0 21.4 %collective-permute-start.18 = (f32[128,512]{1,0:T(8,128)S(1)}, f32[128,512]{1,0:T(8,128)S(1)}, u32[]{:S(2)}, u32[]{:S(2)}) collective-permute-start(f32[128,512]{1,0:T(8,128)S(1)} %get-tuple-element.28), channel_id=1, source_target_pairs={{1,2},{2,1},{3,4},{4,3},{5,6},{6,5},{7,8},{8,7},{9,10},{10,9},{11,... | collective-permute-start | bytes 786440 | tf_op jit(solution)/shard_map/ppermute | solution.py:733
  69.4 7.6 %collective-permute-start.14 = (f32[13,8,128]{2,1,0:T(8,128)S(1)}, f32[13,8,128]{2,1,0:T(8,128)S(1)}, u32[]{:S(2)}, u32[]{:S(2)}) collective-permute-start(f32[13,8,128]{2,1,0:T(8,128)S(1)} %add_add_fusion.2), channel_id=1, source_target_pairs={{0,128},{16,144},{32,160},{48,176},{64,192},{80,208},{96,224},{112... | collective-permute-start | bytes 159752 | tf_op jit(solution)/shard_map/ppermute | solution.py:712
  77.0 6.6 %collective-permute-start.16 = (f32[13,8,128]{2,1,0:T(8,128)S(1)}, f32[13,8,128]{2,1,0:T(8,128)S(1)}, u32[]{:S(2)}, u32[]{:S(2)}) collective-permute-start(f32[13,8,128]{2,1,0:T(8,128)S(1)} %add.54.mine), channel_id=1, source_target_pairs={{0,16},{16,0},{32,48},{48,32},{64,80},{80,64},{96,112},{112,96},{1... | collective-permute-start | bytes 159752 | tf_op jit(solution)/shard_map/ppermute | solution.py:701
  78.8 7.6 %collective-permute-start.15 = (f32[13,8,128]{2,1,0:T(8,128)S(1)}, f32[13,8,128]{2,1,0:T(8,128)S(1)}, u32[]{:S(2)}, u32[]{:S(2)}) collective-permute-start(f32[13,8,128]{2,1,0:T(8,128)S(1)} %add.54.mine), channel_id=1, source_target_pairs={{16,1},{1,16},{17,2},{2,17},{18,3},{3,18},{19,4},{4,19},{20,5},{5,... | collective-permute-start | bytes 159752 | tf_op jit(solution)/shard_map/ppermute | solution.py:743
  86.4 1.2 %collective-permute-start.19 = (f32[13,8,128]{2,1,0:T(8,128)S(1)}, f32[13,8,128]{2,1,0:T(8,128)S(1)}, u32[]{:S(2)}, u32[]{:S(2)}) collective-permute-start(f32[13,8,128]{2,1,0:T(8,128)S(1)} %collective-permute-done.15.got), channel_id=1, source_target_pairs={{0,16},{16,0},{32,48},{48,32},{64,80},{80,64},{96,112},{112,96},{1... | collective-permute-start | bytes 159752 | tf_op jit(solution)/shard_map/ppermute | solution.py:701
  89.8 1.3 %collective-permute-start.20 = (f32[13,8,128]{2,1,0:T(8,128)S(1)}, f32[13,8,128]{2,1,0:T(8,128)S(1)}, u32[]{:S(2)}, u32[]{:S(2)}) collective-permute-start(f32[13,8,128]{2,1,0:T(8,128)S(1)} %get-tuple-element.32), channel_id=1, source_target_pairs={{0,16},{16,0},{32,48},{48,32},{64,80},{80,64},{96,112},{112,96},{1... | collective-permute-start | bytes 159752 | tf_op jit(solution)/shard_map/ppermute | solution.py:701
  91.1 3.9 %collective-permute-start.23 = (f32[13,8,128]{2,1,0:T(8,128)S(1)}, f32[13,8,128]{2,1,0:T(8,128)S(1)}, u32[]{:S(2)}, u32[]{:S(2)}) collective-permute-start(f32[13,8,128]{2,1,0:T(8,128)S(1)} %add.55), channel_id=1, source_target_pairs={{0,96},{16,112},{32,64},{48,80},{64,32},{80,48},{96,0},{112,16},{1... | collective-permute-start | bytes 159752 | tf_op jit(solution)/shard_map/ppermute | solution.py:708
  92.4 4.2 %collective-permute-start.22 = (f32[13,8,128]{2,1,0:T(8,128)S(1)}, f32[13,8,128]{2,1,0:T(8,128)S(1)}, u32[]{:S(2)}, u32[]{:S(2)}) collective-permute-start(f32[13,8,128]{2,1,0:T(8,128)S(1)} %add.55), channel_id=1, source_target_pairs={{0,32},{16,48},{32,0},{48,16},{64,96},{80,112},{96,64},{112,80},{1... | collective-permute-start | bytes 159752 | tf_op jit(solution)/shard_map/ppermute | solution.py:708
  95.1 4.5 %collective-permute-start.21 = (f32[13,8,128]{2,1,0:T(8,128)S(1)}, f32[13,8,128]{2,1,0:T(8,128)S(1)}, u32[]{:S(2)}, u32[]{:S(2)}) collective-permute-start(f32[13,8,128]{2,1,0:T(8,128)S(1)} %add.55), channel_id=1, source_target_pairs={{0,64},{16,80},{32,96},{48,112},{64,0},{80,16},{96,32},{112,48},{1... | collective-permute-start | bytes 159752 | tf_op jit(solution)/shard_map/ppermute | solution.py:708
  99.6 4.8 %collective-permute-start.24 = (f32[13,8,128]{2,1,0:T(8,128)S(1)}, f32[13,8,128]{2,1,0:T(8,128)S(1)}, u32[]{:S(2)}, u32[]{:S(2)}) collective-permute-start(f32[13,8,128]{2,1,0:T(8,128)S(1)} %add_add_fusion.1), channel_id=1, source_target_pairs={{0,128},{16,144},{32,160},{48,176},{64,192},{80,208},{96,224},{112... | collective-permute-start | bytes 159752 | tf_op jit(solution)/shard_map/ppermute | solution.py:712
  104.4 3.7 %collective-permute-start.25 = (f32[13,8,128]{2,1,0:T(8,128)S(1)}, f32[13,8,128]{2,1,0:T(8,128)S(1)}, u32[]{:S(2)}, u32[]{:S(2)}) collective-permute-start(f32[13,8,128]{2,1,0:T(8,128)S(1)} %add.59.mine), channel_id=1, source_target_pairs={{0,16},{16,0},{32,48},{48,32},{64,80},{80,64},{96,112},{112,96},{1... | collective-permute-start | bytes 159752 | tf_op jit(solution)/shard_map/ppermute | solution.py:701

commit v8 on v6

--- a/solution.py
+++ b/solution.py
@@ -527,7 +527,7 @@
 HBM = pl.BlockSpec(memory_space=pltpu.HBM)
 PARAMS = pltpu.CompilerParams(vmem_limit_bytes=12 << 20)
 F32 = jnp.float32
-FIRST_LIMIT = 60_000_000
+FIRST_LIMIT = 12 << 20
 WHOLE = jax.ShapeDtypeStruct((ROWS, DEPTH * SEC), F32)
 WIDE = jax.ShapeDtypeStruct((ROWS, (DEPTH + 2) * SEC), F32)
 RIM = jax.ShapeDtypeStruct((HALF, SEC), F32)
@@ -559,6 +559,37 @@
     )(dist, wall, kind, inflow)
 
 
+def cut_kernel(dist, near, far, sems):
+    even = lax.rem(lax.axis_index("gx"), 2) == 0
+
+    def cut(up, down):
+        copies = [
+            pltpu.make_async_copy(
+                dist.at[pl.ds(HALF, HALF), pl.ds((DEPTH - 1) * SEC, SEC)], up, sems.at[0]
+            ),
+            pltpu.make_async_copy(dist.at[pl.ds(0, HALF), pl.ds(0, SEC)], down, sems.at[1]),
+        ]
+        for copy in copies:
+            copy.start()
+        for copy in copies:
+            copy.wait()
+
+    pl.when(even)(lambda: cut(near, far))
+    pl.when(~even)(lambda: cut(far, near))
+
+
+def cut_rims(dist):
+    return pl.pallas_call(
+        cut_kernel,
+        out_shape=(RIM, RIM),
+        in_specs=[HBM],
+        out_specs=(VM, VM),
+        scratch_shapes=[pltpu.SemaphoreType.DMA((2,))],
+        compiler_params=pltpu.CompilerParams(vmem_limit_bytes=54_000_000),
+        name="cut_rims",
+    )(dist)
+
+
 def move_second(source, halves, faces, kind, inflow, pairs, count):
     outs = (WHOLE, PART, PART, RIM, RIM)
     return pl.pallas_call(
@@ -701,9 +732,8 @@
     count = lax.axis_size("gx")
     inflow = inflow.reshape(2, 128)
     even = lax.rem(lax.axis_index("gx"), 2) == 0
-    up = distribution[HALF:, (DEPTH - 1) * SEC :]
-    down = distribution[:HALF, :SEC]
-    start = swap_rims(jnp.where(even, up, down), jnp.where(even, down, up), count)
+    near, far = cut_rims(distribution)
+    start = swap_rims(near, far, count)
     outs = move_first(distribution, wall_mask, boundary_kind, inflow, count)
     faces, moved, mine, other, *rims = outs
     pairs = swap_rims(*rims, count)

time: 110 us -> 105 us (0.955)
  waiting for transfers between devices: 43.6 us -> 35.9 us
  starting transfers between devices: 47.9 us -> 51.7 us
  local copies, waits for them, and re-layouts: 1.6 us -> 3.87 us
  other arithmetic: 2.07 us -> 0.11 us
  Pallas kernels: 13.1 us -> 11.5 us
    ppermute x3, waiting for transfers between devices: 28.5 us -> 22.1 us  [flip_y(): return lax.ppermute(array, 'vel', [(i, i ^ 8) for i in range(VS)])]
    ppermute x3, starting transfers between devices: 11.7 us -> 15.1 us  [swap_rims(): pair_b = lax.ppermute(pair_b, 'gx', far)]
    ppermute x2, starting transfers between devices: 11.2 us -> 14.2 us  [swap_moments(): return lax.ppermute(half, ('vel', 'gx'), pairs)]
    pallas_call x1, Pallas kernels: 5.31 us -> 2.61 us  [move_first(): pl.pallas_call(functools.partial(first_kernel, count), out_shape=outs, in...]
    ppermute x3, starting transfers between devices: 2.67 us -> 0.34 us  [swap_rims(): pair_a = lax.ppermute(pair_a, 'gx', near)]
    unnamed x8 -> x12, local copies, waits for them, and re-layouts: 1.6 us -> 3.87 us
  transfers between devices with their start and end apart: 28 -> 28, of which waited for: 13 -> 13; matrix products, arithmetic and copies ran while one was open for 1% -> 0% of each run, Pallas kernels for 1% -> 2%
where the time goes in v8:
time: 105 us; the launch traced here: 104 us
  starting transfers between devices  51.7 us (49%)
  waiting for transfers between devices  35.9 us (34%)
  Pallas kernels  11.5 us (11%)
  local copies, waits for them, and re-layouts  3.87 us (4%)
    ppermute x3, waiting for transfers between devices, flip_y(): return lax.ppermute(array, 'vel', [(i, i ^ 8) for i in range(VS)])  22.1 us
    ppermute x3, starting transfers between devices, swap_rims(): pair_b = lax.ppermute(pair_b, 'gx', far)  15.1 us
    ppermute x2, starting transfers between devices, swap_moments(): return lax.ppermute(half, ('vel', 'gx'), pairs)  14.2 us
    ppermute x9, starting transfers between devices, shift_x(): return lax.ppermute(array, 'vel', [(i, mate(i)) for i in range(VS)])  10.7 us
    ppermute x8, waiting for transfers between devices, swap_cores(): return lax.ppermute(array, 'vel', [(i, i ^ 1) for i in range(VS)])  6.44 us
    ppermute x8, starting transfers between devices, swap_cores(): return lax.ppermute(array, 'vel', [(i, i ^ 1) for i in range(VS)])  6.12 us
    ppermute x3, starting transfers between devices, flip_y(): return lax.ppermute(array, 'vel', [(i, i ^ 8) for i in range(VS)])  5.23 us
    ppermute x9, waiting for transfers between devices, shift_x(): return lax.ppermute(array, 'vel', [(i, mate(i)) for i in range(VS)])  4.5 us
  transfers between devices with their start and end apart: 28, of which 13 were waited for; matrix products, arithmetic and copies ran while one was open for 0% of the time, Pallas kernels for 2%

profile of v8, /device:TPU:107, one launch (start us, length us, event | category | flops | bytes accessed | tf_op | source)
XLA Modules:
  0.0 103.5 jit_solution(16934437947561335445)
XLA Ops:
  0.0 1.6 %copy-done = f32[256,2048]{1,0:T(8,128)S(1)} copy-done((f32[256,2048]{1,0:T(8,128)S(1)}, f32[256,2048]{1,0:T(8,128)}, u32[]{:S(2)}) %copy-start) | copy-done | bytes 2097176
  1.6 0.9 copy-done.1
  2.5 0.7 copy-done.2
  3.2 0.7 copy-done.4
  3.9 2.6 %move_first.1 = (f32[5,5,4,8,128]{4,3,2,1,0:T(8,128)S(1)}, f32[256,2048]{1,0:T(8,128)S(1)}, f32[20,8,128]{2,1,0:T(8,128)S(1)}, f32[20,8,128]{2,1,0:T(8,128)S(1)}...) custom-call(f32[256,2048]{1,0:T(8,128)S(1)} %copy-done, s32[64,512]{1,0:T(8,128)S(1)} %copy-done.1, ...), custom_call_target="tpu_custom_call" | custom-call | tf_op jit(solution)/shard_map/move_first/pallas_call | solution.py:543
  6.5 0.8 collective-permute-start
  7.2 0.9 collective-permute-done
  8.2 1.3 %collective-permute-start.3 = (f32[20,8,128]{2,1,0:T(8,128)S(1)}, f32[20,8,128]{2,1,0:T(8,128)S(1)}, u32[]{:S(2)}, u32[]{:S(2)}) collective-permute-start(f32[20,8,128]{2,1,0:T(8,128)S(1)} %add.45), channel_id=1, source_target_pairs={{0,96},{16,112},{32,64},{48,80},{64,32},{80,48},{96,0},{112,16},{1... | collective-permute-start | bytes 245768 | tf_op jit(solution)/shard_map/ppermute | solution.py:693
  9.5 1.5 %collective-permute-start.2 = (f32[20,8,128]{2,1,0:T(8,128)S(1)}, f32[20,8,128]{2,1,0:T(8,128)S(1)}, u32[]{:S(2)}, u32[]{:S(2)}) collective-permute-start(f32[20,8,128]{2,1,0:T(8,128)S(1)} %add.45), channel_id=1, source_target_pairs={{0,32},{16,48},{32,0},{48,16},{64,96},{80,112},{96,64},{112,80},{1... | collective-permute-start | bytes 245768 | tf_op jit(solution)/shard_map/ppermute | solution.py:693
  11.0 0.0 collective-permute-start.1
  11.0 1.0 %cut_rims.1 = (f32[128,512]{1,0:T(8,128)S(1)}, f32[128,512]{1,0:T(8,128)S(1)}) custom-call(f32[256,2048]{1,0:T(8,128)} %dist.3), custom_call_target="tpu_custom_call" | custom-call | tf_op jit(solution)/shard_map/cut_rims/pallas_call | solution.py:582
  12.1 0.2 collective-permute-start.10
  12.3 5.8 %collective-permute-start.11 = (f32[128,512]{1,0:T(8,128)S(1)}, f32[128,512]{1,0:T(8,128)S(1)}, u32[]{:S(2)}, u32[]{:S(2)}) collective-permute-start(f32[128,512]{1,0:T(8,128)S(1)} %get-tuple-element.30), channel_id=1, source_target_pairs={{1,2},{2,1},{3,4},{4,3},{5,6},{6,5},{7,8},{8,7},{9,10},{10,9},{11,... | collective-permute-start | bytes 786440 | tf_op jit(solution)/shard_map/ppermute | solution.py:718
  18.1 0.1 collective-permute-start.8
  18.2 0.0 collective-permute-done.2
  18.2 3.8 %collective-permute-start.9 = (f32[128,512]{1,0:T(8,128)S(1)}, f32[128,512]{1,0:T(8,128)S(1)}, u32[]{:S(2)}, u32[]{:S(2)}) collective-permute-start(f32[128,512]{1,0:T(8,128)S(1)} %get-tuple-element.28), channel_id=1, source_target_pairs={{1,2},{2,1},{3,4},{4,3},{5,6},{6,5},{7,8},{8,7},{9,10},{10,9},{11,... | collective-permute-start | bytes 786440 | tf_op jit(solution)/shard_map/ppermute | solution.py:718
  22.1 2.1 %collective-permute-start.4 = (f32[20,8,128]{2,1,0:T(8,128)S(1)}, f32[20,8,128]{2,1,0:T(8,128)S(1)}, u32[]{:S(2)}, u32[]{:S(2)}) collective-permute-start(f32[20,8,128]{2,1,0:T(8,128)S(1)} %add_add_fusion), channel_id=1, source_target_pairs={{0,128},{16,144},{32,160},{48,176},{64,192},{80,208},{96,224},{112... | collective-permute-start | bytes 245768 | tf_op jit(solution)/shard_map/ppermute | solution.py:697
  24.1 14.1 %collective-permute-done.4 = f32[20,8,128]{2,1,0:T(8,128)S(1)} collective-permute-done((f32[20,8,128]{2,1,0:T(8,128)S(1)}, f32[20,8,128]{2,1,0:T(8,128)S(1)}, u32[]{:S(2)}, u32[]{:S(2)}) %collective-permute-start.4) | collective-permute-done | bytes 81952 | tf_op jit(solution)/shard_map/ppermute | solution.py:697
  38.2 8.2 %collective-permute-start.6 = (f32[20,8,128]{2,1,0:T(8,128)S(1)}, f32[20,8,128]{2,1,0:T(8,128)S(1)}, u32[]{:S(2)}, u32[]{:S(2)}) collective-permute-start(f32[20,8,128]{2,1,0:T(8,128)S(1)} %add.49.mine_in), channel_id=1, source_target_pairs={{16,1},{1,16},{17,2},{2,17},{18,3},{3,18},{19,4},{4,19},{20,5},{5,... | collective-permute-start | bytes 245768 | tf_op jit(solution)/shard_map/ppermute | solution.py:728
  46.5 0.1 collective-permute-start.5
  46.6 2.0 %collective-permute-done.6.got = f32[20,8,128]{2,1,0:T(8,128)S(1)} collective-permute-done((f32[20,8,128]{2,1,0:T(8,128)S(1)}, f32[20,8,128]{2,1,0:T(8,128)S(1)}, u32[]{:S(2)}, u32[]{:S(2)}) %collective-permute-start.6) | collective-permute-done | bytes 81952 | tf_op jit(solution)/shard_map/ppermute | solution.py:728
  48.6 1.2 %collective-permute-done.7.swapped = f32[20,8,128]{2,1,0:T(8,128)S(1)} collective-permute-done((f32[20,8,128]{2,1,0:T(8,128)S(1)}, f32[20,8,128]{2,1,0:T(8,128)S(1)}, u32[]{:S(2)}, u32[]{:S(2)}) %collective-permute-start.7) | collective-permute-done | bytes 81952 | tf_op jit(solution)/shard_map/ppermute | solution.py:686
  49.9 3.1 %move_second.1 = (f32[256,2048]{1,0:T(8,128)S(1)}, f32[13,8,128]{2,1,0:T(8,128)S(1)}, f32[13,8,128]{2,1,0:T(8,128)S(1)}, f32[128,512]{1,0:T(8,128)S(1)}, f32[128,512]{1,0:T(8,128)S(1)}) custom-call(f32[256,2048]{1,0:T(8,128)S(1)} %get-tuple-element.23.source, f32[20,8,128]{2,1,0:T(8,128)S(1)} %add.49.mine_in, ...), custom_call_target="tpu_custom_call" | custom-call | tf_op jit(solution)/shard_map/move_second/pallas_call | solution.py:595
  53.0 0.2 collective-permute-start.12
  53.2 1.1 %collective-permute-done.12 = f32[13,8,128]{2,1,0:T(8,128)S(1)} collective-permute-done((f32[13,8,128]{2,1,0:T(8,128)S(1)}, f32[13,8,128]{2,1,0:T(8,128)S(1)}, u32[]{:S(2)}, u32[]{:S(2)}) %collective-permute-start.12) | collective-permute-done | bytes 53280 | tf_op jit(solution)/shard_map/ppermute | solution.py:686
  54.3 1.3 %collective-permute-start.15 = (f32[13,8,128]{2,1,0:T(8,128)S(1)}, f32[13,8,128]{2,1,0:T(8,128)S(1)}, u32[]{:S(2)}, u32[]{:S(2)}) collective-permute-start(f32[13,8,128]{2,1,0:T(8,128)S(1)} %add.50), channel_id=1, source_target_pairs={{0,96},{16,112},{32,64},{48,80},{64,32},{80,48},{96,0},{112,16},{1... | collective-permute-start | bytes 159752 | tf_op jit(solution)/shard_map/ppermute | solution.py:693
  55.6 2.7 %collective-permute-start.14 = (f32[13,8,128]{2,1,0:T(8,128)S(1)}, f32[13,8,128]{2,1,0:T(8,128)S(1)}, u32[]{:S(2)}, u32[]{:S(2)}) collective-permute-start(f32[13,8,128]{2,1,0:T(8,128)S(1)} %add.50), channel_id=1, source_target_pairs={{0,32},{16,48},{32,0},{48,16},{64,96},{80,112},{96,64},{112,80},{1... | collective-permute-start | bytes 159752 | tf_op jit(solution)/shard_map/ppermute | solution.py:693
  58.3 5.5 %collective-permute-start.20 = (f32[128,512]{1,0:T(8,128)S(1)}, f32[128,512]{1,0:T(8,128)S(1)}, u32[]{:S(2)}, u32[]{:S(2)}) collective-permute-start(f32[128,512]{1,0:T(8,128)S(1)} %get-tuple-element.36), channel_id=1, source_target_pairs={{1,2},{2,1},{3,4},{4,3},{5,6},{6,5},{7,8},{8,7},{9,10},{10,9},{11,... | collective-permute-start | bytes 786440 | tf_op jit(solution)/shard_map/ppermute | solution.py:718
  63.8 0.1 collective-permute-start.16
  63.9 6.5 %collective-permute-done.16 = f32[13,8,128]{2,1,0:T(8,128)S(1)} collective-permute-done((f32[13,8,128]{2,1,0:T(8,128)S(1)}, f32[13,8,128]{2,1,0:T(8,128)S(1)}, u32[]{:S(2)}, u32[]{:S(2)}) %collective-permute-start.16) | collective-permute-done | bytes 53280 | tf_op jit(solution)/shard_map/ppermute | solution.py:697
  70.5 1.7 %collective-permute-start.18 = (f32[13,8,128]{2,1,0:T(8,128)S(1)}, f32[13,8,128]{2,1,0:T(8,128)S(1)}, u32[]{:S(2)}, u32[]{:S(2)}) collective-permute-start(f32[13,8,128]{2,1,0:T(8,128)S(1)} %add.54.mine), channel_id=1, source_target_pairs={{0,16},{16,0},{32,48},{48,32},{64,80},{80,64},{96,112},{112,96},{1... | collective-permute-start | bytes 159752 | tf_op jit(solution)/shard_map/ppermute | solution.py:686
  72.1 6.0 %collective-permute-start.17 = (f32[13,8,128]{2,1,0:T(8,128)S(1)}, f32[13,8,128]{2,1,0:T(8,128)S(1)}, u32[]{:S(2)}, u32[]{:S(2)}) collective-permute-start(f32[13,8,128]{2,1,0:T(8,128)S(1)} %add.54.mine), channel_id=1, source_target_pairs={{16,1},{1,16},{17,2},{2,17},{18,3},{3,18},{19,4},{4,19},{20,5},{5,... | collective-permute-start | bytes 159752 | tf_op jit(solution)/shard_map/ppermute | solution.py:728
  78.2 0.9 relax.1.old
  79.1 0.9 collective-permute-done.17.got
  80.0 0.0 collective-permute-start.21
  80.0 1.2 %collective-permute-done.21.swapped = f32[13,8,128]{2,1,0:T(8,128)S(1)} collective-permute-done((f32[13,8,128]{2,1,0:T(8,128)S(1)}, f32[13,8,128]{2,1,0:T(8,128)S(1)}, u32[]{:S(2)}, u32[]{:S(2)}) %collective-permute-start.21) | collective-permute-done | bytes 53280 | tf_op jit(solution)/shard_map/ppermute | solution.py:686
  81.2 2.0 %move_third.1 = (f32[256,3072]{1,0:T(8,128)S(1)}, f32[256,2048]{1,0:T(8,128)S(1)}, f32[13,8,128]{2,1,0:T(8,128)S(1)}, f32[13,8,128]{2,1,0:T(8,128)S(1)}) custom-call(f32[256,3072]{1,0:T(8,128)S(1)} %relax.1.old, f32[128,512]{1,0:T(8,128)S(1)} %collective-permute-done.19.pair_a, ...), custom_call_target="tpu_custom_call", output_to_operand_aliasing={{0}: (0, {})} | custom-call | tf_op jit(solution)/shard_map/move_third/pallas_call | solution.py:616
  83.2 0.2 collective-permute-start.22
  83.4 1.1 %collective-permute-done.22 = f32[13,8,128]{2,1,0:T(8,128)S(1)} collective-permute-done((f32[13,8,128]{2,1,0:T(8,128)S(1)}, f32[13,8,128]{2,1,0:T(8,128)S(1)}, u32[]{:S(2)}, u32[]{:S(2)}) %collective-permute-start.22) | collective-permute-done | bytes 53280 | tf_op jit(solution)/shard_map/ppermute | solution.py:686
  84.5 1.3 %collective-permute-start.25 = (f32[13,8,128]{2,1,0:T(8,128)S(1)}, f32[13,8,128]{2,1,0:T(8,128)S(1)}, u32[]{:S(2)}, u32[]{:S(2)}) collective-permute-start(f32[13,8,128]{2,1,0:T(8,128)S(1)} %add.55), channel_id=1, source_target_pairs={{0,96},{16,112},{32,64},{48,80},{64,32},{80,48},{96,0},{112,16},{1... | collective-permute-start | bytes 159752 | tf_op jit(solution)/shard_map/ppermute | solution.py:693
  85.8 2.7 %collective-permute-start.24 = (f32[13,8,128]{2,1,0:T(8,128)S(1)}, f32[13,8,128]{2,1,0:T(8,128)S(1)}, u32[]{:S(2)}, u32[]{:S(2)}) collective-permute-start(f32[13,8,128]{2,1,0:T(8,128)S(1)} %add.55), channel_id=1, source_target_pairs={{0,32},{16,48},{32,0},{48,16},{64,96},{80,112},{96,64},{112,80},{1... | collective-permute-start | bytes 159752 | tf_op jit(solution)/shard_map/ppermute | solution.py:693
  88.5 1.5 %collective-permute-done.24 = f32[13,8,128]{2,1,0:T(8,128)S(1)} collective-permute-done((f32[13,8,128]{2,1,0:T(8,128)S(1)}, f32[13,8,128]{2,1,0:T(8,128)S(1)}, u32[]{:S(2)}, u32[]{:S(2)}) %collective-permute-start.24) | collective-permute-done | bytes 53280 | tf_op jit(solution)/shard_map/ppermute | solution.py:693
  90.0 3.0 %collective-permute-done.23 = f32[13,8,128]{2,1,0:T(8,128)S(1)} collective-permute-done((f32[13,8,128]{2,1,0:T(8,128)S(1)}, f32[13,8,128]{2,1,0:T(8,128)S(1)}, u32[]{:S(2)}, u32[]{:S(2)}) %collective-permute-start.23) | collective-permute-done | bytes 53280 | tf_op jit(solution)/shard_map/ppermute | solution.py:693
  93.0 3.0 %collective-permute-start.26 = (f32[13,8,128]{2,1,0:T(8,128)S(1)}, f32[13,8,128]{2,1,0:T(8,128)S(1)}, u32[]{:S(2)}, u32[]{:S(2)}) collective-permute-start(f32[13,8,128]{2,1,0:T(8,128)S(1)} %add_add_fusion.1), channel_id=1, source_target_pairs={{0,128},{16,144},{32,160},{48,176},{64,192},{80,208},{96,224},{112... | collective-permute-start | bytes 159752 | tf_op jit(solution)/shard_map/ppermute | solution.py:697
  96.0 1.5 %collective-permute-done.26 = f32[13,8,128]{2,1,0:T(8,128)S(1)} collective-permute-done((f32[13,8,128]{2,1,0:T(8,128)S(1)}, f32[13,8,128]{2,1,0:T(8,128)S(1)}, u32[]{:S(2)}, u32[]{:S(2)}) %collective-permute-start.26) | collective-permute-done | bytes 53280 | tf_op jit(solution)/shard_map/ppermute | solution.py:697
  97.6 3.1 %collective-permute-start.27 = (f32[13,8,128]{2,1,0:T(8,128)S(1)}, f32[13,8,128]{2,1,0:T(8,128)S(1)}, u32[]{:S(2)}, u32[]{:S(2)}) collective-permute-start(f32[13,8,128]{2,1,0:T(8,128)S(1)} %add.59.mine), channel_id=1, source_target_pairs={{0,16},{16,0},{32,48},{48,32},{64,80},{80,64},{96,112},{112,96},{1... | collective-permute-start | bytes 159752 | tf_op jit(solution)/shard_map/ppermute | solution.py:686
  100.7 0.9 collective-permute-done.27.other
  101.6 1.8 %relax_last.1 = f32[256,2048]{1,0:T(8,128)} custom-call(f32[256,2048]{1,0:T(8,128)S(1)} %get-tuple-element.38.moved, f32[13,8,128]{2,1,0:T(8,128)S(1)} %add.59.mine, f32[13,8,128]{2,1,0:T(8,128)S(1)} %collective-permute-done.27.other), custom_call_target="tpu_custom_call" | custom-call | tf_op jit(solution)/shard_map/relax_last/pallas_call | solution.py:669
  (35 shorter events, 0.2 us)
Async XLA Ops:
  0.0 1.6 %copy-start = (f32[256,2048]{1,0:T(8,128)S(1)}, f32[256,2048]{1,0:T(8,128)}, u32[]{:S(2)}) copy-start(f32[256,2048]{1,0:T(8,128)} %dist.3) | copy-start | bytes 6291460
  1.6 0.9 copy-start.1
  2.5 0.7 copy-start.2
  3.2 0.7 copy-start.4
  3.9 46.0 %copy-start.3 = (s32[2,512]{1,0:T(2,128)S(1)}, s32[2,512]{1,0:T(2,128)}, u32[]{:S(2)}) copy-start(s32[2,512]{1,0:T(2,128)} %kind.5) | copy-start | bytes 12292
  3.9 46.0 %copy-start.5 = (f32[256]{0:T(256)S(1)}, f32[256]{0:T(256)}, u32[]{:S(2)}) copy-start(f32[256]{0:T(256)} %param.7) | copy-start | bytes 3076
  6.5 1.7 %collective-permute-start = (f32[20,8,128]{2,1,0:T(8,128)S(1)}, f32[20,8,128]{2,1,0:T(8,128)S(1)}, u32[]{:S(2)}, u32[]{:S(2)}) collective-permute-start(f32[20,8,128]{2,1,0:T(8,128)S(1)} %get-tuple-element.25), channel_id=1, source_target_pairs={{0,16},{16,0},{32,48},{48,32},{64,80},{80,64},{96,112},{112,96},{1... | collective-permute-start | bytes 245768 | tf_op jit(solution)/shard_map/ppermute | solution.py:686
  8.2 9.9 %collective-permute-start.3 = (f32[20,8,128]{2,1,0:T(8,128)S(1)}, f32[20,8,128]{2,1,0:T(8,128)S(1)}, u32[]{:S(2)}, u32[]{:S(2)}) collective-permute-start(f32[20,8,128]{2,1,0:T(8,128)S(1)} %add.45), channel_id=1, source_target_pairs={{0,96},{16,112},{32,64},{48,80},{64,32},{80,48},{96,0},{112,16},{1... | collective-permute-start | bytes 245768 | tf_op jit(solution)/shard_map/ppermute | solution.py:693
  9.5 8.7 %collective-permute-start.2 = (f32[20,8,128]{2,1,0:T(8,128)S(1)}, f32[20,8,128]{2,1,0:T(8,128)S(1)}, u32[]{:S(2)}, u32[]{:S(2)}) collective-permute-start(f32[20,8,128]{2,1,0:T(8,128)S(1)} %add.45), channel_id=1, source_target_pairs={{0,32},{16,48},{32,0},{48,16},{64,96},{80,112},{96,64},{112,80},{1... | collective-permute-start | bytes 245768 | tf_op jit(solution)/shard_map/ppermute | solution.py:693
  11.0 11.0 %collective-permute-start.1 = (f32[20,8,128]{2,1,0:T(8,128)S(1)}, f32[20,8,128]{2,1,0:T(8,128)S(1)}, u32[]{:S(2)}, u32[]{:S(2)}) collective-permute-start(f32[20,8,128]{2,1,0:T(8,128)S(1)} %add.45), channel_id=1, source_target_pairs={{0,64},{16,80},{32,96},{48,112},{64,0},{80,16},{96,32},{112,48},{1... | collective-permute-start | bytes 245768 | tf_op jit(solution)/shard_map/ppermute | solution.py:693
  12.1 34.4 %collective-permute-start.10 = (f32[128,512]{1,0:T(8,128)S(1)}, f32[128,512]{1,0:T(8,128)S(1)}, u32[]{:S(2)}, u32[]{:S(2)}) collective-permute-start(f32[128,512]{1,0:T(8,128)S(1)} %get-tuple-element.29), channel_id=1, source_target_pairs={{0,1},{1,0},{2,3},{3,2},{4,5},{5,4},{6,7},{7,6},{8,9},{9,8},{10,11... | collective-permute-start | bytes 786440 | tf_op jit(solution)/shard_map/ppermute | solution.py:717
  12.3 36.3 %collective-permute-start.11 = (f32[128,512]{1,0:T(8,128)S(1)}, f32[128,512]{1,0:T(8,128)S(1)}, u32[]{:S(2)}, u32[]{:S(2)}) collective-permute-start(f32[128,512]{1,0:T(8,128)S(1)} %get-tuple-element.30), channel_id=1, source_target_pairs={{1,2},{2,1},{3,4},{4,3},{5,6},{6,5},{7,8},{8,7},{9,10},{10,9},{11,... | collective-permute-start | bytes 786440 | tf_op jit(solution)/shard_map/ppermute | solution.py:718
  18.1 30.5 %collective-permute-start.8 = (f32[128,512]{1,0:T(8,128)S(1)}, f32[128,512]{1,0:T(8,128)S(1)}, u32[]{:S(2)}, u32[]{:S(2)}) collective-permute-start(f32[128,512]{1,0:T(8,128)S(1)} %get-tuple-element.27), channel_id=1, source_target_pairs={{0,1},{1,0},{2,3},{3,2},{4,5},{5,4},{6,7},{7,6},{8,9},{9,8},{10,11... | collective-permute-start | bytes 786440 | tf_op jit(solution)/shard_map/ppermute | solution.py:717
  18.2 30.4 %collective-permute-start.9 = (f32[128,512]{1,0:T(8,128)S(1)}, f32[128,512]{1,0:T(8,128)S(1)}, u32[]{:S(2)}, u32[]{:S(2)}) collective-permute-start(f32[128,512]{1,0:T(8,128)S(1)} %get-tuple-element.28), channel_id=1, source_target_pairs={{1,2},{2,1},{3,4},{4,3},{5,6},{6,5},{7,8},{8,7},{9,10},{10,9},{11,... | collective-permute-start | bytes 786440 | tf_op jit(solution)/shard_map/ppermute | solution.py:718
  22.1 16.2 %collective-permute-start.4 = (f32[20,8,128]{2,1,0:T(8,128)S(1)}, f32[20,8,128]{2,1,0:T(8,128)S(1)}, u32[]{:S(2)}, u32[]{:S(2)}) collective-permute-start(f32[20,8,128]{2,1,0:T(8,128)S(1)} %add_add_fusion), channel_id=1, source_target_pairs={{0,128},{16,144},{32,160},{48,176},{64,192},{80,208},{96,224},{112... | collective-permute-start | bytes 245768 | tf_op jit(solution)/shard_map/ppermute | solution.py:697
  38.2 10.4 %collective-permute-start.6 = (f32[20,8,128]{2,1,0:T(8,128)S(1)}, f32[20,8,128]{2,1,0:T(8,128)S(1)}, u32[]{:S(2)}, u32[]{:S(2)}) collective-permute-start(f32[20,8,128]{2,1,0:T(8,128)S(1)} %add.49.mine_in), channel_id=1, source_target_pairs={{16,1},{1,16},{17,2},{2,17},{18,3},{3,18},{19,4},{4,19},{20,5},{5,... | collective-permute-start | bytes 245768 | tf_op jit(solution)/shard_map/ppermute | solution.py:728
  46.5 2.1 %collective-permute-start.5 = (f32[20,8,128]{2,1,0:T(8,128)S(1)}, f32[20,8,128]{2,1,0:T(8,128)S(1)}, u32[]{:S(2)}, u32[]{:S(2)}) collective-permute-start(f32[20,8,128]{2,1,0:T(8,128)S(1)} %add.49.mine_in), channel_id=1, source_target_pairs={{0,16},{16,0},{32,48},{48,32},{64,80},{80,64},{96,112},{112,96},{1... | collective-permute-start | bytes 245768 | tf_op jit(solution)/shard_map/ppermute | solution.py:686
  48.6 1.3 %collective-permute-start.7 = (f32[20,8,128]{2,1,0:T(8,128)S(1)}, f32[20,8,128]{2,1,0:T(8,128)S(1)}, u32[]{:S(2)}, u32[]{:S(2)}) collective-permute-start(f32[20,8,128]{2,1,0:T(8,128)S(1)} %collective-permute-done.6.got), channel_id=1, source_target_pairs={{0,16},{16,0},{32,48},{48,32},{64,80},{80,64},{96,112},{112,96},{1... | collective-permute-start | bytes 245768 | tf_op jit(solution)/shard_map/ppermute | solution.py:686
  53.0 1.3 %collective-permute-start.12 = (f32[13,8,128]{2,1,0:T(8,128)S(1)}, f32[13,8,128]{2,1,0:T(8,128)S(1)}, u32[]{:S(2)}, u32[]{:S(2)}) collective-permute-start(f32[13,8,128]{2,1,0:T(8,128)S(1)} %get-tuple-element.32), channel_id=1, source_target_pairs={{0,16},{16,0},{32,48},{48,32},{64,80},{80,64},{96,112},{112,96},{1... | collective-permute-start | bytes 159752 | tf_op jit(solution)/shard_map/ppermute | solution.py:686
  54.3 9.5 %collective-permute-start.15 = (f32[13,8,128]{2,1,0:T(8,128)S(1)}, f32[13,8,128]{2,1,0:T(8,128)S(1)}, u32[]{:S(2)}, u32[]{:S(2)}) collective-permute-start(f32[13,8,128]{2,1,0:T(8,128)S(1)} %add.50), channel_id=1, source_target_pairs={{0,96},{16,112},{32,64},{48,80},{64,32},{80,48},{96,0},{112,16},{1... | collective-permute-start | bytes 159752 | tf_op jit(solution)/shard_map/ppermute | solution.py:693
  55.6 8.2 %collective-permute-start.14 = (f32[13,8,128]{2,1,0:T(8,128)S(1)}, f32[13,8,128]{2,1,0:T(8,128)S(1)}, u32[]{:S(2)}, u32[]{:S(2)}) collective-permute-start(f32[13,8,128]{2,1,0:T(8,128)S(1)} %add.50), channel_id=1, source_target_pairs={{0,32},{16,48},{32,0},{48,16},{64,96},{80,112},{96,64},{112,80},{1... | collective-permute-start | bytes 159752 | tf_op jit(solution)/shard_map/ppermute | solution.py:693
  58.3 5.5 %collective-permute-start.13 = (f32[13,8,128]{2,1,0:T(8,128)S(1)}, f32[13,8,128]{2,1,0:T(8,128)S(1)}, u32[]{:S(2)}, u32[]{:S(2)}) collective-permute-start(f32[13,8,128]{2,1,0:T(8,128)S(1)} %add.50), channel_id=1, source_target_pairs={{0,64},{16,80},{32,96},{48,112},{64,0},{80,16},{96,32},{112,48},{1... | collective-permute-start | bytes 159752 | tf_op jit(solution)/shard_map/ppermute | solution.py:693
  58.3 21.7 %collective-permute-start.19 = (f32[128,512]{1,0:T(8,128)S(1)}, f32[128,512]{1,0:T(8,128)S(1)}, u32[]{:S(2)}, u32[]{:S(2)}) collective-permute-start(f32[128,512]{1,0:T(8,128)S(1)} %get-tuple-element.35), channel_id=1, source_target_pairs={{0,1},{1,0},{2,3},{3,2},{4,5},{5,4},{6,7},{7,6},{8,9},{9,8},{10,11... | collective-permute-start | bytes 786440 | tf_op jit(solution)/shard_map/ppermute | solution.py:717
  58.3 21.7 %collective-permute-start.20 = (f32[128,512]{1,0:T(8,128)S(1)}, f32[128,512]{1,0:T(8,128)S(1)}, u32[]{:S(2)}, u32[]{:S(2)}) collective-permute-start(f32[128,512]{1,0:T(8,128)S(1)} %get-tuple-element.36), channel_id=1, source_target_pairs={{1,2},{2,1},{3,4},{4,3},{5,6},{6,5},{7,8},{8,7},{9,10},{10,9},{11,... | collective-permute-start | bytes 786440 | tf_op jit(solution)/shard_map/ppermute | solution.py:718
  63.8 6.6 %collective-permute-start.16 = (f32[13,8,128]{2,1,0:T(8,128)S(1)}, f32[13,8,128]{2,1,0:T(8,128)S(1)}, u32[]{:S(2)}, u32[]{:S(2)}) collective-permute-start(f32[13,8,128]{2,1,0:T(8,128)S(1)} %add_add_fusion.2), channel_id=1, source_target_pairs={{0,128},{16,144},{32,160},{48,176},{64,192},{80,208},{96,224},{112... | collective-permute-start | bytes 159752 | tf_op jit(solution)/shard_map/ppermute | solution.py:697
  70.5 7.7 %collective-permute-start.18 = (f32[13,8,128]{2,1,0:T(8,128)S(1)}, f32[13,8,128]{2,1,0:T(8,128)S(1)}, u32[]{:S(2)}, u32[]{:S(2)}) collective-permute-start(f32[13,8,128]{2,1,0:T(8,128)S(1)} %add.54.mine), channel_id=1, source_target_pairs={{0,16},{16,0},{32,48},{48,32},{64,80},{80,64},{96,112},{112,96},{1... | collective-permute-start | bytes 159752 | tf_op jit(solution)/shard_map/ppermute | solution.py:686
  72.1 7.8 %collective-permute-start.17 = (f32[13,8,128]{2,1,0:T(8,128)S(1)}, f32[13,8,128]{2,1,0:T(8,128)S(1)}, u32[]{:S(2)}, u32[]{:S(2)}) collective-permute-start(f32[13,8,128]{2,1,0:T(8,128)S(1)} %add.54.mine), channel_id=1, source_target_pairs={{16,1},{1,16},{17,2},{2,17},{18,3},{3,18},{19,4},{4,19},{20,5},{5,... | collective-permute-start | bytes 159752 | tf_op jit(solution)/shard_map/ppermute | solution.py:728
  80.0 1.2 %collective-permute-start.21 = (f32[13,8,128]{2,1,0:T(8,128)S(1)}, f32[13,8,128]{2,1,0:T(8,128)S(1)}, u32[]{:S(2)}, u32[]{:S(2)}) collective-permute-start(f32[13,8,128]{2,1,0:T(8,128)S(1)} %collective-permute-done.17.got), channel_id=1, source_target_pairs={{0,16},{16,0},{32,48},{48,32},{64,80},{80,64},{96,112},{112,96},{1... | collective-permute-start | bytes 159752 | tf_op jit(solution)/shard_map/ppermute | solution.py:686
  83.2 1.3 %collective-permute-start.22 = (f32[13,8,128]{2,1,0:T(8,128)S(1)}, f32[13,8,128]{2,1,0:T(8,128)S(1)}, u32[]{:S(2)}, u32[]{:S(2)}) collective-permute-start(f32[13,8,128]{2,1,0:T(8,128)S(1)} %get-tuple-element.40), channel_id=1, source_target_pairs={{0,16},{16,0},{32,48},{48,32},{64,80},{80,64},{96,112},{112,96},{1... | collective-permute-start | bytes 159752 | tf_op jit(solution)/shard_map/ppermute | solution.py:686
  84.5 3.9 %collective-permute-start.25 = (f32[13,8,128]{2,1,0:T(8,128)S(1)}, f32[13,8,128]{2,1,0:T(8,128)S(1)}, u32[]{:S(2)}, u32[]{:S(2)}) collective-permute-start(f32[13,8,128]{2,1,0:T(8,128)S(1)} %add.55), channel_id=1, source_target_pairs={{0,96},{16,112},{32,64},{48,80},{64,32},{80,48},{96,0},{112,16},{1... | collective-permute-start | bytes 159752 | tf_op jit(solution)/shard_map/ppermute | solution.py:693
  85.8 4.2 %collective-permute-start.24 = (f32[13,8,128]{2,1,0:T(8,128)S(1)}, f32[13,8,128]{2,1,0:T(8,128)S(1)}, u32[]{:S(2)}, u32[]{:S(2)}) collective-permute-start(f32[13,8,128]{2,1,0:T(8,128)S(1)} %add.55), channel_id=1, source_target_pairs={{0,32},{16,48},{32,0},{48,16},{64,96},{80,112},{96,64},{112,80},{1... | collective-permute-start | bytes 159752 | tf_op jit(solution)/shard_map/ppermute | solution.py:693
  88.5 4.5 %collective-permute-start.23 = (f32[13,8,128]{2,1,0:T(8,128)S(1)}, f32[13,8,128]{2,1,0:T(8,128)S(1)}, u32[]{:S(2)}, u32[]{:S(2)}) collective-permute-start(f32[13,8,128]{2,1,0:T(8,128)S(1)} %add.55), channel_id=1, source_target_pairs={{0,64},{16,80},{32,96},{48,112},{64,0},{80,16},{96,32},{112,48},{1... | collective-permute-start | bytes 159752 | tf_op jit(solution)/shard_map/ppermute | solution.py:693
  93.0 4.6 %collective-permute-start.26 = (f32[13,8,128]{2,1,0:T(8,128)S(1)}, f32[13,8,128]{2,1,0:T(8,128)S(1)}, u32[]{:S(2)}, u32[]{:S(2)}) collective-permute-start(f32[13,8,128]{2,1,0:T(8,128)S(1)} %add_add_fusion.1), channel_id=1, source_target_pairs={{0,128},{16,144},{32,160},{48,176},{64,192},{80,208},{96,224},{112... | collective-permute-start | bytes 159752 | tf_op jit(solution)/shard_map/ppermute | solution.py:697
  97.6 4.0 %collective-permute-start.27 = (f32[13,8,128]{2,1,0:T(8,128)S(1)}, f32[13,8,128]{2,1,0:T(8,128)S(1)}, u32[]{:S(2)}, u32[]{:S(2)}) collective-permute-start(f32[13,8,128]{2,1,0:T(8,128)S(1)} %add.59.mine), channel_id=1, source_target_pairs={{0,16},{16,0},{32,48},{48,32},{64,80},{80,64},{96,112},{112,96},{1... | collective-permute-start | bytes 159752 | tf_op jit(solution)/shard_map/ppermute | solution.py:686
